TPU v7x, 32 devices: a whole 2x2x4 slice. The times are simulated.
32 devices in a mesh: fsdp: 4 (over y, x), tp: 8 (over z, core).
Axes of the slice: x: 2, y: 2, z: 4, core: 2. Of those that a mesh axis runs over, the one named last changes fastest.
Arguments:
- activations: float32 [8192, 2048], P(('fsdp', 'tp')), may hold values from -6 to 6
- gain_attn: float32 [2048], replicated, may hold values from 0.1 to 1.9
- w_query: bfloat16 [2048, 2048], P('fsdp', 'tp'), may hold values from -0.1875 to 0.1875
- w_key: bfloat16 [2048, 2048], P('fsdp', 'tp'), may hold values from -0.1875 to 0.1875
- w_value: bfloat16 [2048, 2048], P('fsdp', 'tp'), may hold values from -0.125 to 0.125
- w_out: bfloat16 [2048, 2048], P('tp', 'fsdp'), may hold values from -0.25 to 0.25
- gain_mlp: float32 [2048], replicated, may hold values from 0.1 to 1.9
- w_gate: bfloat16 [2048, 8192], P('fsdp', 'tp'), may hold values from -0.125 to 0.125
- w_up: bfloat16 [2048, 8192], P('fsdp', 'tp'), may hold values from -0.125 to 0.125
- w_down: bfloat16 [8192, 2048], P('tp', 'fsdp'), may hold values from -0.0625 to 0.0625
- cotangent: float32 [8192, 2048], P(('fsdp', 'tp')), may hold values from -6 to 6
Outputs:
- output: float32 [8192, 2048], P(('fsdp', 'tp'))
- input_grad: float32 [8192, 2048], P(('fsdp', 'tp'))
- grad_gain_attn: float32 [2048], replicated
- grad_query: float32 [2048, 2048], P('fsdp', 'tp')
- grad_key: float32 [2048, 2048], P('fsdp', 'tp')
- grad_value: float32 [2048, 2048], P('fsdp', 'tp')
- grad_out: float32 [2048, 2048], P('tp', 'fsdp')
- grad_gain_mlp: float32 [2048], replicated
- grad_gate: float32 [2048, 8192], P('fsdp', 'tp')
- grad_up: float32 [2048, 8192], P('fsdp', 'tp')
- grad_down: float32 [8192, 2048], P('tp', 'fsdp')
All inputs are finite; a program needn't handle non-finite values.
Results may differ from a plain program's by a relative error of at most 0.019.
Values may be sent and summed in bfloat16 or wider, within the bound.
A program may use at most 320 MiB of HBM per device.

v0:
```python
import jax
import jax.numpy as jnp
from jax import lax
from jax.sharding import PartitionSpec as P

HEAD_DIM = 64
SEQ_LEN = 2048
BLOCK = 512


rope_base = 130000.0
norm_eps = 1e-05
masked_score = -1e30


def rms_norm(values, gain):
    return values * lax.rsqrt(jnp.mean(values * values, axis=-1, keepdims=True) + norm_eps) * gain


def contract_rows(left, right):
    return lax.dot_general(
        left, right, (((0,), (0,)), ((), ())), preferred_element_type=jnp.float32
    )


def contract_cols(left, right):
    return lax.dot_general(
        left, right, (((1,), (1,)), ((), ())), preferred_element_type=jnp.float32
    )


def rope_tables(count, width):
    half = HEAD_DIM // 2
    positions = (jnp.arange(count, dtype=jnp.int32) % SEQ_LEN).astype(jnp.float32)
    column = jnp.arange(width, dtype=jnp.int32) % HEAD_DIM % half
    inverse = jnp.power(jnp.float32(rope_base), -2.0 * column.astype(jnp.float32) / HEAD_DIM)
    angle = positions[:, None] * inverse[None, :]
    return (jnp.cos(angle), jnp.sin(angle))


def rotation(width):
    half = HEAD_DIM // 2
    source = jnp.arange(width, dtype=jnp.int32)[:, None]
    target = jnp.arange(width, dtype=jnp.int32)[None, :]
    within = target % HEAD_DIM
    lower = jnp.logical_and(within < half, source == target + half)
    upper = jnp.logical_and(within >= half, source == target - half)
    return jnp.where(lower, -1.0, 0.0).astype(jnp.float32) + jnp.where(upper, 1.0, 0.0).astype(
        jnp.float32
    )


def rotate(values, cosine, sine, turn):
    return values * cosine + jnp.dot(values, turn, precision=lax.Precision.HIGHEST) * sine


def unrotate(grads, cosine, sine, turn):
    turned = lax.dot_general(
        grads * sine, turn, (((1,), (1,)), ((), ())), precision=lax.Precision.HIGHEST
    )
    return grads * cosine + turned


def split_heads(block):
    return block.reshape(block.shape[0], block.shape[1] // HEAD_DIM, HEAD_DIM)


def block_scores(query_block, key_seq, offset):
    raw = jnp.einsum(
        "bhd,lhd->hbl",
        split_heads(query_block),
        split_heads(key_seq),
        preferred_element_type=jnp.float32,
    )
    raw = raw * HEAD_DIM ** (-0.5)
    query_pos = offset + jnp.arange(query_block.shape[0], dtype=jnp.int32)
    key_pos = jnp.arange(key_seq.shape[0], dtype=jnp.int32)
    return jnp.where(key_pos[None, None, :] <= query_pos[None, :, None], raw, masked_score)


def body(
    activations,
    gain_attn,
    w_query,
    w_key,
    w_value,
    w_out,
    gain_mlp,
    w_gate,
    w_up,
    w_down,
    cotangent,
):
    full_query, full_key, full_value, out_part, full_gate, full_up, down_rows = (
        lax.all_gather(w_query, "fsdp", axis=0, tiled=True),
        lax.all_gather(w_key, "fsdp", axis=0, tiled=True),
        lax.all_gather(w_value, "fsdp", axis=0, tiled=True),
        lax.all_gather(w_out, "fsdp", axis=1, tiled=True),
        lax.all_gather(w_gate, "fsdp", axis=0, tiled=True),
        lax.all_gather(w_up, "fsdp", axis=0, tiled=True),
        lax.all_gather(w_down, "fsdp", axis=1, tiled=True),
    )
    head_cols = full_query.shape[1]
    turn = rotation(head_cols)
    scale = HEAD_DIM ** (-0.5)
    normed_attn = rms_norm(activations, gain_attn).astype(jnp.bfloat16)
    piece = lax.all_gather(normed_attn, "tp", axis=0, tiled=True)
    cosine, sine = rope_tables(piece.shape[0], head_cols)
    query_rows = rotate(
        jnp.dot(piece, full_query, preferred_element_type=jnp.float32), cosine, sine, turn
    )
    key_rows = rotate(
        jnp.dot(piece, full_key, preferred_element_type=jnp.float32), cosine, sine, turn
    )
    value_rows = jnp.dot(piece, full_value, preferred_element_type=jnp.float32)
    query = query_rows.astype(jnp.bfloat16)
    keys = key_rows.astype(jnp.bfloat16)
    values = value_rows.astype(jnp.bfloat16)
    seen_attn = piece
    group_rows = query.shape[0]
    blocks = group_rows // BLOCK

    def block_inputs(index):
        start = index * BLOCK
        seq_start = start // SEQ_LEN * SEQ_LEN
        query_block = lax.dynamic_slice_in_dim(query, start, BLOCK, 0)
        key_seq = lax.dynamic_slice_in_dim(keys, seq_start, SEQ_LEN, 0)
        value_seq = lax.dynamic_slice_in_dim(values, seq_start, SEQ_LEN, 0)
        return (start, seq_start, query_block, key_seq, value_seq)

    def forward_block(index):
        start, seq_start, query_block, key_seq, value_seq = block_inputs(index)
        scores = block_scores(query_block, key_seq, start - seq_start)
        top = jnp.max(scores, axis=-1, keepdims=True)
        weights = jnp.exp(scores - top)
        total = jnp.sum(weights, axis=-1, keepdims=True)
        probs = (weights / total).astype(jnp.bfloat16)
        mixed_block = jnp.einsum(
            "hbl,lhd->bhd", probs, split_heads(value_seq), preferred_element_type=jnp.float32
        )
        return (
            mixed_block.reshape(BLOCK, head_cols).astype(jnp.bfloat16),
            (top + jnp.log(total))[..., 0],
        )

    mixed_blocks, log_totals = lax.map(forward_block, jnp.arange(blocks, dtype=jnp.int32))
    mixed = mixed_blocks.reshape(group_rows, head_cols)
    attn_branch = lax.psum_scatter(
        jnp.dot(mixed, out_part, preferred_element_type=jnp.float32),
        "tp",
        scatter_dimension=0,
        tiled=True,
    )
    hidden_state = activations + attn_branch
    normed_mlp = rms_norm(hidden_state, gain_mlp).astype(jnp.bfloat16)
    piece = lax.all_gather(normed_mlp, "tp", axis=0, tiled=True)
    gate_rows = jnp.dot(piece, full_gate, preferred_element_type=jnp.float32)
    up_rows = jnp.dot(piece, full_up, preferred_element_type=jnp.float32)
    gate = gate_rows
    up_value = up_rows
    seen_mlp = piece
    inner = (jax.nn.silu(gate) * up_value).astype(jnp.bfloat16)
    output = hidden_state + lax.psum_scatter(
        jnp.dot(inner, down_rows, preferred_element_type=jnp.float32).astype(jnp.bfloat16),
        "tp",
        scatter_dimension=0,
        tiled=True,
    ).astype(jnp.float32)
    piece = lax.all_gather(cotangent.astype(jnp.bfloat16), "tp", axis=0, tiled=True)
    inner_grad = contract_cols(piece, down_rows)
    seen_grad = piece
    grad_down = contract_rows(inner, seen_grad)
    _, pull_inner = jax.vjp(lambda gate_in, up_in: jax.nn.silu(gate_in) * up_in, gate, up_value)
    gate_grad, up_grad = pull_inner(inner_grad)
    gate_grad = gate_grad.astype(jnp.bfloat16)
    up_grad = up_grad.astype(jnp.bfloat16)
    grad_gate = contract_rows(seen_mlp, gate_grad)
    grad_up = contract_rows(seen_mlp, up_grad)
    gate_rows = gate_grad
    up_rows = up_grad
    normed_mlp_grad = lax.psum_scatter(
        contract_cols(gate_rows, full_gate) + contract_cols(up_rows, full_up),
        "tp",
        scatter_dimension=0,
        tiled=True,
    )
    _, pull_norm_mlp = jax.vjp(rms_norm, hidden_state, gain_mlp)
    hidden_norm_grad, gain_mlp_part = pull_norm_mlp(normed_mlp_grad)
    hidden_grad = cotangent + hidden_norm_grad
    branch_grad = hidden_grad.astype(jnp.bfloat16)
    piece = lax.all_gather(branch_grad, "tp", axis=0, tiled=True)
    mixed_grad = contract_cols(piece, out_part)
    grad_out = contract_rows(mixed, piece)
    mixed_grad = mixed_grad.astype(jnp.bfloat16)

    def backward_block(index, carry):
        query_grad, key_grad, value_grad = carry
        start, seq_start, query_block, key_seq, value_seq = block_inputs(index)
        scores = block_scores(query_block, key_seq, start - seq_start)
        probs = jnp.exp(scores - log_totals[index][..., None])
        out_grad = split_heads(lax.dynamic_slice_in_dim(mixed_grad, start, BLOCK, 0))
        prob_grad = jnp.einsum(
            "bhd,lhd->hbl", out_grad, split_heads(value_seq), preferred_element_type=jnp.float32
        )
        score_grad = probs * (prob_grad - jnp.sum(prob_grad * probs, axis=-1, keepdims=True))
        score_grad = score_grad.astype(jnp.bfloat16)
        block_query = (
            jnp.einsum(
                "hbl,lhd->bhd", score_grad, split_heads(key_seq), preferred_element_type=jnp.float32
            )
            * scale
        )
        block_key = (
            jnp.einsum(
                "hbl,bhd->lhd",
                score_grad,
                split_heads(query_block),
                preferred_element_type=jnp.float32,
            )
            * scale
        )
        block_value = jnp.einsum(
            "hbl,bhd->lhd", probs.astype(jnp.bfloat16), out_grad, preferred_element_type=jnp.float32
        )
        query_grad = lax.dynamic_update_slice_in_dim(
            query_grad, block_query.reshape(BLOCK, head_cols), start, 0
        )
        key_old = lax.dynamic_slice_in_dim(key_grad, seq_start, SEQ_LEN, 0)
        key_grad = lax.dynamic_update_slice_in_dim(
            key_grad, key_old + block_key.reshape(SEQ_LEN, head_cols), seq_start, 0
        )
        value_old = lax.dynamic_slice_in_dim(value_grad, seq_start, SEQ_LEN, 0)
        value_grad = lax.dynamic_update_slice_in_dim(
            value_grad, value_old + block_value.reshape(SEQ_LEN, head_cols), seq_start, 0
        )
        return (query_grad, key_grad, value_grad)

    empty = jnp.zeros((group_rows, head_cols), jnp.float32)
    query_grad, key_grad, value_grad = lax.fori_loop(
        0, blocks, backward_block, (empty, empty, empty)
    )
    cosine_all, sine_all = rope_tables(group_rows, head_cols)
    query_pre_grad = unrotate(query_grad, cosine_all, sine_all, turn).astype(jnp.bfloat16)
    key_pre_grad = unrotate(key_grad, cosine_all, sine_all, turn).astype(jnp.bfloat16)
    value_pre_grad = value_grad.astype(jnp.bfloat16)
    grad_query = contract_rows(seen_attn, query_pre_grad)
    grad_key = contract_rows(seen_attn, key_pre_grad)
    grad_value = contract_rows(seen_attn, value_pre_grad)
    query_rows = query_pre_grad
    key_rows = key_pre_grad
    value_rows = value_pre_grad
    normed_attn_grad = lax.psum_scatter(
        (
            contract_cols(query_rows, full_query)
            + contract_cols(key_rows, full_key)
            + contract_cols(value_rows, full_value)
        ).astype(jnp.bfloat16),
        "tp",
        scatter_dimension=0,
        tiled=True,
    ).astype(jnp.float32)
    _, pull_norm_attn = jax.vjp(rms_norm, activations, gain_attn)
    input_norm_grad, gain_attn_part = pull_norm_attn(normed_attn_grad)
    input_grad = hidden_grad + input_norm_grad
    summed = (
        lax.psum_scatter(
            grad_query.astype(jnp.bfloat16), "fsdp", scatter_dimension=0, tiled=True
        ).astype(jnp.float32),
        lax.psum_scatter(
            grad_key.astype(jnp.bfloat16), "fsdp", scatter_dimension=0, tiled=True
        ).astype(jnp.float32),
        lax.psum_scatter(
            grad_value.astype(jnp.bfloat16), "fsdp", scatter_dimension=0, tiled=True
        ).astype(jnp.float32),
        lax.psum_scatter(
            grad_out.astype(jnp.bfloat16), "fsdp", scatter_dimension=1, tiled=True
        ).astype(jnp.float32),
        lax.psum_scatter(
            grad_gate.astype(jnp.bfloat16), "fsdp", scatter_dimension=0, tiled=True
        ).astype(jnp.float32),
        lax.psum_scatter(
            grad_up.astype(jnp.bfloat16), "fsdp", scatter_dimension=0, tiled=True
        ).astype(jnp.float32),
        lax.psum_scatter(
            grad_down.astype(jnp.bfloat16), "fsdp", scatter_dimension=1, tiled=True
        ).astype(jnp.float32),
    )
    gain_sums = lax.psum((gain_attn_part, gain_mlp_part), ("fsdp", "tp"))
    return (
        output,
        input_grad,
        gain_sums[0],
        summed[0],
        summed[1],
        summed[2],
        summed[3],
        gain_sums[1],
        summed[4],
        summed[5],
        summed[6],
    )


def solution(mesh):
    in_specs = (
        P(("fsdp", "tp"), None),
        P(),
        P("fsdp", "tp"),
        P("fsdp", "tp"),
        P("fsdp", "tp"),
        P("tp", "fsdp"),
        P(),
        P("fsdp", "tp"),
        P("fsdp", "tp"),
        P("tp", "fsdp"),
        P(("fsdp", "tp"), None),
    )
    out_specs = (
        P(("fsdp", "tp"), None),
        P(("fsdp", "tp"), None),
        P(),
        P("fsdp", "tp"),
        P("fsdp", "tp"),
        P("fsdp", "tp"),
        P("tp", "fsdp"),
        P(),
        P("fsdp", "tp"),
        P("fsdp", "tp"),
        P("tp", "fsdp"),
    )
    return jax.shard_map(body, mesh=mesh, in_specs=in_specs, out_specs=out_specs, check_vma=False)
```

profile of v0, /device:TPU:0, one launch (start us, length us, event | category | flops | bytes accessed | tf_op | source)
XLA Modules:
  0.0 1654.9 jit_solution(3708394938445229087)
XLA Ops:
  15.9 23.4 %all-gather.18.cloned.1.call-done = bf16[2048,256]{1,0:T(8,128)(2,1)} async-done(((bf16[512,256]{1,0:T(8,128)(2,1)}), bf16[2048,256]{1,0:T(8,128)(2,1)}) %all-gather.18.cloned.1.call-update) | async-done | bytes 1048592 | tf_op jit(solution)/shard_map/all_gather | solution.py:97
  39.2 84.3 %all-gather.12.cloned.1.call-done = bf16[2048,2048]{1,0:T(8,128)(2,1)} async-done(((bf16[256,2048]{1,0:T(8,128)(2,1)}), bf16[2048,2048]{1,0:T(8,128)(2,1)}) %all-gather.12.cloned.1.call-update) | async-done | bytes 8388624 | tf_op jit(solution)/shard_map/all_gather | solution.py:107
  131.1 19.5 %all-gather.16.cloned.1.call-done = bf16[2048,256]{1,0:T(8,128)(2,1)} async-done(((bf16[512,256]{1,0:T(8,128)(2,1)}), bf16[2048,256]{1,0:T(8,128)(2,1)}) %all-gather.16.cloned.1.call-update) | async-done | bytes 1048592 | tf_op jit(solution)/shard_map/all_gather | solution.py:96
  167.1 11.8 all-gather.14.cloned.1.call-done
  196.2 69.2 %while.34 = (s32[]{:T(128)}, bf16[4,512,256]{2,1,0:T(8,128)(2,1)S(1)}, f32[4,4,512]{2,1,0:T(4,128)}, s32[4]{0:T(128)S(1)}, bf16[2048,256]{0,1:T(8,128)(2,1)}, /*...) while((s32[]{:T(128)}, ...), condition=%wide.region_4.5_spmd, body=%wide.region_1.4_spmd.sunk | while | flops 1125251584 | bytes 58790268 | solution.py:146
  276.4 167.6 %reduce-scatter.12.cloned.1.call-done = f32[256,2048]{1,0:T(8,128)} async-done(((f32[2048,2048]{1,0:T(8,128)}), f32[256,2048]{1,0:T(8,128)}) %reduce-scatter.12.cloned.1.call-update) | async-done | bytes 2097168 | tf_op jit(solution)/shard_map/reduce_scatter | solution.py:148
  451.0 45.9 %all-gather.26.cloned.1.call-done = bf16[2048,1024]{1,0:T(8,128)(2,1)} async-done(((bf16[512,1024]{1,0:T(8,128)(2,1)}), bf16[2048,1024]{1,0:T(8,128)(2,1)}) %all-gather.26.cloned.1.call-update) | async-done | bytes 4194320 | tf_op jit(solution)/shard_map/all_gather | solution.py:100
  496.9 84.3 %all-gather.22.cloned.1.call-done = bf16[2048,2048]{1,0:T(8,128)(2,1)} async-done(((bf16[256,2048]{1,0:T(8,128)(2,1)}), bf16[2048,2048]{1,0:T(8,128)(2,1)}) %all-gather.22.cloned.1.call-update) | async-done | bytes 8388624 | tf_op jit(solution)/shard_map/all_gather | solution.py:156
  581.2 14.5 fusion.111
  595.7 38.6 %all-gather.24.cloned.1.call-done = bf16[2048,1024]{1,0:T(8,128)(2,1)} async-done(((bf16[512,1024]{1,0:T(8,128)(2,1)}), bf16[2048,1024]{1,0:T(8,128)(2,1)}) %all-gather.24.cloned.1.call-update) | async-done | bytes 4194320 | tf_op jit(solution)/shard_map/all_gather | solution.py:99
  634.3 14.5 fusion.110
  648.8 39.8 %all-gather.28.cloned.1.call-done = bf16[1024,2048]{1,0:T(8,128)(2,1)} async-done(((bf16[1024,512]{1,0:T(8,128)(2,1)}), bf16[1024,2048]{1,0:T(8,128)(2,1)}) %all-gather.28.cloned.1.call-update) | async-done | bytes 4194320 | tf_op jit(solution)/shard_map/all_gather | solution.py:101
  688.6 84.3 %all-gather.30.cloned.1.call-done = bf16[2048,2048]{1,0:T(8,128)(2,1)} async-done(((bf16[256,2048]{1,0:T(8,128)(2,1)}), bf16[2048,2048]{1,0:T(8,128)(2,1)}) %all-gather.30.cloned.1.call-update) | async-done | bytes 8388624 | tf_op jit(solution)/shard_map/all_gather | solution.py:169
  772.9 23.4 %multiply_convert_fusion.1 = (bf16[2048,1024]{1,0:T(8,128)(2,1)}, bf16[2048,1024]{1,0:T(8,128)(2,1)}, bf16[2048,1024]{1,0:T(8,128)(2,1)}) fusion(f32[2048,1024]{1,0:T(8,128)} %fusion.110, f32[2048,1024]{1,0:T(8,128)} %fusion.111, bf16[2048,2048]{1,0:T(8,128)(2,1)} %all-gather.30.cloned.1.call-done, bf16[1024,2048]{1,0:T(8,128)(2,1)} %all-gather.28.cloned.1.call-done), kind=kOutput, calls=%fused_computation.37 | convolution fusion | flops 8623489024 | bytes 41943040 | tf_op jit(solution)/shard_map/dot_general | solution.py:27
  796.2 15.5 fusion.112
  811.7 17.3 %convolution_add_fusion = f32[2048,2048]{1,0:T(8,128)} fusion(f32[2048,2048]{1,0:T(8,128)} %fusion.112, bf16[2048,1024]{1,0:T(8,128)(2,1)S(1)} %copy-done.47, bf16[2048,1024]{1,0:T(8,128)(2,1)S(1)} %copy-done.40), kind=kOutput, calls=%fused_computation.42 | convolution fusion | flops 8594128896 | bytes 41943040 | tf_op jit(solution)/shard_map/dot_general | solution.py:27
  829.1 14.0 convolution_convert_fusion
  843.1 152.8 %reduce-scatter.16.cloned.1.call-done = f32[256,2048]{1,0:T(8,128)} async-done(((f32[2048,2048]{1,0:T(8,128)}), f32[256,2048]{1,0:T(8,128)}) %reduce-scatter.16.cloned.1.call-update) | async-done | bytes 2097168 | tf_op jit(solution)/shard_map/reduce_scatter | solution.py:181
  998.7 87.6 %reduce-scatter.14.cloned.1.call-done = bf16[256,2048]{1,0:T(8,128)(2,1)} async-done(((bf16[2048,2048]{1,0:T(8,128)(2,1)}), bf16[256,2048]{1,0:T(8,128)(2,1)}) %reduce-scatter.14.cloned.1.call-update) | async-done | bytes 1048592 | tf_op jit(solution)/shard_map/reduce_scatter | solution.py:163
  1091.8 14.5 convolution_convert_fusion.1
  1106.4 14.0 convolution_convert_fusion.2
  1120.5 14.3 convolution_convert_fusion.3
  1134.9 37.4 %all-gather.32.cloned.1.call-done = bf16[2048,2048]{1,0:T(8,128)(2,1)} async-done(((bf16[256,2048]{1,0:T(8,128)(2,1)}), bf16[2048,2048]{1,0:T(8,128)(2,1)}) %all-gather.32.cloned.1.call-update) | async-done | bytes 8388624 | tf_op jit(solution)/shard_map/all_gather | solution.py:191
  1188.2 209.2 %while.35 = (s32[]{:T(128)}, f32[2048,256]{1,0:T(8,128)}, f32[2048,256]{0,1:T(8,128)}, f32[2048,256]{0,1:T(8,128)}, bf16[2048,256]{0,1:T(8,128)(2,1)}, /*index=5...) while((s32[]{:T(128)}, f32[2048,256]{1,0:T(8,128)}, ...), condition=%wide.region_12.13_spmd.clone, body=%wide.region_10.12_spmd.clone.sunk | while | flops 2751068672 | bytes 238088880 | solution.py:239
  1201.3 11.6 multiply_reduce_fusion.6
  1253.4 11.6 multiply_reduce_fusion.6
  1305.7 11.8 multiply_reduce_fusion.6
  1397.5 18.4 %fusion.26 = bf16[2048,256]{1,0:T(8,128)(2,1)S(1)} fusion(f32[2048,256]{1,0:T(8,128)} %get-tuple-element.327, f32[256]{0:T(256)} %copy-done.41, f32[2048]{0:T(1024)} %copy-done.34, s32[256]{0:T(256)S(1)} %copy-done.37, s32[256]{0:T(256)} %copy-done.38, pred[256]{0:T(512)(128)(4,1)} %copy-done.43, pred[256]{0:T(512)(128)(4,1)} %copy-done.45), kind=kOutput, calls=%fused_computation.64 | convolution fusion | flops 1614217216 | bytes 3157504 | tf_op jit(solution)/shard_map/dot_general | solution.py:58
  1433.9 18.2 %fusion.27 = bf16[2048,256]{1,0:T(8,128)(2,1)S(1)} fusion(f32[2048,256]{1,0:T(8,128)} %copy.43, f32[256]{0:T(256)S(1)} %copy-done.42, f32[2048]{0:T(1024)S(1)} %copy-done.35, s32[256]{0:T(256)S(1)} %copy-done.37, s32[256]{0:T(256)S(1)} %copy-done.39, pred[256]{0:T(512)(128)(4,1)S(1)} %copy-done.44, pred[256]{0:T(512)(128)(4,1)S(1)} %copy-done.46), kind=kOutput, calls=%fused_computation.65 | convolution fusion | flops 1614217216 | bytes 3157504 | tf_op jit(solution)/shard_map/dot_general | solution.py:58
  1478.1 15.5 add_convert_fusion
  1513.9 90.3 %reduce-scatter.18.cloned.1.call-done = bf16[256,2048]{1,0:T(8,128)(2,1)} async-done(((bf16[2048,2048]{1,0:T(8,128)(2,1)}), bf16[256,2048]{1,0:T(8,128)(2,1)}) %reduce-scatter.18.cloned.1.call-update) | async-done | bytes 1048592 | tf_op jit(solution)/shard_map/reduce_scatter | solution.py:252
  1606.1 38.0 %all-reduce = (f32[2048]{0:T(1024)}, f32[2048]{0:T(1024)}) all-reduce(f32[2048]{0:T(1024)S(1)} %get-tuple-element.394, f32[2048]{0:T(1024)S(1)} %copy-done.29), channel_id=1, replica_groups=mesh['fsdp'=4,'tp'=8] {'fsdp','tp'}, use_global_device_ids=true, to_apply=%region_16.17 | all-reduce | flops 4096 | bytes 32768 | tf_op jit(solution)/shard_map/psum | solution.py:288
  (352 shorter events, 401.1 us)
Async XLA Ops:
  7.2 32.0 %all-gather.18.cloned.1.call-start = ((), (), s32[]{:S(2)}) async-start(), calls=%async_computation.14 | async-start | bytes 1310720 | tf_op jit(solution)/shard_map/all_gather | solution.py:97
  7.9 115.6 %all-gather.12.cloned.1.call-start = ((), (), s32[]{:S(2)}) async-start(), calls=%async_computation.11 | async-start | bytes 9437184 | tf_op jit(solution)/shard_map/all_gather | solution.py:107
  13.8 136.7 %all-gather.16.cloned.1.call-start = ((), (), s32[]{:S(2)}) async-start(), calls=%async_computation.13 | async-start | bytes 1310720 | tf_op jit(solution)/shard_map/all_gather | solution.py:96
  14.5 164.4 %all-gather.14.cloned.1.call-start = ((), (), s32[]{:S(2)}) async-start(), calls=%async_computation.12 | async-start | bytes 1310720 | tf_op jit(solution)/shard_map/all_gather | solution.py:95
  15.1 250.4 %all-gather.20.cloned.1.call-start = ((), (), s32[]{:S(2)}) async-start(), calls=%async_computation.15 | async-start | bytes 1310720 | tf_op jit(solution)/shard_map/all_gather | solution.py:98
  15.7 428.3 %reduce-scatter.12.cloned.1.call-start = ((), (), s32[]{:S(2)}) async-start(), calls=%async_computation.16 | async-start | bytes 18874368 | tf_op jit(solution)/shard_map/reduce_scatter | solution.py:148
  15.7 169.2 %copy-start.41 = (f32[256]{0:T(256)}, f32[256]{0:T(256)S(1)}, u32[]{:S(2)}) copy-start(f32[256]{0:T(256)S(1)} %fusion.88) | copy-start | bytes 3076
  15.8 169.2 %copy-start.43 = (pred[256]{0:T(512)(128)(4,1)}, pred[256]{0:T(512)(128)(4,1)S(1)}, u32[]{:S(2)}) copy-start(pred[256]{0:T(512)(128)(4,1)S(1)} %get-tuple-element.446) | copy-start | bytes 772
  15.8 169.2 %copy-start.45 = (pred[256]{0:T(512)(128)(4,1)}, pred[256]{0:T(512)(128)(4,1)S(1)}, u32[]{:S(2)}) copy-start(pred[256]{0:T(512)(128)(4,1)S(1)} %get-tuple-element.447) | copy-start | bytes 772
  15.8 169.2 %copy-start.36 = (s32[256]{0:T(256)}, s32[256]{0:T(256)S(1)}, u32[]{:S(2)}) copy-start(s32[256]{0:T(256)S(1)} %get-tuple-element.444) | copy-start | bytes 3076
  15.8 169.2 %copy-start.38 = (s32[256]{0:T(256)}, s32[256]{0:T(256)S(1)}, u32[]{:S(2)}) copy-start(s32[256]{0:T(256)S(1)} %get-tuple-element.445) | copy-start | bytes 3076
  15.8 169.2 %copy-start.34 = (f32[2048]{0:T(1024)}, f32[2048]{0:T(1024)S(1)}, u32[]{:S(2)}) copy-start(f32[2048]{0:T(1024)S(1)} %fusion.82) | copy-start | bytes 24580
  275.6 168.4 %copy-start.12 = (f32[256,2048]{1,0:T(8,128)S(1)}, f32[256,2048]{1,0:T(8,128)}, u32[]{:S(2)}) copy-start(f32[256,2048]{1,0:T(8,128)} %param.15) | copy-start | bytes 6291460
  275.6 171.6 %copy-start.27 = (f32[2048]{0:T(1024)S(1)}, f32[2048]{0:T(1024)}, u32[]{:S(2)}) copy-start(f32[2048]{0:T(1024)} %param.21) | copy-start | bytes 24580
  275.6 221.3 %all-gather.26.cloned.1.call-start = ((), (), s32[]{:S(2)}) async-start(), calls=%async_computation.19 | async-start | bytes 5242880 | tf_op jit(solution)/shard_map/all_gather | solution.py:100
  276.4 304.8 %all-gather.22.cloned.1.call-start = ((), (), s32[]{:S(2)}) async-start(), calls=%async_computation.17 | async-start | bytes 9437184 | tf_op jit(solution)/shard_map/all_gather | solution.py:156
  448.5 185.8 %all-gather.24.cloned.1.call-start = ((), (), s32[]{:S(2)}) async-start(), calls=%async_computation.18 | async-start | bytes 5242880 | tf_op jit(solution)/shard_map/all_gather | solution.py:99
  449.2 239.4 %all-gather.28.cloned.1.call-start = ((), (), s32[]{:S(2)}) async-start(), calls=%async_computation.20 | async-start | bytes 5242880 | tf_op jit(solution)/shard_map/all_gather | solution.py:101
  449.8 323.1 %all-gather.30.cloned.1.call-start = ((), (), s32[]{:S(2)}) async-start(), calls=%async_computation.22 | async-start | bytes 9437184 | tf_op jit(solution)/shard_map/all_gather | solution.py:169
  451.0 545.0 %reduce-scatter.16.cloned.1.call-start = ((), (), s32[]{:S(2)}) async-start(), calls=%async_computation.23 | async-start | bytes 18874368 | tf_op jit(solution)/shard_map/reduce_scatter | solution.py:181
  829.0 257.2 %reduce-scatter.14.cloned.1.call-start = ((), (), s32[]{:S(2)}) async-start(), calls=%async_computation.21 | async-start | bytes 9437184 | tf_op jit(solution)/shard_map/reduce_scatter | solution.py:163
  843.1 152.9 %copy-start.15 = (f32[256,2048]{1,0:T(8,128)S(1)}, f32[256,2048]{1,0:T(8,128)}, u32[]{:S(2)}) copy-start(f32[256,2048]{1,0:T(8,128)} %copy-done.14) | copy-start | bytes 6291460
  843.1 329.3 %all-gather.32.cloned.1.call-start = ((), (), s32[]{:S(2)}) async-start(), calls=%async_computation.24 | async-start | bytes 9437184 | tf_op jit(solution)/shard_map/all_gather | solution.py:191
  1091.8 401.9 %reduce-scatter.32.cloned.1.call-start = ((), (), s32[]{:S(2)}) async-start(), calls=%async_computation.32 | async-start | bytes 5242880 | tf_op jit(solution)/shard_map/reduce_scatter | solution.py:284
  1106.4 390.1 %reduce-scatter.30.cloned.1.call-start = ((), (), s32[]{:S(2)}) async-start(), calls=%async_computation.31 | async-start | bytes 5242880 | tf_op jit(solution)/shard_map/reduce_scatter | solution.py:281
  1120.4 379.0 %reduce-scatter.28.cloned.1.call-start = ((), (), s32[]{:S(2)}) async-start(), calls=%async_computation.30 | async-start | bytes 5242880 | tf_op jit(solution)/shard_map/reduce_scatter | solution.py:278
  1134.8 367.5 %reduce-scatter.26.cloned.1.call-start = ((), (), s32[]{:S(2)}) async-start(), calls=%async_computation.29 | async-start | bytes 1310720 | tf_op jit(solution)/shard_map/reduce_scatter | solution.py:275
  1179.1 325.0 %reduce-scatter.20.cloned.1.call-start = ((), (), s32[]{:S(2)}) async-start(), calls=%async_computation.26 | async-start | bytes 1310720 | tf_op jit(solution)/shard_map/reduce_scatter | solution.py:266
  1188.2 209.2 %copy-start.37 = (s32[256]{0:T(256)S(1)}, s32[256]{0:T(256)}, u32[]{:S(2)}) copy-start(s32[256]{0:T(256)} %copy-done.36) | copy-start | bytes 3076
  1423.9 82.0 %reduce-scatter.24.cloned.1.call-start = ((), (), s32[]{:S(2)}) async-start(), calls=%async_computation.28 | async-start | bytes 1310720 | tf_op jit(solution)/shard_map/reduce_scatter | solution.py:272
  1430.9 81.2 %reduce-scatter.22.cloned.1.call-start = ((), (), s32[]{:S(2)}) async-start(), calls=%async_computation.27 | async-start | bytes 1310720 | tf_op jit(solution)/shard_map/reduce_scatter | solution.py:269
  1460.1 144.1 %reduce-scatter.18.cloned.1.call-start = ((), (), s32[]{:S(2)}) async-start(), calls=%async_computation.25 | async-start | bytes 9437184 | tf_op jit(solution)/shard_map/reduce_scatter | solution.py:252
  (68 other events, 881.1 us)
Sparse Core Ops, SparseCore 0:
  9.9 29.3 all-gather.17
  41.4 82.0 all-gather.11
  125.3 25.1 all-gather.15
  152.2 26.6 all-gather.13
  180.5 26.4 all-gather.19
  275.7 168.2 reduce-scatter.11
  445.8 51.0 all-gather.25
  499.1 82.0 all-gather.21
  583.0 51.2 all-gather.23
  636.0 52.5 all-gather.27
  690.8 82.0 all-gather.29
  829.2 166.7 reduce-scatter.15
  998.2 87.9 reduce-scatter.13
  1091.9 80.3 all-gather.31
  1175.2 51.1 reduce-scatter.31
  1229.5 52.6 reduce-scatter.29
  1285.0 52.6 reduce-scatter.27
  1340.8 27.6 reduce-scatter.25
  1424.0 26.7 reduce-scatter.19
  1453.8 27.6 reduce-scatter.23
  1484.4 27.6 reduce-scatter.21
  1514.5 89.5 reduce-scatter.17
where the time goes:
time: 1660 us; the launch traced here: 1650 us
  waiting for transfers between devices  976 us (59%)
  matrix products  446 us (27%)
  other arithmetic  112 us (7%)
  local copies, waits for them, and re-layouts  61.1 us (4%)
  blocking collectives  38 us (2%)
    reduce_scatter x1, waiting for transfers between devices, body(): lax.psum_scatter(jnp.dot(mixed, out_part, preferred_element_type=jnp.floa...  168 us
    reduce_scatter x1, waiting for transfers between devices, body(): lax.psum_scatter(contract_cols(gate_rows, full_gate) + contract_cols(up_r...  153 us
    dot_general x7, matrix products, contract_cols(): lax.dot_general(left, right, (((1,), (1,)), ((), ())), preferred_element_...  97 us
    reduce_scatter x1, waiting for transfers between devices, body(): lax.psum_scatter((contract_cols(query_rows, full_query) + contract_cols(k...  90.3 us
    reduce_scatter x1, waiting for transfers between devices, body(): lax.psum_scatter(jnp.dot(inner, down_rows, preferred_element_type=jnp.flo...  87.6 us
    all_gather x1, waiting for transfers between devices, body(): lax.all_gather(cotangent.astype(jnp.bfloat16), 'tp', axis=0, tiled=True)  84.3 us
    all_gather x1, waiting for transfers between devices, body(): piece = lax.all_gather(normed_mlp, 'tp', axis=0, tiled=True)  84.3 us
    all_gather x1, waiting for transfers between devices, body(): piece = lax.all_gather(normed_attn, 'tp', axis=0, tiled=True)  84.3 us
  transfers between devices with their start and end apart: 22, of which 15 were waited for; matrix products, arithmetic and copies ran while one was open for 32% of the time, Pallas kernels for 0%

commit v1 on v0

v1 whole, which is shorter than its diff:
```python
import jax
import jax.numpy as jnp
from jax import lax
from jax.experimental import pallas as pl
from jax.experimental.pallas import tpu as pltpu
from jax.sharding import PartitionSpec as P

HEAD_DIM = 64
SEQ_LEN = 2048
rope_base = 130000.0
norm_eps = 1e-05
masked_score = -1e30

NT = (((1,), (1,)), ((), ()))
NN = (((1,), (0,)), ((), ()))


def dot(left, right, dims=NN):
    return lax.dot_general(left, right, dims, preferred_element_type=jnp.float32)


def only_head(block, head):
    lane = lax.broadcasted_iota(jnp.int32, block.shape, 1)
    return jnp.where(lane // HEAD_DIM == head, block, jnp.zeros_like(block))


def causal(tile):
    key = lax.broadcasted_iota(jnp.int32, tile.shape, 0)
    query = lax.broadcasted_iota(jnp.int32, tile.shape, 1)
    return jnp.where(key <= query, tile, masked_score)


def attend_kernel(place_ref, query_ref, keys_ref, values_t_ref, mixed_ref, total_ref, heads_ref, acc_ref, out_ref, top_ref, sum_ref):
    rows, width = query_ref.shape
    half = rows // 2
    heads = width // HEAD_DIM
    core = place_ref[0]
    start = place_ref[1] * rows
    first = start // SEQ_LEN * SEQ_LEN
    full = (start - first) // rows
    scaled = query_ref[...] * jnp.bfloat16(HEAD_DIM**-0.5)
    for head in range(heads):
        heads_ref[head] = only_head(scaled, head)
    acc_ref[...] = jnp.zeros_like(acc_ref)
    top_ref[...] = jnp.full_like(top_ref, masked_score)
    sum_ref[...] = jnp.zeros_like(sum_ref)

    def visit(offset, diagonal):
        key_block = keys_ref[pl.ds(offset, rows), :]
        for head in range(heads):
            feature = pl.ds(head * HEAD_DIM, HEAD_DIM)
            scores = dot(key_block, heads_ref[head], NT)
            if diagonal:
                scores = causal(scores)
            old = top_ref[pl.ds(head, 1), :]
            top = jnp.maximum(old, jnp.max(scores, axis=0, keepdims=True))
            shrink = jnp.exp(old - top)
            weights = jnp.exp(scores - top)
            top_ref[pl.ds(head, 1), :] = top
            sum_ref[pl.ds(head, 1), :] = sum_ref[pl.ds(head, 1), :] * shrink + jnp.sum(weights, axis=0, keepdims=True)
            value_t = values_t_ref[feature, pl.ds(offset, rows)]
            acc_ref[feature, :] = acc_ref[feature, :] * shrink + dot(value_t, weights.astype(jnp.bfloat16))

    def step(index, carry):
        visit(pl.multiple_of(first + index * rows, rows), False)
        return carry

    lax.fori_loop(0, full, step, 0)
    visit(pl.multiple_of(start, rows), True)
    for head in range(heads):
        feature = pl.ds(head * HEAD_DIM, HEAD_DIM)
        acc_ref[feature, :] = acc_ref[feature, :] / sum_ref[pl.ds(head, 1), :]
    out_ref[...] = acc_ref[...].T
    for side, part in enumerate((core, 1 - core)):
        mixed_ref[side] = out_ref[pl.ds(pl.multiple_of(part * half, half), half), :].astype(jnp.bfloat16)
    total_ref[...] = top_ref[...] + jnp.log(sum_ref[...])


def attend(place, qkv, values_t, rows):
    group_rows, width = qkv.shape[0], qkv.shape[1] // 3
    heads = width // HEAD_DIM
    return pl.pallas_call(
        attend_kernel,
        grid_spec=pltpu.PrefetchScalarGridSpec(
            num_scalar_prefetch=1,
            grid=(1,),
            in_specs=[
                pl.BlockSpec((rows, width), lambda i, s: (s[1], 0)),
                pl.BlockSpec((group_rows, width), lambda i, s: (0, 1)),
                pl.BlockSpec(values_t.shape, lambda i, s: (0, 0)),
            ],
            out_specs=[
                pl.BlockSpec((2, rows // 2, width), lambda i, s: (0, 0, 0)),
                pl.BlockSpec((heads, rows), lambda i, s: (0, 0)),
            ],
            scratch_shapes=[
                pltpu.VMEM((heads, rows, width), jnp.bfloat16),
                pltpu.VMEM((width, rows), jnp.float32),
                pltpu.VMEM((rows, width), jnp.float32),
                pltpu.VMEM((heads, rows), jnp.float32),
                pltpu.VMEM((heads, rows), jnp.float32),
            ],
        ),
        out_shape=[
            jax.ShapeDtypeStruct((2, rows // 2, width), jnp.bfloat16),
            jax.ShapeDtypeStruct((heads, rows), jnp.float32),
        ],
        cost_estimate=pl.CostEstimate(flops=4 * rows * SEQ_LEN * width, bytes_accessed=4 * rows * width + 4 * group_rows * width, transcendentals=rows * SEQ_LEN * heads // 2),
        name="attend",
    )(place, qkv, qkv, values_t)


def attend_back_kernel(place_ref, query_ref, mixed_in, grad_same, grad_other, total_ref, keys_ref, keys_t_ref, values_ref, dquery_in, dkey_in, dvalue_in, dquery_ref, dkey_ref, dvalue_ref, heads_ref, grads_ref, acc_ref, inner_ref, mixed_ref, grad_ref):
    rows, width = query_ref.shape
    half = rows // 2
    heads = width // HEAD_DIM
    core = place_ref[0]
    start = place_ref[1] * rows
    for side, part in enumerate((core, 1 - core)):
        span = pl.ds(pl.multiple_of(part * half, half), half)
        mixed_ref[span, :] = mixed_in[side]
        grad_ref[span, :] = (grad_same, grad_other)[side][...]
    first = start // SEQ_LEN * SEQ_LEN
    full = (start - first) // rows
    scaled = query_ref[...] * jnp.bfloat16(HEAD_DIM**-0.5)
    grad = grad_ref[...]
    product = grad.astype(jnp.float32) * mixed_ref[...].astype(jnp.float32)
    pick = (lax.broadcasted_iota(jnp.int32, inner_ref.shape[:1] + (width,), 1) // HEAD_DIM == lax.broadcasted_iota(jnp.int32, inner_ref.shape[:1] + (width,), 0)).astype(jnp.float32)
    inner_ref[...] = lax.dot_general(pick, product, NT, precision=lax.Precision.HIGHEST, preferred_element_type=jnp.float32)
    for head in range(heads):
        heads_ref[head] = only_head(scaled, head)
        grads_ref[head] = only_head(grad, head)
    acc_ref[...] = jnp.zeros_like(acc_ref)

    def visit(offset, diagonal):
        span = pl.ds(offset, rows)
        key_block = keys_ref[span, :]
        value_block = values_ref[span, :]
        dkey = dkey_in[span, :]
        dvalue = dvalue_in[span, :]
        for head in range(heads):
            feature = pl.ds(head * HEAD_DIM, HEAD_DIM)
            scores = dot(key_block, heads_ref[head], NT)
            if diagonal:
                scores = causal(scores)
            probs = jnp.exp(scores - total_ref[pl.ds(head, 1), :])
            dprobs = dot(value_block, grads_ref[head], NT)
            dscores = (probs * (dprobs - inner_ref[pl.ds(head, 1), :])).astype(jnp.bfloat16)
            dvalue = dvalue + dot(probs.astype(jnp.bfloat16), grads_ref[head])
            dkey = dkey + dot(dscores, heads_ref[head])
            acc_ref[feature, :] = acc_ref[feature, :] + dot(keys_t_ref[feature, span], dscores)
        dkey_ref[span, :] = dkey
        dvalue_ref[span, :] = dvalue

    def step(index, carry):
        visit(pl.multiple_of(first + index * rows, rows), False)
        return carry

    dkey_ref[...] = dkey_in[...]
    dvalue_ref[...] = dvalue_in[...]
    lax.fori_loop(0, full, step, 0)
    visit(pl.multiple_of(start, rows), True)
    dquery_ref[...] = acc_ref[...].T * HEAD_DIM**-0.5


def attend_back(place, qkv, mixed, grad_same, grad_other, total, keys_t, dquery, dkey, dvalue):
    _, half, width = mixed.shape
    rows = 2 * half
    group_rows = qkv.shape[0]
    heads = width // HEAD_DIM
    whole = lambda a: pl.BlockSpec(a.shape, lambda i, s: (0,) * a.ndim)
    return pl.pallas_call(
        attend_back_kernel,
        grid_spec=pltpu.PrefetchScalarGridSpec(
            num_scalar_prefetch=1,
            grid=(1,),
            in_specs=[
                pl.BlockSpec((rows, width), lambda i, s: (s[1], 0)),
                whole(mixed),
                whole(grad_same),
                whole(grad_other),
                whole(total),
                pl.BlockSpec((group_rows, width), lambda i, s: (0, 1)),
                whole(keys_t),
                pl.BlockSpec((group_rows, width), lambda i, s: (0, 2)),
                pl.BlockSpec(memory_space=pl.ANY),
                whole(dkey),
                whole(dvalue),
            ],
            out_specs=[
                pl.BlockSpec((rows, width), lambda i, s: (s[1], 0)),
                whole(dkey),
                whole(dvalue),
            ],
            scratch_shapes=[
                pltpu.VMEM((heads, rows, width), jnp.bfloat16),
                pltpu.VMEM((heads, rows, width), jnp.bfloat16),
                pltpu.VMEM((width, rows), jnp.float32),
                pltpu.VMEM((8, rows), jnp.float32),
                pltpu.VMEM((rows, width), jnp.bfloat16),
                pltpu.VMEM((rows, width), jnp.bfloat16),
            ],
        ),
        out_shape=[jax.ShapeDtypeStruct(a.shape, jnp.float32) for a in (dquery, dkey, dvalue)],
        input_output_aliases={9: 0, 10: 1, 11: 2},
        cost_estimate=pl.CostEstimate(flops=10 * rows * SEQ_LEN * width, bytes_accessed=8 * rows * width + 20 * group_rows * width, transcendentals=rows * SEQ_LEN * heads // 2),
        name="attend_back",
    )(place, qkv, mixed, grad_same, grad_other, total, qkv, keys_t, qkv, dquery, dkey, dvalue)


def turned(block, sign):
    half = HEAD_DIM // 2
    lane = lax.broadcasted_iota(jnp.int32, block.shape, 1)
    width = block.shape[1]
    up = pltpu.roll(block, width - half, 1)
    down = pltpu.roll(block, half, 1)
    return jnp.where(lane % HEAD_DIM < half, -sign * up, sign * down)


def project_kernel(place_ref, same_ref, other_ref, weight_ref, cosine_ref, sine_ref, out_in, out_ref, acc_ref):
    rows = same_ref.shape[0]
    core = place_ref[0]
    same = pl.ds(pl.multiple_of(core * rows, rows), rows)
    other = pl.ds(pl.multiple_of((1 - core) * rows, rows), rows)
    acc_ref[same, :] = dot(same_ref[...], weight_ref[...])
    acc_ref[other, :] = dot(other_ref[...], weight_ref[...])

    @pl.when(pl.program_id(0) < 2)
    def _():
        block = acc_ref[...]
        out_ref[...] = (block * cosine_ref[...] + turned(block, 1.0) * sine_ref[...]).astype(jnp.bfloat16)

    @pl.when(pl.program_id(0) == 2)
    def _():
        out_ref[...] = acc_ref[...].astype(jnp.bfloat16)


def project(place, same, other, weight, cosine, sine, out):
    rows, depth = same.shape
    pair = 2 * rows
    width = weight.shape[1] // 3
    cycle = SEQ_LEN // pair
    fixed = lambda shape: pl.BlockSpec(shape, lambda i, s: (0, 0))
    table = pl.BlockSpec((pair, width), lambda i, s: (s[1] % cycle, 0))
    return pl.pallas_call(
        project_kernel,
        grid_spec=pltpu.PrefetchScalarGridSpec(
            num_scalar_prefetch=1,
            grid=(3,),
            in_specs=[
                fixed(same.shape),
                fixed(other.shape),
                pl.BlockSpec((depth, width), lambda i, s: (0, i)),
                table,
                table,
                pl.BlockSpec(memory_space=pl.ANY),
            ],
            out_specs=pl.BlockSpec((pair, width), lambda i, s: (s[1], i)),
            scratch_shapes=[pltpu.VMEM((pair, width), jnp.float32)],
        ),
        out_shape=jax.ShapeDtypeStruct(out.shape, jnp.bfloat16),
        input_output_aliases={6: 0},
        cost_estimate=pl.CostEstimate(flops=12 * rows * depth * width, bytes_accessed=4 * rows * depth + 6 * depth * width, transcendentals=0),
        name="project",
    )(place, same, other, weight, cosine, sine, out)


def unrotate_kernel(order_ref, dquery_ref, dkey_ref, dvalue_ref, cosine_ref, sine_ref, out_ref):
    width = dquery_ref.shape[1]
    for place, ref in enumerate((dquery_ref, dkey_ref)):
        block = ref[...]
        out_ref[:, pl.ds(place * width, width)] = (block * cosine_ref[...] + turned(block * sine_ref[...], -1.0)).astype(jnp.bfloat16)
    out_ref[:, pl.ds(2 * width, width)] = dvalue_ref[...].astype(jnp.bfloat16)


def unrotate(order, dquery, dkey, dvalue, cosine, sine):
    group_rows, width = dquery.shape
    blocks = order.shape[0]
    rows = group_rows // blocks
    cycle = SEQ_LEN // rows
    spec = pl.BlockSpec((rows, width), lambda i, s: (s[i], 0))
    table = pl.BlockSpec((rows, width), lambda i, s: (s[i] % cycle, 0))
    return pl.pallas_call(
        unrotate_kernel,
        grid_spec=pltpu.PrefetchScalarGridSpec(
            num_scalar_prefetch=1,
            grid=(blocks,),
            in_specs=[spec, spec, spec, table, table],
            out_specs=pl.BlockSpec((rows, 3 * width), lambda i, s: (i, 0)),
        ),
        out_shape=jax.ShapeDtypeStruct((group_rows, 3 * width), jnp.bfloat16),
        cost_estimate=pl.CostEstimate(flops=20 * group_rows * width, bytes_accessed=18 * group_rows * width, transcendentals=0),
        name="unrotate",
    )(order, dquery, dkey, dvalue, cosine, sine)


def rms_norm(values, gain):
    return values * lax.rsqrt(jnp.mean(values * values, axis=-1, keepdims=True) + norm_eps) * gain


def rope_tables(width):
    half = HEAD_DIM // 2
    positions = jnp.arange(SEQ_LEN, dtype=jnp.int32).astype(jnp.float32)
    column = jnp.arange(width, dtype=jnp.int32) % half
    inverse = jnp.power(jnp.float32(rope_base), -2.0 * column.astype(jnp.float32) / HEAD_DIM)
    angle = positions[:, None] * inverse[None, :]
    return (jnp.cos(angle), jnp.sin(angle))


class Ring:
    def __init__(self, size):
        self.chips = size // 2
        self.order = [2 * p if 2 * p < self.chips else 2 * (self.chips - 1 - p) + 1 for p in range(self.chips)]
        place = [self.order.index(chip) for chip in range(self.chips)]
        follower = [self.order[(place[chip] + 1) % self.chips] for chip in range(self.chips)]
        self.forward = [(2 * chip + core, 2 * follower[chip] + core) for chip in range(self.chips) for core in range(2)]
        self.swap = [(device, device ^ 1) for device in range(size)]
        index = lax.axis_index("tp")
        self.chip, self.core = index // 2, index % 2
        table = [[self.order[(place[chip] - slot) % self.chips] for chip in range(self.chips)] for slot in range(self.chips)]
        self.sources = [jnp.array(row, jnp.int32)[self.chip] for row in table]

    def exchange(self, block):
        return lax.ppermute(block, "tp", self.swap)

    def gather(self, block):
        slots = []
        for slot in range(self.chips):
            following = lax.ppermute(block, "tp", self.forward) if slot < self.chips - 1 else None
            slots.append((block, self.exchange(block)))
            block = following
        return slots

    def scatter(self, parts):
        total = None
        for slot in list(range(1, self.chips)) + [0]:
            same, other = parts(slot)
            term = same.astype(jnp.float32) + self.exchange(other).astype(jnp.float32)
            if total is not None:
                term = term + lax.ppermute(total, "tp", self.forward).astype(jnp.float32)
            total = term.astype(jnp.bfloat16) if slot else term
        return total


def swap_sum(values, mesh):
    for axis in ("tp", "fsdp"):
        step = 1
        while step < mesh[axis]:
            values = values + lax.ppermute(values, axis, [(i, i ^ step) for i in range(mesh[axis])])
            step *= 2
    return values


def make_body(mesh):
    sizes = dict(mesh.shape)

    def body(activations, gain_attn, w_query, w_key, w_value, w_out, gain_mlp, w_gate, w_up, w_down, cotangent):
        ring = Ring(sizes["tp"])
        chips, core = ring.chips, ring.core
        rows = activations.shape[0]
        width = w_query.shape[1]
        pair = 2 * rows
        group_rows = chips * pair
        w_qkv = lax.all_gather(jnp.concatenate([w_query, w_key, w_value], axis=1), "fsdp", axis=0, tiled=True)
        full_out = lax.all_gather(w_out, "fsdp", axis=1, tiled=True)
        full_gate = lax.all_gather(w_gate, "fsdp", axis=0, tiled=True)
        full_up = lax.all_gather(w_up, "fsdp", axis=0, tiled=True)
        full_down = lax.all_gather(w_down, "fsdp", axis=1, tiled=True)
        cosine, sine = rope_tables(width)
        places = [jnp.stack([core, source]) for source in ring.sources]
        order = jnp.stack([2 * source + part for source in ring.sources for part in (core, 1 - core)])

        normed_attn = rms_norm(activations, gain_attn).astype(jnp.bfloat16)
        seen_attn = ring.gather(normed_attn)
        qkv = jnp.zeros((group_rows, 3 * width), jnp.bfloat16)
        for slot, (same, other) in enumerate(seen_attn):
            qkv = project(places[slot], same, other, w_qkv, cosine, sine, qkv)
        keys_t, values_t = qkv[:, width : 2 * width].T, qkv[:, 2 * width :].T

        seen_grad = ring.gather(cotangent.astype(jnp.bfloat16))

        kept = {}

        def attention_part(slot):
            kept[slot] = attend(places[slot], qkv, values_t, pair)
            mixed = kept[slot][0]
            return [dot(mixed[side], full_out).astype(jnp.bfloat16) for side in range(2)]

        attn_branch = ring.scatter(attention_part)
        hidden_state = activations + attn_branch
        normed_mlp = rms_norm(hidden_state, gain_mlp).astype(jnp.bfloat16)
        seen_mlp = ring.gather(normed_mlp)
        mlp = {}

        def mlp_part(slot):
            tokens = jnp.concatenate(seen_mlp[slot], axis=0)
            grads = jnp.concatenate(seen_grad[slot], axis=0)
            gate = dot(tokens, full_gate)
            up = dot(tokens, full_up)
            act, pull = jax.vjp(lambda g, u: jax.nn.silu(g) * u, gate, up)
            gate_grad, up_grad = pull(dot(grads, full_down, NT))
            gate_grad = gate_grad.astype(jnp.bfloat16)
            up_grad = up_grad.astype(jnp.bfloat16)
            mlp[slot] = (tokens, grads, act.astype(jnp.bfloat16), gate_grad, up_grad)
            back = (dot(gate_grad, full_gate, NT) + dot(up_grad, full_up, NT)).astype(jnp.bfloat16)
            return back[:rows], back[rows:]

        normed_mlp_grad = ring.scatter(mlp_part)

        def down_part(slot):
            part = dot(mlp[slot][2], full_down).astype(jnp.bfloat16)
            return part[:rows], part[rows:]

        output = hidden_state + ring.scatter(down_part)
        all_tokens, all_grads, inner, gate_grad, up_grad = [
            jnp.concatenate([mlp[slot][item] for slot in range(chips)], axis=0) for item in range(5)
        ]
        _, pull_norm_mlp = jax.vjp(rms_norm, hidden_state, gain_mlp)
        hidden_norm_grad, gain_mlp_part = pull_norm_mlp(normed_mlp_grad)
        hidden_grad = cotangent + hidden_norm_grad
        seen_branch = ring.gather(hidden_grad.astype(jnp.bfloat16))

        def over_fsdp(grad, dimension):
            return lax.psum_scatter(grad.astype(jnp.bfloat16), "fsdp", scatter_dimension=dimension, tiled=True).astype(jnp.float32)

        TN = (((0,), (0,)), ((), ()))
        grad_down = over_fsdp(dot(inner, all_grads, TN), 1)
        grad_gate = over_fsdp(dot(all_tokens, gate_grad, TN), 0)
        grad_up = over_fsdp(dot(all_tokens, up_grad, TN), 0)

        empty = jnp.zeros((group_rows, width), jnp.float32)
        dquery, dkey, dvalue = empty, empty, empty
        mixed_parts, branch_parts = [], []
        for slot in range(chips):
            mixed, totals = kept[slot]
            same, other = seen_branch[slot]
            grad_same = dot(same, full_out, NT).astype(jnp.bfloat16)
            grad_other = dot(other, full_out, NT).astype(jnp.bfloat16)
            mixed_parts.append(mixed.reshape(pair, width))
            branch_parts.extend((same, other))
            dquery, dkey, dvalue = attend_back(places[slot], qkv, mixed, grad_same, grad_other, totals, keys_t, dquery, dkey, dvalue)
        grad_out = over_fsdp(dot(jnp.concatenate(mixed_parts, axis=0), jnp.concatenate(branch_parts, axis=0), TN), 1)
        qkv_grad = unrotate(order, dquery, dkey, dvalue, cosine, sine)

        def qkv_part(slot):
            part = dot(qkv_grad[slot * pair : (slot + 1) * pair], w_qkv, NT).astype(jnp.bfloat16)
            return part[:rows], part[rows:]

        normed_attn_grad = ring.scatter(qkv_part)
        flat_attn = jnp.concatenate([half for slot in range(chips) for half in seen_attn[slot]], axis=0)
        grad_qkv = over_fsdp(dot(flat_attn, qkv_grad, TN), 0)
        _, pull_norm_attn = jax.vjp(rms_norm, activations, gain_attn)
        input_norm_grad, gain_attn_part = pull_norm_attn(normed_attn_grad)
        input_grad = hidden_grad + input_norm_grad
        gain_sums = swap_sum(jnp.stack([gain_attn_part, gain_mlp_part]), sizes)
        return (
            output,
            input_grad,
            gain_sums[0],
            grad_qkv[:, :width],
            grad_qkv[:, width : 2 * width],
            grad_qkv[:, 2 * width :],
            grad_out,
            gain_sums[1],
            grad_gate,
            grad_up,
            grad_down,
        )

    return body


def solution(mesh):
    tokens = P(("fsdp", "tp"), None)
    column = P("fsdp", "tp")
    row = P("tp", "fsdp")
    in_specs = (tokens, P(), column, column, column, row, P(), column, column, row, tokens)
    out_specs = (tokens, tokens, P(), column, column, column, row, P(), column, column, row)
    return jax.shard_map(make_body(mesh), mesh=mesh, in_specs=in_specs, out_specs=out_specs, check_vma=False)
```

time: 1660 us -> 867 us (0.52)
  waiting for transfers between devices: 976 us -> 313 us
  matrix products: 446 us -> 191 us
  Pallas kernels: 0 us -> 141 us
  other arithmetic: 112 us -> 60.4 us
  starting transfers between devices: 1.1 us -> 48.6 us
  blocking collectives: 38 us -> 0 us
  local copies, waits for them, and re-layouts: 61.1 us -> 85.2 us
    reduce_scatter x11 -> x5, waiting for transfers between devices: 503 us -> 0.01 us  [over_fsdp(): lax.psum_scatter(grad.astype(jnp.bfloat16), 'fsdp', scatter_dimension=dim...]
    all_gather x11 -> x5, waiting for transfers between devices: 469 us -> 0.02 us  [the longest x1 0.01 us: body(): lax.all_gather(jnp.concatenate([w_query, w_key, w_value], axis=1), 'fsdp'...]
    ppermute x0 -> x61, waiting for transfers between devices: none -> 311 us  [the longest x12 160 us: scatter(): term = term + lax.ppermute(total, 'tp', self.forward).astype(jnp.float32)]
    dot_general x53 -> x49, matrix products: 446 us -> 191 us  [dot(): lax.dot_general(left, right, dims, preferred_element_type=jnp.float32)]
    pallas_call x0 -> x13, Pallas kernels: none -> 141 us  [the longest x4 58.8 us: attend_back(): pl.pallas_call(attend_back_kernel, grid_spec=pltpu.PrefetchScalarGridSpec...]
    unnamed x76 -> x194, local copies, waits for them, and re-layouts: 4.53 us -> 57 us
    ppermute x0 -> x61, starting transfers between devices: none -> 48.2 us  [the longest x12 18 us: scatter(): term = term + lax.ppermute(total, 'tp', self.forward).astype(jnp.float32)]
    convert_element_type x16 -> x14, other arithmetic: 71 us -> 26 us  [the longest x9 15.8 us: scatter(): total = term.astype(jnp.bfloat16) if slot else term]
  transfers between devices with their start and end apart: 22 -> 71, of which waited for: 15 -> 26; matrix products, arithmetic and copies ran while one was open for 32% -> 38% of each run, Pallas kernels for 0% -> 17%
where the time goes in v1:
time: 867 us; the launch traced here: 856 us
  waiting for transfers between devices  313 us (36%)
  matrix products  191 us (22%)
  Pallas kernels  141 us (16%)
  local copies, waits for them, and re-layouts  85.2 us (10%)
  other arithmetic  60.4 us (7%)
  starting transfers between devices  48.6 us (6%)
  between operations  17.4 us (2%)
    dot_general x49, matrix products, dot(): lax.dot_general(left, right, dims, preferred_element_type=jnp.float32)  191 us
    ppermute x12, waiting for transfers between devices, scatter(): term = term + lax.ppermute(total, 'tp', self.forward).astype(jnp.float32)  160 us
    ppermute x12, waiting for transfers between devices, gather(): lax.ppermute(block, 'tp', self.forward)  144 us
    pallas_call x4, Pallas kernels, attend_back(): pl.pallas_call(attend_back_kernel, grid_spec=pltpu.PrefetchScalarGridSpec...  58.8 us
    unnamed x194, local copies, waits for them, and re-layouts  57 us
    pallas_call x4, Pallas kernels, attend(): pl.pallas_call(attend_kernel, grid_spec=pltpu.PrefetchScalarGridSpec(num_...  45.4 us
    pallas_call x4, Pallas kernels, project(): pl.pallas_call(project_kernel, grid_spec=pltpu.PrefetchScalarGridSpec(num...  27.4 us
    ppermute x12, starting transfers between devices, scatter(): term = term + lax.ppermute(total, 'tp', self.forward).astype(jnp.float32)  18 us
  transfers between devices with their start and end apart: 71, of which 26 were waited for; matrix products, arithmetic and copies ran while one was open for 38% of the time, Pallas kernels for 17%

profile of v1, /device:TPU:0, one launch (start us, length us, event | category | flops | bytes accessed | tf_op | source)
XLA Modules:
  0.0 856.2 jit_solution(6414723855358242155)
XLA Ops:
  17.1 22.4 %collective-permute-done.same_ref = bf16[256,2048]{1,0:T(8,128)(2,1)} collective-permute-done((bf16[256,2048]{1,0:T(8,128)(2,1)S(1)}, bf16[256,2048]{1,0:T(8,128)(2,1)}, u32[]{:S(2)}, u32[]{:S(2)}) %collective-permute-start) | collective-permute-done | bytes 1048608 | tf_op jit(solution)/shard_map/ppermute | solution.py:329
  43.1 21.8 %collective-permute-done.1.same_ref = bf16[256,2048]{1,0:T(8,128)(2,1)} collective-permute-done((bf16[256,2048]{1,0:T(8,128)(2,1)}, bf16[256,2048]{1,0:T(8,128)(2,1)}, u32[]{:S(2)}, u32[]{:S(2)}) %collective-permute-start.1) | collective-permute-done | bytes 1048608 | tf_op jit(solution)/shard_map/ppermute | solution.py:329
  73.2 16.0 %collective-permute-done.2.same_ref = bf16[256,2048]{1,0:T(8,128)(2,1)} collective-permute-done((bf16[256,2048]{1,0:T(8,128)(2,1)}, bf16[256,2048]{1,0:T(8,128)(2,1)}, u32[]{:S(2)}, u32[]{:S(2)}) %collective-permute-start.2) | collective-permute-done | bytes 1048608 | tf_op jit(solution)/shard_map/ppermute | solution.py:329
  90.5 8.8 %multiply_sine_fusion = (f32[2048,256]{1,0:T(8,128)}, f32[2048,256]{1,0:T(8,128)}) fusion(f32[256]{0:T(256)S(1)} %fusion.110, f32[2048]{0:T(1024)S(1)} %iota_convert_fusion), kind=kLoop, calls=%fused_computation.38 | loop fusion | flops 524288 | bytes 4203520 | tf_op jit(solution)/shard_map/sin | solution.py:307
  146.4 12.8 %attend.6 = (bf16[2,256,256]{2,1,0:T(8,128)(2,1)}, f32[4,512]{1,0:T(4,128)}) custom-call(s32[2]{0:T(128)} %get-tuple-element.101.place_ref, bf16[2048,768]{1,0:T(8,128)(2,1)} %project.7.query_ref.keys_ref.values_ref, bf16[2048,768]{1,0:T(8,128)(2,1)} %project.7.query_ref.keys_ref.values_ref, bf16[256,2048]{1,0:T(8,128)(2,1)} %bitcast.139), custom_call_target="tpu_custom_call" | custom-call | flops 1073741824 | bytes 2621440 | tf_op jit(solution)/shard_map/attend/pallas_call | solution.py:82
  164.4 12.2 %collective-permute-done.30 = bf16[256,2048]{1,0:T(8,128)(2,1)} collective-permute-done((bf16[256,2048]{1,0:T(8,128)(2,1)}, bf16[256,2048]{1,0:T(8,128)(2,1)}, u32[]{:S(2)}, u32[]{:S(2)}) %collective-permute-start.30) | collective-permute-done | bytes 1048608 | tf_op jit(solution)/shard_map/ppermute | solution.py:329
  176.7 10.0 %attend.5 = (bf16[2,256,256]{2,1,0:T(8,128)(2,1)}, f32[4,512]{1,0:T(4,128)}) custom-call(s32[2]{0:T(128)} %pad_add_fusion.1.place_ref, bf16[2048,768]{1,0:T(8,128)(2,1)} %project.7.query_ref.keys_ref.values_ref, bf16[2048,768]{1,0:T(8,128)(2,1)} %project.7.query_ref.keys_ref.values_ref, bf16[256,2048]{1,0:T(8,128)(2,1)} %bitcast.140), custom_call_target="tpu_custom_call" | custom-call | flops 1073741824 | bytes 2621440 | tf_op jit(solution)/shard_map/attend/pallas_call | solution.py:82
  189.0 10.1 %collective-permute-done.11 = bf16[256,2048]{1,0:T(8,128)(2,1)} collective-permute-done((bf16[256,2048]{1,0:T(8,128)(2,1)}, bf16[256,2048]{1,0:T(8,128)(2,1)}, u32[]{:S(2)}, u32[]{:S(2)}) %collective-permute-start.11) | collective-permute-done | bytes 1048608 | tf_op jit(solution)/shard_map/ppermute | solution.py:340
  205.3 16.3 %collective-permute-done.31 = bf16[256,2048]{1,0:T(8,128)(2,1)} collective-permute-done((bf16[256,2048]{1,0:T(8,128)(2,1)}, bf16[256,2048]{1,0:T(8,128)(2,1)}, u32[]{:S(2)}, u32[]{:S(2)}) %collective-permute-start.31) | collective-permute-done | bytes 1048608 | tf_op jit(solution)/shard_map/ppermute | solution.py:329
  221.6 14.9 %attend.4 = (bf16[2,256,256]{2,1,0:T(8,128)(2,1)}, f32[4,512]{1,0:T(4,128)}) custom-call(s32[2]{0:T(128)} %get-tuple-element.100.place_ref, bf16[2048,768]{1,0:T(8,128)(2,1)} %project.7.query_ref.keys_ref.values_ref, bf16[2048,768]{1,0:T(8,128)(2,1)} %project.7.query_ref.keys_ref.values_ref, bf16[256,2048]{1,0:T(8,128)(2,1)} %bitcast.141), custom_call_target="tpu_custom_call" | custom-call | flops 1073741824 | bytes 2621440 | tf_op jit(solution)/shard_map/attend/pallas_call | solution.py:82
  266.6 21.7 %collective-permute-done.13 = bf16[256,2048]{1,0:T(8,128)(2,1)S(1)} collective-permute-done((bf16[256,2048]{1,0:T(8,128)(2,1)S(1)}, bf16[256,2048]{1,0:T(8,128)(2,1)S(1)}, u32[]{:S(2)}, u32[]{:S(2)}) %collective-permute-start.13) | collective-permute-done | bytes 1048608 | tf_op jit(solution)/shard_map/ppermute | solution.py:340
  312.9 8.2 multiply_convert_fusion.3
  341.4 12.9 %collective-permute-done.17 = bf16[256,2048]{1,0:T(8,128)(2,1)S(1)} collective-permute-done((bf16[256,2048]{1,0:T(8,128)(2,1)S(1)}, bf16[256,2048]{1,0:T(8,128)(2,1)S(1)}, u32[]{:S(2)}, u32[]{:S(2)}) %collective-permute-start.17) | collective-permute-done | bytes 1048608 | tf_op jit(solution)/shard_map/ppermute | solution.py:329
  377.5 12.7 %collective-permute-done.18 = bf16[256,2048]{1,0:T(8,128)(2,1)S(1)} collective-permute-done((bf16[256,2048]{1,0:T(8,128)(2,1)S(1)}, bf16[256,2048]{1,0:T(8,128)(2,1)S(1)}, u32[]{:S(2)}, u32[]{:S(2)}) %collective-permute-start.18) | collective-permute-done | bytes 1048608 | tf_op jit(solution)/shard_map/ppermute | solution.py:329
  412.8 10.6 %fusion.30 = bf16[1024,2048]{1,0:T(8,128)(2,1)} fusion(bf16[2048,2048]{1,0:T(8,128)(2,1)S(1)} %bitcast.154, bf16[512,1024]{1,0:T(8,128)(2,1)S(1)} %get-tuple-element.69, bf16[512,1024]{1,0:T(8,128)(2,1)S(1)} %get-tuple-element.72, bf16[512,1024]{1,0:T(8,128)(2,1)S(1)} %get-tuple-element.75, bf16[512,1024]{1,0:T(8,128)(2,1)S(1)} %get-tuple-element.66), kind=kOutput, calls=%fused_computation.30 | convolution fusion | flops 8608808960 | bytes 16777216 | tf_op jit(solution)/shard_map/dot_general | solution.py:19
  447.4 10.6 %fusion.24 = bf16[2048,1024]{1,0:T(8,128)(2,1)} fusion(bf16[2048,2048]{1,0:T(8,128)(2,1)S(1)} %bitcast.150, bf16[512,1024]{1,0:T(8,128)(2,1)S(1)} %copy-done.73, bf16[512,1024]{1,0:T(8,128)(2,1)S(1)} %copy-done.75, bf16[512,1024]{1,0:T(8,128)(2,1)S(1)} %copy-done.72, bf16[512,1024]{1,0:T(8,128)(2,1)S(1)} %copy-done.70), kind=kOutput, calls=%fused_computation.28 | convolution fusion | flops 8608808960 | bytes 16777216 | tf_op jit(solution)/shard_map/dot_general | solution.py:19
  477.6 8.0 collective-permute-done.39
  494.5 13.5 %collective-permute-done.26 = bf16[256,2048]{1,0:T(8,128)(2,1)S(1)} collective-permute-done((bf16[256,2048]{1,0:T(8,128)(2,1)S(1)}, bf16[256,2048]{1,0:T(8,128)(2,1)S(1)}, u32[]{:S(2)}, u32[]{:S(2)}) %collective-permute-start.26) | collective-permute-done | bytes 1048608 | tf_op jit(solution)/shard_map/ppermute | solution.py:340
  510.1 20.3 %collective-permute-done.40 = bf16[256,2048]{1,0:T(8,128)(2,1)S(1)} collective-permute-done((bf16[256,2048]{1,0:T(8,128)(2,1)S(1)}, bf16[256,2048]{1,0:T(8,128)(2,1)S(1)}, u32[]{:S(2)}, u32[]{:S(2)}) %collective-permute-start.40) | collective-permute-done | bytes 1048608 | tf_op jit(solution)/shard_map/ppermute | solution.py:340
  532.7 11.0 %fusion.27 = bf16[2048,1024]{1,0:T(8,128)(2,1)} fusion(bf16[2048,2048]{1,0:T(8,128)(2,1)S(1)} %bitcast.152, bf16[512,1024]{1,0:T(8,128)(2,1)S(1)} %copy-done.66, bf16[512,1024]{1,0:T(8,128)(2,1)S(1)} %copy-done.65, bf16[512,1024]{1,0:T(8,128)(2,1)S(1)} %copy-done.63, bf16[512,1024]{1,0:T(8,128)(2,1)S(1)} %copy-done.61), kind=kOutput, calls=%fused_computation.29 | convolution fusion | flops 8608808960 | bytes 16777216 | tf_op jit(solution)/shard_map/dot_general | solution.py:19
  543.9 9.2 %collective-permute-done.27 = bf16[256,2048]{1,0:T(8,128)(2,1)} collective-permute-done((bf16[256,2048]{1,0:T(8,128)(2,1)}, bf16[256,2048]{1,0:T(8,128)(2,1)}, u32[]{:S(2)}, u32[]{:S(2)}) %collective-permute-start.27) | collective-permute-done | bytes 1048608 | tf_op jit(solution)/shard_map/ppermute | solution.py:340
  553.0 22.3 %collective-permute-done.41 = bf16[256,2048]{1,0:T(8,128)(2,1)} collective-permute-done((bf16[256,2048]{1,0:T(8,128)(2,1)}, bf16[256,2048]{1,0:T(8,128)(2,1)}, u32[]{:S(2)}, u32[]{:S(2)}) %collective-permute-start.41) | collective-permute-done | bytes 1048608 | tf_op jit(solution)/shard_map/ppermute | solution.py:340
  598.7 12.8 %collective-permute-done.42 = bf16[256,2048]{1,0:T(8,128)(2,1)S(1)} collective-permute-done((bf16[256,2048]{1,0:T(8,128)(2,1)}, bf16[256,2048]{1,0:T(8,128)(2,1)S(1)}, u32[]{:S(2)}, u32[]{:S(2)}) %collective-permute-start.42) | collective-permute-done | bytes 1048608 | tf_op jit(solution)/shard_map/ppermute | solution.py:329
  622.2 10.3 %attend_back.4 = (f32[2048,256]{1,0:T(8,128)}, f32[2048,256]{1,0:T(8,128)}, f32[2048,256]{1,0:T(8,128)}) custom-call(s32[2]{0:T(128)} %get-tuple-element.100.place_ref, bf16[2048,768]{1,0:T(8,128)(2,1)} %project.7.query_ref.keys_ref.values_ref, ...), custom_call_target="tpu_custom_call", output_to_operand_aliasing={{0}: (9, {}), {1}: (10, {}), {2}: (11, {})} | custom-call | flops 2684354560 | bytes 11534336 | tf_op jit(solution)/shard_map/attend_back/pallas_call | solution.py:172
  647.1 13.5 %attend_back.5 = (f32[2048,256]{1,0:T(8,128)}, f32[2048,256]{1,0:T(8,128)}, f32[2048,256]{1,0:T(8,128)}) custom-call(s32[2]{0:T(128)} %pad_add_fusion.3.place_ref, bf16[2048,768]{1,0:T(8,128)(2,1)} %project.7.query_ref.keys_ref.values_ref, ...), custom_call_target="tpu_custom_call", output_to_operand_aliasing={{0}: (9, {}), {1}: (10, {}), {2}: (11, {})} | custom-call | flops 2684354560 | bytes 11534336 | tf_op jit(solution)/shard_map/attend_back/pallas_call | solution.py:172
  671.5 18.9 %attend_back.6 = (f32[2048,256]{1,0:T(8,128)}, f32[2048,256]{1,0:T(8,128)}, f32[2048,256]{1,0:T(8,128)}) custom-call(s32[2]{0:T(128)} %get-tuple-element.101.place_ref, bf16[2048,768]{1,0:T(8,128)(2,1)} %project.7.query_ref.keys_ref.values_ref, ...), custom_call_target="tpu_custom_call", output_to_operand_aliasing={{0}: (9, {}), {1}: (10, {}), {2}: (11, {})} | custom-call | flops 2684354560 | bytes 11534336 | tf_op jit(solution)/shard_map/attend_back/pallas_call | solution.py:172
  694.0 16.1 %attend_back.7 = (f32[2048,256]{1,0:T(8,128)}, f32[2048,256]{1,0:T(8,128)}, f32[2048,256]{1,0:T(8,128)}) custom-call(s32[2]{0:T(128)} %pad_add_fusion.1.place_ref, bf16[2048,768]{1,0:T(8,128)(2,1)} %project.7.query_ref.keys_ref.values_ref, ...), custom_call_target="tpu_custom_call", output_to_operand_aliasing={{0}: (9, {}), {1}: (10, {}), {2}: (11, {})} | custom-call | flops 2684354560 | bytes 11534336 | tf_op jit(solution)/shard_map/attend_back/pallas_call | solution.py:172
  710.0 9.7 %unrotate.1 = bf16[2048,768]{1,0:T(8,128)(2,1)} custom-call(s32[8]{0:T(128)} %stack.63.order_ref, f32[2048,256]{1,0:T(8,128)} %get-tuple-element.48.dquery_ref, f32[2048,256]{1,0:T(8,128)} %get-tuple-element.49.dkey_ref, f32[2048,256]{1,0:T(8,128)} %get-tuple-element.50.dvalue_ref, f32[2048,256]{1,0:T(8,128)} %get-tuple-element.97.cosine_ref, ...), custom_call_target="tpu_custom_call" | custom-call | flops 10485760 | bytes 9437184 | tf_op jit(solution)/shard_map/unrotate/pallas_call | solution.py:283
  740.4 10.7 %convolution_convert_fusion = bf16[2048,768]{1,0:T(8,128)(2,1)} fusion(bf16[2048,2048]{1,0:T(8,128)(2,1)} %constant_dynamic-update-slice_fusion.6, bf16[2048,768]{1,0:T(8,128)(2,1)S(1)} %copy-done.17), kind=kOutput, calls=%fused_computation.31 | convolution fusion | flops 6444023808 | bytes 14680064 | tf_op jit(solution)/shard_map/dot_general | solution.py:19
  754.3 9.3 %collective-permute-done.53 = bf16[256,2048]{1,0:T(8,128)(2,1)} collective-permute-done((bf16[256,2048]{1,0:T(8,128)(2,1)}, bf16[256,2048]{1,0:T(8,128)(2,1)}, u32[]{:S(2)}, u32[]{:S(2)}) %collective-permute-start.53) | collective-permute-done | bytes 1048608 | tf_op jit(solution)/shard_map/ppermute | solution.py:340
  772.3 18.9 %collective-permute-done.54 = bf16[256,2048]{1,0:T(8,128)(2,1)S(1)} collective-permute-done((bf16[256,2048]{1,0:T(8,128)(2,1)S(1)}, bf16[256,2048]{1,0:T(8,128)(2,1)S(1)}, u32[]{:S(2)}, u32[]{:S(2)}) %collective-permute-start.54) | collective-permute-done | bytes 1048608 | tf_op jit(solution)/shard_map/ppermute | solution.py:340
  795.3 21.2 %collective-permute-done.55 = bf16[256,2048]{1,0:T(8,128)(2,1)S(1)} collective-permute-done((bf16[256,2048]{1,0:T(8,128)(2,1)S(1)}, bf16[256,2048]{1,0:T(8,128)(2,1)S(1)}, u32[]{:S(2)}, u32[]{:S(2)}) %collective-permute-start.55) | collective-permute-done | bytes 1048608 | tf_op jit(solution)/shard_map/ppermute | solution.py:340
  (445 shorter events, 390.8 us)
Async XLA Ops:
  7.2 92.1 %all-gather.6.cloned.1.call-start = ((), (), s32[]{:S(2)}) async-start(), calls=%async_computation.5 | async-start | bytes 3932160 | tf_op jit(solution)/shard_map/all_gather | solution.py:364
  9.4 131.0 %all-gather.8.cloned.1.call-start = ((), (), s32[]{:S(2)}) async-start(), calls=%async_computation.6 | async-start | bytes 1310720 | tf_op jit(solution)/shard_map/all_gather | solution.py:365
  10.2 291.0 %all-gather.12.cloned.1.call-start = ((), (), s32[]{:S(2)}) async-start(), calls=%async_computation.8 | async-start | bytes 5242880 | tf_op jit(solution)/shard_map/all_gather | solution.py:367
  10.9 296.1 %all-gather.10.cloned.1.call-start = ((), (), s32[]{:S(2)}) async-start(), calls=%async_computation.7 | async-start | bytes 5242880 | tf_op jit(solution)/shard_map/all_gather | solution.py:366
  43.0 269.9 %all-gather.14.cloned.1.call-start = ((), (), s32[]{:S(2)}) async-start(), calls=%async_computation.9 | async-start | bytes 5242880 | tf_op jit(solution)/shard_map/all_gather | solution.py:368
  68.9 39.1 %collective-permute-start.5 = (bf16[256,2048]{1,0:T(8,128)(2,1)}, bf16[256,2048]{1,0:T(8,128)(2,1)}, u32[]{:S(2)}, u32[]{:S(2)}) collective-permute-start(bf16[256,2048]{1,0:T(8,128)(2,1)} %collective-permute-done.same_ref), channel_id=1, source_target_pairs={{0,1},{1,0},{2,3},{3,2},{4,5},{5,4},{6,7},{7,6},{8,9},{9,8},{10,11... | collective-permute-start | bytes 3145736 | tf_op jit(solution)/shard_map/ppermute | solution.py:324
  71.8 43.1 %collective-permute-start.4 = (bf16[256,2048]{1,0:T(8,128)(2,1)}, bf16[256,2048]{1,0:T(8,128)(2,1)}, u32[]{:S(2)}, u32[]{:S(2)}) collective-permute-start(bf16[256,2048]{1,0:T(8,128)(2,1)} %collective-permute-done.1.same_ref), channel_id=1, source_target_pairs={{0,1},{1,0},{2,3},{3,2},{4,5},{5,4},{6,7},{7,6},{8,9},{9,8},{10,11... | collective-permute-start | bytes 3145736 | tf_op jit(solution)/shard_map/ppermute | solution.py:324
  164.2 34.9 %collective-permute-start.11 = (bf16[256,2048]{1,0:T(8,128)(2,1)}, bf16[256,2048]{1,0:T(8,128)(2,1)}, u32[]{:S(2)}, u32[]{:S(2)}) collective-permute-start(bf16[256,2048]{1,0:T(8,128)(2,1)} %add_convert_fusion.15), channel_id=1, source_target_pairs={{0,4},{1,5},{2,0},{3,1},{4,6},{5,7},{6,2},{7,3},{8,12},{9,13},{10,... | collective-permute-start | bytes 3145736 | tf_op jit(solution)/shard_map/ppermute | solution.py:340
  164.4 661.7 %reduce-scatter.14.cloned.1.call-start = ((), (), s32[]{:S(2)}) async-start(), calls=%async_computation.14 | async-start | bytes 5242880 | tf_op jit(solution)/shard_map/reduce_scatter | solution.py:424
  176.7 44.9 %collective-permute-start.31 = (bf16[256,2048]{1,0:T(8,128)(2,1)}, bf16[256,2048]{1,0:T(8,128)(2,1)}, u32[]{:S(2)}, u32[]{:S(2)}) collective-permute-start(bf16[256,2048]{1,0:T(8,128)(2,1)} %collective-permute-done.30), channel_id=1, source_target_pairs={{0,4},{1,5},{2,0},{3,1},{4,6},{5,7},{6,2},{7,3},{8,12},{9,13},{10,... | collective-permute-start | bytes 3145736 | tf_op jit(solution)/shard_map/ppermute | solution.py:329
  189.0 48.9 %collective-permute-start.8 = (bf16[256,2048]{1,0:T(8,128)(2,1)}, bf16[256,2048]{1,0:T(8,128)(2,1)}, u32[]{:S(2)}, u32[]{:S(2)}) collective-permute-start(bf16[256,2048]{1,0:T(8,128)(2,1)} %convolution_convert_fusion.13), channel_id=1, source_target_pairs={{0,1},{1,0},{2,3},{3,2},{4,5},{5,4},{6,7},{7,6},{8,9},{9,8},{10,11... | collective-permute-start | bytes 3145736 | tf_op jit(solution)/shard_map/ppermute | solution.py:324
  202.2 41.9 %collective-permute-start.12 = (bf16[256,2048]{1,0:T(8,128)(2,1)}, bf16[256,2048]{1,0:T(8,128)(2,1)}, u32[]{:S(2)}, u32[]{:S(2)}) collective-permute-start(bf16[256,2048]{1,0:T(8,128)(2,1)} %add_convert_fusion.14), channel_id=1, source_target_pairs={{0,4},{1,5},{2,0},{3,1},{4,6},{5,7},{6,2},{7,3},{8,12},{9,13},{10,... | collective-permute-start | bytes 3145736 | tf_op jit(solution)/shard_map/ppermute | solution.py:340
  202.2 49.8 %collective-permute-start.28 = (bf16[256,2048]{1,0:T(8,128)(2,1)}, bf16[256,2048]{1,0:T(8,128)(2,1)}, u32[]{:S(2)}, u32[]{:S(2)}) collective-permute-start(bf16[256,2048]{1,0:T(8,128)(2,1)} %get-tuple-element.56), channel_id=1, source_target_pairs={{0,1},{1,0},{2,3},{3,2},{4,5},{5,4},{6,7},{7,6},{8,9},{9,8},{10,11... | collective-permute-start | bytes 3145736 | tf_op jit(solution)/shard_map/ppermute | solution.py:324
  204.8 86.2 %collective-permute-start.37 = (bf16[256,2048]{1,0:T(8,128)(2,1)}, bf16[256,2048]{1,0:T(8,128)(2,1)}, u32[]{:S(2)}, u32[]{:S(2)}) collective-permute-start(bf16[256,2048]{1,0:T(8,128)(2,1)} %collective-permute-done.30), channel_id=1, source_target_pairs={{0,1},{1,0},{2,3},{3,2},{4,5},{5,4},{6,7},{7,6},{8,9},{9,8},{10,11... | collective-permute-start | bytes 3145736 | tf_op jit(solution)/shard_map/ppermute | solution.py:324
  221.6 44.9 %collective-permute-start.32 = (bf16[256,2048]{1,0:T(8,128)(2,1)}, bf16[256,2048]{1,0:T(8,128)(2,1)}, u32[]{:S(2)}, u32[]{:S(2)}) collective-permute-start(bf16[256,2048]{1,0:T(8,128)(2,1)} %collective-permute-done.31), channel_id=1, source_target_pairs={{0,4},{1,5},{2,0},{3,1},{4,6},{5,7},{6,2},{7,3},{8,12},{9,13},{10,... | collective-permute-start | bytes 3145736 | tf_op jit(solution)/shard_map/ppermute | solution.py:329
  246.2 42.1 %collective-permute-start.13 = (bf16[256,2048]{1,0:T(8,128)(2,1)S(1)}, bf16[256,2048]{1,0:T(8,128)(2,1)S(1)}, u32[]{:S(2)}, u32[]{:S(2)}) collective-permute-start(bf16[256,2048]{1,0:T(8,128)(2,1)S(1)} %add_convert_fusion.13), channel_id=1, source_target_pairs={{0,4},{1,5},{2,0},{3,1},{4,6},{5,7},{6,2},{7,3},{8,12},{9,13},{10,... | collective-permute-start | bytes 3145736 | tf_op jit(solution)/shard_map/ppermute | solution.py:340
  256.7 38.9 %collective-permute-start.35 = (bf16[256,2048]{1,0:T(8,128)(2,1)}, bf16[256,2048]{1,0:T(8,128)(2,1)S(1)}, u32[]{:S(2)}, u32[]{:S(2)}) collective-permute-start(bf16[256,2048]{1,0:T(8,128)(2,1)} %collective-permute-done.31), channel_id=1, source_target_pairs={{0,1},{1,0},{2,3},{3,2},{4,5},{5,4},{6,7},{7,6},{8,9},{9,8},{10,11... | collective-permute-start | bytes 3145736 | tf_op jit(solution)/shard_map/ppermute | solution.py:324
  324.6 219.2 %collective-permute-start.15 = (bf16[256,2048]{1,0:T(8,128)(2,1)}, bf16[256,2048]{1,0:T(8,128)(2,1)}, u32[]{:S(2)}, u32[]{:S(2)}) collective-permute-start(bf16[256,2048]{1,0:T(8,128)(2,1)} %slice.174), channel_id=1, source_target_pairs={{0,1},{1,0},{2,3},{3,2},{4,5},{5,4},{6,7},{7,6},{8,9},{9,8},{10,11... | collective-permute-start | bytes 3145736 | tf_op jit(solution)/shard_map/ppermute | solution.py:324
  363.4 71.4 %collective-permute-start.24 = (bf16[256,2048]{1,0:T(8,128)(2,1)}, bf16[256,2048]{1,0:T(8,128)(2,1)S(1)}, u32[]{:S(2)}, u32[]{:S(2)}) collective-permute-start(bf16[256,2048]{1,0:T(8,128)(2,1)} %slice.180), channel_id=1, source_target_pairs={{0,1},{1,0},{2,3},{3,2},{4,5},{5,4},{6,7},{7,6},{8,9},{9,8},{10,11... | collective-permute-start | bytes 3145736 | tf_op jit(solution)/shard_map/ppermute | solution.py:324
  423.4 405.5 %reduce-scatter.12.cloned.1.call-start = ((), (), s32[]{:S(2)}) async-start(), calls=%async_computation.13 | async-start | bytes 5242880 | tf_op jit(solution)/shard_map/reduce_scatter | solution.py:424
  437.4 48.2 %collective-permute-start.39 = (bf16[256,2048]{1,0:T(8,128)(2,1)S(1)}, bf16[256,2048]{1,0:T(8,128)(2,1)}, u32[]{:S(2)}, u32[]{:S(2)}) collective-permute-start(bf16[256,2048]{1,0:T(8,128)(2,1)S(1)} %add_convert_fusion.9), channel_id=1, source_target_pairs={{0,4},{1,5},{2,0},{3,1},{4,6},{5,7},{6,2},{7,3},{8,12},{9,13},{10,... | collective-permute-start | bytes 3145736 | tf_op jit(solution)/shard_map/ppermute | solution.py:340
  446.5 39.1 %collective-permute-start.36 = (bf16[256,2048]{1,0:T(8,128)(2,1)}, bf16[256,2048]{1,0:T(8,128)(2,1)}, u32[]{:S(2)}, u32[]{:S(2)}) collective-permute-start(bf16[256,2048]{1,0:T(8,128)(2,1)} %slice.186), channel_id=1, source_target_pairs={{0,1},{1,0},{2,3},{3,2},{4,5},{5,4},{6,7},{7,6},{8,9},{9,8},{10,11... | collective-permute-start | bytes 3145736 | tf_op jit(solution)/shard_map/ppermute | solution.py:324
  464.0 367.7 %reduce-scatter.10.cloned.1.call-start = ((), (), s32[]{:S(2)}) async-start(), calls=%async_computation.12 | async-start | bytes 5242880 | tf_op jit(solution)/shard_map/reduce_scatter | solution.py:424
  466.6 41.3 %collective-permute-start.26 = (bf16[256,2048]{1,0:T(8,128)(2,1)S(1)}, bf16[256,2048]{1,0:T(8,128)(2,1)S(1)}, u32[]{:S(2)}, u32[]{:S(2)}) collective-permute-start(bf16[256,2048]{1,0:T(8,128)(2,1)S(1)} %add_convert_fusion.11), channel_id=1, source_target_pairs={{0,4},{1,5},{2,0},{3,1},{4,6},{5,7},{6,2},{7,3},{8,12},{9,13},{10,... | collective-permute-start | bytes 3145736 | tf_op jit(solution)/shard_map/ppermute | solution.py:340
  470.2 37.8 %collective-permute-start.20 = (bf16[256,2048]{1,0:T(8,128)(2,1)S(1)}, bf16[256,2048]{1,0:T(8,128)(2,1)S(1)}, u32[]{:S(2)}, u32[]{:S(2)}) collective-permute-start(bf16[256,2048]{1,0:T(8,128)(2,1)S(1)} %copy-done.37), channel_id=1, source_target_pairs={{0,1},{1,0},{2,3},{3,2},{4,5},{5,4},{6,7},{7,6},{8,9},{9,8},{10,11... | collective-permute-start | bytes 3145736 | tf_op jit(solution)/shard_map/ppermute | solution.py:324
  488.4 42.0 %collective-permute-start.40 = (bf16[256,2048]{1,0:T(8,128)(2,1)S(1)}, bf16[256,2048]{1,0:T(8,128)(2,1)S(1)}, u32[]{:S(2)}, u32[]{:S(2)}) collective-permute-start(bf16[256,2048]{1,0:T(8,128)(2,1)S(1)} %add_convert_fusion.8), channel_id=1, source_target_pairs={{0,4},{1,5},{2,0},{3,1},{4,6},{5,7},{6,2},{7,3},{8,12},{9,13},{10,... | collective-permute-start | bytes 3145736 | tf_op jit(solution)/shard_map/ppermute | solution.py:340
  488.5 42.0 %collective-permute-start.34 = (bf16[256,2048]{1,0:T(8,128)(2,1)S(1)}, bf16[256,2048]{1,0:T(8,128)(2,1)S(1)}, u32[]{:S(2)}, u32[]{:S(2)}) collective-permute-start(bf16[256,2048]{1,0:T(8,128)(2,1)S(1)} %slice.184), channel_id=1, source_target_pairs={{0,1},{1,0},{2,3},{3,2},{4,5},{5,4},{6,7},{7,6},{8,9},{9,8},{10,11... | collective-permute-start | bytes 3145736 | tf_op jit(solution)/shard_map/ppermute | solution.py:324
  508.0 35.9 %collective-permute-start.29 = (bf16[256,2048]{1,0:T(8,128)(2,1)}, bf16[256,2048]{1,0:T(8,128)(2,1)S(1)}, u32[]{:S(2)}, u32[]{:S(2)}) collective-permute-start(bf16[256,2048]{1,0:T(8,128)(2,1)} %slice.182), channel_id=1, source_target_pairs={{0,1},{1,0},{2,3},{3,2},{4,5},{5,4},{6,7},{7,6},{8,9},{9,8},{10,11... | collective-permute-start | bytes 3145736 | tf_op jit(solution)/shard_map/ppermute | solution.py:324
  509.5 43.5 %collective-permute-start.27 = (bf16[256,2048]{1,0:T(8,128)(2,1)}, bf16[256,2048]{1,0:T(8,128)(2,1)}, u32[]{:S(2)}, u32[]{:S(2)}) collective-permute-start(bf16[256,2048]{1,0:T(8,128)(2,1)} %add_convert_fusion.10), channel_id=1, source_target_pairs={{0,4},{1,5},{2,0},{3,1},{4,6},{5,7},{6,2},{7,3},{8,12},{9,13},{10,... | collective-permute-start | bytes 3145736 | tf_op jit(solution)/shard_map/ppermute | solution.py:340
  531.9 43.3 %collective-permute-start.41 = (bf16[256,2048]{1,0:T(8,128)(2,1)}, bf16[256,2048]{1,0:T(8,128)(2,1)}, u32[]{:S(2)}, u32[]{:S(2)}) collective-permute-start(bf16[256,2048]{1,0:T(8,128)(2,1)} %add_convert_fusion.7), channel_id=1, source_target_pairs={{0,4},{1,5},{2,0},{3,1},{4,6},{5,7},{6,2},{7,3},{8,12},{9,13},{10,... | collective-permute-start | bytes 3145736 | tf_op jit(solution)/shard_map/ppermute | solution.py:340
  543.8 290.7 %reduce-scatter.8.cloned.1.call-start = ((), (), s32[]{:S(2)}) async-start(), calls=%async_computation.11 | async-start | bytes 1310720 | tf_op jit(solution)/shard_map/reduce_scatter | solution.py:424
  734.1 112.7 %reduce-scatter.6.cloned.1.call-start = ((), (), s32[]{:S(2)}) async-start(), calls=%async_computation.10 | async-start | bytes 3932160 | tf_op jit(solution)/shard_map/reduce_scatter | solution.py:424
  (123 other events, 2040.7 us)
Sparse Core Ops, SparseCore 0:
  10.4 46.6 all-gather.5
  59.0 26.5 all-gather.7
  87.4 52.7 all-gather.11
  141.8 52.6 all-gather.9
  196.2 52.5 all-gather.13
  423.6 53.0 reduce-scatter.13
  479.9 52.6 reduce-scatter.11
  543.9 54.9 reduce-scatter.9
  734.2 28.4 reduce-scatter.7
  765.5 43.9 reduce-scatter.5

commit v2 on v1

--- a/solution.py
+++ b/solution.py
@@ -294,6 +294,231 @@
     )(order, dquery, dkey, dvalue, cosine, sine)
 
 
+def chip_at(place, chips):
+    return jnp.where(2 * place < chips, 2 * place, 2 * (chips - 1 - place) + 1)
+
+
+def place_of(chip, chips):
+    return jnp.where(chip % 2 == 0, chip // 2, chips - 1 - chip // 2)
+
+
+def remote(source, target, send, receive, device):
+    return pltpu.make_async_remote_copy(
+        src_ref=source, dst_ref=target, send_sem=send, recv_sem=receive,
+        device_id={"tp": device}, device_id_type=pl.DeviceIdType.MESH,
+    )
+
+
+def greet(devices):
+    barrier = pltpu.get_barrier_semaphore()
+    for device in devices:
+        pl.semaphore_signal(barrier, inc=1, device_id={"tp": device}, device_id_type=pl.DeviceIdType.MESH)
+    pl.semaphore_wait(barrier, len(devices))
+
+
+def feed_kernel(
+    chips,
+    tokens_ref, grads_hbm, gate_hbm, up_hbm, down_hbm,
+    back_ref, tokens_out, inner_out, gate_out, up_out,
+    tokens_all, gate_w, up_w, down_w, grads, inner, gate_grad, up_grad, own, term, stage, from_core, from_ring, total,
+    load_sem, grad_sem, keep_sem, store_sem, ring_send, ring_recv, core_send, core_recv, stage_send, stage_recv, total_send, total_recv,
+):
+    rows, depth = tokens_ref.shape
+    pair = 2 * rows
+    hidden = gate_w.shape[1]
+    me = lax.axis_index("tp")
+    chip, core = me // 2, me % 2
+    place = place_of(chip, chips)
+    following = 2 * chip_at((place + 1) % chips, chips) + core
+    before = 2 * chip_at((place + chips - 1) % chips, chips) + core
+    partner = 2 * chip + 1 - core
+
+    loads = [pltpu.make_async_copy(a, b, load_sem.at[i]) for i, (a, b) in enumerate(((gate_hbm, gate_w), (up_hbm, up_w), (down_hbm, down_w)))]
+    for load in loads:
+        load.start()
+
+    def source(slot):
+        return chip_at((place + chips - slot) % chips, chips)
+
+    def fetch(slot):
+        start = pl.multiple_of(source(slot) * pair, pair)
+        return pltpu.make_async_copy(grads_hbm.at[pl.ds(start, pair)], grads.at[slot % 2], grad_sem.at[slot % 2])
+
+    def block(ref, index):
+        return ref.at[pl.ds(pl.multiple_of(index * rows, rows), rows)]
+
+    def to_ring(slot):
+        index = 2 * source(slot) + core
+        return remote(block(tokens_all, index), block(tokens_all, index), ring_send.at[slot], ring_recv.at[slot], following)
+
+    def to_core(slot):
+        index = 2 * source(slot) + core
+        return remote(block(tokens_all, index), block(tokens_all, index), core_send.at[slot], core_recv.at[slot], partner)
+
+    def keep(slot):
+        start = pl.multiple_of(source(slot) * pair, pair)
+        span = pl.ds(start, pair)
+        return pltpu.make_async_copy(tokens_all.at[span], tokens_out.at[span], keep_sem.at[slot])
+
+    def stores(slot):
+        span = pl.ds(pl.multiple_of(source(slot) * pair, pair), pair)
+        return [
+            pltpu.make_async_copy(ref.at[slot % 2], out.at[span], store_sem.at[i, slot % 2])
+            for i, (ref, out) in enumerate(((inner, inner_out), (gate_grad, gate_out), (up_grad, up_out)))
+        ]
+
+    def stage_copy(slot):
+        return remote(stage.at[slot % 2], from_core.at[slot], stage_send.at[slot % 2], stage_recv.at[slot], partner)
+
+    def total_copy(slot):
+        return remote(total.at[slot - 1], from_ring.at[slot - 1], total_send.at[slot - 1], total_recv.at[slot - 1], following)
+
+    fetch(0).start()
+    tokens_all[pl.ds(pl.multiple_of(me * rows, rows), rows), :] = tokens_ref[...]
+    greet((following, before, partner))
+
+    def step(slot, carry):
+        @pl.when(slot > 0)
+        def _():
+            to_ring(slot - 1).wait_recv()
+
+        @pl.when(slot < chips - 1)
+        def _():
+            to_ring(slot).start()
+            fetch(slot + 1).start()
+
+        to_core(slot).start()
+
+        @pl.when(slot == 0)
+        def _():
+            for load in loads:
+                load.wait()
+
+        @pl.when(slot > 1)
+        def _():
+            for store in stores(slot - 2):
+                store.wait()
+
+        to_core(slot).wait_recv()
+        keep(slot).start()
+        fetch(slot).wait()
+        here = slot % 2
+        span = pl.ds(pl.multiple_of(source(slot) * pair, pair), pair)
+
+        def narrow(tile, carry):
+            columns = pl.ds(pl.multiple_of(tile * 256, 256), 256)
+            token = tokens_all[span, :]
+            gate = dot(token, gate_w[:, columns])
+            up = dot(token, up_w[:, columns])
+            grad = dot(grads[here], down_w[columns, :], NT)
+            squash = jax.nn.sigmoid(gate)
+            act = gate * squash
+            inner[here, :, columns] = (act * up).astype(jnp.bfloat16)
+            up_grad[here, :, columns] = (grad * act).astype(jnp.bfloat16)
+            gate_grad[here, :, columns] = (grad * up * squash * (1.0 + gate * (1.0 - squash))).astype(jnp.bfloat16)
+            return carry
+
+        lax.fori_loop(0, hidden // 256, narrow, 0)
+        for store in stores(slot):
+            store.start()
+
+        @pl.when(slot > 1)
+        def _():
+            stage_copy(slot - 2).wait_send()
+
+        def wide(tile, carry):
+            columns = pl.ds(pl.multiple_of(tile * 256, 256), 256)
+            part = dot(gate_grad[here], gate_w[columns, :], NT) + dot(up_grad[here], up_w[columns, :], NT)
+            term[:, columns] = part.astype(jnp.bfloat16)
+            return carry
+
+        lax.fori_loop(0, depth // 256, wide, 0)
+        stage[here] = term[pl.ds(pl.multiple_of((1 - core) * rows, rows), rows), :]
+        stage_copy(slot).start()
+        mine = pl.ds(pl.multiple_of(core * rows, rows), rows)
+
+        @pl.when(slot == 0)
+        def _():
+            own[...] = term[mine, :].astype(jnp.float32)
+
+        @pl.when(slot > 0)
+        def _():
+            stage_copy(slot).wait_recv()
+
+        @pl.when(slot == 1)
+        def _():
+            total[slot - 1] = (term[mine, :].astype(jnp.float32) + from_core[slot].astype(jnp.float32)).astype(jnp.bfloat16)
+
+        @pl.when(slot > 1)
+        def _():
+            total_copy(slot - 1).wait_recv()
+            total[slot - 1] = (term[mine, :].astype(jnp.float32) + from_core[slot].astype(jnp.float32) + from_ring[slot - 2].astype(jnp.float32)).astype(jnp.bfloat16)
+
+        @pl.when(slot > 0)
+        def _():
+            total_copy(slot).start()
+
+        return carry
+
+    lax.fori_loop(0, chips, step, 0)
+    stage_copy(0).wait_recv()
+    total_copy(chips - 1).wait_recv()
+    back_ref[...] = own[...] + from_core[0].astype(jnp.float32) + from_ring[chips - 2].astype(jnp.float32)
+    for slot in range(chips):
+        to_core(slot).wait_send()
+        keep(slot).wait()
+        if slot < chips - 1:
+            to_ring(slot).wait_send()
+        if slot > 0:
+            total_copy(slot).wait_send()
+        if slot >= chips - 2:
+            stage_copy(slot).wait_send()
+            for store in stores(slot):
+                store.wait()
+
+
+def feed(chips, tokens, grads, gate_w, up_w, down_w):
+    rows, depth = tokens.shape
+    pair = 2 * rows
+    group_rows = chips * pair
+    hidden = gate_w.shape[1]
+    low = jnp.bfloat16
+    anywhere = pl.BlockSpec(memory_space=pl.ANY)
+    vmem = pl.BlockSpec(memory_space=pltpu.VMEM)
+    dma = pltpu.SemaphoreType.DMA
+    return pl.pallas_call(
+        lambda *refs: feed_kernel(chips, *refs),
+        in_specs=[vmem] + [anywhere] * 4,
+        out_specs=[vmem] + [anywhere] * 4,
+        out_shape=[
+            jax.ShapeDtypeStruct((rows, depth), jnp.float32),
+            jax.ShapeDtypeStruct((group_rows, depth), low),
+        ] + [jax.ShapeDtypeStruct((group_rows, hidden), low)] * 3,
+        scratch_shapes=[
+            pltpu.VMEM((group_rows, depth), low),
+            pltpu.VMEM(gate_w.shape, low),
+            pltpu.VMEM(up_w.shape, low),
+            pltpu.VMEM(down_w.shape, low),
+            pltpu.VMEM((2, pair, depth), low),
+            pltpu.VMEM((2, pair, hidden), low),
+            pltpu.VMEM((2, pair, hidden), low),
+            pltpu.VMEM((2, pair, hidden), low),
+            pltpu.VMEM((rows, depth), jnp.float32),
+            pltpu.VMEM((pair, depth), low),
+            pltpu.VMEM((2, rows, depth), low),
+            pltpu.VMEM((chips, rows, depth), low),
+            pltpu.VMEM((chips - 1, rows, depth), low),
+            pltpu.VMEM((chips - 1, rows, depth), low),
+            dma((3,)), dma((2,)), dma((chips,)), dma((3, 2)),
+            dma((chips,)), dma((chips,)), dma((chips,)), dma((chips,)),
+            dma((2,)), dma((chips,)), dma((chips - 1,)), dma((chips - 1,)),
+        ],
+        compiler_params=pltpu.CompilerParams(collective_id=3, has_side_effects=True, vmem_limit_bytes=63 << 20),
+        cost_estimate=pl.CostEstimate(flops=12 * group_rows * depth * hidden, bytes_accessed=10 * group_rows * depth, transcendentals=group_rows * hidden),
+        name="feed",
+    )(tokens, grads, gate_w, up_w, down_w)
+
+
 def rms_norm(values, gain):
     return values * lax.rsqrt(jnp.mean(values * values, axis=-1, keepdims=True) + norm_eps) * gain
 
@@ -367,6 +592,7 @@
         full_up = lax.all_gather(w_up, "fsdp", axis=0, tiled=True)
         full_down = lax.all_gather(w_down, "fsdp", axis=1, tiled=True)
         cosine, sine = rope_tables(width)
+        starts = [source * pair for source in ring.sources]
         places = [jnp.stack([core, source]) for source in ring.sources]
         order = jnp.stack([2 * source + part for source in ring.sources for part in (core, 1 - core)])
 
@@ -389,32 +615,20 @@
         attn_branch = ring.scatter(attention_part)
         hidden_state = activations + attn_branch
         normed_mlp = rms_norm(hidden_state, gain_mlp).astype(jnp.bfloat16)
-        seen_mlp = ring.gather(normed_mlp)
-        mlp = {}
-
-        def mlp_part(slot):
-            tokens = jnp.concatenate(seen_mlp[slot], axis=0)
-            grads = jnp.concatenate(seen_grad[slot], axis=0)
-            gate = dot(tokens, full_gate)
-            up = dot(tokens, full_up)
-            act, pull = jax.vjp(lambda g, u: jax.nn.silu(g) * u, gate, up)
-            gate_grad, up_grad = pull(dot(grads, full_down, NT))
-            gate_grad = gate_grad.astype(jnp.bfloat16)
-            up_grad = up_grad.astype(jnp.bfloat16)
-            mlp[slot] = (tokens, grads, act.astype(jnp.bfloat16), gate_grad, up_grad)
-            back = (dot(gate_grad, full_gate, NT) + dot(up_grad, full_up, NT)).astype(jnp.bfloat16)
-            return back[:rows], back[rows:]
-
-        normed_mlp_grad = ring.scatter(mlp_part)
+        all_grads = jnp.zeros((group_rows, activations.shape[1]), jnp.bfloat16)
+        for slot, (same, other) in enumerate(seen_grad):
+            all_grads = lax.dynamic_update_slice_in_dim(all_grads, same, starts[slot] + core * rows, 0)
+            all_grads = lax.dynamic_update_slice_in_dim(all_grads, other, starts[slot] + (1 - core) * rows, 0)
+        normed_mlp_grad, all_tokens, inner, gate_grad, up_grad = feed(chips, normed_mlp, all_grads, full_gate, full_up, full_down)
+        down = dot(inner, full_down).astype(jnp.bfloat16)
 
         def down_part(slot):
-            part = dot(mlp[slot][2], full_down).astype(jnp.bfloat16)
-            return part[:rows], part[rows:]
+            return (
+                lax.dynamic_slice_in_dim(down, starts[slot] + core * rows, rows, 0),
+                lax.dynamic_slice_in_dim(down, starts[slot] + (1 - core) * rows, rows, 0),
+            )
 
         output = hidden_state + ring.scatter(down_part)
-        all_tokens, all_grads, inner, gate_grad, up_grad = [
-            jnp.concatenate([mlp[slot][item] for slot in range(chips)], axis=0) for item in range(5)
-        ]
         _, pull_norm_mlp = jax.vjp(rms_norm, hidden_state, gain_mlp)
         hidden_norm_grad, gain_mlp_part = pull_norm_mlp(normed_mlp_grad)
         hidden_grad = cotangent + hidden_norm_grad

time: 867 us -> 836 us (0.964)
  Pallas kernels: 141 us -> 274 us
  matrix products: 191 us -> 113 us
  waiting for transfers between devices: 313 us -> 239 us
  local copies, waits for them, and re-layouts: 85.2 us -> 73.5 us
    pallas_call x0 -> x1, Pallas kernels: none -> 142 us  [feed(): pl.pallas_call(lambda *refs: feed_kernel(chips, *refs), in_specs=[vmem] +...]
    dot_general x49 -> x26, matrix products: 191 us -> 113 us  [dot(): lax.dot_general(left, right, dims, preferred_element_type=jnp.float32)]
    ppermute x12 -> x9, waiting for transfers between devices: 144 us -> 95.9 us  [gather(): lax.ppermute(block, 'tp', self.forward)]
    ppermute x12 -> x9, waiting for transfers between devices: 160 us -> 132 us  [scatter(): term = term + lax.ppermute(total, 'tp', self.forward).astype(jnp.float32)]
    unnamed x194 -> x100, local copies, waits for them, and re-layouts: 57 us -> 36.5 us
    dynamic_update_slice x0 -> x7, local copies, waits for them, and re-layouts: none -> 16.4 us  [the longest x4 9.32 us: body(): lax.dynamic_update_slice_in_dim(all_grads, other, starts[slot] + (1 - cor...]
    pallas_call x4, Pallas kernels: 45.4 us -> 36 us  [attend(): pl.pallas_call(attend_kernel, grid_spec=pltpu.PrefetchScalarGridSpec(num_...]
    ppermute x12 -> x9, starting transfers between devices: 17.4 us -> 23.1 us  [gather(): lax.ppermute(block, 'tp', self.forward)]
  transfers between devices with their start and end apart: 71 -> 57, of which waited for: 26 -> 20; matrix products, arithmetic and copies ran while one was open for 38% -> 26% of each run, Pallas kernels for 17% -> 16%
where the time goes in v2:
time: 836 us; the launch traced here: 827 us
  Pallas kernels  274 us (33%)
  waiting for transfers between devices  239 us (29%)
  matrix products  113 us (14%)
  local copies, waits for them, and re-layouts  73.5 us (9%)
  starting transfers between devices  56.9 us (7%)
  other arithmetic  52.1 us (6%)
  between operations  18.9 us (2%)
    pallas_call x1, Pallas kernels, feed(): pl.pallas_call(lambda *refs: feed_kernel(chips, *refs), in_specs=[vmem] +...  142 us
    ppermute x9, waiting for transfers between devices, scatter(): term = term + lax.ppermute(total, 'tp', self.forward).astype(jnp.float32)  132 us
    dot_general x26, matrix products, dot(): lax.dot_general(left, right, dims, preferred_element_type=jnp.float32)  113 us
    ppermute x9, waiting for transfers between devices, gather(): lax.ppermute(block, 'tp', self.forward)  95.9 us
    pallas_call x4, Pallas kernels, attend_back(): pl.pallas_call(attend_back_kernel, grid_spec=pltpu.PrefetchScalarGridSpec...  59 us
    unnamed x100, local copies, waits for them, and re-layouts  36.5 us
    pallas_call x4, Pallas kernels, attend(): pl.pallas_call(attend_kernel, grid_spec=pltpu.PrefetchScalarGridSpec(num_...  36 us
    pallas_call x4, Pallas kernels, project(): pl.pallas_call(project_kernel, grid_spec=pltpu.PrefetchScalarGridSpec(num...  27.5 us
  transfers between devices with their start and end apart: 57, of which 20 were waited for; matrix products, arithmetic and copies ran while one was open for 26% of the time, Pallas kernels for 16%

profile of v2, /device:TPU:0, one launch (start us, length us, event | category | flops | bytes accessed | tf_op | source)
XLA Modules:
  0.0 827.0 jit_solution(1537072987718703861)
XLA Ops:
  17.7 22.4 %collective-permute-done.same_ref = bf16[256,2048]{1,0:T(8,128)(2,1)} collective-permute-done((bf16[256,2048]{1,0:T(8,128)(2,1)S(1)}, bf16[256,2048]{1,0:T(8,128)(2,1)}, u32[]{:S(2)}, u32[]{:S(2)}) %collective-permute-start) | collective-permute-done | bytes 1048608 | tf_op jit(solution)/shard_map/ppermute | solution.py:554
  43.6 21.9 %collective-permute-done.1.same_ref = bf16[256,2048]{1,0:T(8,128)(2,1)} collective-permute-done((bf16[256,2048]{1,0:T(8,128)(2,1)}, bf16[256,2048]{1,0:T(8,128)(2,1)}, u32[]{:S(2)}, u32[]{:S(2)}) %collective-permute-start.1) | collective-permute-done | bytes 1048608 | tf_op jit(solution)/shard_map/ppermute | solution.py:554
  79.9 12.9 %collective-permute-done.2.same_ref = bf16[256,2048]{1,0:T(8,128)(2,1)} collective-permute-done((bf16[256,2048]{1,0:T(8,128)(2,1)}, bf16[256,2048]{1,0:T(8,128)(2,1)}, u32[]{:S(2)}, u32[]{:S(2)}) %collective-permute-start.2) | collective-permute-done | bytes 1048608 | tf_op jit(solution)/shard_map/ppermute | solution.py:554
  93.9 8.8 %multiply_sine_fusion = (f32[2048,256]{1,0:T(8,128)}, f32[2048,256]{1,0:T(8,128)}) fusion(f32[256]{0:T(256)S(1)} %fusion.43, f32[2048]{0:T(1024)S(1)} %iota_convert_fusion), kind=kLoop, calls=%fused_computation.7 | loop fusion | flops 524288 | bytes 4203520 | tf_op jit(solution)/shard_map/sin | solution.py:532
  104.6 6.8 project.4.out_in
  111.4 7.0 project.5.out_in
  136.1 7.9 attend.7
  148.2 12.6 %attend.6 = (bf16[2,256,256]{2,1,0:T(8,128)(2,1)}, f32[4,512]{1,0:T(4,128)}) custom-call(s32[2]{0:T(128)} %get-tuple-element.89.place_ref, bf16[2048,768]{1,0:T(8,128)(2,1)} %project.7.query_ref.keys_ref.values_ref, bf16[2048,768]{1,0:T(8,128)(2,1)} %project.7.query_ref.keys_ref.values_ref, bf16[256,2048]{1,0:T(8,128)(2,1)} %bitcast.106), custom_call_target="tpu_custom_call" | custom-call | flops 1073741824 | bytes 2621440 | tf_op jit(solution)/shard_map/attend/pallas_call | solution.py:82
  166.4 12.2 %collective-permute-done.17 = bf16[256,2048]{1,0:T(8,128)(2,1)} collective-permute-done((bf16[256,2048]{1,0:T(8,128)(2,1)}, bf16[256,2048]{1,0:T(8,128)(2,1)}, u32[]{:S(2)}, u32[]{:S(2)}) %collective-permute-start.17) | collective-permute-done | bytes 1048608 | tf_op jit(solution)/shard_map/ppermute | solution.py:554
  178.6 10.0 %attend.5 = (bf16[2,256,256]{2,1,0:T(8,128)(2,1)}, f32[4,512]{1,0:T(4,128)}) custom-call(s32[2]{0:T(128)} %pad_add_fusion.1.place_ref, bf16[2048,768]{1,0:T(8,128)(2,1)} %project.7.query_ref.keys_ref.values_ref, bf16[2048,768]{1,0:T(8,128)(2,1)} %project.7.query_ref.keys_ref.values_ref, bf16[256,2048]{1,0:T(8,128)(2,1)} %bitcast.107), custom_call_target="tpu_custom_call" | custom-call | flops 1073741824 | bytes 2621440 | tf_op jit(solution)/shard_map/attend/pallas_call | solution.py:82
  191.0 10.1 %collective-permute-done.11 = bf16[256,2048]{1,0:T(8,128)(2,1)} collective-permute-done((bf16[256,2048]{1,0:T(8,128)(2,1)}, bf16[256,2048]{1,0:T(8,128)(2,1)}, u32[]{:S(2)}, u32[]{:S(2)}) %collective-permute-start.11) | collective-permute-done | bytes 1048608 | tf_op jit(solution)/shard_map/ppermute | solution.py:565
  211.8 11.8 %collective-permute-done.19 = bf16[256,2048]{1,0:T(8,128)(2,1)} collective-permute-done((bf16[256,2048]{1,0:T(8,128)(2,1)}, bf16[256,2048]{1,0:T(8,128)(2,1)}, u32[]{:S(2)}, u32[]{:S(2)}) %collective-permute-start.19) | collective-permute-done | bytes 1048608 | tf_op jit(solution)/shard_map/ppermute | solution.py:554
  231.0 14.4 %collective-permute-done.12 = bf16[256,2048]{1,0:T(8,128)(2,1)} collective-permute-done((bf16[256,2048]{1,0:T(8,128)(2,1)}, bf16[256,2048]{1,0:T(8,128)(2,1)}, u32[]{:S(2)}, u32[]{:S(2)}) %collective-permute-start.12) | collective-permute-done | bytes 1048608 | tf_op jit(solution)/shard_map/ppermute | solution.py:565
  259.3 13.4 %collective-permute-done.13 = bf16[256,2048]{1,0:T(8,128)(2,1)S(1)} collective-permute-done((bf16[256,2048]{1,0:T(8,128)(2,1)S(1)}, bf16[256,2048]{1,0:T(8,128)(2,1)S(1)}, u32[]{:S(2)}, u32[]{:S(2)}) %collective-permute-start.13) | collective-permute-done | bytes 1048608 | tf_op jit(solution)/shard_map/ppermute | solution.py:565
  276.1 142.2 %feed.1 = (f32[256,2048]{1,0:T(8,128)}, bf16[2048,2048]{1,0:T(8,128)(2,1)}, bf16[2048,1024]{1,0:T(8,128)(2,1)}, bf16[2048,1024]{1,0:T(8,128)(2,1)}, bf16[2048,1024]{1,0:T(8,128)(2,1)}) custom-call(bf16[256,2048]{1,0:T(8,128)(2,1)} %multiply_convert_fusion.refs_0_, bf16[2048,2048]{1,0:T(8,128)(2,1)} %constant_dynamic-update-slice_fusion.16.refs_1_, ...), custom_call_target="tpu_custom_call" | custom-call | flops 51539607552 | bytes 41943040 | tf_op jit(solution)/shard_map/feed/pallas_call | solution.py:489
  418.3 14.1 %convolution_convert_fusion.1 = bf16[1024,2048]{1,0:T(8,128)(2,1)} fusion(bf16[2048,1024]{1,0:T(8,128)(2,1)} %get-tuple-element.40, bf16[2048,2048]{1,0:T(8,128)(2,1)} %constant_dynamic-update-slice_fusion.16.refs_1_), kind=kOutput, calls=%fused_computation.1 | convolution fusion | flops 8592031744 | bytes 16777216 | tf_op jit(solution)/shard_map/dot_general | solution.py:19
  432.7 14.0 %convolution_convert_fusion.3 = bf16[2048,1024]{1,0:T(8,128)(2,1)} fusion(bf16[2048,2048]{1,0:T(8,128)(2,1)} %get-tuple-element.58, bf16[2048,1024]{1,0:T(8,128)(2,1)} %get-tuple-element.59), kind=kOutput, calls=%fused_computation.3 | convolution fusion | flops 8592031744 | bytes 16777216 | tf_op jit(solution)/shard_map/dot_general | solution.py:19
  446.7 12.2 %convolution_convert_fusion = bf16[2048,2048]{1,0:T(8,128)(2,1)S(1)} fusion(bf16[2048,1024]{1,0:T(8,128)(2,1)} %get-tuple-element.40, bf16[1024,2048]{1,0:T(8,128)(2,1)} %all-gather.14.cloned.1.call-done.refs_4_), kind=kOutput, calls=%fused_computation | convolution fusion | flops 8594128896 | bytes 16777216 | tf_op jit(solution)/shard_map/dot_general | solution.py:19
  466.1 22.7 %collective-permute-done.25 = bf16[256,2048]{1,0:T(8,128)(2,1)S(1)} collective-permute-done((bf16[256,2048]{1,0:T(8,128)(2,1)S(1)}, bf16[256,2048]{1,0:T(8,128)(2,1)S(1)}, u32[]{:S(2)}, u32[]{:S(2)}) %collective-permute-start.25) | collective-permute-done | bytes 1048608 | tf_op jit(solution)/shard_map/ppermute | solution.py:565
  503.3 13.3 %collective-permute-done.26 = bf16[256,2048]{1,0:T(8,128)(2,1)} collective-permute-done((bf16[256,2048]{1,0:T(8,128)(2,1)}, bf16[256,2048]{1,0:T(8,128)(2,1)}, u32[]{:S(2)}, u32[]{:S(2)}) %collective-permute-start.26) | collective-permute-done | bytes 1048608 | tf_op jit(solution)/shard_map/ppermute | solution.py:565
  522.6 12.9 %convolution_convert_fusion.2 = bf16[2048,1024]{1,0:T(8,128)(2,1)} fusion(bf16[2048,2048]{1,0:T(8,128)(2,1)} %get-tuple-element.58, bf16[2048,1024]{1,0:T(8,128)(2,1)S(1)} %copy-done.40), kind=kOutput, calls=%fused_computation.2 | convolution fusion | flops 8592031744 | bytes 16777216 | tf_op jit(solution)/shard_map/dot_general | solution.py:19
  535.6 9.2 %collective-permute-done.27 = bf16[256,2048]{1,0:T(8,128)(2,1)} collective-permute-done((bf16[256,2048]{1,0:T(8,128)(2,1)}, bf16[256,2048]{1,0:T(8,128)(2,1)}, u32[]{:S(2)}, u32[]{:S(2)}) %collective-permute-start.27) | collective-permute-done | bytes 1048608 | tf_op jit(solution)/shard_map/ppermute | solution.py:565
  566.6 12.1 %collective-permute-done.28 = bf16[256,2048]{1,0:T(8,128)(2,1)} collective-permute-done((bf16[256,2048]{1,0:T(8,128)(2,1)S(1)}, bf16[256,2048]{1,0:T(8,128)(2,1)}, u32[]{:S(2)}, u32[]{:S(2)}) %collective-permute-start.28) | collective-permute-done | bytes 1048608 | tf_op jit(solution)/shard_map/ppermute | solution.py:554
  592.6 10.7 %attend_back.4 = (f32[2048,256]{1,0:T(8,128)}, f32[2048,256]{1,0:T(8,128)}, f32[2048,256]{1,0:T(8,128)}) custom-call(s32[2]{0:T(128)} %get-tuple-element.88.place_ref, bf16[2048,768]{1,0:T(8,128)(2,1)} %project.7.query_ref.keys_ref.values_ref, ...), custom_call_target="tpu_custom_call", output_to_operand_aliasing={{0}: (9, {}), {1}: (10, {}), {2}: (11, {})} | custom-call | flops 2684354560 | bytes 11534336 | tf_op jit(solution)/shard_map/attend_back/pallas_call | solution.py:172
  617.7 13.1 %attend_back.5 = (f32[2048,256]{1,0:T(8,128)}, f32[2048,256]{1,0:T(8,128)}, f32[2048,256]{1,0:T(8,128)}) custom-call(s32[2]{0:T(128)} %pad_add_fusion.3.place_ref, bf16[2048,768]{1,0:T(8,128)(2,1)} %project.7.query_ref.keys_ref.values_ref, ...), custom_call_target="tpu_custom_call", output_to_operand_aliasing={{0}: (9, {}), {1}: (10, {}), {2}: (11, {})} | custom-call | flops 2684354560 | bytes 11534336 | tf_op jit(solution)/shard_map/attend_back/pallas_call | solution.py:172
  641.6 19.0 %attend_back.6 = (f32[2048,256]{1,0:T(8,128)}, f32[2048,256]{1,0:T(8,128)}, f32[2048,256]{1,0:T(8,128)}) custom-call(s32[2]{0:T(128)} %get-tuple-element.89.place_ref, bf16[2048,768]{1,0:T(8,128)(2,1)} %project.7.query_ref.keys_ref.values_ref, ...), custom_call_target="tpu_custom_call", output_to_operand_aliasing={{0}: (9, {}), {1}: (10, {}), {2}: (11, {})} | custom-call | flops 2684354560 | bytes 11534336 | tf_op jit(solution)/shard_map/attend_back/pallas_call | solution.py:172
  664.0 16.2 %attend_back.7 = (f32[2048,256]{1,0:T(8,128)}, f32[2048,256]{1,0:T(8,128)}, f32[2048,256]{1,0:T(8,128)}) custom-call(s32[2]{0:T(128)} %pad_add_fusion.1.place_ref, bf16[2048,768]{1,0:T(8,128)(2,1)} %project.7.query_ref.keys_ref.values_ref, ...), custom_call_target="tpu_custom_call", output_to_operand_aliasing={{0}: (9, {}), {1}: (10, {}), {2}: (11, {})} | custom-call | flops 2684354560 | bytes 11534336 | tf_op jit(solution)/shard_map/attend_back/pallas_call | solution.py:172
  680.3 9.7 %unrotate.1 = bf16[2048,768]{1,0:T(8,128)(2,1)} custom-call(s32[8]{0:T(128)} %stack.63.order_ref, f32[2048,256]{1,0:T(8,128)} %get-tuple-element.55.dquery_ref, f32[2048,256]{1,0:T(8,128)} %get-tuple-element.56.dkey_ref, f32[2048,256]{1,0:T(8,128)} %get-tuple-element.57.dvalue_ref, f32[2048,256]{1,0:T(8,128)} %get-tuple-element.85.cosine_ref, ...), custom_call_target="tpu_custom_call" | custom-call | flops 10485760 | bytes 9437184 | tf_op jit(solution)/shard_map/unrotate/pallas_call | solution.py:283
  711.1 10.8 %convolution_convert_fusion.4 = bf16[2048,768]{1,0:T(8,128)(2,1)} fusion(bf16[2048,2048]{1,0:T(8,128)(2,1)} %constant_dynamic-update-slice_fusion, bf16[2048,768]{1,0:T(8,128)(2,1)S(1)} %copy-done.18), kind=kOutput, calls=%fused_computation.4 | convolution fusion | flops 6444023808 | bytes 14680064 | tf_op jit(solution)/shard_map/dot_general | solution.py:19
  725.1 9.2 %collective-permute-done.39 = bf16[256,2048]{1,0:T(8,128)(2,1)} collective-permute-done((bf16[256,2048]{1,0:T(8,128)(2,1)}, bf16[256,2048]{1,0:T(8,128)(2,1)}, u32[]{:S(2)}, u32[]{:S(2)}) %collective-permute-start.39) | collective-permute-done | bytes 1048608 | tf_op jit(solution)/shard_map/ppermute | solution.py:565
  743.0 18.9 %collective-permute-done.40 = bf16[256,2048]{1,0:T(8,128)(2,1)S(1)} collective-permute-done((bf16[256,2048]{1,0:T(8,128)(2,1)S(1)}, bf16[256,2048]{1,0:T(8,128)(2,1)S(1)}, u32[]{:S(2)}, u32[]{:S(2)}) %collective-permute-start.40) | collective-permute-done | bytes 1048608 | tf_op jit(solution)/shard_map/ppermute | solution.py:565
  766.0 21.2 %collective-permute-done.41 = bf16[256,2048]{1,0:T(8,128)(2,1)S(1)} collective-permute-done((bf16[256,2048]{1,0:T(8,128)(2,1)S(1)}, bf16[256,2048]{1,0:T(8,128)(2,1)S(1)}, u32[]{:S(2)}, u32[]{:S(2)}) %collective-permute-start.41) | collective-permute-done | bytes 1048608 | tf_op jit(solution)/shard_map/ppermute | solution.py:565
  (294 shorter events, 254.5 us)
Async XLA Ops:
  7.2 95.5 %all-gather.6.cloned.1.call-start = ((), (), s32[]{:S(2)}) async-start(), calls=%async_computation.5 | async-start | bytes 3932160 | tf_op jit(solution)/shard_map/all_gather | solution.py:589
  9.4 134.6 %all-gather.8.cloned.1.call-start = ((), (), s32[]{:S(2)}) async-start(), calls=%async_computation.6 | async-start | bytes 1310720 | tf_op jit(solution)/shard_map/all_gather | solution.py:590
  10.2 265.9 %all-gather.10.cloned.1.call-start = ((), (), s32[]{:S(2)}) async-start(), calls=%async_computation.7 | async-start | bytes 5242880 | tf_op jit(solution)/shard_map/all_gather | solution.py:591
  10.9 265.2 %all-gather.12.cloned.1.call-start = ((), (), s32[]{:S(2)}) async-start(), calls=%async_computation.8 | async-start | bytes 5242880 | tf_op jit(solution)/shard_map/all_gather | solution.py:592
  11.5 264.6 %all-gather.14.cloned.1.call-start = ((), (), s32[]{:S(2)}) async-start(), calls=%async_computation.9 | async-start | bytes 5242880 | tf_op jit(solution)/shard_map/all_gather | solution.py:593
  68.8 33.9 %collective-permute-start.6 = (bf16[256,2048]{1,0:T(8,128)(2,1)S(1)}, bf16[256,2048]{1,0:T(8,128)(2,1)}, u32[]{:S(2)}, u32[]{:S(2)}) collective-permute-start(bf16[256,2048]{1,0:T(8,128)(2,1)S(1)} %get-tuple-element.69.same_ref), channel_id=1, source_target_pairs={{0,1},{1,0},{2,3},{3,2},{4,5},{5,4},{6,7},{7,6},{8,9},{9,8},{10,11... | collective-permute-start | bytes 3145736 | tf_op jit(solution)/shard_map/ppermute | solution.py:549
  74.9 72.3 %collective-permute-start.15 = (bf16[256,2048]{1,0:T(8,128)(2,1)}, bf16[256,2048]{1,0:T(8,128)(2,1)}, u32[]{:S(2)}, u32[]{:S(2)}) collective-permute-start(bf16[256,2048]{1,0:T(8,128)(2,1)} %get-tuple-element.71), channel_id=1, source_target_pairs={{0,4},{1,5},{2,0},{3,1},{4,6},{5,7},{6,2},{7,3},{8,12},{9,13},{10,... | collective-permute-start | bytes 3145736 | tf_op jit(solution)/shard_map/ppermute | solution.py:554
  75.6 35.8 %collective-permute-start.5 = (bf16[256,2048]{1,0:T(8,128)(2,1)}, bf16[256,2048]{1,0:T(8,128)(2,1)}, u32[]{:S(2)}, u32[]{:S(2)}) collective-permute-start(bf16[256,2048]{1,0:T(8,128)(2,1)} %collective-permute-done.same_ref), channel_id=1, source_target_pairs={{0,1},{1,0},{2,3},{3,2},{4,5},{5,4},{6,7},{7,6},{8,9},{9,8},{10,11... | collective-permute-start | bytes 3145736 | tf_op jit(solution)/shard_map/ppermute | solution.py:549
  78.6 39.8 %collective-permute-start.4 = (bf16[256,2048]{1,0:T(8,128)(2,1)}, bf16[256,2048]{1,0:T(8,128)(2,1)}, u32[]{:S(2)}, u32[]{:S(2)}) collective-permute-start(bf16[256,2048]{1,0:T(8,128)(2,1)} %collective-permute-done.1.same_ref), channel_id=1, source_target_pairs={{0,1},{1,0},{2,3},{3,2},{4,5},{5,4},{6,7},{7,6},{8,9},{9,8},{10,11... | collective-permute-start | bytes 3145736 | tf_op jit(solution)/shard_map/ppermute | solution.py:549
  92.7 32.5 %collective-permute-start.3 = (bf16[256,2048]{1,0:T(8,128)(2,1)}, bf16[256,2048]{1,0:T(8,128)(2,1)}, u32[]{:S(2)}, u32[]{:S(2)}) collective-permute-start(bf16[256,2048]{1,0:T(8,128)(2,1)} %collective-permute-done.2.same_ref), channel_id=1, source_target_pairs={{0,1},{1,0},{2,3},{3,2},{4,5},{5,4},{6,7},{7,6},{8,9},{9,8},{10,11... | collective-permute-start | bytes 3145736 | tf_op jit(solution)/shard_map/ppermute | solution.py:549
  147.2 649.6 %reduce-scatter.14.cloned.1.call-start = ((), (), s32[]{:S(2)}) async-start(), calls=%async_computation.14 | async-start | bytes 5242880 | tf_op jit(solution)/shard_map/reduce_scatter | solution.py:638
  147.2 31.4 %collective-permute-start.17 = (bf16[256,2048]{1,0:T(8,128)(2,1)}, bf16[256,2048]{1,0:T(8,128)(2,1)}, u32[]{:S(2)}, u32[]{:S(2)}) collective-permute-start(bf16[256,2048]{1,0:T(8,128)(2,1)} %collective-permute-done.15), channel_id=1, source_target_pairs={{0,4},{1,5},{2,0},{3,1},{4,6},{5,7},{6,2},{7,3},{8,12},{9,13},{10,... | collective-permute-start | bytes 3145736 | tf_op jit(solution)/shard_map/ppermute | solution.py:554
  165.9 35.2 %collective-permute-start.11 = (bf16[256,2048]{1,0:T(8,128)(2,1)}, bf16[256,2048]{1,0:T(8,128)(2,1)}, u32[]{:S(2)}, u32[]{:S(2)}) collective-permute-start(bf16[256,2048]{1,0:T(8,128)(2,1)} %add_convert_fusion.8), channel_id=1, source_target_pairs={{0,4},{1,5},{2,0},{3,1},{4,6},{5,7},{6,2},{7,3},{8,12},{9,13},{10,... | collective-permute-start | bytes 3145736 | tf_op jit(solution)/shard_map/ppermute | solution.py:565
  165.9 40.7 %collective-permute-start.14 = (bf16[256,2048]{1,0:T(8,128)(2,1)}, bf16[256,2048]{1,0:T(8,128)(2,1)}, u32[]{:S(2)}, u32[]{:S(2)}) collective-permute-start(bf16[256,2048]{1,0:T(8,128)(2,1)} %get-tuple-element.71), channel_id=1, source_target_pairs={{0,1},{1,0},{2,3},{3,2},{4,5},{5,4},{6,7},{7,6},{8,9},{9,8},{10,11... | collective-permute-start | bytes 3145736 | tf_op jit(solution)/shard_map/ppermute | solution.py:549
  178.6 44.9 %collective-permute-start.19 = (bf16[256,2048]{1,0:T(8,128)(2,1)}, bf16[256,2048]{1,0:T(8,128)(2,1)}, u32[]{:S(2)}, u32[]{:S(2)}) collective-permute-start(bf16[256,2048]{1,0:T(8,128)(2,1)} %collective-permute-done.17), channel_id=1, source_target_pairs={{0,4},{1,5},{2,0},{3,1},{4,6},{5,7},{6,2},{7,3},{8,12},{9,13},{10,... | collective-permute-start | bytes 3145736 | tf_op jit(solution)/shard_map/ppermute | solution.py:554
  191.0 39.4 %collective-permute-start.8 = (bf16[256,2048]{1,0:T(8,128)(2,1)}, bf16[256,2048]{1,0:T(8,128)(2,1)}, u32[]{:S(2)}, u32[]{:S(2)}) collective-permute-start(bf16[256,2048]{1,0:T(8,128)(2,1)} %convolution_convert_fusion.13), channel_id=1, source_target_pairs={{0,1},{1,0},{2,3},{3,2},{4,5},{5,4},{6,7},{7,6},{8,9},{9,8},{10,11... | collective-permute-start | bytes 3145736 | tf_op jit(solution)/shard_map/ppermute | solution.py:549
  204.2 41.2 %collective-permute-start.12 = (bf16[256,2048]{1,0:T(8,128)(2,1)}, bf16[256,2048]{1,0:T(8,128)(2,1)}, u32[]{:S(2)}, u32[]{:S(2)}) collective-permute-start(bf16[256,2048]{1,0:T(8,128)(2,1)} %add_convert_fusion.7), channel_id=1, source_target_pairs={{0,4},{1,5},{2,0},{3,1},{4,6},{5,7},{6,2},{7,3},{8,12},{9,13},{10,... | collective-permute-start | bytes 3145736 | tf_op jit(solution)/shard_map/ppermute | solution.py:565
  206.5 41.1 %collective-permute-start.16 = (bf16[256,2048]{1,0:T(8,128)(2,1)}, bf16[256,2048]{1,0:T(8,128)(2,1)}, u32[]{:S(2)}, u32[]{:S(2)}) collective-permute-start(bf16[256,2048]{1,0:T(8,128)(2,1)} %collective-permute-done.15), channel_id=1, source_target_pairs={{0,1},{1,0},{2,3},{3,2},{4,5},{5,4},{6,7},{7,6},{8,9},{9,8},{10,11... | collective-permute-start | bytes 3145736 | tf_op jit(solution)/shard_map/ppermute | solution.py:549
  211.3 41.1 %collective-permute-start.18 = (bf16[256,2048]{1,0:T(8,128)(2,1)}, bf16[256,2048]{1,0:T(8,128)(2,1)}, u32[]{:S(2)}, u32[]{:S(2)}) collective-permute-start(bf16[256,2048]{1,0:T(8,128)(2,1)} %collective-permute-done.17), channel_id=1, source_target_pairs={{0,1},{1,0},{2,3},{3,2},{4,5},{5,4},{6,7},{7,6},{8,9},{9,8},{10,11... | collective-permute-start | bytes 3145736 | tf_op jit(solution)/shard_map/ppermute | solution.py:549
  223.5 33.5 %collective-permute-start.20 = (bf16[256,2048]{1,0:T(8,128)(2,1)}, bf16[256,2048]{1,0:T(8,128)(2,1)}, u32[]{:S(2)}, u32[]{:S(2)}) collective-permute-start(bf16[256,2048]{1,0:T(8,128)(2,1)} %collective-permute-done.19), channel_id=1, source_target_pairs={{0,1},{1,0},{2,3},{3,2},{4,5},{5,4},{6,7},{7,6},{8,9},{9,8},{10,11... | collective-permute-start | bytes 3145736 | tf_op jit(solution)/shard_map/ppermute | solution.py:549
  230.4 28.9 %collective-permute-start.7 = (bf16[256,2048]{1,0:T(8,128)(2,1)S(1)}, bf16[256,2048]{1,0:T(8,128)(2,1)S(1)}, u32[]{:S(2)}, u32[]{:S(2)}) collective-permute-start(bf16[256,2048]{1,0:T(8,128)(2,1)S(1)} %convolution_convert_fusion.15), channel_id=1, source_target_pairs={{0,1},{1,0},{2,3},{3,2},{4,5},{5,4},{6,7},{7,6},{8,9},{9,8},{10,11... | collective-permute-start | bytes 3145736 | tf_op jit(solution)/shard_map/ppermute | solution.py:549
  432.4 367.2 %reduce-scatter.10.cloned.1.call-start = ((), (), s32[]{:S(2)}) async-start(), calls=%async_computation.12 | async-start | bytes 5242880 | tf_op jit(solution)/shard_map/reduce_scatter | solution.py:638
  446.6 355.8 %reduce-scatter.12.cloned.1.call-start = ((), (), s32[]{:S(2)}) async-start(), calls=%async_computation.13 | async-start | bytes 5242880 | tf_op jit(solution)/shard_map/reduce_scatter | solution.py:638
  466.1 37.1 %collective-permute-start.22 = (bf16[256,2048]{1,0:T(8,128)(2,1)S(1)}, bf16[256,2048]{1,0:T(8,128)(2,1)S(1)}, u32[]{:S(2)}, u32[]{:S(2)}) collective-permute-start(bf16[256,2048]{1,0:T(8,128)(2,1)S(1)} %get-tuple-element.75), channel_id=1, source_target_pairs={{0,1},{1,0},{2,3},{3,2},{4,5},{5,4},{6,7},{7,6},{8,9},{9,8},{10,11... | collective-permute-start | bytes 3145736 | tf_op jit(solution)/shard_map/ppermute | solution.py:549
  503.3 32.3 %collective-permute-start.21 = (bf16[256,2048]{1,0:T(8,128)(2,1)S(1)}, bf16[256,2048]{1,0:T(8,128)(2,1)}, u32[]{:S(2)}, u32[]{:S(2)}) collective-permute-start(bf16[256,2048]{1,0:T(8,128)(2,1)S(1)} %get-tuple-element.72), channel_id=1, source_target_pairs={{0,1},{1,0},{2,3},{3,2},{4,5},{5,4},{6,7},{7,6},{8,9},{9,8},{10,11... | collective-permute-start | bytes 3145736 | tf_op jit(solution)/shard_map/ppermute | solution.py:549
  535.5 269.7 %reduce-scatter.8.cloned.1.call-start = ((), (), s32[]{:S(2)}) async-start(), calls=%async_computation.11 | async-start | bytes 1310720 | tf_op jit(solution)/shard_map/reduce_scatter | solution.py:638
  552.0 29.1 %collective-permute-start.34 = (bf16[256,2048]{1,0:T(8,128)(2,1)S(1)}, bf16[256,2048]{1,0:T(8,128)(2,1)}, u32[]{:S(2)}, u32[]{:S(2)}) collective-permute-start(bf16[256,2048]{1,0:T(8,128)(2,1)S(1)} %get-tuple-element.66), channel_id=1, source_target_pairs={{0,1},{1,0},{2,3},{3,2},{4,5},{5,4},{6,7},{7,6},{8,9},{9,8},{10,11... | collective-permute-start | bytes 3145736 | tf_op jit(solution)/shard_map/ppermute | solution.py:549
  578.6 33.4 %collective-permute-start.33 = (bf16[256,2048]{1,0:T(8,128)(2,1)}, bf16[256,2048]{1,0:T(8,128)(2,1)}, u32[]{:S(2)}, u32[]{:S(2)}) collective-permute-start(bf16[256,2048]{1,0:T(8,128)(2,1)} %collective-permute-done.28), channel_id=1, source_target_pairs={{0,1},{1,0},{2,3},{3,2},{4,5},{5,4},{6,7},{7,6},{8,9},{9,8},{10,11... | collective-permute-start | bytes 3145736 | tf_op jit(solution)/shard_map/ppermute | solution.py:549
  605.6 28.9 %collective-permute-start.32 = (bf16[256,2048]{1,0:T(8,128)(2,1)S(1)}, bf16[256,2048]{1,0:T(8,128)(2,1)}, u32[]{:S(2)}, u32[]{:S(2)}) collective-permute-start(bf16[256,2048]{1,0:T(8,128)(2,1)S(1)} %collective-permute-done.29), channel_id=1, source_target_pairs={{0,1},{1,0},{2,3},{3,2},{4,5},{5,4},{6,7},{7,6},{8,9},{9,8},{10,11... | collective-permute-start | bytes 3145736 | tf_op jit(solution)/shard_map/ppermute | solution.py:549
  605.8 28.7 %collective-permute-start.30 = (bf16[256,2048]{1,0:T(8,128)(2,1)S(1)}, bf16[256,2048]{1,0:T(8,128)(2,1)}, u32[]{:S(2)}, u32[]{:S(2)}) collective-permute-start(bf16[256,2048]{1,0:T(8,128)(2,1)S(1)} %collective-permute-done.29), channel_id=1, source_target_pairs={{0,4},{1,5},{2,0},{3,1},{4,6},{5,7},{6,2},{7,3},{8,12},{9,13},{10,... | collective-permute-start | bytes 3145736 | tf_op jit(solution)/shard_map/ppermute | solution.py:554
  634.6 28.3 %collective-permute-start.31 = (bf16[256,2048]{1,0:T(8,128)(2,1)}, bf16[256,2048]{1,0:T(8,128)(2,1)S(1)}, u32[]{:S(2)}, u32[]{:S(2)}) collective-permute-start(bf16[256,2048]{1,0:T(8,128)(2,1)} %collective-permute-done.30), channel_id=1, source_target_pairs={{0,1},{1,0},{2,3},{3,2},{4,5},{5,4},{6,7},{7,6},{8,9},{9,8},{10,11... | collective-permute-start | bytes 3145736 | tf_op jit(solution)/shard_map/ppermute | solution.py:549
  704.3 113.2 %reduce-scatter.6.cloned.1.call-start = ((), (), s32[]{:S(2)}) async-start(), calls=%async_computation.10 | async-start | bytes 3932160 | tf_op jit(solution)/shard_map/reduce_scatter | solution.py:638
  (68 other events, 977.9 us)
Sparse Core Ops, SparseCore 0:
  10.4 46.6 all-gather.5
  59.0 26.4 all-gather.7
  87.4 52.7 all-gather.9
  141.8 52.6 all-gather.11
  196.3 52.5 all-gather.13
  432.6 55.8 reduce-scatter.13
  491.6 52.6 reduce-scatter.9
  547.3 52.6 reduce-scatter.11
  704.4 28.9 reduce-scatter.7
  736.2 43.9 reduce-scatter.5

commit v3 on v2

v3 whole, which is shorter than its diff:
```python
import jax
import jax.numpy as jnp
from jax import lax
from jax.experimental import pallas as pl
from jax.experimental.pallas import tpu as pltpu
from jax.sharding import PartitionSpec as P

HEAD_DIM = 64
SEQ_LEN = 2048
LANES = 128
rope_base = 130000.0
norm_eps = 1e-05
masked_score = -1e30

NT = (((1,), (1,)), ((), ()))
NN = (((1,), (0,)), ((), ()))
TN = (((0,), (0,)), ((), ()))
MESH = pl.DeviceIdType.MESH
DMA = pltpu.SemaphoreType.DMA
ANYWHERE = pl.BlockSpec(memory_space=pl.ANY)
VMEM = pl.BlockSpec(memory_space=pltpu.VMEM)
low = jnp.bfloat16


def dot(left, right, dims=NN):
    return lax.dot_general(left, right, dims, preferred_element_type=jnp.float32)


def span(index, size):
    return pl.ds(pl.multiple_of(index * size, size), size)


def remote(source, target, send, receive, device):
    return pltpu.make_async_remote_copy(
        src_ref=source, dst_ref=target, send_sem=send, recv_sem=receive,
        device_id=device, device_id_type=MESH,
    )


def hello(device):
    pl.semaphore_signal(pltpu.get_barrier_semaphore(), inc=1, device_id=device, device_id_type=MESH)


class Line:
    def __init__(self, chips):
        self.chips = chips
        self.me = lax.axis_index("tp")
        self.chip, self.core = self.me // 2, self.me % 2
        self.partner = 2 * self.chip + 1 - self.core
        self.has_left, self.has_right = self.chip > 0, self.chip < chips - 1

    def greet(self, more=()):
        hello({"tp": self.partner})

        @pl.when(self.has_left)
        def _():
            hello({"tp": self.me - 2})

        @pl.when(self.has_right)
        def _():
            hello({"tp": self.me + 2})

        for device in more:
            hello(device)
        count = 1 + len(more) + jnp.where(self.has_left, 1, 0) + jnp.where(self.has_right, 1, 0)
        pl.semaphore_wait(pltpu.get_barrier_semaphore(), count)

    def target(self, step):
        after = self.chips - 1 - self.chip
        most, least = jnp.maximum(self.chip, after), jnp.minimum(self.chip, after)
        sign = jnp.where(after >= self.chip, 1, -1)
        late = step - (most - least)
        side = jnp.where(late % 2 == 0, sign, -sign)
        return jnp.where(late < 0, self.chip + sign * (most - step), self.chip + side * (least - late // 2))


class Gather:
    scratch = staticmethod(lambda chips: [DMA((2 * chips,)), DMA((chips,)), DMA((chips,)), DMA((chips,)), DMA])

    def __init__(self, line, own, out, received, right, left, across, local):
        self.line, self.own, self.out = line, own, out
        self.received, self.right, self.left, self.across, self.local = received, right, left, across, local
        self.rows = own.shape[0]

    def block(self, index):
        return self.out.at[span(index, self.rows)]

    def copy(self, source, sems, chip, device, mine):
        index = 2 * chip + self.line.core
        return remote(source if mine else self.block(index), self.block(index), sems.at[chip], self.received.at[index], {"tp": device})

    def keep(self):
        return pltpu.make_async_copy(self.own, self.block(self.line.me), self.local)

    def start(self):
        line = self.line
        self.keep().start()

        @pl.when(line.has_right)
        def _():
            self.copy(self.own, self.right, line.chip, line.me + 2, True).start()

        @pl.when(line.has_left)
        def _():
            self.copy(self.own, self.left, line.chip, line.me - 2, True).start()

        self.copy(self.own, self.across, line.chip, line.partner, True).start()

    def arrive(self, index):
        remote(self.own, self.block(index), self.right.at[0], self.received.at[index], {"tp": self.line.partner}).wait_recv()

    def arrive_across(self, chip):
        self.arrive(2 * chip + 1 - self.line.core)

    def step(self, distance):
        line = self.line
        before, after = line.chip - distance, line.chip + distance

        @pl.when(before >= 0)
        def _():
            self.arrive(2 * before + line.core)

            @pl.when(line.has_right)
            def _():
                self.copy(None, self.right, before, line.me + 2, False).start()

            self.copy(None, self.across, before, line.partner, False).start()

        @pl.when(after < line.chips)
        def _():
            self.arrive(2 * after + line.core)

            @pl.when(line.has_left)
            def _():
                self.copy(None, self.left, after, line.me - 2, False).start()

            self.copy(None, self.across, after, line.partner, False).start()

    def finish(self, arrivals):
        line = self.line
        if arrivals:
            self.keep().wait()
        for chip in range(line.chips):
            if arrivals:
                self.arrive_across(chip)
            self.copy(self.own, self.across, chip, line.partner, True).wait_send()

            @pl.when(jnp.logical_and(line.has_right, chip <= line.chip))
            def _():
                self.copy(self.own, self.right, chip, line.me + 2, True).wait_send()

            @pl.when(jnp.logical_and(line.has_left, chip >= line.chip))
            def _():
                self.copy(self.own, self.left, chip, line.me - 2, True).wait_send()


class Scatter:
    @staticmethod
    def scratch(chips, rows, depth):
        shares = min(chips, 4)
        return [
            pltpu.VMEM((2, 2 * rows, depth), low),
            pltpu.VMEM((shares, rows, depth), low),
            pltpu.VMEM((chips + 1, rows, depth), low),
            pltpu.VMEM((2, rows, depth), low),
            DMA((2,)), DMA((shares,)), DMA((2,)), DMA((chips + 1,)),
        ]

    def __init__(self, line, out, term, shares, lines, total, share_send, share_recv, line_send, line_recv):
        self.line, self.out = line, out
        self.term, self.shares, self.lines, self.total = term, shares, lines, total
        self.share_send, self.share_recv, self.line_send, self.line_recv = share_send, share_recv, line_send, line_recv
        self.rows = out.shape[0]

    def share(self, step):
        slot = step % self.shares.shape[0]
        source = self.term.at[step % 2, span(1 - self.line.core, self.rows)]
        return remote(source, self.shares.at[slot], self.share_send.at[step % 2], self.share_recv.at[slot], {"tp": self.line.partner})

    def pass_on(self, step):
        line, target = self.line, self.line.target(step)
        onward = target > line.chip
        slot = jnp.where(onward, target, jnp.where(target == line.chip - 1, line.chips, target))
        device = jnp.where(onward, line.me + 2, line.me - 2)
        return remote(self.total.at[step % 2], self.lines.at[slot], self.line_send.at[step % 2], self.line_recv.at[slot], {"tp": device})

    def add(self, slot):
        remote(self.total.at[0], self.lines.at[slot], self.line_send.at[0], self.line_recv.at[slot], {"tp": self.line.partner}).wait_recv()
        self.out[...] += self.lines[slot].astype(jnp.float32)

    def free(self, step):
        @pl.when(step >= 2)
        def _():
            self.share(step - 2).wait_send()

    def step(self, step):
        line, target = self.line, self.line.target(step)
        self.share(step).wait_recv()
        mine = self.term[step % 2, span(line.core, self.rows), :].astype(jnp.float32)
        self.out[...] = mine + self.shares[step % self.shares.shape[0]].astype(jnp.float32)

        @pl.when(jnp.logical_and(target >= line.chip, line.has_left))
        def _():
            self.add(target)

        @pl.when(jnp.logical_and(target <= line.chip, line.has_right))
        def _():
            self.add(jnp.where(target == line.chip, line.chips, target))

        @pl.when(step < line.chips - 1)
        def _():
            @pl.when(step >= 2)
            def _():
                self.pass_on(step - 2).wait_send()

            self.total[step % 2] = self.out[...].astype(low)
            self.pass_on(step).start()

    def finish(self):
        chips = self.line.chips
        for step in range(max(0, chips - 3), chips - 1):
            self.pass_on(step).wait_send()
        for step in range(max(0, chips - 2), chips):
            self.share(step).wait_send()


def turned(block, sign):
    half = HEAD_DIM // 2
    lane = lax.broadcasted_iota(jnp.int32, block.shape, 1)
    width = block.shape[1]
    up = pltpu.roll(block, width - half, 1)
    down = pltpu.roll(block, half, 1)
    return jnp.where(lane % HEAD_DIM < half, -sign * up, sign * down)


def widened(table, width):
    return table if table.shape[1] == width else jnp.concatenate([table] * (width // table.shape[1]), axis=1)


def only_head(block, head):
    lane = lax.broadcasted_iota(jnp.int32, block.shape, 1)
    return jnp.where(lane // HEAD_DIM == head, block, jnp.zeros_like(block))


def causal(tile):
    key = lax.broadcasted_iota(jnp.int32, tile.shape, 0)
    query = lax.broadcasted_iota(jnp.int32, tile.shape, 1)
    return jnp.where(key <= query, tile, masked_score)


def over_keys(chunk, rows, visit):
    start = chunk * rows
    first = start // SEQ_LEN * SEQ_LEN

    def step(index, carry):
        visit(pl.multiple_of(first + index * rows, rows), False)
        return carry

    lax.fori_loop(0, (start - first) // rows, step, 0)
    visit(pl.multiple_of(start, rows), True)


def project_kernel(
    chips, shards,
    tokens, w_query, w_key, w_value, cosine, sine,
    tokens_out, weight, qkv, keys_t, values_t,
    chunks, chunk_sem, weight_send, weight_recv, weight_keep, *gather_sems,
):
    line = Line(chips)
    rows = tokens.shape[0]
    pair = 2 * rows
    depth, width = w_query.shape
    shard = lax.axis_index("fsdp")
    others = [(shard + ahead) % shards for ahead in range(1, shards)]
    gather = Gather(line, tokens, tokens_out, *gather_sems)
    parts = (w_query, w_key, w_value)

    def place(index, part):
        return weight.at[span(index, depth), pl.ds(part * width, width)]

    def give(ahead, part):
        return remote(parts[part], place(shard, part), weight_send.at[ahead, part], weight_recv.at[ahead, part], {"fsdp": others[ahead]})

    def keep(part):
        return pltpu.make_async_copy(parts[part], place(shard, part), weight_keep.at[part])

    line.greet([{"fsdp": other} for other in others])
    gather.start()
    for part in range(3):
        keep(part).start()
        for ahead in range(shards - 1):
            give(ahead, part).start()

    def project(chip):
        @pl.when(jnp.logical_and(chip >= 0, chip < chips))
        def _():
            gather.arrive_across(chip)
            load = pltpu.make_async_copy(tokens_out.at[span(chip, pair)], chunks, chunk_sem)
            load.start()
            load.wait()
            here = span(chip, pair)
            table = span(chip % (SEQ_LEN // pair), pair)
            for part in range(3):
                columns = pl.ds(part * width, width)
                block = dot(chunks[...], weight[:, columns])
                if part < 2:
                    block = block * widened(cosine[table, :], width) + turned(block, 1.0) * widened(sine[table, :], width)
                qkv[here, columns] = block.astype(low)
                if part:
                    (keys_t, values_t)[part - 1][:, here] = block.T.astype(low)

    def step(index, carry):
        @pl.when(jnp.logical_and(index >= 1, index < chips))
        def _():
            gather.step(index)

        @pl.when(index == 1)
        def _():
            gather.keep().wait()
            for part in range(3):
                keep(part).wait()
                for ahead in range(shards - 1):
                    give(ahead, part).wait_recv()

        def side(which, carry):
            distance = index - 1

            @pl.when(jnp.logical_and(distance >= 0, jnp.logical_or(which == 0, distance > 0)))
            def _():
                project(jnp.where(which == 0, line.chip - distance, line.chip + distance))

            return carry

        lax.fori_loop(0, 2, side, 0)
        return carry

    lax.fori_loop(0, chips + 1, step, 0)
    gather.finish(False)
    for part in range(3):
        for ahead in range(shards - 1):
            give(ahead, part).wait_send()


def project(chips, shards, tokens, w_query, w_key, w_value, cosine, sine):
    rows, depth = tokens.shape
    group_rows = 2 * chips * rows
    shard_rows, width = w_query.shape
    shape = jax.ShapeDtypeStruct
    return pl.pallas_call(
        lambda *refs: project_kernel(chips, shards, *refs),
        in_specs=[VMEM] * 6,
        out_specs=[ANYWHERE] + [VMEM] * 4,
        out_shape=[
            shape((group_rows, depth), low),
            shape((depth, 3 * width), low),
            shape((group_rows, 3 * width), low),
            shape((width, group_rows), low),
            shape((width, group_rows), low),
        ],
        scratch_shapes=[pltpu.VMEM((2 * rows, depth), low), DMA, DMA((shards - 1, 3)), DMA((shards - 1, 3)), DMA((3,))] + Gather.scratch(chips),
        compiler_params=pltpu.CompilerParams(collective_id=1, has_side_effects=True, vmem_limit_bytes=40 << 20),
        cost_estimate=pl.CostEstimate(flops=6 * group_rows * depth * width, bytes_accessed=4 * group_rows * depth, transcendentals=0),
        name="project",
    )(tokens, w_query, w_key, w_value, cosine, sine)


def attend_chunk(chunk, rows, qkv, values_t, heads_ref, acc, out, top_ref, sum_ref):
    width = acc.shape[0]
    heads = width // HEAD_DIM
    scaled = qkv[span(chunk, rows), pl.ds(0, width)] * low(HEAD_DIM**-0.5)
    for head in range(heads):
        heads_ref[head] = only_head(scaled, head)
    acc[...] = jnp.zeros_like(acc)
    top_ref[...] = jnp.full_like(top_ref, masked_score)
    sum_ref[...] = jnp.zeros_like(sum_ref)

    def visit(offset, diagonal):
        key_block = qkv[pl.ds(offset, rows), pl.ds(width, width)]
        for head in range(heads):
            feature = pl.ds(head * HEAD_DIM, HEAD_DIM)
            one = pl.ds(head, 1)
            scores = dot(key_block, heads_ref[head], NT)
            if diagonal:
                scores = causal(scores)
            old = top_ref[one, :]
            top = jnp.maximum(old, jnp.max(scores, axis=0, keepdims=True))
            shrink = jnp.exp(old - top)
            weights = jnp.exp(scores - top)
            top_ref[one, :] = top
            sum_ref[one, :] = sum_ref[one, :] * shrink + jnp.sum(weights, axis=0, keepdims=True)
            acc[feature, :] = acc[feature, :] * shrink + dot(values_t[feature, pl.ds(offset, rows)], weights.astype(low))

    over_keys(chunk, rows, visit)
    for head in range(heads):
        feature = pl.ds(head * HEAD_DIM, HEAD_DIM)
        acc[feature, :] = acc[feature, :] / sum_ref[pl.ds(head, 1), :]
    out[...] = acc[...].T.astype(low)


def attend_kernel(
    chips,
    qkv, values_t, w_out, grads,
    branch, mixed, totals, grads_out,
    heads_ref, acc, out, top_ref, sum_ref, *sems,
):
    line = Line(chips)
    rows, depth = branch.shape
    pair = 2 * rows
    scatter = Scatter(line, branch, *sems[:8])
    gather = Gather(line, grads, grads_out, *sems[8:])
    line.greet()
    gather.start()

    def step(index, carry):
        work = jnp.where(index == chips, chips - 1, index)

        @pl.when(jnp.logical_or(index < chips - 1, index == chips))
        def _():
            chunk = line.target(work)
            attend_chunk(chunk, pair, qkv, values_t, heads_ref, acc, out, top_ref, sum_ref)
            mixed[span(chunk, pair), :] = out[...]
            totals[:, span(chunk, pair)] = top_ref[...] + jnp.log(sum_ref[...])
            scatter.free(work)

            def tile(place, carry):
                columns = span(place, 512)
                scatter.term[work % 2, :, columns] = dot(out[...], w_out[:, columns]).astype(low)
                return carry

            lax.fori_loop(0, depth // 512, tile, 0)
            scatter.share(work).start()

        @pl.when(jnp.logical_and(index >= 1, index < chips))
        def _():
            gather.step(index)

        @pl.when(index >= 1)
        def _():
            scatter.step(index - 1)

        return carry

    lax.fori_loop(0, chips + 1, step, 0)
    scatter.finish()
    gather.finish(True)


def attend(chips, qkv, values_t, w_out, grads):
    rows, depth = grads.shape
    pair = 2 * rows
    group_rows = chips * pair
    width = w_out.shape[0]
    heads = width // HEAD_DIM
    shape = jax.ShapeDtypeStruct
    return pl.pallas_call(
        lambda *refs: attend_kernel(chips, *refs),
        in_specs=[VMEM] * 4,
        out_specs=[VMEM] * 3 + [ANYWHERE],
        out_shape=[
            shape((rows, depth), jnp.float32),
            shape((group_rows, width), low),
            shape((heads, group_rows), jnp.float32),
            shape((group_rows, depth), low),
        ],
        scratch_shapes=[
            pltpu.VMEM((heads, pair, width), low),
            pltpu.VMEM((width, pair), jnp.float32),
            pltpu.VMEM((pair, width), low),
            pltpu.VMEM((heads, pair), jnp.float32),
            pltpu.VMEM((heads, pair), jnp.float32),
        ] + Scatter.scratch(chips, rows, depth) + Gather.scratch(chips),
        compiler_params=pltpu.CompilerParams(collective_id=2, has_side_effects=True, vmem_limit_bytes=60 << 20),
        cost_estimate=pl.CostEstimate(flops=2 * group_rows * (SEQ_LEN + depth) * width, bytes_accessed=4 * group_rows * depth, transcendentals=group_rows * SEQ_LEN * heads // 2),
        name="attend",
    )(qkv, values_t, w_out, grads)


def back_chunk(chunk, rows, grad, qkv, keys_t, mixed, totals, dkey, dvalue, heads_ref, grads_ref, acc, inner_ref):
    width = acc.shape[0]
    heads = width // HEAD_DIM
    here = span(chunk, rows)
    scaled = qkv[here, pl.ds(0, width)] * low(HEAD_DIM**-0.5)
    product = grad.astype(jnp.float32) * mixed[here, :].astype(jnp.float32)
    shape = (inner_ref.shape[0], width)
    pick = (lax.broadcasted_iota(jnp.int32, shape, 1) // HEAD_DIM == lax.broadcasted_iota(jnp.int32, shape, 0)).astype(jnp.float32)
    inner_ref[...] = lax.dot_general(pick, product, NT, precision=lax.Precision.HIGHEST, preferred_element_type=jnp.float32)
    for head in range(heads):
        heads_ref[head] = only_head(scaled, head)
        grads_ref[head] = only_head(grad, head)
    acc[...] = jnp.zeros_like(acc)

    def visit(offset, diagonal):
        keys = pl.ds(offset, rows)
        key_block = qkv[keys, pl.ds(width, width)]
        value_block = qkv[keys, pl.ds(2 * width, width)]
        key_sum, value_sum = dkey[keys, :], dvalue[keys, :]
        for head in range(heads):
            feature = pl.ds(head * HEAD_DIM, HEAD_DIM)
            scores = dot(key_block, heads_ref[head], NT)
            if diagonal:
                scores = causal(scores)
            probs = jnp.exp(scores - totals[pl.ds(head, 1), here])
            dprobs = dot(value_block, grads_ref[head], NT)
            dscores = (probs * (dprobs - inner_ref[pl.ds(head, 1), :])).astype(low)
            value_sum = value_sum + dot(probs.astype(low), grads_ref[head])
            key_sum = key_sum + dot(dscores, heads_ref[head])
            acc[feature, :] = acc[feature, :] + dot(keys_t[feature, keys], dscores)
        dkey[keys, :] = key_sum
        dvalue[keys, :] = value_sum

    over_keys(chunk, rows, visit)


def back_kernel(
    chips,
    branch, inner, w_down, w_out, qkv, keys_t, mixed, totals, cosine, sine,
    down, branch_out, qkv_grad,
    down_w, inner_chunk, branch_chunk, dkey, dvalue, heads_ref, grads_ref, acc, inner_ref, load_sem, inner_sem, branch_sem, *sems,
):
    line = Line(chips)
    rows, depth = down.shape
    pair = 2 * rows
    width = w_out.shape[0]
    scatter = Scatter(line, down, *sems[:8])
    gather = Gather(line, branch, branch_out, *sems[8:])

    def load():
        return pltpu.make_async_copy(w_down, down_w, load_sem)

    def fetch(step):
        return pltpu.make_async_copy(inner.at[span(line.target(step), pair)], inner_chunk.at[step % 2], inner_sem.at[step % 2])

    load().start()
    fetch(0).start()
    line.greet()
    gather.start()
    dkey[...] = jnp.zeros_like(dkey)
    dvalue[...] = jnp.zeros_like(dvalue)

    def unrotated(block, chunk):
        table = span(chunk % (SEQ_LEN // pair), pair)
        return (block * widened(cosine[table, :], width) + turned(block * widened(sine[table, :], width), -1.0)).astype(low)

    def attention(chunk):
        gather.arrive_across(chunk)
        copy = pltpu.make_async_copy(branch_out.at[span(chunk, pair)], branch_chunk, branch_sem)
        copy.start()
        copy.wait()
        grad = dot(branch_chunk[...], w_out[...], NT).astype(low)
        back_chunk(chunk, pair, grad, qkv, keys_t, mixed, totals, dkey, dvalue, heads_ref, grads_ref, acc, inner_ref)
        qkv_grad[span(chunk, pair), pl.ds(0, width)] = unrotated(acc[...].T * HEAD_DIM**-0.5, chunk)

    def step(index, carry):
        @pl.when(index == 0)
        def _():
            load().wait()
            gather.keep().wait()

        @pl.when(index < chips)
        def _():
            @pl.when(index < chips - 1)
            def _():
                fetch(index + 1).start()

            fetch(index).wait()
            scatter.free(index)

            def tile(place, carry):
                columns = span(place, 256)
                scatter.term[index % 2, :, columns] = dot(inner_chunk[index % 2], down_w[:, columns]).astype(low)
                return carry

            lax.fori_loop(0, depth // 256, tile, 0)
            scatter.share(index).start()

        @pl.when(jnp.logical_and(index >= 1, index < chips))
        def _():
            gather.step(index)

        def side(which, carry):
            chunk = jnp.where(which == 0, line.chip - index, line.chip + index)
            there = jnp.logical_and(chunk >= 0, chunk < chips)

            @pl.when(jnp.logical_and(there, jnp.logical_or(which == 0, index > 0)))
            def _():
                attention(chunk)

            return carry

        lax.fori_loop(0, 2, side, 0)

        @pl.when(index >= 1)
        def _():
            scatter.step(index - 1)

        return carry

    lax.fori_loop(0, chips + 1, step, 0)

    def close(chunk, carry):
        here = span(chunk, pair)
        qkv_grad[here, pl.ds(width, width)] = unrotated(dkey[here, :], chunk)
        qkv_grad[here, pl.ds(2 * width, width)] = dvalue[here, :].astype(low)
        return carry

    lax.fori_loop(0, chips, close, 0)
    scatter.finish()
    gather.finish(False)


def back(chips, branch, inner, w_down, w_out, qkv, keys_t, mixed, totals, cosine, sine):
    rows, depth = branch.shape
    pair = 2 * rows
    group_rows = chips * pair
    width = w_out.shape[0]
    hidden = w_down.shape[0]
    heads = width // HEAD_DIM
    shape = jax.ShapeDtypeStruct
    return pl.pallas_call(
        lambda *refs: back_kernel(chips, *refs),
        in_specs=[VMEM, ANYWHERE, ANYWHERE] + [VMEM] * 7,
        out_specs=[VMEM, ANYWHERE, VMEM],
        out_shape=[
            shape((rows, depth), jnp.float32),
            shape((group_rows, depth), low),
            shape((group_rows, 3 * width), low),
        ],
        scratch_shapes=[
            pltpu.VMEM((hidden, depth), low),
            pltpu.VMEM((2, pair, hidden), low),
            pltpu.VMEM((pair, depth), low),
            pltpu.VMEM((group_rows, width), jnp.float32),
            pltpu.VMEM((group_rows, width), jnp.float32),
            pltpu.VMEM((heads, pair, width), low),
            pltpu.VMEM((heads, pair, width), low),
            pltpu.VMEM((width, pair), jnp.float32),
            pltpu.VMEM((8, pair), jnp.float32),
            DMA, DMA((2,)), DMA,
        ] + Scatter.scratch(chips, rows, depth) + Gather.scratch(chips),
        compiler_params=pltpu.CompilerParams(collective_id=4, has_side_effects=True, vmem_limit_bytes=63 << 20),
        cost_estimate=pl.CostEstimate(flops=2 * group_rows * (depth * hidden + depth * width + 5 * SEQ_LEN * width // 2), bytes_accessed=6 * group_rows * depth, transcendentals=group_rows * SEQ_LEN * heads // 2),
        name="back",
    )(branch, inner, w_down, w_out, qkv, keys_t, mixed, totals, cosine, sine)


def spread_kernel(chips, qkv_grad, weight, out, *sems):
    line = Line(chips)
    rows, depth = out.shape
    pair = 2 * rows
    scatter = Scatter(line, out, *sems)
    line.greet()

    def step(index, carry):
        @pl.when(index < chips)
        def _():
            here = span(line.target(index), pair)
            scatter.free(index)

            def tile(place, carry):
                columns = span(place, 512)
                scatter.term[index % 2, :, columns] = dot(qkv_grad[here, :], weight[columns, :], NT).astype(low)
                return carry

            lax.fori_loop(0, depth // 512, tile, 0)
            scatter.share(index).start()

        @pl.when(index >= 1)
        def _():
            scatter.step(index - 1)

        return carry

    lax.fori_loop(0, chips + 1, step, 0)
    scatter.finish()


def spread(chips, qkv_grad, weight):
    group_rows = qkv_grad.shape[0]
    rows = group_rows // (2 * chips)
    depth = weight.shape[0]
    return pl.pallas_call(
        lambda *refs: spread_kernel(chips, *refs),
        in_specs=[VMEM] * 2,
        out_specs=VMEM,
        out_shape=jax.ShapeDtypeStruct((rows, depth), jnp.float32),
        scratch_shapes=Scatter.scratch(chips, rows, depth),
        compiler_params=pltpu.CompilerParams(collective_id=5, has_side_effects=True, vmem_limit_bytes=48 << 20),
        cost_estimate=pl.CostEstimate(flops=2 * group_rows * weight.size, bytes_accessed=4 * weight.size, transcendentals=0),
        name="spread",
    )(qkv_grad, weight)


def chip_at(place, chips):
    return jnp.where(2 * place < chips, 2 * place, 2 * (chips - 1 - place) + 1)


def place_of(chip, chips):
    return jnp.where(chip % 2 == 0, chip // 2, chips - 1 - chip // 2)


def feed_kernel(
    chips,
    tokens_ref, grads_hbm, gate_hbm, up_hbm, down_hbm,
    back_ref, tokens_out, inner_out, gate_out, up_out,
    tokens_all, gate_w, up_w, down_w, grads, inner, gate_grad, up_grad, own, term, stage, from_core, from_ring, total,
    load_sem, grad_sem, keep_sem, store_sem, ring_send, ring_recv, core_send, core_recv, stage_send, stage_recv, total_send, total_recv,
):
    rows, depth = tokens_ref.shape
    pair = 2 * rows
    hidden = gate_w.shape[1]
    me = lax.axis_index("tp")
    chip, core = me // 2, me % 2
    place = place_of(chip, chips)
    following = 2 * chip_at((place + 1) % chips, chips) + core
    before = 2 * chip_at((place + chips - 1) % chips, chips) + core
    partner = 2 * chip + 1 - core

    loads = [pltpu.make_async_copy(a, b, load_sem.at[i]) for i, (a, b) in enumerate(((gate_hbm, gate_w), (up_hbm, up_w), (down_hbm, down_w)))]
    for load in loads:
        load.start()

    def source(slot):
        return chip_at((place + chips - slot) % chips, chips)

    def fetch(slot):
        start = pl.multiple_of(source(slot) * pair, pair)
        return pltpu.make_async_copy(grads_hbm.at[pl.ds(start, pair)], grads.at[slot % 2], grad_sem.at[slot % 2])

    def block(ref, index):
        return ref.at[pl.ds(pl.multiple_of(index * rows, rows), rows)]

    def to_ring(slot):
        index = 2 * source(slot) + core
        return remote(block(tokens_all, index), block(tokens_all, index), ring_send.at[slot], ring_recv.at[slot], {"tp": following})

    def to_core(slot):
        index = 2 * source(slot) + core
        return remote(block(tokens_all, index), block(tokens_all, index), core_send.at[slot], core_recv.at[slot], {"tp": partner})

    def keep(slot):
        start = pl.multiple_of(source(slot) * pair, pair)
        span = pl.ds(start, pair)
        return pltpu.make_async_copy(tokens_all.at[span], tokens_out.at[span], keep_sem.at[slot])

    def stores(slot):
        span = pl.ds(pl.multiple_of(source(slot) * pair, pair), pair)
        return [
            pltpu.make_async_copy(ref.at[slot % 2], out.at[span], store_sem.at[i, slot % 2])
            for i, (ref, out) in enumerate(((inner, inner_out), (gate_grad, gate_out), (up_grad, up_out)))
        ]

    def stage_copy(slot):
        return remote(stage.at[slot % 2], from_core.at[slot], stage_send.at[slot % 2], stage_recv.at[slot], {"tp": partner})

    def total_copy(slot):
        return remote(total.at[slot - 1], from_ring.at[slot - 1], total_send.at[slot - 1], total_recv.at[slot - 1], {"tp": following})

    fetch(0).start()
    tokens_all[pl.ds(pl.multiple_of(me * rows, rows), rows), :] = tokens_ref[...]
    for device in (following, before, partner):
        hello({"tp": device})
    pl.semaphore_wait(pltpu.get_barrier_semaphore(), 3)

    def step(slot, carry):
        @pl.when(slot > 0)
        def _():
            to_ring(slot - 1).wait_recv()

        @pl.when(slot < chips - 1)
        def _():
            to_ring(slot).start()
            fetch(slot + 1).start()

        to_core(slot).start()

        @pl.when(slot == 0)
        def _():
            for load in loads:
                load.wait()

        @pl.when(slot > 1)
        def _():
            for store in stores(slot - 2):
                store.wait()

        to_core(slot).wait_recv()
        keep(slot).start()
        fetch(slot).wait()
        here = slot % 2
        span = pl.ds(pl.multiple_of(source(slot) * pair, pair), pair)

        def narrow(tile, carry):
            columns = pl.ds(pl.multiple_of(tile * 256, 256), 256)
            token = tokens_all[span, :]
            gate = dot(token, gate_w[:, columns])
            up = dot(token, up_w[:, columns])
            grad = dot(grads[here], down_w[columns, :], NT)
            squash = jax.nn.sigmoid(gate)
            act = gate * squash
            inner[here, :, columns] = (act * up).astype(jnp.bfloat16)
            up_grad[here, :, columns] = (grad * act).astype(jnp.bfloat16)
            gate_grad[here, :, columns] = (grad * up * squash * (1.0 + gate * (1.0 - squash))).astype(jnp.bfloat16)
            return carry

        lax.fori_loop(0, hidden // 256, narrow, 0)
        for store in stores(slot):
            store.start()

        @pl.when(slot > 1)
        def _():
            stage_copy(slot - 2).wait_send()

        def wide(tile, carry):
            columns = pl.ds(pl.multiple_of(tile * 256, 256), 256)
            part = dot(gate_grad[here], gate_w[columns, :], NT) + dot(up_grad[here], up_w[columns, :], NT)
            term[:, columns] = part.astype(jnp.bfloat16)
            return carry

        lax.fori_loop(0, depth // 256, wide, 0)
        stage[here] = term[pl.ds(pl.multiple_of((1 - core) * rows, rows), rows), :]
        stage_copy(slot).start()
        mine = pl.ds(pl.multiple_of(core * rows, rows), rows)

        @pl.when(slot == 0)
        def _():
            own[...] = term[mine, :].astype(jnp.float32)

        @pl.when(slot > 0)
        def _():
            stage_copy(slot).wait_recv()

        @pl.when(slot == 1)
        def _():
            total[slot - 1] = (term[mine, :].astype(jnp.float32) + from_core[slot].astype(jnp.float32)).astype(jnp.bfloat16)

        @pl.when(slot > 1)
        def _():
            total_copy(slot - 1).wait_recv()
            total[slot - 1] = (term[mine, :].astype(jnp.float32) + from_core[slot].astype(jnp.float32) + from_ring[slot - 2].astype(jnp.float32)).astype(jnp.bfloat16)

        @pl.when(slot > 0)
        def _():
            total_copy(slot).start()

        return carry

    lax.fori_loop(0, chips, step, 0)
    stage_copy(0).wait_recv()
    total_copy(chips - 1).wait_recv()
    back_ref[...] = own[...] + from_core[0].astype(jnp.float32) + from_ring[chips - 2].astype(jnp.float32)
    for slot in range(chips):
        to_core(slot).wait_send()
        keep(slot).wait()
        if slot < chips - 1:
            to_ring(slot).wait_send()
        if slot > 0:
            total_copy(slot).wait_send()
        if slot >= chips - 2:
            stage_copy(slot).wait_send()
            for store in stores(slot):
                store.wait()


def feed(chips, tokens, grads, gate_w, up_w, down_w):
    rows, depth = tokens.shape
    pair = 2 * rows
    group_rows = chips * pair
    hidden = gate_w.shape[1]
    return pl.pallas_call(
        lambda *refs: feed_kernel(chips, *refs),
        in_specs=[VMEM] + [ANYWHERE] * 4,
        out_specs=[VMEM] + [ANYWHERE] * 4,
        out_shape=[
            jax.ShapeDtypeStruct((rows, depth), jnp.float32),
            jax.ShapeDtypeStruct((group_rows, depth), low),
        ] + [jax.ShapeDtypeStruct((group_rows, hidden), low)] * 3,
        scratch_shapes=[
            pltpu.VMEM((group_rows, depth), low),
            pltpu.VMEM(gate_w.shape, low),
            pltpu.VMEM(up_w.shape, low),
            pltpu.VMEM(down_w.shape, low),
            pltpu.VMEM((2, pair, depth), low),
            pltpu.VMEM((2, pair, hidden), low),
            pltpu.VMEM((2, pair, hidden), low),
            pltpu.VMEM((2, pair, hidden), low),
            pltpu.VMEM((rows, depth), jnp.float32),
            pltpu.VMEM((pair, depth), low),
            pltpu.VMEM((2, rows, depth), low),
            pltpu.VMEM((chips, rows, depth), low),
            pltpu.VMEM((chips - 1, rows, depth), low),
            pltpu.VMEM((chips - 1, rows, depth), low),
            DMA((3,)), DMA((2,)), DMA((chips,)), DMA((3, 2)),
            DMA((chips,)), DMA((chips,)), DMA((chips,)), DMA((chips,)),
            DMA((2,)), DMA((chips,)), DMA((chips - 1,)), DMA((chips - 1,)),
        ],
        compiler_params=pltpu.CompilerParams(collective_id=3, has_side_effects=True, vmem_limit_bytes=63 << 20),
        cost_estimate=pl.CostEstimate(flops=12 * group_rows * depth * hidden, bytes_accessed=10 * group_rows * depth, transcendentals=group_rows * hidden),
        name="feed",
    )(tokens, grads, gate_w, up_w, down_w)


def rms_norm(values, gain):
    return values * lax.rsqrt(jnp.mean(values * values, axis=-1, keepdims=True) + norm_eps) * gain


def rope_tables(width):
    half = HEAD_DIM // 2
    positions = jnp.arange(SEQ_LEN, dtype=jnp.int32).astype(jnp.float32)
    column = jnp.arange(width, dtype=jnp.int32) % half
    inverse = jnp.power(jnp.float32(rope_base), -2.0 * column.astype(jnp.float32) / HEAD_DIM)
    angle = positions[:, None] * inverse[None, :]
    return (jnp.cos(angle), jnp.sin(angle))


def swap_sum(values, mesh):
    for axis in ("tp", "fsdp"):
        step = 1
        while step < mesh[axis]:
            values = values + lax.ppermute(values, axis, [(i, i ^ step) for i in range(mesh[axis])])
            step *= 2
    return values


def make_body(mesh):
    sizes = dict(mesh.shape)
    chips, shards = sizes["tp"] // 2, sizes["fsdp"]

    def body(activations, gain_attn, w_query, w_key, w_value, w_out, gain_mlp, w_gate, w_up, w_down, cotangent):
        width = w_query.shape[1]
        full_out = lax.all_gather(w_out, "fsdp", axis=1, tiled=True)
        full_gate = lax.all_gather(w_gate, "fsdp", axis=0, tiled=True)
        full_up = lax.all_gather(w_up, "fsdp", axis=0, tiled=True)
        full_down = lax.all_gather(w_down, "fsdp", axis=1, tiled=True)
        cosine, sine = rope_tables(LANES)

        normed_attn = rms_norm(activations, gain_attn).astype(low)
        seen_attn, w_qkv, qkv, keys_t, values_t = project(chips, shards, normed_attn, w_query, w_key, w_value, cosine, sine)
        attn_branch, mixed, totals, seen_grad = attend(chips, qkv, values_t, full_out, cotangent.astype(low))
        hidden_state = activations + attn_branch
        normed_mlp = rms_norm(hidden_state, gain_mlp).astype(low)
        normed_mlp_grad, seen_mlp, inner, gate_grad, up_grad = feed(chips, normed_mlp, seen_grad, full_gate, full_up, full_down)
        _, pull_norm_mlp = jax.vjp(rms_norm, hidden_state, gain_mlp)
        hidden_norm_grad, gain_mlp_part = pull_norm_mlp(normed_mlp_grad)
        hidden_grad = cotangent + hidden_norm_grad

        def over_fsdp(grad, dimension):
            return lax.psum_scatter(grad, "fsdp", scatter_dimension=dimension, tiled=True)

        branch_grad, grad_down, grad_gate, grad_up = lax.optimization_barrier(
            (
                hidden_grad.astype(low),
                dot(inner, seen_grad, TN).astype(low),
                dot(seen_mlp, gate_grad, TN).astype(low),
                dot(seen_mlp, up_grad, TN).astype(low),
            )
        )
        grad_down, grad_gate, grad_up = over_fsdp(grad_down, 1), over_fsdp(grad_gate, 0), over_fsdp(grad_up, 0)
        down, seen_branch, qkv_grad = back(
            chips, branch_grad, inner, full_down, full_out, qkv, keys_t, mixed, totals, cosine, sine
        )
        output = hidden_state + down
        qkv_grad, grad_out, grad_qkv, grad_down, grad_gate, grad_up = lax.optimization_barrier(
            (
                qkv_grad,
                dot(mixed, seen_branch, TN).astype(low),
                dot(seen_attn, qkv_grad, TN).astype(low),
                grad_down,
                grad_gate,
                grad_up,
            )
        )
        grad_out, grad_qkv = over_fsdp(grad_out, 1), over_fsdp(grad_qkv, 0)
        normed_attn_grad = spread(chips, qkv_grad, w_qkv)
        _, pull_norm_attn = jax.vjp(rms_norm, activations, gain_attn)
        input_norm_grad, gain_attn_part = pull_norm_attn(normed_attn_grad)
        input_grad = hidden_grad + input_norm_grad
        gain_sums = swap_sum(jnp.stack([gain_attn_part, gain_mlp_part]), sizes)
        grad_query, grad_key, grad_value = [grad_qkv[:, part * width : (part + 1) * width] for part in range(3)]
        weights = [
            grad.astype(jnp.float32)
            for grad in (grad_query, grad_key, grad_value, grad_out, grad_gate, grad_up, grad_down)
        ]
        return (output, input_grad, gain_sums[0], *weights[:4], gain_sums[1], *weights[4:])

    return body


def solution(mesh):
    tokens = P(("fsdp", "tp"), None)
    column = P("fsdp", "tp")
    row = P("tp", "fsdp")
    in_specs = (tokens, P(), column, column, column, row, P(), column, column, row, tokens)
    out_specs = (tokens, tokens, P(), column, column, column, row, P(), column, column, row)
    return jax.shard_map(make_body(mesh), mesh=mesh, in_specs=in_specs, out_specs=out_specs, check_vma=False)
```

time: 836 us -> 703 us (0.84)
  Pallas kernels: 274 us -> 548 us
  waiting for transfers between devices: 239 us -> 31.8 us
  local copies, waits for them, and re-layouts: 73.5 us -> 9.79 us
  starting transfers between devices: 56.9 us -> 4.34 us
  matrix products: 113 us -> 60.8 us
  other arithmetic: 52.1 us -> 27.5 us
    pallas_call x14 -> x5, Pallas kernels: 274 us -> 548 us  [the longest x1 144 us: feed(): pl.pallas_call(lambda *refs: feed_kernel(chips, *refs), in_specs=[VMEM] +...]
    ppermute x42 -> x0, waiting for transfers between devices: 231 us -> none  [the longest x9 132 us: scatter(): term = term + lax.ppermute(total, 'tp', self.forward).astype(jnp.float32)]
    dot_general x26 -> x5, matrix products: 113 us -> 60.8 us  [dot(): lax.dot_general(left, right, dims, preferred_element_type=jnp.float32)]
    ppermute x42 -> x0, starting transfers between devices: 48.6 us -> none  [the longest x9 23.1 us: gather(): lax.ppermute(block, 'tp', self.forward)]
    unnamed x100 -> x58, local copies, waits for them, and re-layouts: 36.5 us -> 9.17 us
    dynamic_update_slice x7 -> x0, local copies, waits for them, and re-layouts: 16.4 us -> none  [the longest x4 9.32 us: body(): lax.dynamic_update_slice_in_dim(all_grads, other, starts[slot] + (1 - cor...]
    reduce_scatter x5, waiting for transfers between devices: 0.01 us -> 9.9 us  [over_fsdp(): lax.psum_scatter(grad, 'fsdp', scatter_dimension=dimension, tiled=True)]
    convert_element_type x11 -> x9, other arithmetic: 22.1 us -> 15.3 us  [the longest x5 8.84 us: body(): grad.astype(jnp.float32)]
  transfers between devices with their start and end apart: 57 -> 14, of which waited for: 20 -> 6; matrix products, arithmetic and copies ran while one was open for 26% -> 6% of each run, Pallas kernels for 16% -> 58%
where the time goes in v3:
time: 703 us; the launch traced here: 697 us
  Pallas kernels  548 us (78%)
  matrix products  60.8 us (9%)
  waiting for transfers between devices  31.8 us (5%)
  other arithmetic  27.5 us (4%)
  between operations  14.4 us (2%)
  local copies, waits for them, and re-layouts  9.79 us (1%)
    pallas_call x1, Pallas kernels, feed(): pl.pallas_call(lambda *refs: feed_kernel(chips, *refs), in_specs=[VMEM] +...  144 us
    pallas_call x1, Pallas kernels, back(): pl.pallas_call(lambda *refs: back_kernel(chips, *refs), in_specs=[VMEM, A...  135 us
    pallas_call x1, Pallas kernels, attend(): pl.pallas_call(lambda *refs: attend_kernel(chips, *refs), in_specs=[VMEM]...  102 us
    pallas_call x1, Pallas kernels, project(): pl.pallas_call(lambda *refs: project_kernel(chips, shards, *refs), in_spe...  84.5 us
    pallas_call x1, Pallas kernels, spread(): pl.pallas_call(lambda *refs: spread_kernel(chips, *refs), in_specs=[VMEM]...  83.4 us
    dot_general x5, matrix products, dot(): lax.dot_general(left, right, dims, preferred_element_type=jnp.float32)  60.8 us
  transfers between devices with their start and end apart: 14, of which 6 were waited for; matrix products, arithmetic and copies ran while one was open for 6% of the time, Pallas kernels for 58%

profile of v3, /device:TPU:0, one launch (start us, length us, event | category | flops | bytes accessed | tf_op | source)
XLA Modules:
  0.0 696.8 jit_solution(2838600006125497425)
XLA Ops:
  10.0 2.7 convert_element_type.77.refs_3_
  13.6 3.7 multiply_sine_fusion
  19.0 84.5 %project.1 = (bf16[2048,2048]{1,0:T(8,128)(2,1)}, bf16[2048,768]{1,0:T(8,128)(2,1)S(1)}, bf16[2048,768]{1,0:T(8,128)(2,1)S(1)}, bf16[256,2048]{1,0:T(8,128)(2,1)S(1)}, bf16[256,2048]{1,0:T(8,128)(2,1)S(1)}) custom-call(bf16[256,2048]{1,0:T(8,128)(2,1)S(1)} %multiply_convert_fusion.1.refs_0_, bf16[512,256]{1,0:T(8,128)(2,1)S(1)} %copy-done.2, ...), custom_call_target="tpu_custom_call" | custom-call | flops 6442450944 | bytes 16777216 | tf_op jit(solution)/shard_map/project/pallas_call | solution.py:349
  103.5 1.6 copy-done.5
  105.1 1.7 copy-done.6
  108.7 101.7 %attend.1 = (f32[256,2048]{1,0:T(8,128)}, bf16[2048,256]{1,0:T(8,128)(2,1)}, f32[4,2048]{1,0:T(4,128)}, bf16[2048,2048]{1,0:T(8,128)(2,1)}) custom-call(bf16[2048,768]{1,0:T(8,128)(2,1)} %copy-done.5, bf16[256,2048]{1,0:T(8,128)(2,1)} %copy-done.8, bf16[256,2048]{1,0:T(8,128)(2,1)} %all-gather.5.cloned.1.call-done.refs_2_.refs_3_, ...), custom_call_target="tpu_custom_call" | custom-call | flops 4294967296 | bytes 16777216 | tf_op jit(solution)/shard_map/attend/pallas_call | solution.py:455
  210.4 1.9 multiply_reduce_fusion.4
  212.4 1.3 copy-done.12
  214.9 8.0 %all-gather.11.cloned.1.call-done.refs_4_.refs_2_ = bf16[1024,2048]{1,0:T(8,128)(2,1)} async-done(((bf16[1024,512]{1,0:T(8,128)(2,1)}), bf16[1024,2048]{1,0:T(8,128)(2,1)}) %all-gather.11.cloned.1.call-update) | async-done | bytes 4194320 | tf_op jit(solution)/shard_map/all_gather | solution.py:933
  222.9 143.9 %feed.1 = (f32[256,2048]{1,0:T(8,128)}, bf16[2048,2048]{1,0:T(8,128)(2,1)}, bf16[2048,1024]{1,0:T(8,128)(2,1)}, bf16[2048,1024]{1,0:T(8,128)(2,1)}, bf16[2048,1024]{1,0:T(8,128)(2,1)}) custom-call(bf16[256,2048]{1,0:T(8,128)(2,1)} %multiply_convert_fusion.refs_0_, bf16[2048,2048]{1,0:T(8,128)(2,1)} %get-tuple-element.41.refs_1_, ...), custom_call_target="tpu_custom_call" | custom-call | flops 51539607552 | bytes 41943040 | tf_op jit(solution)/shard_map/feed/pallas_call | solution.py:869
  366.8 14.3 %convolution_convert_fusion = bf16[1024,2048]{1,0:T(8,128)(2,1)} fusion(bf16[2048,1024]{1,0:T(8,128)(2,1)} %get-tuple-element.43.refs_1_, bf16[2048,2048]{1,0:T(8,128)(2,1)} %get-tuple-element.41.refs_1_), kind=kOutput, calls=%fused_computation | convolution fusion | flops 8592031744 | bytes 16777216 | tf_op jit(solution)/shard_map/dot_general | solution.py:26
  381.1 14.0 %convolution_convert_fusion.2 = bf16[2048,1024]{1,0:T(8,128)(2,1)} fusion(bf16[2048,2048]{1,0:T(8,128)(2,1)} %get-tuple-element.44, bf16[2048,1024]{1,0:T(8,128)(2,1)} %get-tuple-element.45), kind=kOutput, calls=%fused_computation.2 | convolution fusion | flops 8592031744 | bytes 16777216 | tf_op jit(solution)/shard_map/dot_general | solution.py:26
  395.1 14.6 %convolution_convert_fusion.1 = bf16[2048,1024]{1,0:T(8,128)(2,1)} fusion(bf16[2048,2048]{1,0:T(8,128)(2,1)} %get-tuple-element.44, bf16[2048,1024]{1,0:T(8,128)(2,1)} %get-tuple-element.46), kind=kOutput, calls=%fused_computation.1 | convolution fusion | flops 8592031744 | bytes 16777216 | tf_op jit(solution)/shard_map/dot_general | solution.py:26
  409.8 2.3 multiply_reduce_fusion
  412.6 2.3 fusion.8
  416.3 134.8 %back.1 = (f32[256,2048]{1,0:T(8,128)}, bf16[2048,2048]{1,0:T(8,128)(2,1)}, bf16[2048,768]{1,0:T(8,128)(2,1)}) custom-call(bf16[256,2048]{1,0:T(8,128)(2,1)} %get-tuple-element.47.refs_0_, bf16[2048,1024]{1,0:T(8,128)(2,1)} %get-tuple-element.43.refs_1_, bf16[1024,2048]{1,0:T(8,128)(2,1)} %all-gather.11.cloned.1.call-done.refs_4_.refs_2_, ...), custom_call_target="tpu_custom_call" | custom-call | flops 16106127360 | bytes 25165824 | tf_op jit(solution)/shard_map/back/pallas_call | solution.py:619
  551.1 7.3 %convolution_convert_fusion.4 = bf16[256,2048]{1,0:T(8,128)(2,1)} fusion(bf16[2048,256]{1,0:T(8,128)(2,1)} %get-tuple-element.49.refs_6_, bf16[2048,2048]{1,0:T(8,128)(2,1)} %get-tuple-element.53), kind=kOutput, calls=%fused_computation.6 | convolution fusion | flops 2148007936 | bytes 10485760 | tf_op jit(solution)/shard_map/dot_general | solution.py:26
  558.4 10.6 %convolution_convert_fusion.3 = bf16[2048,768]{1,0:T(8,128)(2,1)} fusion(bf16[2048,2048]{1,0:T(8,128)(2,1)} %get-tuple-element.54, bf16[2048,768]{1,0:T(8,128)(2,1)S(1)} %copy-done.7), kind=kOutput, calls=%fused_computation.3 | convolution fusion | flops 6444023808 | bytes 14680064 | tf_op jit(solution)/shard_map/dot_general | solution.py:26
  569.0 9.9 %reduce-scatter.10.cloned.1.call-done = bf16[512,1024]{1,0:T(8,128)(2,1)} async-done(((bf16[2048,1024]{1,0:T(8,128)(2,1)}), bf16[512,1024]{1,0:T(8,128)(2,1)}) %reduce-scatter.10.cloned.1.call-update) | async-done | bytes 1048592 | tf_op jit(solution)/shard_map/reduce_scatter | solution.py:947
  579.7 83.4 %spread.1 = f32[256,2048]{1,0:T(8,128)S(1)} custom-call(bf16[2048,768]{1,0:T(8,128)(2,1)S(1)} %copy-done.7, bf16[2048,768]{1,0:T(8,128)(2,1)} %copy-done.6), custom_call_target="tpu_custom_call" | custom-call | flops 6442450944 | bytes 6291456 | tf_op jit(solution)/shard_map/spread/pallas_call | solution.py:681
  665.1 3.7 collective-permute-done.1
  669.8 1.6 add.80
  671.4 2.1 collective-permute-done.2
  673.5 1.4 collective-permute-start.3
  675.0 2.4 collective-permute-done.3
  677.3 1.4 collective-permute-start.4
  678.8 1.8 fusion.1
  680.6 1.6 convert_element_type.89
  682.2 1.6 convert_element_type.90
  683.7 1.6 convert_element_type.91
  686.0 1.8 convert_element_type.88
  687.8 2.3 slice_convert_fusion
  (102 shorter events, 14.7 us)
Async XLA Ops:
  7.2 101.5 %all-gather.5.cloned.1.call-start = ((), (), s32[]{:S(2)}) async-start(), calls=%async_computation.5 | async-start | bytes 1310720 | tf_op jit(solution)/shard_map/all_gather | solution.py:930
  7.9 207.0 %all-gather.7.cloned.1.call-start = ((), (), s32[]{:S(2)}) async-start(), calls=%async_computation.6 | async-start | bytes 5242880 | tf_op jit(solution)/shard_map/all_gather | solution.py:931
  8.7 206.2 %all-gather.9.cloned.1.call-start = ((), (), s32[]{:S(2)}) async-start(), calls=%async_computation.7 | async-start | bytes 5242880 | tf_op jit(solution)/shard_map/all_gather | solution.py:932
  9.4 3.4 copy-start.10
  9.4 213.5 %all-gather.11.cloned.1.call-start = ((), (), s32[]{:S(2)}) async-start(), calls=%async_computation.8 | async-start | bytes 5242880 | tf_op jit(solution)/shard_map/all_gather | solution.py:933
  10.0 559.0 %reduce-scatter.6.cloned.1.call-start = ((), (), s32[]{:S(2)}) async-start(), calls=%async_computation.9 | async-start | bytes 5242880 | tf_op jit(solution)/shard_map/reduce_scatter | solution.py:947
  12.8 4.5 copy-start.23
  13.6 4.0 copy-start.25
  17.3 1.7 copy-start.4
  105.1 1.7 copy-start.6
  210.4 3.2 copy-start.22
  395.1 14.6 %copy-start.13 = (f32[256,2048]{1,0:T(8,128)S(1)}, f32[256,2048]{1,0:T(8,128)}, u32[]{:S(2)}) copy-start(f32[256,2048]{1,0:T(8,128)} %copy-done.12) | copy-start | bytes 6291460
  409.7 2.3 copy-start.15
  409.7 2.9 copy-start.17
  415.0 154.0 %reduce-scatter.8.cloned.1.call-start = ((), (), s32[]{:S(2)}) async-start(), calls=%async_computation.10 | async-start | bytes 5242880 | tf_op jit(solution)/shard_map/reduce_scatter | solution.py:947
  415.5 163.3 %reduce-scatter.10.cloned.1.call-start = ((), (), s32[]{:S(2)}) async-start(), calls=%async_computation.11 | async-start | bytes 5242880 | tf_op jit(solution)/shard_map/reduce_scatter | solution.py:947
  416.3 269.7 %reduce-scatter.14.cloned.1.call-start = ((), (), s32[]{:S(2)}) async-start(), calls=%async_computation.13 | async-start | bytes 1310720 | tf_op jit(solution)/shard_map/reduce_scatter | solution.py:947
  551.1 7.3 %copy-start.7 = (bf16[2048,768]{1,0:T(8,128)(2,1)S(1)}, bf16[2048,768]{1,0:T(8,128)(2,1)}, u32[]{:S(2)}) copy-start(bf16[2048,768]{1,0:T(8,128)(2,1)} %get-tuple-element.58.refs_0_) | copy-start | bytes 9437188
  578.9 108.9 %reduce-scatter.12.cloned.1.call-start = ((), (), s32[]{:S(2)}) async-start(), calls=%async_computation.12 | async-start | bytes 3932160 | tf_op jit(solution)/shard_map/reduce_scatter | solution.py:947
  579.6 83.4 %copy-start.11 = (f32[256,2048]{1,0:T(8,128)S(1)}, f32[256,2048]{1,0:T(8,128)}, u32[]{:S(2)}) copy-start(f32[256,2048]{1,0:T(8,128)} %param.11) | copy-start | bytes 6291460
  579.6 83.4 %copy-start.24 = (f32[2048]{0:T(1024)S(1)}, f32[2048]{0:T(1024)}, u32[]{:S(2)}) copy-start(f32[2048]{0:T(1024)} %param.12) | copy-start | bytes 24580
  579.6 83.4 %copy-start.26 = (f32[256]{0:T(256)S(1)}, f32[256]{0:T(256)}, u32[]{:S(2)}) copy-start(f32[256]{0:T(256)} %copy-done.25) | copy-start | bytes 3076
  663.1 6.7 copy-start.14
  663.1 6.7 copy-start.18
  663.7 1.2 collective-permute-start
  665.0 3.8 collective-permute-start.1
  668.8 4.7 collective-permute-start.2
  669.8 5.2 copy-start.28
  669.8 9.0 %copy-start.16 = (f32[256,2048]{1,0:T(8,128)S(1)}, f32[256,2048]{1,0:T(8,128)}, u32[]{:S(2)}) copy-start(f32[256,2048]{1,0:T(8,128)} %get-tuple-element.70) | copy-start | bytes 6291460
  673.5 3.8 collective-permute-start.3
  677.3 8.0 %collective-permute-start.4 = (f32[2,2048]{1,0:T(2,128)S(1)}, f32[2,2048]{1,0:T(2,128)S(1)}, u32[]{:S(2)}, u32[]{:S(2)}) collective-permute-start(f32[2,2048]{1,0:T(2,128)S(1)} %add.85), channel_id=1, source_target_pairs={{0,16},{8,24},{16,0},{24,8},{1,17},{9,25},{17,1},{25,9},{2,18},{10... | collective-permute-start | bytes 49160 | tf_op jit(solution)/shard_map/ppermute | solution.py:919
  678.8 1.8 copy-start.20
  (11 other events, 13.6 us)
Sparse Core Ops, SparseCore 0:
  9.8 50.3 all-gather.4
  62.1 51.9 all-gather.6
  115.9 52.7 all-gather.8
  170.3 52.5 all-gather.10
  415.1 52.2 reduce-scatter.5
  470.4 52.6 reduce-scatter.7
  526.1 52.6 reduce-scatter.9
  582.0 27.7 reduce-scatter.13
  612.8 43.9 reduce-scatter.11

commit v4 on v3

--- a/solution.py
+++ b/solution.py
@@ -72,6 +72,11 @@
         late = step - (most - least)
         side = jnp.where(late % 2 == 0, sign, -sign)
         return jnp.where(late < 0, self.chip + sign * (most - step), self.chip + side * (least - late // 2))
+
+
+    def fed(self, target):
+        after, before = jnp.logical_and(target >= self.chip, self.has_left), jnp.logical_and(target <= self.chip, self.has_right)
+        return jnp.logical_or(after, before)
 
 
 class Gather:
@@ -224,6 +229,28 @@
             self.share(step).wait_send()
 
 
+NORM_ROWS = 64
+
+
+def normed(value, gain):
+    return value * lax.rsqrt(jnp.mean(value * value, axis=-1, keepdims=True) + norm_eps) * gain
+
+
+def norm_back(value, gain, grad):
+    scale = lax.rsqrt(jnp.mean(value * value, axis=-1, keepdims=True) + norm_eps)
+    unit = value * scale
+    scaled = grad * gain
+    return scale * (scaled - unit * jnp.mean(scaled * unit, axis=-1, keepdims=True)), jnp.sum(grad * unit, axis=0, keepdims=True)
+
+
+def by_rows(rows, work):
+    def step(index, carry):
+        work(span(index, NORM_ROWS))
+        return carry
+
+    lax.fori_loop(0, rows // NORM_ROWS, step, 0)
+
+
 def turned(block, sign):
     half = HEAD_DIM // 2
     lane = lax.broadcasted_iota(jnp.int32, block.shape, 1)
@@ -262,9 +289,9 @@
 
 def project_kernel(
     chips, shards,
-    tokens, w_query, w_key, w_value, cosine, sine,
-    tokens_out, weight, qkv, keys_t, values_t,
-    chunks, chunk_sem, weight_send, weight_recv, weight_keep, *gather_sems,
+    activations, gain, w_query, w_key, w_value, cosine_t, sine_t,
+    tokens_out, weight, qkv, keys_t, values_t, cosine, sine,
+    tokens, chunks, chunk_sem, weight_send, weight_recv, weight_keep, *gather_sems,
 ):
     line = Line(chips)
     rows = tokens.shape[0]
@@ -275,21 +302,28 @@
     gather = Gather(line, tokens, tokens_out, *gather_sems)
     parts = (w_query, w_key, w_value)
 
-    def place(index, part):
-        return weight.at[span(index, depth), pl.ds(part * width, width)]
+    def place(part):
+        return weight.at[span(shard, depth), pl.ds(part * width, width)]
 
     def give(ahead, part):
-        return remote(parts[part], place(shard, part), weight_send.at[ahead, part], weight_recv.at[ahead, part], {"fsdp": others[ahead]})
+        return remote(parts[part], place(part), weight_send.at[ahead, part], weight_recv.at[ahead, part], {"fsdp": others[ahead]})
 
     def keep(part):
-        return pltpu.make_async_copy(parts[part], place(shard, part), weight_keep.at[part])
-
+        return pltpu.make_async_copy(parts[part], place(part), weight_keep.at[part])
+
+    def norm(here):
+        tokens[here, :] = normed(activations[here, :], gain[...]).astype(low)
+
+    by_rows(rows, norm)
     line.greet([{"fsdp": other} for other in others])
     gather.start()
     for part in range(3):
         keep(part).start()
         for ahead in range(shards - 1):
             give(ahead, part).start()
+    for table, table_t in ((cosine, cosine_t), (sine, sine_t)):
+        turn = table_t[...].T
+        table[...] = jnp.concatenate([turn] * (LANES // turn.shape[1]), axis=1)
 
     def project(chip):
         @pl.when(jnp.logical_and(chip >= 0, chip < chips))
@@ -341,27 +375,33 @@
             give(ahead, part).wait_send()
 
 
-def project(chips, shards, tokens, w_query, w_key, w_value, cosine, sine):
-    rows, depth = tokens.shape
+def project(chips, shards, activations, gain, w_query, w_key, w_value, cosine_t, sine_t):
+    rows, depth = activations.shape
     group_rows = 2 * chips * rows
-    shard_rows, width = w_query.shape
+    width = w_query.shape[1]
     shape = jax.ShapeDtypeStruct
     return pl.pallas_call(
         lambda *refs: project_kernel(chips, shards, *refs),
-        in_specs=[VMEM] * 6,
-        out_specs=[ANYWHERE] + [VMEM] * 4,
+        in_specs=[VMEM] * 7,
+        out_specs=[ANYWHERE] + [VMEM] * 6,
         out_shape=[
             shape((group_rows, depth), low),
             shape((depth, 3 * width), low),
             shape((group_rows, 3 * width), low),
             shape((width, group_rows), low),
             shape((width, group_rows), low),
+            shape((SEQ_LEN, LANES), jnp.float32),
+            shape((SEQ_LEN, LANES), jnp.float32),
         ],
-        scratch_shapes=[pltpu.VMEM((2 * rows, depth), low), DMA, DMA((shards - 1, 3)), DMA((shards - 1, 3)), DMA((3,))] + Gather.scratch(chips),
-        compiler_params=pltpu.CompilerParams(collective_id=1, has_side_effects=True, vmem_limit_bytes=40 << 20),
+        scratch_shapes=[
+            pltpu.VMEM((rows, depth), low),
+            pltpu.VMEM((2 * rows, depth), low),
+            DMA, DMA((shards - 1, 3)), DMA((shards - 1, 3)), DMA((3,)),
+        ] + Gather.scratch(chips),
+        compiler_params=pltpu.CompilerParams(collective_id=1, has_side_effects=True, vmem_limit_bytes=63 << 20),
         cost_estimate=pl.CostEstimate(flops=6 * group_rows * depth * width, bytes_accessed=4 * group_rows * depth, transcendentals=0),
         name="project",
-    )(tokens, w_query, w_key, w_value, cosine, sine)
+    )(activations, gain, w_query, w_key, w_value, cosine_t, sine_t)
 
 
 def attend_chunk(chunk, rows, qkv, values_t, heads_ref, acc, out, top_ref, sum_ref):
@@ -399,14 +439,15 @@
 
 def attend_kernel(
     chips,
-    qkv, values_t, w_out, grads,
-    branch, mixed, totals, grads_out,
-    heads_ref, acc, out, top_ref, sum_ref, *sems,
+    qkv, values_t, w_out, activations, cotangent, gain,
+    hidden, tokens, mixed, totals, grads_out,
+    heads_ref, acc, out, top_ref, sum_ref, grads, *sems,
 ):
     line = Line(chips)
-    rows, depth = branch.shape
+    rows, depth = hidden.shape
     pair = 2 * rows
-    scatter = Scatter(line, branch, *sems[:8])
+    scatter = Scatter(line, hidden, *sems[:8])
+    grads[...] = cotangent[...].astype(low)
     gather = Gather(line, grads, grads_out, *sems[8:])
     line.greet()
     gather.start()
@@ -441,12 +482,19 @@
         return carry
 
     lax.fori_loop(0, chips + 1, step, 0)
+
+    def norm(here):
+        state = activations[here, :] + hidden[here, :]
+        hidden[here, :] = state
+        tokens[here, :] = normed(state, gain[...]).astype(low)
+
+    by_rows(rows, norm)
     scatter.finish()
     gather.finish(True)
 
 
-def attend(chips, qkv, values_t, w_out, grads):
-    rows, depth = grads.shape
+def attend(chips, qkv, values_t, w_out, activations, cotangent, gain):
+    rows, depth = activations.shape
     pair = 2 * rows
     group_rows = chips * pair
     width = w_out.shape[0]
@@ -454,10 +502,11 @@
     shape = jax.ShapeDtypeStruct
     return pl.pallas_call(
         lambda *refs: attend_kernel(chips, *refs),
-        in_specs=[VMEM] * 4,
-        out_specs=[VMEM] * 3 + [ANYWHERE],
+        in_specs=[VMEM] * 6,
+        out_specs=[VMEM] * 4 + [ANYWHERE],
         out_shape=[
             shape((rows, depth), jnp.float32),
+            shape((rows, depth), low),
             shape((group_rows, width), low),
             shape((heads, group_rows), jnp.float32),
             shape((group_rows, depth), low),
@@ -468,11 +517,12 @@
             pltpu.VMEM((pair, width), low),
             pltpu.VMEM((heads, pair), jnp.float32),
             pltpu.VMEM((heads, pair), jnp.float32),
+            pltpu.VMEM((rows, depth), low),
         ] + Scatter.scratch(chips, rows, depth) + Gather.scratch(chips),
-        compiler_params=pltpu.CompilerParams(collective_id=2, has_side_effects=True, vmem_limit_bytes=60 << 20),
+        compiler_params=pltpu.CompilerParams(collective_id=2, has_side_effects=True, vmem_limit_bytes=63 << 20),
         cost_estimate=pl.CostEstimate(flops=2 * group_rows * (SEQ_LEN + depth) * width, bytes_accessed=4 * group_rows * depth, transcendentals=group_rows * SEQ_LEN * heads // 2),
         name="attend",
-    )(qkv, values_t, w_out, grads)
+    )(qkv, values_t, w_out, activations, cotangent, gain)
 
 
 def back_chunk(chunk, rows, grad, qkv, keys_t, mixed, totals, dkey, dvalue, heads_ref, grads_ref, acc, inner_ref):
@@ -512,10 +562,11 @@
 
 
 def back_kernel(
-    chips,
-    branch, inner, w_down, w_out, qkv, keys_t, mixed, totals, cosine, sine,
-    down, branch_out, qkv_grad,
-    down_w, inner_chunk, branch_chunk, dkey, dvalue, heads_ref, grads_ref, acc, inner_ref, load_sem, inner_sem, branch_sem, *sems,
+    chips, shards,
+    branch, inner, grads, w_down, w_out, qkv, keys_t, mixed, totals, cosine, sine,
+    down, branch_out, qkv_grad, grad_down, grad_out,
+    down_w, inner_chunk, grad_chunk, down_sum, down_tile, out_sum, out_stage, out_from, branch_chunk, dkey, dvalue, heads_ref, grads_ref, acc, inner_ref,
+    load_sem, inner_sem, grad_sem, branch_sem, tile_sem, out_send, out_recv, *sems,
 ):
     line = Line(chips)
     rows, depth = down.shape
@@ -530,10 +581,24 @@
     def fetch(step):
         return pltpu.make_async_copy(inner.at[span(line.target(step), pair)], inner_chunk.at[step % 2], inner_sem.at[step % 2])
 
+    def fetch_grad(step):
+        return pltpu.make_async_copy(grads.at[span(line.target(step), pair)], grad_chunk, grad_sem)
+
+    shard = lax.axis_index("fsdp")
+    columns_out = depth // shards
+    others = [(shard + ahead) % shards for ahead in range(1, shards)]
+
+    def give(turn):
+        return remote(out_stage.at[turn], out_from.at[turn], out_send.at[turn], out_recv.at[turn], {"fsdp": others[turn]})
+
+    def keep_tile(place):
+        return pltpu.make_async_copy(down_tile, grad_down.at[span(place, 256)], tile_sem)
+
     load().start()
     fetch(0).start()
-    line.greet()
+    line.greet([{"fsdp": other} for other in others])
     gather.start()
+    out_sum[...] = jnp.zeros_like(out_sum)
     dkey[...] = jnp.zeros_like(dkey)
     dvalue[...] = jnp.zeros_like(dvalue)
 
@@ -546,9 +611,19 @@
         copy = pltpu.make_async_copy(branch_out.at[span(chunk, pair)], branch_chunk, branch_sem)
         copy.start()
         copy.wait()
+        out_sum[...] += dot(mixed[span(chunk, pair), :], branch_chunk[...], TN)
         grad = dot(branch_chunk[...], w_out[...], NT).astype(low)
         back_chunk(chunk, pair, grad, qkv, keys_t, mixed, totals, dkey, dvalue, heads_ref, grads_ref, acc, inner_ref)
         qkv_grad[span(chunk, pair), pl.ds(0, width)] = unrotated(acc[...].T * HEAD_DIM**-0.5, chunk)
+
+    def close():
+        def part(chunk, carry):
+            here = span(chunk, pair)
+            qkv_grad[here, pl.ds(width, width)] = unrotated(dkey[here, :], chunk)
+            qkv_grad[here, pl.ds(2 * width, width)] = dvalue[here, :].astype(low)
+            return carry
+
+        lax.fori_loop(0, chips, part, 0)
 
     def step(index, carry):
         @pl.when(index == 0)
@@ -577,38 +652,83 @@
         def _():
             gather.step(index)
 
-        def side(which, carry):
-            chunk = jnp.where(which == 0, line.chip - index, line.chip + index)
+        @pl.when(index < chips)
+        def _():
+            fetch_grad(index).start()
+
+        @pl.when(index == chips)
+        def _():
+            for turn in range(shards - 1):
+                out_stage[turn] = out_sum[:, span(others[turn], columns_out)].astype(low)
+                give(turn).start()
+            close()
+
+        def phase(which, carry):
+            done = jnp.maximum(index - 1, 0)
+            late = line.fed(line.target(done))
+            turn = jnp.logical_or(jnp.logical_and(which == 0, jnp.logical_not(late)), jnp.logical_and(which == 3, late))
+
+            @pl.when(jnp.logical_and(index >= 1, turn))
+            def _():
+                scatter.step(done)
+
+            chunk = jnp.where(which == 1, line.chip - index, line.chip + index)
             there = jnp.logical_and(chunk >= 0, chunk < chips)
-
-            @pl.when(jnp.logical_and(there, jnp.logical_or(which == 0, index > 0)))
+            turn = jnp.logical_or(which == 1, jnp.logical_and(which == 2, index > 0))
+
+            @pl.when(jnp.logical_and(there, turn))
             def _():
                 attention(chunk)
 
             return carry
 
-        lax.fori_loop(0, 2, side, 0)
-
-        @pl.when(index >= 1)
-        def _():
-            scatter.step(index - 1)
+        lax.fori_loop(0, 4, phase, 0)
+
+        @pl.when(index < chips)
+        def _():
+            fetch_grad(index).wait()
+
+            def tile(place, carry):
+                here = span(place, 256)
+                part = dot(inner_chunk[index % 2, :, here], grad_chunk[...], TN)
+
+                @pl.when(index == 0)
+                def _():
+                    down_sum[here, :] = part
+
+                @pl.when(index > 0)
+                def _():
+                    down_sum[here, :] += part
+
+                @pl.when(index == chips - 1)
+                def _():
+                    @pl.when(place > 0)
+                    def _():
+                        keep_tile(place - 1).wait()
+
+                    down_tile[...] = down_sum[here, :].astype(low)
+                    keep_tile(place).start()
+
+                return carry
+
+            lax.fori_loop(0, down_sum.shape[0] // 256, tile, 0)
 
         return carry
 
     lax.fori_loop(0, chips + 1, step, 0)
-
-    def close(chunk, carry):
-        here = span(chunk, pair)
-        qkv_grad[here, pl.ds(width, width)] = unrotated(dkey[here, :], chunk)
-        qkv_grad[here, pl.ds(2 * width, width)] = dvalue[here, :].astype(low)
-        return carry
-
-    lax.fori_loop(0, chips, close, 0)
+    total = out_sum[:, span(shard, columns_out)]
+    for turn in range(shards - 1):
+        give(turn).wait_recv()
+        total = total + out_from[turn].astype(jnp.float32)
+    grad_out[...] = total
+    for turn in range(shards - 1):
+        give(turn).wait_send()
+    keep_tile(down_sum.shape[0] // 256 - 1).wait()
     scatter.finish()
     gather.finish(False)
 
 
-def back(chips, branch, inner, w_down, w_out, qkv, keys_t, mixed, totals, cosine, sine):
+def back(chips, shards, branch, inner, grads, w_down, w_out, qkv, keys_t, mixed, totals, cosine, sine):
     rows, depth = branch.shape
     pair = 2 * rows
     group_rows = chips * pair
@@ -617,17 +737,25 @@
     heads = width // HEAD_DIM
     shape = jax.ShapeDtypeStruct
     return pl.pallas_call(
-        lambda *refs: back_kernel(chips, *refs),
-        in_specs=[VMEM, ANYWHERE, ANYWHERE] + [VMEM] * 7,
-        out_specs=[VMEM, ANYWHERE, VMEM],
+        lambda *refs: back_kernel(chips, shards, *refs),
+        in_specs=[VMEM] + [ANYWHERE] * 3 + [VMEM] * 7,
+        out_specs=[VMEM, ANYWHERE, VMEM, ANYWHERE, VMEM],
         out_shape=[
             shape((rows, depth), jnp.float32),
             shape((group_rows, depth), low),
             shape((group_rows, 3 * width), low),
+            shape((hidden, depth), low),
+            shape((width, depth // shards), jnp.float32),
         ],
         scratch_shapes=[
             pltpu.VMEM((hidden, depth), low),
             pltpu.VMEM((2, pair, hidden), low),
+            pltpu.VMEM((pair, depth), low),
+            pltpu.VMEM((hidden, depth), jnp.float32),
+            pltpu.VMEM((256, depth), low),
+            pltpu.VMEM((width, depth), jnp.float32),
+            pltpu.VMEM((shards - 1, width, depth // shards), low),
+            pltpu.VMEM((shards - 1, width, depth // shards), low),
             pltpu.VMEM((pair, depth), low),
             pltpu.VMEM((group_rows, width), jnp.float32),
             pltpu.VMEM((group_rows, width), jnp.float32),
@@ -635,20 +763,69 @@
             pltpu.VMEM((heads, pair, width), low),
             pltpu.VMEM((width, pair), jnp.float32),
             pltpu.VMEM((8, pair), jnp.float32),
-            DMA, DMA((2,)), DMA,
+            DMA, DMA((2,)), DMA, DMA, DMA, DMA((shards - 1,)), DMA((shards - 1,)),
         ] + Scatter.scratch(chips, rows, depth) + Gather.scratch(chips),
-        compiler_params=pltpu.CompilerParams(collective_id=4, has_side_effects=True, vmem_limit_bytes=63 << 20),
-        cost_estimate=pl.CostEstimate(flops=2 * group_rows * (depth * hidden + depth * width + 5 * SEQ_LEN * width // 2), bytes_accessed=6 * group_rows * depth, transcendentals=group_rows * SEQ_LEN * heads // 2),
+        compiler_params=pltpu.CompilerParams(collective_id=4, has_side_effects=True, vmem_limit_bytes=67043328),
+        cost_estimate=pl.CostEstimate(flops=1 << 20, bytes_accessed=1 << 20, transcendentals=0),
         name="back",
-    )(branch, inner, w_down, w_out, qkv, keys_t, mixed, totals, cosine, sine)
-
-
-def spread_kernel(chips, qkv_grad, weight, out, *sems):
+    )(branch, inner, grads, w_down, w_out, qkv, keys_t, mixed, totals, cosine, sine)
+
+
+def spread_kernel(
+    chips, shards,
+    qkv_grad, weight, activations, gain, gain_part, attn_tokens,
+    input_part, grad_qkv, gain_sum,
+    attn_cols, qkv_stage, qkv_from, gains, gains_tp, gains_fsdp,
+    attn_sem, qkv_send, qkv_recv, tp_send, tp_recv, fsdp_send, fsdp_recv, *sems,
+):
     line = Line(chips)
-    rows, depth = out.shape
+    size = 2 * chips
+    rows, depth = input_part.shape
     pair = 2 * rows
-    scatter = Scatter(line, out, *sems)
-    line.greet()
+    shard = lax.axis_index("fsdp")
+    columns = depth // shards
+    scatter = Scatter(line, input_part, *sems)
+
+    def peer(turn):
+        return (shard + 1 + turn) % shards
+
+    def fetch(turn):
+        return pltpu.make_async_copy(attn_tokens.at[:, span(peer(turn), columns)], attn_cols.at[turn % 2], attn_sem.at[turn % 2])
+
+    def give(turn):
+        return remote(qkv_stage.at[turn], qkv_from.at[turn], qkv_send.at[turn], qkv_recv.at[turn], {"fsdp": peer(turn)})
+
+    def tell_tp(ahead):
+        return remote(gains, gains_tp.at[line.me], tp_send.at[ahead - 1], tp_recv.at[line.me], {"tp": (line.me + ahead) % size})
+
+    def tell_fsdp(ahead):
+        return remote(gains, gains_fsdp.at[shard], fsdp_send.at[ahead - 1], fsdp_recv.at[shard], {"fsdp": (shard + ahead) % shards})
+
+    fetch(0).start()
+    for ahead in range(1, size):
+        hello({"tp": (line.me + ahead) % size})
+    for ahead in range(1, shards):
+        hello({"fsdp": (shard + ahead) % shards})
+    pl.semaphore_wait(pltpu.get_barrier_semaphore(), size - 1 + shards - 1)
+
+    def weights(turn, carry):
+        @pl.when(turn < shards - 1)
+        def _():
+            fetch(turn + 1).start()
+
+        fetch(turn).wait()
+        part = dot(attn_cols[turn % 2], qkv_grad[...], TN)
+
+        @pl.when(turn < shards - 1)
+        def _():
+            qkv_stage[turn] = part.astype(low)
+            give(turn).start()
+
+        @pl.when(turn == shards - 1)
+        def _():
+            grad_qkv[...] = part
+
+        return carry
 
     def step(index, carry):
         @pl.when(index < chips)
@@ -657,37 +834,104 @@
             scatter.free(index)
 
             def tile(place, carry):
-                columns = span(place, 512)
-                scatter.term[index % 2, :, columns] = dot(qkv_grad[here, :], weight[columns, :], NT).astype(low)
+                there = span(place, 512)
+                scatter.term[index % 2, :, there] = dot(qkv_grad[here, :], weight[there, :], NT).astype(low)
                 return carry
 
             lax.fori_loop(0, depth // 512, tile, 0)
             scatter.share(index).start()
 
-        @pl.when(index >= 1)
-        def _():
-            scatter.step(index - 1)
-
+        def phase(which, carry):
+            done = jnp.maximum(index - 1, 0)
+            late = line.fed(line.target(done))
+            turn = jnp.logical_or(jnp.logical_and(which == 0, jnp.logical_not(late)), jnp.logical_and(which == 2, late))
+
+            @pl.when(jnp.logical_and(index >= 1, turn))
+            def _():
+                scatter.step(done)
+
+            @pl.when(jnp.logical_and(which == 1, index < 2))
+            def _():
+                lax.fori_loop(index, jnp.where(index == 0, 1, shards), weights, 0)
+
+            return carry
+
+        lax.fori_loop(0, 3, phase, 0)
         return carry
 
     lax.fori_loop(0, chips + 1, step, 0)
+    for turn in range(shards - 1):
+        give(turn).wait_recv()
+        grad_qkv[...] += qkv_from[turn].astype(jnp.float32)
+    gains[0:1, :] = jnp.zeros((1, depth), jnp.float32)
+    gains[1:2, :] = gain_part[...]
+
+    def norm(here):
+        part, grad = norm_back(activations[here, :], gain[...], input_part[here, :])
+        input_part[here, :] = part
+        gains[0:1, :] += grad
+
+    by_rows(rows, norm)
+
+    gains_tp[line.me] = gains[...]
+    for ahead in range(1, size):
+        tell_tp(ahead).start()
+    for ahead in range(1, size):
+        source = (line.me + ahead) % size
+        remote(gains, gains_tp.at[source], tp_send.at[0], tp_recv.at[source], {"tp": source}).wait_recv()
+    total = gains_tp[0]
+    for source in range(1, size):
+        total = total + gains_tp[source]
+    for ahead in range(1, size):
+        tell_tp(ahead).wait_send()
+    gains[...] = total
+    gains_fsdp[shard] = total
+    for ahead in range(1, shards):
+        tell_fsdp(ahead).start()
+    for ahead in range(1, shards):
+        source = (shard + ahead) % shards
+        remote(gains, gains_fsdp.at[source], fsdp_send.at[0], fsdp_recv.at[source], {"fsdp": source}).wait_recv()
+    total = gains_fsdp[0]
+    for source in range(1, shards):
+        total = total + gains_fsdp[source]
+    gain_sum[...] = total
+    for ahead in range(1, shards):
+        tell_fsdp(ahead).wait_send()
+    for turn in range(shards - 1):
+        give(turn).wait_send()
     scatter.finish()
 
 
-def spread(chips, qkv_grad, weight):
+def spread(chips, shards, qkv_grad, weight, activations, gain, gain_part, attn_tokens):
     group_rows = qkv_grad.shape[0]
-    rows = group_rows // (2 * chips)
-    depth = weight.shape[0]
+    rows, depth = activations.shape
+    width = qkv_grad.shape[1] // 3
+    columns = depth // shards
+    size = 2 * chips
+    shape = jax.ShapeDtypeStruct
     return pl.pallas_call(
-        lambda *refs: spread_kernel(chips, *refs),
-        in_specs=[VMEM] * 2,
-        out_specs=VMEM,
-        out_shape=jax.ShapeDtypeStruct((rows, depth), jnp.float32),
-        scratch_shapes=Scatter.scratch(chips, rows, depth),
-        compiler_params=pltpu.CompilerParams(collective_id=5, has_side_effects=True, vmem_limit_bytes=48 << 20),
-        cost_estimate=pl.CostEstimate(flops=2 * group_rows * weight.size, bytes_accessed=4 * weight.size, transcendentals=0),
+        lambda *refs: spread_kernel(chips, shards, *refs),
+        in_specs=[VMEM] * 5 + [ANYWHERE],
+        out_specs=[VMEM] * 3,
+        out_shape=[
+            shape((rows, depth), jnp.float32),
+            shape((columns, 3 * width), jnp.float32),
+            shape((2, depth), jnp.float32),
+        ],
+        scratch_shapes=[
+            pltpu.VMEM((2, group_rows, columns), low),
+            pltpu.VMEM((shards - 1, columns, 3 * width), low),
+            pltpu.VMEM((shards - 1, columns, 3 * width), low),
+            pltpu.VMEM((2, depth), jnp.float32),
+            pltpu.VMEM((size, 2, depth), jnp.float32),
+            pltpu.VMEM((shards, 2, depth), jnp.float32),
+            DMA((2,)), DMA((shards - 1,)), DMA((shards - 1,)),
+            DMA((size - 1,)), DMA((size,)), DMA((shards - 1,)), DMA((shards,)),
+        ] + Scatter.scratch(chips, rows, depth),
+        compiler_params=pltpu.CompilerParams(collective_id=5, has_side_effects=True, vmem_limit_bytes=63 << 20),
+        cost_estimate=pl.CostEstimate(flops=1 << 20, bytes_accessed=1 << 20, transcendentals=0),
         name="spread",
-    )(qkv_grad, weight)
+    )(qkv_grad, weight, activations, gain, gain_part, attn_tokens)
 
 
 def chip_at(place, chips):
@@ -700,68 +944,64 @@
 
 def feed_kernel(
     chips,
-    tokens_ref, grads_hbm, gate_hbm, up_hbm, down_hbm,
-    back_ref, tokens_out, inner_out, gate_out, up_out,
-    tokens_all, gate_w, up_w, down_w, grads, inner, gate_grad, up_grad, own, term, stage, from_core, from_ring, total,
-    load_sem, grad_sem, keep_sem, store_sem, ring_send, ring_recv, core_send, core_recv, stage_send, stage_recv, total_send, total_recv,
+    hidden_state, cotangent, gain, tokens, grads_hbm, both_hbm, down_hbm,
+    hidden_grad, branch, gain_part, inner_out, grad_both,
+    tokens_all, gate_w, up_w, down_w, grads, inner, gate_grad, up_grad, term, from_core, from_ring, total, tile_gate, tile_up,
+    load_sem, own_sem, grad_sem, store_sem, tile_sem,
+    ring_send, ring_recv, core_send, core_recv, share_send, share_recv, total_send, total_recv,
 ):
-    rows, depth = tokens_ref.shape
+    rows, depth = hidden_state.shape
     pair = 2 * rows
-    hidden = gate_w.shape[1]
+    width = gate_w.shape[1]
     me = lax.axis_index("tp")
     chip, core = me // 2, me % 2
     place = place_of(chip, chips)
-    following = 2 * chip_at((place + 1) % chips, chips) + core
-    before = 2 * chip_at((place + chips - 1) % chips, chips) + core
-    partner = 2 * chip + 1 - core
-
-    loads = [pltpu.make_async_copy(a, b, load_sem.at[i]) for i, (a, b) in enumerate(((gate_hbm, gate_w), (up_hbm, up_w), (down_hbm, down_w)))]
+    following = {"tp": 2 * chip_at((place + 1) % chips, chips) + core}
+    before = {"tp": 2 * chip_at((place + chips - 1) % chips, chips) + core}
+    partner = {"tp": 2 * chip + 1 - core}
+
+    loads = [pltpu.make_async_copy(a, b, load_sem.at[i]) for i, (a, b) in enumerate(((both_hbm.at[:, pl.ds(0, width)], gate_w), (both_hbm.at[:, pl.ds(width, width)], up_w), (down_hbm, down_w)))]
+    own = pltpu.make_async_copy(tokens, tokens_all.at[span(me, rows)], own_sem)
+
+    def source(slot):
+        return chip_at((place + chips - slot) % chips, chips)
+
+    def fetch(slot):
+        return pltpu.make_async_copy(grads_hbm.at[span(source(slot), pair)], grads.at[slot % 2], grad_sem.at[slot % 2])
+
+    def block(slot):
+        return tokens_all.at[span(2 * source(slot) + core, rows)]
+
+    def to_ring(slot):
+        return remote(block(slot), block(slot), ring_send.at[slot], ring_recv.at[slot], following)
+
+    def to_core(slot):
+        return remote(block(slot), block(slot), core_send.at[slot], core_recv.at[slot], partner)
+
+    def store(slot):
+        return pltpu.make_async_copy(inner.at[slot % 2], inner_out.at[span(source(slot), pair)], store_sem.at[slot % 2])
+
+    def share(slot):
+        place = jnp.where(slot == 0, 0, 1 + slot % 2)
+        return remote(term.at[span(1 - core, rows)], from_core.at[place], share_send, share_recv.at[place], partner)
+
+    def pass_on(slot):
+        return remote(total.at[slot % 2], from_ring.at[slot - 1], total_send.at[slot % 2], total_recv.at[slot - 1], following)
+
+    own.start()
+    fetch(0).start()
     for load in loads:
         load.start()
-
-    def source(slot):
-        return chip_at((place + chips - slot) % chips, chips)
-
-    def fetch(slot):
-        start = pl.multiple_of(source(slot) * pair, pair)
-        return pltpu.make_async_copy(grads_hbm.at[pl.ds(start, pair)], grads.at[slot % 2], grad_sem.at[slot % 2])
-
-    def block(ref, index):
-        return ref.at[pl.ds(pl.multiple_of(index * rows, rows), rows)]
-
-    def to_ring(slot):
-        index = 2 * source(slot) + core
-        return remote(block(tokens_all, index), block(tokens_all, index), ring_send.at[slot], ring_recv.at[slot], {"tp": following})
-
-    def to_core(slot):
-        index = 2 * source(slot) + core
-        return remote(block(tokens_all, index), block(tokens_all, index), core_send.at[slot], core_recv.at[slot], {"tp": partner})
-
-    def keep(slot):
-        start = pl.multiple_of(source(slot) * pair, pair)
-        span = pl.ds(start, pair)
-        return pltpu.make_async_copy(tokens_all.at[span], tokens_out.at[span], keep_sem.at[slot])
-
-    def stores(slot):
-        span = pl.ds(pl.multiple_of(source(slot) * pair, pair), pair)
-        return [
-            pltpu.make_async_copy(ref.at[slot % 2], out.at[span], store_sem.at[i, slot % 2])
-            for i, (ref, out) in enumerate(((inner, inner_out), (gate_grad, gate_out), (up_grad, up_out)))
-        ]
-
-    def stage_copy(slot):
-        return remote(stage.at[slot % 2], from_core.at[slot], stage_send.at[slot % 2], stage_recv.at[slot], {"tp": partner})
-
-    def total_copy(slot):
-        return remote(total.at[slot - 1], from_ring.at[slot - 1], total_send.at[slot - 1], total_recv.at[slot - 1], {"tp": following})
-
-    fetch(0).start()
-    tokens_all[pl.ds(pl.multiple_of(me * rows, rows), rows), :] = tokens_ref[...]
+    own.wait()
     for device in (following, before, partner):
-        hello({"tp": device})
+        hello(device)
     pl.semaphore_wait(pltpu.get_barrier_semaphore(), 3)
 
     def step(slot, carry):
+        here = slot % 2
+        wide_rows = span(source(slot), pair)
+        mine = span(core, rows)
+
         @pl.when(slot > 0)
         def _():
             to_ring(slot - 1).wait_recv()
@@ -780,207 +1020,203 @@
 
         @pl.when(slot > 1)
         def _():
-            for store in stores(slot - 2):
-                store.wait()
+            store(slot - 2).wait()
 
         to_core(slot).wait_recv()
-        keep(slot).start()
         fetch(slot).wait()
-        here = slot % 2
-        span = pl.ds(pl.multiple_of(source(slot) * pair, pair), pair)
 
         def narrow(tile, carry):
-            columns = pl.ds(pl.multiple_of(tile * 256, 256), 256)
-            token = tokens_all[span, :]
+            columns = span(tile, 256)
+            token = tokens_all[wide_rows, :]
             gate = dot(token, gate_w[:, columns])
             up = dot(token, up_w[:, columns])
             grad = dot(grads[here], down_w[columns, :], NT)
             squash = jax.nn.sigmoid(gate)
             act = gate * squash
-            inner[here, :, columns] = (act * up).astype(jnp.bfloat16)
-            up_grad[here, :, columns] = (grad * act).astype(jnp.bfloat16)
-            gate_grad[here, :, columns] = (grad * up * squash * (1.0 + gate * (1.0 - squash))).astype(jnp.bfloat16)
+            inner[here, :, columns] = (act * up).astype(low)
+            up_grad[wide_rows, columns] = (grad * act).astype(low)
+            gate_grad[wide_rows, columns] = (grad * up * squash * (1.0 + gate * (1.0 - squash))).astype(low)
             return carry
 
-        lax.fori_loop(0, hidden // 256, narrow, 0)
-        for store in stores(slot):
-            store.start()
-
-        @pl.when(slot > 1)
-        def _():
-            stage_copy(slot - 2).wait_send()
+        lax.fori_loop(0, width // 256, narrow, 0)
+        store(slot).start()
+
+        @pl.when(slot > 0)
+        def _():
+            share(slot - 1).wait_send()
 
         def wide(tile, carry):
-            columns = pl.ds(pl.multiple_of(tile * 256, 256), 256)
-            part = dot(gate_grad[here], gate_w[columns, :], NT) + dot(up_grad[here], up_w[columns, :], NT)
-            term[:, columns] = part.astype(jnp.bfloat16)
+            columns = span(tile, 256)
+            part = dot(gate_grad[wide_rows, :], gate_w[columns, :], NT) + dot(up_grad[wide_rows, :], up_w[columns, :], NT)
+            term[:, columns] = part.astype(low)
             return carry
 
         lax.fori_loop(0, depth // 256, wide, 0)
-        stage[here] = term[pl.ds(pl.multiple_of((1 - core) * rows, rows), rows), :]
-        stage_copy(slot).start()
-        mine = pl.ds(pl.multiple_of(core * rows, rows), rows)
+        share(slot).start()
 
         @pl.when(slot == 0)
         def _():
-            own[...] = term[mine, :].astype(jnp.float32)
+            hidden_grad[...] = term[mine, :].astype(jnp.float32)
 
         @pl.when(slot > 0)
         def _():
-            stage_copy(slot).wait_recv()
-
-        @pl.when(slot == 1)
-        def _():
-            total[slot - 1] = (term[mine, :].astype(jnp.float32) + from_core[slot].astype(jnp.float32)).astype(jnp.bfloat16)
-
-        @pl.when(slot > 1)
-        def _():
-            total_copy(slot - 1).wait_recv()
-            total[slot - 1] = (term[mine, :].astype(jnp.float32) + from_core[slot].astype(jnp.float32) + from_ring[slot - 2].astype(jnp.float32)).astype(jnp.bfloat16)
-
-        @pl.when(slot > 0)
-        def _():
-            total_copy(slot).start()
+            share(slot).wait_recv()
+
+            @pl.when(slot > 2)
+            def _():
+                pass_on(slot - 2).wait_send()
+
+            @pl.when(slot == 1)
+            def _():
+                total[here] = (term[mine, :].astype(jnp.float32) + from_core[1 + here].astype(jnp.float32)).astype(low)
+
+            @pl.when(slot > 1)
+            def _():
+                pass_on(slot - 1).wait_recv()
+                total[here] = (term[mine, :].astype(jnp.float32) + from_core[1 + here].astype(jnp.float32) + from_ring[slot - 2].astype(jnp.float32)).astype(low)
+
+            pass_on(slot).start()
 
         return carry
 
     lax.fori_loop(0, chips, step, 0)
-    stage_copy(0).wait_recv()
-    total_copy(chips - 1).wait_recv()
-    back_ref[...] = own[...] + from_core[0].astype(jnp.float32) + from_ring[chips - 2].astype(jnp.float32)
+
+    def tiles(index):
+        there = span(index, 256)
+        return (
+            pltpu.make_async_copy(tile_gate.at[index % 2], grad_both.at[there, pl.ds(0, width)], tile_sem.at[0, index % 2]),
+            pltpu.make_async_copy(tile_up.at[index % 2], grad_both.at[there, pl.ds(width, width)], tile_sem.at[1, index % 2]),
+        )
+
+    def weights(index, carry):
+        @pl.when(index > 1)
+        def _():
+            for copy in tiles(index - 2):
+                copy.wait()
+
+        token = tokens_all[:, span(index, 256)]
+        tile_gate[index % 2] = dot(token, gate_grad[...], TN).astype(low)
+        tile_up[index % 2] = dot(token, up_grad[...], TN).astype(low)
+        for copy in tiles(index):
+            copy.start()
+        return carry
+
+    lax.fori_loop(0, depth // 256, weights, 0)
+    share(0).wait_recv()
+    pass_on(chips - 1).wait_recv()
+    gain_part[...] = jnp.zeros_like(gain_part)
+
+    def norm(here):
+        grad = hidden_grad[here, :] + from_core[0, here, :].astype(jnp.float32) + from_ring[chips - 2, here, :].astype(jnp.float32)
+        part, gain_grad = norm_back(hidden_state[here, :], gain[...], grad)
+        full = cotangent[here, :] + part
+        hidden_grad[here, :] = full
+        branch[here, :] = full.astype(low)
+        gain_part[...] += gain_grad
+
+    by_rows(rows, norm)
+    share(chips - 1).wait_send()
     for slot in range(chips):
         to_core(slot).wait_send()
-        keep(slot).wait()
         if slot < chips - 1:
             to_ring(slot).wait_send()
-        if slot > 0:
-            total_copy(slot).wait_send()
+        if slot >= max(1, chips - 2):
+            pass_on(slot).wait_send()
         if slot >= chips - 2:
-            stage_copy(slot).wait_send()
-            for store in stores(slot):
-                store.wait()
-
-
-def feed(chips, tokens, grads, gate_w, up_w, down_w):
+            store(slot).wait()
+    for index in range(depth // 256 - 2, depth // 256):
+        for copy in tiles(index):
+            copy.wait()
+
+
+def feed(chips, hidden_state, cotangent, gain, tokens, grads, both_w, down_w):
     rows, depth = tokens.shape
     pair = 2 * rows
     group_rows = chips * pair
-    hidden = gate_w.shape[1]
+    width = down_w.shape[0]
+    shape = jax.ShapeDtypeStruct
     return pl.pallas_call(
         lambda *refs: feed_kernel(chips, *refs),
-        in_specs=[VMEM] + [ANYWHERE] * 4,
-        out_specs=[VMEM] + [ANYWHERE] * 4,
+        in_specs=[VMEM] * 3 + [ANYWHERE] * 4,
+        out_specs=[VMEM] * 3 + [ANYWHERE] * 2,
         out_shape=[
-            jax.ShapeDtypeStruct((rows, depth), jnp.float32),
-            jax.ShapeDtypeStruct((group_rows, depth), low),
-        ] + [jax.ShapeDtypeStruct((group_rows, hidden), low)] * 3,
+            shape((rows, depth), jnp.float32),
+            shape((rows, depth), low),
+            shape((1, depth), jnp.float32),
+            shape((group_rows, width), low),
+            shape((depth, 2 * width), low),
+        ],
         scratch_shapes=[
             pltpu.VMEM((group_rows, depth), low),
-            pltpu.VMEM(gate_w.shape, low),
-            pltpu.VMEM(up_w.shape, low),
+            pltpu.VMEM((depth, width), low),
+            pltpu.VMEM((depth, width), low),
             pltpu.VMEM(down_w.shape, low),
             pltpu.VMEM((2, pair, depth), low),
-            pltpu.VMEM((2, pair, hidden), low),
-            pltpu.VMEM((2, pair, hidden), low),
-            pltpu.VMEM((2, pair, hidden), low),
-            pltpu.VMEM((rows, depth), jnp.float32),
+            pltpu.VMEM((2, pair, width), low),
+            pltpu.VMEM((group_rows, width), low),
+            pltpu.VMEM((group_rows, width), low),
             pltpu.VMEM((pair, depth), low),
+            pltpu.VMEM((3, rows, depth), low),
+            pltpu.VMEM((chips - 1, rows, depth), low),
             pltpu.VMEM((2, rows, depth), low),
-            pltpu.VMEM((chips, rows, depth), low),
-            pltpu.VMEM((chips - 1, rows, depth), low),
-            pltpu.VMEM((chips - 1, rows, depth), low),
-            DMA((3,)), DMA((2,)), DMA((chips,)), DMA((3, 2)),
+            pltpu.VMEM((2, 256, width), low),
+            pltpu.VMEM((2, 256, width), low),
+            DMA((3,)), DMA, DMA((2,)), DMA((2,)), DMA((2, 2)),
             DMA((chips,)), DMA((chips,)), DMA((chips,)), DMA((chips,)),
-            DMA((2,)), DMA((chips,)), DMA((chips - 1,)), DMA((chips - 1,)),
+            DMA, DMA((3,)), DMA((2,)), DMA((chips - 1,)),
         ],
         compiler_params=pltpu.CompilerParams(collective_id=3, has_side_effects=True, vmem_limit_bytes=63 << 20),
-        cost_estimate=pl.CostEstimate(flops=12 * group_rows * depth * hidden, bytes_accessed=10 * group_rows * depth, transcendentals=group_rows * hidden),
+        cost_estimate=pl.CostEstimate(flops=16 * group_rows * depth * width, bytes_accessed=10 * group_rows * depth, transcendentals=group_rows * width),
         name="feed",
-    )(tokens, grads, gate_w, up_w, down_w)
-
-
-def rms_norm(values, gain):
-    return values * lax.rsqrt(jnp.mean(values * values, axis=-1, keepdims=True) + norm_eps) * gain
-
-
-def rope_tables(width):
+    )(hidden_state, cotangent, gain, tokens, grads, both_w, down_w)
+
+
+def rope_tables():
     half = HEAD_DIM // 2
     positions = jnp.arange(SEQ_LEN, dtype=jnp.int32).astype(jnp.float32)
-    column = jnp.arange(width, dtype=jnp.int32) % half
+    column = jnp.arange(half, dtype=jnp.int32)
     inverse = jnp.power(jnp.float32(rope_base), -2.0 * column.astype(jnp.float32) / HEAD_DIM)
-    angle = positions[:, None] * inverse[None, :]
+    angle = positions[None, :] * inverse[:, None]
     return (jnp.cos(angle), jnp.sin(angle))
 
 
-def swap_sum(values, mesh):
-    for axis in ("tp", "fsdp"):
-        step = 1
-        while step < mesh[axis]:
-            values = values + lax.ppermute(values, axis, [(i, i ^ step) for i in range(mesh[axis])])
-            step *= 2
-    return values
-
-
 def make_body(mesh):
-    sizes = dict(mesh.shape)
-    chips, shards = sizes["tp"] // 2, sizes["fsdp"]
+    chips, shards = mesh.shape["tp"] // 2, mesh.shape["fsdp"]
 
     def body(activations, gain_attn, w_query, w_key, w_value, w_out, gain_mlp, w_gate, w_up, w_down, cotangent):
         width = w_query.shape[1]
         full_out = lax.all_gather(w_out, "fsdp", axis=1, tiled=True)
-        full_gate = lax.all_gather(w_gate, "fsdp", axis=0, tiled=True)
-        full_up = lax.all_gather(w_up, "fsdp", axis=0, tiled=True)
+        full_both = lax.all_gather(jnp.concatenate([w_gate, w_up], axis=1), "fsdp", axis=0, tiled=True)
         full_down = lax.all_gather(w_down, "fsdp", axis=1, tiled=True)
-        cosine, sine = rope_tables(LANES)
-
-        normed_attn = rms_norm(activations, gain_attn).astype(low)
-        seen_attn, w_qkv, qkv, keys_t, values_t = project(chips, shards, normed_attn, w_query, w_key, w_value, cosine, sine)
-        attn_branch, mixed, totals, seen_grad = attend(chips, qkv, values_t, full_out, cotangent.astype(low))
-        hidden_state = activations + attn_branch
-        normed_mlp = rms_norm(hidden_state, gain_mlp).astype(low)
-        normed_mlp_grad, seen_mlp, inner, gate_grad, up_grad = feed(chips, normed_mlp, seen_grad, full_gate, full_up, full_down)
-        _, pull_norm_mlp = jax.vjp(rms_norm, hidden_state, gain_mlp)
-        hidden_norm_grad, gain_mlp_part = pull_norm_mlp(normed_mlp_grad)
-        hidden_grad = cotangent + hidden_norm_grad
+        gain_attn, gain_mlp = gain_attn[None, :], gain_mlp[None, :]
+        seen_attn, w_qkv, qkv, keys_t, values_t, cosine, sine = project(
+            chips, shards, activations, gain_attn, w_query, w_key, w_value, *rope_tables()
+        )
+        hidden_state, normed_mlp, mixed, totals, seen_grad = attend(chips, qkv, values_t, full_out, activations, cotangent, gain_mlp)
+        hidden_grad, branch_grad, gain_part, inner, grad_both = feed(
+            chips, hidden_state, cotangent, gain_mlp, normed_mlp, seen_grad, full_both, full_down
+        )
 
         def over_fsdp(grad, dimension):
             return lax.psum_scatter(grad, "fsdp", scatter_dimension=dimension, tiled=True)
 
-        branch_grad, grad_down, grad_gate, grad_up = lax.optimization_barrier(
-            (
-                hidden_grad.astype(low),
-                dot(inner, seen_grad, TN).astype(low),
-                dot(seen_mlp, gate_grad, TN).astype(low),
-                dot(seen_mlp, up_grad, TN).astype(low),
-            )
-        )
-        grad_down, grad_gate, grad_up = over_fsdp(grad_down, 1), over_fsdp(grad_gate, 0), over_fsdp(grad_up, 0)
-        down, seen_branch, qkv_grad = back(
-            chips, branch_grad, inner, full_down, full_out, qkv, keys_t, mixed, totals, cosine, sine
+        grad_both = over_fsdp(grad_both, 0)
+        down, _, qkv_grad, grad_down, grad_out = back(
+            chips, shards, branch_grad, inner, seen_grad, full_down, full_out, qkv, keys_t, mixed, totals, cosine, sine
         )
         output = hidden_state + down
-        qkv_grad, grad_out, grad_qkv, grad_down, grad_gate, grad_up = lax.optimization_barrier(
-            (
-                qkv_grad,
-                dot(mixed, seen_branch, TN).astype(low),
-                dot(seen_attn, qkv_grad, TN).astype(low),
-                grad_down,
-                grad_gate,
-                grad_up,
-            )
+        grad_down = over_fsdp(grad_down, 1)
+        input_part, grad_qkv, gain_sums = spread(chips, shards, qkv_grad, w_qkv, activations, gain_attn, gain_part, seen_attn)
+        input_grad = hidden_grad + input_part
+        grad_query, grad_key, grad_value = [grad_qkv[:, part * width : (part + 1) * width] for part in range(3)]
+        hidden = w_gate.shape[1]
+        grad_gate, grad_up = grad_both[:, :hidden].astype(jnp.float32), grad_both[:, hidden:].astype(jnp.float32)
+        grad_down, grad_gate, grad_up = lax.optimization_barrier((grad_down, grad_gate, grad_up))
+        grad_down = grad_down.astype(jnp.float32)
+        return (
+            output, input_grad, gain_sums[0], grad_query, grad_key, grad_value, grad_out, gain_sums[1],
+            grad_gate, grad_up, grad_down,
         )
-        grad_out, grad_qkv = over_fsdp(grad_out, 1), over_fsdp(grad_qkv, 0)
-        normed_attn_grad = spread(chips, qkv_grad, w_qkv)
-        _, pull_norm_attn = jax.vjp(rms_norm, activations, gain_attn)
-        input_norm_grad, gain_attn_part = pull_norm_attn(normed_attn_grad)
-        input_grad = hidden_grad + input_norm_grad
-        gain_sums = swap_sum(jnp.stack([gain_attn_part, gain_mlp_part]), sizes)
-        grad_query, grad_key, grad_value = [grad_qkv[:, part * width : (part + 1) * width] for part in range(3)]
-        weights = [
-            grad.astype(jnp.float32)
-            for grad in (grad_query, grad_key, grad_value, grad_out, grad_gate, grad_up, grad_down)
-        ]
-        return (output, input_grad, gain_sums[0], *weights[:4], gain_sums[1], *weights[4:])
 
     return body
 

time: 703 us -> 614 us (0.87)
  matrix products: 60.8 us -> 0 us
  waiting for transfers between devices: 31.8 us -> 1.49 us
  Pallas kernels: 548 us -> 574 us
  other arithmetic: 27.5 us -> 19 us
    dot_general x5 -> x0, matrix products: 60.8 us -> none  [dot(): lax.dot_general(left, right, dims, preferred_element_type=jnp.float32)]
    pallas_call x3, Pallas kernels: 362 us -> 380 us  [the longest x1 155 us: feed(): pl.pallas_call(lambda *refs: feed_kernel(chips, *refs), in_specs=[VMEM] *...]
    reduce_scatter x5 -> x2, waiting for transfers between devices: 9.9 us -> 0.01 us  [over_fsdp(): lax.psum_scatter(grad, 'fsdp', scatter_dimension=dimension, tiled=True)]
    ppermute x5 -> x0, waiting for transfers between devices: 9.39 us -> none  [swap_sum(): lax.ppermute(values, axis, [(i, i ^ step) for i in range(mesh[axis])])]
    convert_element_type x9 -> x2, other arithmetic: 15.3 us -> 6.91 us  [the longest x1 4.01 us: body(): grad_both[:, hidden:].astype(jnp.float32)]
    all_gather x1, waiting for transfers between devices: 8.02 us -> 0.02 us  [body(): full_down = lax.all_gather(w_down, 'fsdp', axis=1, tiled=True)]
  transfers between devices with their start and end apart: 14 -> 5, of which waited for: 6 -> 0; matrix products, arithmetic and copies ran while one was open for 6% -> 3% of each run, Pallas kernels for 58% -> 68%
where the time goes in v4:
time: 614 us; the launch traced here: 613 us
  Pallas kernels  574 us (93%)
  other arithmetic  19 us (3%)
  between operations  13.9 us (2%)
    pallas_call x1, Pallas kernels, feed(): pl.pallas_call(lambda *refs: feed_kernel(chips, *refs), in_specs=[VMEM] *...  155 us
    pallas_call x1, Pallas kernels, back(): pl.pallas_call(lambda *refs: back_kernel(chips, shards, *refs), in_specs=...  124 us
    pallas_call x1, Pallas kernels, attend(): pl.pallas_call(lambda *refs: attend_kernel(chips, *refs), in_specs=[VMEM]...  104 us
    pallas_call x1, Pallas kernels, spread(): pl.pallas_call(lambda *refs: spread_kernel(chips, shards, *refs), in_spec...  100 us
    pallas_call x1, Pallas kernels, project(): pl.pallas_call(lambda *refs: project_kernel(chips, shards, *refs), in_spe...  90.9 us
  transfers between devices with their start and end apart: 5, of which 0 were waited for; matrix products, arithmetic and copies ran while one was open for 3% of the time, Pallas kernels for 68%

profile of v4, /device:TPU:0, one launch (start us, length us, event | category | flops | bytes accessed | tf_op | source)
XLA Modules:
  0.0 613.1 jit_solution(3123563627791762345)
XLA Ops:
  7.2 0.0 all-gather.4.cloned.1.call-start
  7.2 0.7 all-gather.4.cloned.1.call-update
  7.9 0.0 all-gather.8.cloned.1.call-start
  8.0 0.7 all-gather.8.cloned.1.call-update
  8.7 0.0 all-gather.6.cloned.1.call-start
  8.7 3.1 pad_maximum_fusion
  11.8 0.0 all-gather.6.cloned.1.call-update
  11.8 0.0 reduce-scatter.5.cloned.1.call-start
  11.9 1.8 multiply_sine_fusion
  13.7 90.9 %project.1 = (bf16[2048,2048]{1,0:T(8,128)(2,1)}, bf16[2048,768]{1,0:T(8,128)(2,1)}, bf16[2048,768]{1,0:T(8,128)(2,1)}, bf16[256,2048]{1,0:T(8,128)(2,1)}, bf16[...) custom-call(f32[256,2048]{1,0:T(8,128)} %refs_2_.3, f32[1,2048]{1,0:T(1,128)} %bitcast.4, ...), custom_call_target="tpu_custom_call" | custom-call | flops 6442450944 | bytes 16777216 | tf_op jit(solution)/shard_map/project/pallas_call | solution.py:383
  104.6 0.0 all-gather.4.cloned.1.call-done.refs_2_.refs_4_
  104.6 103.7 %attend.1 = (f32[256,2048]{1,0:T(8,128)}, bf16[256,2048]{1,0:T(8,128)(2,1)}, bf16[2048,256]{1,0:T(8,128)(2,1)}, f32[4,2048]{1,0:T(4,128)}, bf16[2048,2048]{1,0:T(8,128)(2,1)}) custom-call(bf16[2048,768]{1,0:T(8,128)(2,1)} %get-tuple-element.38.refs_0_.refs_5_, bf16[256,2048]{1,0:T(8,128)(2,1)} %get-tuple-element.39.refs_1_, ...), custom_call_target="tpu_custom_call" | custom-call | flops 4294967296 | bytes 16777216 | tf_op jit(solution)/shard_map/attend/pallas_call | solution.py:503
  208.3 0.0 all-gather.8.cloned.1.call-done.refs_6_.refs_3_
  208.3 0.0 all-gather.6.cloned.1.call-done.refs_5_
  208.3 155.5 %feed.1 = (f32[256,2048]{1,0:T(8,128)}, bf16[256,2048]{1,0:T(8,128)(2,1)}, f32[1,2048]{1,0:T(1,128)}, bf16[2048,1024]{1,0:T(8,128)(2,1)}, bf16[2048,2048]{1,0:T(8,128)(2,1)}) custom-call(f32[256,2048]{1,0:T(8,128)} %get-tuple-element.40.refs_0_, f32[256,2048]{1,0:T(8,128)} %refs_1_.1, f32[1,2048]{1,0:T(1,128)} %bitcast.9, ...), custom_call_target="tpu_custom_call" | custom-call | flops 68719476736 | bytes 41943040 | tf_op jit(solution)/shard_map/feed/pallas_call | solution.py:1138
  363.8 0.0 reduce-scatter.5.cloned.1.call-update
  363.8 0.0 reduce-scatter.3.cloned.1.call-start
  363.9 124.3 %back.1 = (f32[256,2048]{1,0:T(8,128)}, bf16[2048,2048]{1,0:T(8,128)(2,1)}, bf16[2048,768]{1,0:T(8,128)(2,1)}, bf16[1024,2048]{1,0:T(8,128)(2,1)}, f32[256,512]{1,0:T(8,128)}) custom-call(bf16[256,2048]{1,0:T(8,128)(2,1)} %get-tuple-element.43.refs_0_, bf16[2048,1024]{1,0:T(8,128)(2,1)} %get-tuple-element.44.refs_1_, ...), custom_call_target="tpu_custom_call" | custom-call | flops 1048576 | bytes 1048576 | tf_op jit(solution)/shard_map/back/pallas_call | solution.py:739
  488.2 0.0 copy-start
  488.2 0.0 reduce-scatter.3.cloned.1.call-update
  488.2 1.6 copy-done
  489.8 3.2 add.10
  492.9 100.2 %spread.1 = (f32[256,2048]{1,0:T(8,128)}, f32[512,768]{1,0:T(8,128)}, f32[2,2048]{1,0:T(2,128)}) custom-call(bf16[2048,768]{1,0:T(8,128)(2,1)} %get-tuple-element.52.refs_0_, bf16[2048,768]{1,0:T(8,128)(2,1)} %get-tuple-element.53.refs_1_, f32[256,2048]{1,0:T(8,128)} %refs_2_.3, f32[1,2048]{1,0:T(1,128)} %bitcast.5, f32[1,2048]{1,0:T(1,128)} %get-tuple-element.54.refs_4_, ...), custom_call_target="tpu_custom_call" | custom-call | flops 1048576 | bytes 1048576 | tf_op jit(solution)/shard_map/spread/pallas_call | solution.py:912
  593.1 0.0 copy-start.1
  593.1 4.0 add.11
  597.1 0.0 copy-done.1
  597.1 1.2 fusion
  598.3 0.0 copy-done.3
  598.3 0.6 fusion.1
  598.9 4.0 slice_convert_fusion
  602.9 2.9 convert_element_type.31
  605.8 0.8 copy.23
  (7 shorter events, 0.0 us)
Async XLA Ops:
  7.2 97.4 %all-gather.4.cloned.1.call-start = ((), (), s32[]{:S(2)}) async-start(), calls=%async_computation.2 | async-start | bytes 1310720 | tf_op jit(solution)/shard_map/all_gather | solution.py:1188
  7.9 200.4 %all-gather.8.cloned.1.call-start = ((), (), s32[]{:S(2)}) async-start(), calls=%async_computation.4 | async-start | bytes 5242880 | tf_op jit(solution)/shard_map/all_gather | solution.py:1190
  8.7 199.6 %all-gather.6.cloned.1.call-start = ((), (), s32[]{:S(2)}) async-start(), calls=%async_computation.3 | async-start | bytes 10485760 | tf_op jit(solution)/shard_map/all_gather | solution.py:1189
  11.8 587.1 %reduce-scatter.5.cloned.1.call-start = ((), (), s32[]{:S(2)}) async-start(), calls=%async_computation.6 | async-start | bytes 10485760 | tf_op jit(solution)/shard_map/reduce_scatter | solution.py:1201
  363.8 239.1 %reduce-scatter.3.cloned.1.call-start = ((), (), s32[]{:S(2)}) async-start(), calls=%async_computation.5 | async-start | bytes 5242880 | tf_op jit(solution)/shard_map/reduce_scatter | solution.py:1201
  488.2 1.6 copy-start
  593.1 4.0 copy-start.1
  597.1 1.2 copy-start.3
  602.9 2.9 copy-start.2
Sparse Core Ops, SparseCore 0:
  9.8 48.2 all-gather.3
  60.0 51.7 all-gather.7
  114.2 87.6 all-gather.5
  364.0 87.2 reduce-scatter.4
  488.3 81.6 reduce-scatter.2

commit v5 on v4

--- a/solution.py
+++ b/solution.py
@@ -182,6 +182,9 @@
         source = self.term.at[step % 2, span(1 - self.line.core, self.rows)]
         return remote(source, self.shares.at[slot], self.share_send.at[step % 2], self.share_recv.at[slot], {"tp": self.line.partner})
 
+    def mine(self, step):
+        return self.term[step % 2, span(self.line.core, self.rows), :]
+
     def pass_on(self, step):
         line, target = self.line, self.line.target(step)
         onward = target > line.chip
@@ -201,8 +204,7 @@
     def step(self, step):
         line, target = self.line, self.line.target(step)
         self.share(step).wait_recv()
-        mine = self.term[step % 2, span(line.core, self.rows), :].astype(jnp.float32)
-        self.out[...] = mine + self.shares[step % self.shares.shape[0]].astype(jnp.float32)
+        self.out[...] = self.mine(step).astype(jnp.float32) + self.shares[step % self.shares.shape[0]].astype(jnp.float32)
 
         @pl.when(jnp.logical_and(target >= line.chip, line.has_left))
         def _():
@@ -249,6 +251,47 @@
         return carry
 
     lax.fori_loop(0, rows // NORM_ROWS, step, 0)
+
+
+class HeldScatter(Scatter):
+    @staticmethod
+    def scratch(chips, rows, depth):
+        return [pltpu.VMEM((2, rows, depth), low)] + Scatter.scratch(chips, rows, depth)[1:] + [DMA((2,))]
+
+    def __init__(self, line, out, held, *refs):
+        super().__init__(line, out, *refs[:-1])
+        self.held, self.load_sem = held, refs[-1]
+
+    def load(self, step):
+        source = self.held.at[span(2 * self.line.target(step) + self.line.core, self.rows)]
+        return pltpu.make_async_copy(source, self.term.at[step % 2], self.load_sem.at[step % 2])
+
+    def share(self, step):
+        slot = step % self.shares.shape[0]
+        source = self.held.at[span(2 * self.line.target(step) + 1 - self.line.core, self.rows)]
+        return remote(source, self.shares.at[slot], self.share_send.at[step % 2], self.share_recv.at[slot], {"tp": self.line.partner})
+
+    def mine(self, step):
+        self.load(step).wait()
+        return self.term[step % 2]
+
+
+class Loads:
+    @staticmethod
+    def scratch(*operands):
+        return [pltpu.VMEM(a.shape, a.dtype) for a in operands] + [DMA((len(operands),))]
+
+    def __init__(self, sources, refs):
+        self.refs = refs[: len(sources)]
+        self.copies = [pltpu.make_async_copy(source, ref, refs[-1].at[i]) for i, (source, ref) in enumerate(zip(sources, self.refs))]
+
+    def start(self):
+        for copy in self.copies:
+            copy.start()
+
+    def wait(self, *which):
+        for i in which:
+            self.copies[i].wait()
 
 
 def turned(block, sign):
@@ -289,9 +332,10 @@
 
 def project_kernel(
     chips, shards,
-    activations, gain, w_query, w_key, w_value, cosine_t, sine_t,
-    tokens_out, weight, qkv, keys_t, values_t, cosine, sine,
-    tokens, chunks, chunk_sem, weight_send, weight_recv, weight_keep, *gather_sems,
+    activations, gain, w_query, w_key, w_value, cosine_t, sine_t, w_gate, w_up,
+    tokens_out, weight_out, qkv_out, keys_out, values_out, cosine_out, sine_out, both_out,
+    weight, qkv, keys_t, values_t, cosine, sine, both, tokens, chunks,
+    chunk_sem, weight_send, weight_recv, weight_keep, table_sem, both_sem, store_sem, *gather_sems,
 ):
     line = Line(chips)
     rows = tokens.shape[0]
@@ -310,6 +354,25 @@
 
     def keep(part):
         return pltpu.make_async_copy(parts[part], place(part), weight_keep.at[part])
+
+    hidden = w_gate.shape[1]
+    joins = [
+        pltpu.make_async_copy(source, both.at[:, pl.ds(side * hidden, hidden)], both_sem.at[side])
+        for side, source in enumerate((w_gate, w_up))
+    ]
+    joined = pltpu.make_async_copy(both, both_out, both_sem.at[2])
+    tables = [
+        pltpu.make_async_copy(source, out, table_sem.at[i])
+        for i, (source, out) in enumerate(((cosine, cosine_out), (sine, sine_out), (weight, weight_out)))
+    ]
+
+    def stores(chip):
+        here = span(chip, pair)
+        return [
+            pltpu.make_async_copy(qkv.at[here], qkv_out.at[here], store_sem.at[0, chip]),
+            pltpu.make_async_copy(keys_t.at[:, here], keys_out.at[:, here], store_sem.at[1, chip]),
+            pltpu.make_async_copy(values_t.at[:, here], values_out.at[:, here], store_sem.at[2, chip]),
+        ]
 
     def norm(here):
         tokens[here, :] = normed(activations[here, :], gain[...]).astype(low)
@@ -324,6 +387,8 @@
     for table, table_t in ((cosine, cosine_t), (sine, sine_t)):
         turn = table_t[...].T
         table[...] = jnp.concatenate([turn] * (LANES // turn.shape[1]), axis=1)
+    for copy in joins + tables[:2]:
+        copy.start()
 
     def project(chip):
         @pl.when(jnp.logical_and(chip >= 0, chip < chips))
@@ -342,6 +407,8 @@
                 qkv[here, columns] = block.astype(low)
                 if part:
                     (keys_t, values_t)[part - 1][:, here] = block.T.astype(low)
+            for copy in stores(chip):
+                copy.start()
 
     def step(index, carry):
         @pl.when(jnp.logical_and(index >= 1, index < chips))
@@ -355,6 +422,10 @@
                 keep(part).wait()
                 for ahead in range(shards - 1):
                     give(ahead, part).wait_recv()
+            tables[2].start()
+            for copy in joins:
+                copy.wait()
+            joined.start()
 
         def side(which, carry):
             distance = index - 1
@@ -373,35 +444,42 @@
     for part in range(3):
         for ahead in range(shards - 1):
             give(ahead, part).wait_send()
-
-
-def project(chips, shards, activations, gain, w_query, w_key, w_value, cosine_t, sine_t):
+    joined.wait()
+    for copy in tables:
+        copy.wait()
+    for chip in range(chips):
+        for copy in stores(chip):
+            copy.wait()
+
+
+def project(chips, shards, activations, gain, w_query, w_key, w_value, cosine_t, sine_t, w_gate, w_up):
     rows, depth = activations.shape
     group_rows = 2 * chips * rows
     width = w_query.shape[1]
     shape = jax.ShapeDtypeStruct
+    held = [
+        shape((depth, 3 * width), low),
+        shape((group_rows, 3 * width), low),
+        shape((width, group_rows), low),
+        shape((width, group_rows), low),
+        shape((SEQ_LEN, LANES), jnp.float32),
+        shape((SEQ_LEN, LANES), jnp.float32),
+        shape((w_gate.shape[0], 2 * w_gate.shape[1]), low),
+    ]
     return pl.pallas_call(
         lambda *refs: project_kernel(chips, shards, *refs),
-        in_specs=[VMEM] * 7,
-        out_specs=[ANYWHERE] + [VMEM] * 6,
-        out_shape=[
-            shape((group_rows, depth), low),
-            shape((depth, 3 * width), low),
-            shape((group_rows, 3 * width), low),
-            shape((width, group_rows), low),
-            shape((width, group_rows), low),
-            shape((SEQ_LEN, LANES), jnp.float32),
-            shape((SEQ_LEN, LANES), jnp.float32),
-        ],
-        scratch_shapes=[
+        in_specs=[VMEM] * 7 + [ANYWHERE] * 2,
+        out_specs=[ANYWHERE] * 8,
+        out_shape=[shape((group_rows, depth), low)] + held,
+        scratch_shapes=[pltpu.VMEM(a.shape, a.dtype) for a in held] + [
             pltpu.VMEM((rows, depth), low),
             pltpu.VMEM((2 * rows, depth), low),
-            DMA, DMA((shards - 1, 3)), DMA((shards - 1, 3)), DMA((3,)),
+            DMA, DMA((shards - 1, 3)), DMA((shards - 1, 3)), DMA((3,)), DMA((3,)), DMA((3,)), DMA((3, chips)),
         ] + Gather.scratch(chips),
         compiler_params=pltpu.CompilerParams(collective_id=1, has_side_effects=True, vmem_limit_bytes=63 << 20),
         cost_estimate=pl.CostEstimate(flops=6 * group_rows * depth * width, bytes_accessed=4 * group_rows * depth, transcendentals=0),
         name="project",
-    )(activations, gain, w_query, w_key, w_value, cosine_t, sine_t)
+    )(activations, gain, w_query, w_key, w_value, cosine_t, sine_t, w_gate, w_up)
 
 
 def attend_chunk(chunk, rows, qkv, values_t, heads_ref, acc, out, top_ref, sum_ref):
@@ -439,10 +517,14 @@
 
 def attend_kernel(
     chips,
-    qkv, values_t, w_out, activations, cotangent, gain,
-    hidden, tokens, mixed, totals, grads_out,
-    heads_ref, acc, out, top_ref, sum_ref, grads, *sems,
+    cotangent, gain, *refs,
 ):
+    sources, (hidden, tokens, mixed, totals, grads_out) = refs[:4], refs[4:9]
+    loads = Loads(sources, refs[9:14])
+    qkv, values_t, w_out, activations = loads.refs
+    heads_ref, acc, out, top_ref, sum_ref, grads = refs[14:20]
+    sems = refs[20:]
+    loads.start()
     line = Line(chips)
     rows, depth = hidden.shape
     pair = 2 * rows
@@ -451,6 +533,7 @@
     gather = Gather(line, grads, grads_out, *sems[8:])
     line.greet()
     gather.start()
+    loads.wait(0, 1, 2, 3)
 
     def step(index, carry):
         work = jnp.where(index == chips, chips - 1, index)
@@ -502,7 +585,7 @@
     shape = jax.ShapeDtypeStruct
     return pl.pallas_call(
         lambda *refs: attend_kernel(chips, *refs),
-        in_specs=[VMEM] * 6,
+        in_specs=[VMEM] * 2 + [ANYWHERE] * 4,
         out_specs=[VMEM] * 4 + [ANYWHERE],
         out_shape=[
             shape((rows, depth), jnp.float32),
@@ -511,7 +594,7 @@
             shape((heads, group_rows), jnp.float32),
             shape((group_rows, depth), low),
         ],
-        scratch_shapes=[
+        scratch_shapes=Loads.scratch(qkv, values_t, w_out, activations) + [
             pltpu.VMEM((heads, pair, width), low),
             pltpu.VMEM((width, pair), jnp.float32),
             pltpu.VMEM((pair, width), low),
@@ -522,7 +605,7 @@
         compiler_params=pltpu.CompilerParams(collective_id=2, has_side_effects=True, vmem_limit_bytes=63 << 20),
         cost_estimate=pl.CostEstimate(flops=2 * group_rows * (SEQ_LEN + depth) * width, bytes_accessed=4 * group_rows * depth, transcendentals=group_rows * SEQ_LEN * heads // 2),
         name="attend",
-    )(qkv, values_t, w_out, activations, cotangent, gain)
+    )(cotangent, gain, qkv, values_t, w_out, activations)
 
 
 def back_chunk(chunk, rows, grad, qkv, keys_t, mixed, totals, dkey, dvalue, heads_ref, grads_ref, acc, inner_ref):
@@ -563,23 +646,23 @@
 
 def back_kernel(
     chips, shards,
-    branch, inner, grads, w_down, w_out, qkv, keys_t, mixed, totals, cosine, sine,
-    down, branch_out, qkv_grad, grad_down, grad_out,
-    down_w, inner_chunk, grad_chunk, down_sum, down_tile, out_sum, out_stage, out_from, branch_chunk, dkey, dvalue, heads_ref, grads_ref, acc, inner_ref,
-    load_sem, inner_sem, grad_sem, branch_sem, tile_sem, out_send, out_recv, *sems,
+    branch, terms, inner, grads, *refs,
 ):
+    sources, (down, branch_out, qkv_grad, grad_down, grad_out) = refs[:7], refs[7:12]
+    loads = Loads(sources, refs[12:20])
+    w_out, qkv, keys_t, mixed, totals, cosine, sine = loads.refs
+    inner_chunk, grad_chunk, down_sum, down_tile, out_sum, out_stage, out_from, branch_chunk, dkey, dvalue = refs[20:30]
+    heads_ref, grads_ref, acc, inner_ref, inner_sem, grad_sem, branch_sem, tile_sem, out_send, out_recv = refs[30:40]
+    sems = refs[40:]
     line = Line(chips)
     rows, depth = down.shape
     pair = 2 * rows
     width = w_out.shape[0]
-    scatter = Scatter(line, down, *sems[:8])
-    gather = Gather(line, branch, branch_out, *sems[8:])
-
-    def load():
-        return pltpu.make_async_copy(w_down, down_w, load_sem)
+    scatter = HeldScatter(line, down, terms, *sems[:9])
+    gather = Gather(line, branch, branch_out, *sems[9:])
 
     def fetch(step):
-        return pltpu.make_async_copy(inner.at[span(line.target(step), pair)], inner_chunk.at[step % 2], inner_sem.at[step % 2])
+        return pltpu.make_async_copy(inner.at[span(line.target(step), pair)], inner_chunk, inner_sem)
 
     def fetch_grad(step):
         return pltpu.make_async_copy(grads.at[span(line.target(step), pair)], grad_chunk, grad_sem)
@@ -594,8 +677,7 @@
     def keep_tile(place):
         return pltpu.make_async_copy(down_tile, grad_down.at[span(place, 256)], tile_sem)
 
-    load().start()
-    fetch(0).start()
+    loads.start()
     line.greet([{"fsdp": other} for other in others])
     gather.start()
     out_sum[...] = jnp.zeros_like(out_sum)
@@ -628,33 +710,20 @@
     def step(index, carry):
         @pl.when(index == 0)
         def _():
-            load().wait()
+            loads.wait(*range(7))
             gather.keep().wait()
 
         @pl.when(index < chips)
         def _():
-            @pl.when(index < chips - 1)
-            def _():
-                fetch(index + 1).start()
-
-            fetch(index).wait()
+            fetch(index).start()
+            fetch_grad(index).start()
             scatter.free(index)
-
-            def tile(place, carry):
-                columns = span(place, 256)
-                scatter.term[index % 2, :, columns] = dot(inner_chunk[index % 2], down_w[:, columns]).astype(low)
-                return carry
-
-            lax.fori_loop(0, depth // 256, tile, 0)
+            scatter.load(index).start()
             scatter.share(index).start()
 
         @pl.when(jnp.logical_and(index >= 1, index < chips))
         def _():
             gather.step(index)
-
-        @pl.when(index < chips)
-        def _():
-            fetch_grad(index).start()
 
         @pl.when(index == chips)
         def _():
@@ -686,11 +755,12 @@
 
         @pl.when(index < chips)
         def _():
+            fetch(index).wait()
             fetch_grad(index).wait()
 
             def tile(place, carry):
                 here = span(place, 256)
-                part = dot(inner_chunk[index % 2, :, here], grad_chunk[...], TN)
+                part = dot(inner_chunk[:, here], grad_chunk[...], TN)
 
                 @pl.when(index == 0)
                 def _():
@@ -728,17 +798,18 @@
     gather.finish(False)
 
 
-def back(chips, shards, branch, inner, grads, w_down, w_out, qkv, keys_t, mixed, totals, cosine, sine):
+def back(chips, shards, branch, terms, inner, grads, w_out, qkv, keys_t, mixed, totals, cosine, sine):
     rows, depth = branch.shape
     pair = 2 * rows
     group_rows = chips * pair
     width = w_out.shape[0]
-    hidden = w_down.shape[0]
+    hidden = inner.shape[1]
     heads = width // HEAD_DIM
     shape = jax.ShapeDtypeStruct
+    held = (w_out, qkv, keys_t, mixed, totals, cosine, sine)
     return pl.pallas_call(
         lambda *refs: back_kernel(chips, shards, *refs),
-        in_specs=[VMEM] + [ANYWHERE] * 3 + [VMEM] * 7,
+        in_specs=[VMEM] + [ANYWHERE] * 10,
         out_specs=[VMEM, ANYWHERE, VMEM, ANYWHERE, VMEM],
         out_shape=[
             shape((rows, depth), jnp.float32),
@@ -747,9 +818,8 @@
             shape((hidden, depth), low),
             shape((width, depth // shards), jnp.float32),
         ],
-        scratch_shapes=[
-            pltpu.VMEM((hidden, depth), low),
-            pltpu.VMEM((2, pair, hidden), low),
+        scratch_shapes=Loads.scratch(*held) + [
+            pltpu.VMEM((pair, hidden), low),
             pltpu.VMEM((pair, depth), low),
             pltpu.VMEM((hidden, depth), jnp.float32),
             pltpu.VMEM((256, depth), low),
@@ -763,12 +833,12 @@
             pltpu.VMEM((heads, pair, width), low),
             pltpu.VMEM((width, pair), jnp.float32),
             pltpu.VMEM((8, pair), jnp.float32),
-            DMA, DMA((2,)), DMA, DMA, DMA, DMA((shards - 1,)), DMA((shards - 1,)),
-        ] + Scatter.scratch(chips, rows, depth) + Gather.scratch(chips),
+            DMA, DMA, DMA, DMA, DMA((shards - 1,)), DMA((shards - 1,)),
+        ] + HeldScatter.scratch(chips, rows, depth) + Gather.scratch(chips),
         compiler_params=pltpu.CompilerParams(collective_id=4, has_side_effects=True, vmem_limit_bytes=67043328),
         cost_estimate=pl.CostEstimate(flops=1 << 20, bytes_accessed=1 << 20, transcendentals=0),
         name="back",
-    )(branch, inner, grads, w_down, w_out, qkv, keys_t, mixed, totals, cosine, sine)
+    )(branch, terms, inner, grads, *held)
 
 
 def spread_kernel(
@@ -944,13 +1014,13 @@
 
 def feed_kernel(
     chips,
-    hidden_state, cotangent, gain, tokens, grads_hbm, both_hbm, down_hbm,
-    hidden_grad, branch, gain_part, inner_out, grad_both,
-    tokens_all, gate_w, up_w, down_w, grads, inner, gate_grad, up_grad, term, from_core, from_ring, total, tile_gate, tile_up,
+    gain, hidden_hbm, cotangent_hbm, tokens, grads_hbm, both_hbm, down_hbm,
+    hidden_grad, branch, gain_part, inner_out, grad_both, down_out,
+    hidden_state, cotangent, state_sem, down_tile, down_sem, tokens_all, gate_w, up_w, down_w, grads, inner, gate_grad, up_grad, term, from_core, from_ring, total, tile_gate, tile_up,
     load_sem, own_sem, grad_sem, store_sem, tile_sem,
     ring_send, ring_recv, core_send, core_recv, share_send, share_recv, total_send, total_recv,
 ):
-    rows, depth = hidden_state.shape
+    rows, depth = hidden_grad.shape
     pair = 2 * rows
     width = gate_w.shape[1]
     me = lax.axis_index("tp")
@@ -962,6 +1032,7 @@
 
     loads = [pltpu.make_async_copy(a, b, load_sem.at[i]) for i, (a, b) in enumerate(((both_hbm.at[:, pl.ds(0, width)], gate_w), (both_hbm.at[:, pl.ds(width, width)], up_w), (down_hbm, down_w)))]
     own = pltpu.make_async_copy(tokens, tokens_all.at[span(me, rows)], own_sem)
+    states = Loads((hidden_hbm, cotangent_hbm), (hidden_state, cotangent, state_sem))
 
     def source(slot):
         return chip_at((place + chips - slot) % chips, chips)
@@ -979,7 +1050,26 @@
         return remote(block(slot), block(slot), core_send.at[slot], core_recv.at[slot], partner)
 
     def store(slot):
-        return pltpu.make_async_copy(inner.at[slot % 2], inner_out.at[span(source(slot), pair)], store_sem.at[slot % 2])
+        return pltpu.make_async_copy(inner.at[slot], inner_out.at[span(source(slot), pair)], store_sem.at[slot])
+
+    def keep_down(slot, tile):
+        there = down_out.at[span(source(slot), pair), span(tile, 256)]
+        return pltpu.make_async_copy(down_tile.at[tile % 2], there, down_sem.at[tile % 2])
+
+    def down_term(slot, carry):
+        def tile(index, carry):
+            @pl.when(index > 1)
+            def _():
+                keep_down(slot, index - 2).wait()
+
+            down_tile[index % 2] = dot(inner[slot], down_w[:, span(index, 256)]).astype(low)
+            keep_down(slot, index).start()
+            return carry
+
+        lax.fori_loop(0, depth // 256, tile, 0)
+        for index in range(depth // 256 - 2, depth // 256):
+            keep_down(slot, index).wait()
+        return carry
 
     def share(slot):
         place = jnp.where(slot == 0, 0, 1 + slot % 2)
@@ -1018,9 +1108,9 @@
             for load in loads:
                 load.wait()
 
-        @pl.when(slot > 1)
-        def _():
-            store(slot - 2).wait()
+        @pl.when(slot == 1)
+        def _():
+            states.start()
 
         to_core(slot).wait_recv()
         fetch(slot).wait()
@@ -1033,7 +1123,7 @@
             grad = dot(grads[here], down_w[columns, :], NT)
             squash = jax.nn.sigmoid(gate)
             act = gate * squash
-            inner[here, :, columns] = (act * up).astype(low)
+            inner[slot, :, columns] = (act * up).astype(low)
             up_grad[wide_rows, columns] = (grad * act).astype(low)
             gate_grad[wide_rows, columns] = (grad * up * squash * (1.0 + gate * (1.0 - squash))).astype(low)
             return carry
@@ -1057,6 +1147,9 @@
         @pl.when(slot == 0)
         def _():
             hidden_grad[...] = term[mine, :].astype(jnp.float32)
+
+        middle = jnp.logical_and(slot >= 2, slot < chips - 1)
+        lax.fori_loop(jnp.where(slot == 2, 0, slot), jnp.where(middle, slot + 1, 0), down_term, 0)
 
         @pl.when(slot > 0)
         def _():
@@ -1101,7 +1194,9 @@
             copy.start()
         return carry
 
+    lax.fori_loop(0 if chips < 4 else chips - 1, chips, down_term, 0)
     lax.fori_loop(0, depth // 256, weights, 0)
+    states.wait(0, 1)
     share(0).wait_recv()
     pass_on(chips - 1).wait_recv()
     gain_part[...] = jnp.zeros_like(gain_part)
@@ -1122,8 +1217,7 @@
             to_ring(slot).wait_send()
         if slot >= max(1, chips - 2):
             pass_on(slot).wait_send()
-        if slot >= chips - 2:
-            store(slot).wait()
+        store(slot).wait()
     for index in range(depth // 256 - 2, depth // 256):
         for copy in tiles(index):
             copy.wait()
@@ -1137,22 +1231,25 @@
     shape = jax.ShapeDtypeStruct
     return pl.pallas_call(
         lambda *refs: feed_kernel(chips, *refs),
-        in_specs=[VMEM] * 3 + [ANYWHERE] * 4,
-        out_specs=[VMEM] * 3 + [ANYWHERE] * 2,
+        in_specs=[VMEM] + [ANYWHERE] * 6,
+        out_specs=[VMEM] * 3 + [ANYWHERE] * 3,
         out_shape=[
             shape((rows, depth), jnp.float32),
             shape((rows, depth), low),
             shape((1, depth), jnp.float32),
             shape((group_rows, width), low),
             shape((depth, 2 * width), low),
+            shape((group_rows, depth), low),
         ],
-        scratch_shapes=[
+        scratch_shapes=Loads.scratch(hidden_state, cotangent) + [
+            pltpu.VMEM((2, pair, 256), low),
+            DMA((2,)),
             pltpu.VMEM((group_rows, depth), low),
             pltpu.VMEM((depth, width), low),
             pltpu.VMEM((depth, width), low),
             pltpu.VMEM(down_w.shape, low),
             pltpu.VMEM((2, pair, depth), low),
-            pltpu.VMEM((2, pair, width), low),
+            pltpu.VMEM((chips, pair, width), low),
             pltpu.VMEM((group_rows, width), low),
             pltpu.VMEM((group_rows, width), low),
             pltpu.VMEM((pair, depth), low),
@@ -1161,14 +1258,43 @@
             pltpu.VMEM((2, rows, depth), low),
             pltpu.VMEM((2, 256, width), low),
             pltpu.VMEM((2, 256, width), low),
-            DMA((3,)), DMA, DMA((2,)), DMA((2,)), DMA((2, 2)),
+            DMA((3,)), DMA, DMA((2,)), DMA((chips,)), DMA((2, 2)),
             DMA((chips,)), DMA((chips,)), DMA((chips,)), DMA((chips,)),
             DMA, DMA((3,)), DMA((2,)), DMA((chips - 1,)),
         ],
-        compiler_params=pltpu.CompilerParams(collective_id=3, has_side_effects=True, vmem_limit_bytes=63 << 20),
+        compiler_params=pltpu.CompilerParams(collective_id=3, has_side_effects=True, vmem_limit_bytes=67043328),
         cost_estimate=pl.CostEstimate(flops=16 * group_rows * depth * width, bytes_accessed=10 * group_rows * depth, transcendentals=group_rows * width),
         name="feed",
-    )(hidden_state, cotangent, gain, tokens, grads, both_w, down_w)
+    )(gain, hidden_state, cotangent, tokens, grads, both_w, down_w)
+
+
+def finish_kernel(hidden, down, hidden_grad, input_part, both, grad_down, grad_qkv, grad_out, output, input_grad, query, key, value, out, gate, up, down_out):
+    output[...] = hidden[...] + down[...]
+    input_grad[...] = hidden_grad[...] + input_part[...]
+    width = query.shape[1]
+    for part, ref in enumerate((query, key, value)):
+        ref[...] = grad_qkv[:, pl.ds(part * width, width)]
+    out[...] = grad_out[...]
+    wide = gate.shape[1]
+    gate[...] = both[:, pl.ds(0, wide)].astype(jnp.float32)
+    up[...] = both[:, pl.ds(wide, wide)].astype(jnp.float32)
+    down_out[...] = grad_down[...].astype(jnp.float32)
+
+
+def finish(*operands):
+    steps = 8
+    hidden, _, _, _, both, grad_down, grad_qkv, grad_out = operands
+    shape = lambda a, parts: jax.ShapeDtypeStruct((a.shape[0], a.shape[1] // parts), jnp.float32)
+    results = [shape(hidden, 1)] * 2 + [shape(grad_qkv, 3)] * 3 + [shape(grad_out, 1)] + [shape(both, 2)] * 2 + [shape(grad_down, 1)]
+    spec = lambda a: pl.BlockSpec((a.shape[0] // steps, a.shape[1]), lambda i: (i, 0))
+    return pl.pallas_call(
+        finish_kernel,
+        grid=(steps,),
+        in_specs=[spec(a) for a in operands],
+        out_specs=[spec(a) for a in results],
+        out_shape=results,
+        name="finish",
+    )(*operands)
 
 
 def rope_tables():
@@ -1186,14 +1312,14 @@
     def body(activations, gain_attn, w_query, w_key, w_value, w_out, gain_mlp, w_gate, w_up, w_down, cotangent):
         width = w_query.shape[1]
         full_out = lax.all_gather(w_out, "fsdp", axis=1, tiled=True)
-        full_both = lax.all_gather(jnp.concatenate([w_gate, w_up], axis=1), "fsdp", axis=0, tiled=True)
         full_down = lax.all_gather(w_down, "fsdp", axis=1, tiled=True)
         gain_attn, gain_mlp = gain_attn[None, :], gain_mlp[None, :]
-        seen_attn, w_qkv, qkv, keys_t, values_t, cosine, sine = project(
-            chips, shards, activations, gain_attn, w_query, w_key, w_value, *rope_tables()
+        seen_attn, w_qkv, qkv, keys_t, values_t, cosine, sine, both = project(
+            chips, shards, activations, gain_attn, w_query, w_key, w_value, *rope_tables(), w_gate, w_up
         )
+        full_both = lax.all_gather(both, "fsdp", axis=0, tiled=True)
         hidden_state, normed_mlp, mixed, totals, seen_grad = attend(chips, qkv, values_t, full_out, activations, cotangent, gain_mlp)
-        hidden_grad, branch_grad, gain_part, inner, grad_both = feed(
+        hidden_grad, branch_grad, gain_part, inner, grad_both, terms = feed(
             chips, hidden_state, cotangent, gain_mlp, normed_mlp, seen_grad, full_both, full_down
         )
 
@@ -1202,17 +1328,14 @@
 
         grad_both = over_fsdp(grad_both, 0)
         down, _, qkv_grad, grad_down, grad_out = back(
-            chips, shards, branch_grad, inner, seen_grad, full_down, full_out, qkv, keys_t, mixed, totals, cosine, sine
+            chips, shards, branch_grad, terms, inner, seen_grad, full_out, qkv, keys_t, mixed, totals, cosine, sine
         )
-        output = hidden_state + down
         grad_down = over_fsdp(grad_down, 1)
+        qkv_grad, grad_both = lax.optimization_barrier((qkv_grad, grad_both))
         input_part, grad_qkv, gain_sums = spread(chips, shards, qkv_grad, w_qkv, activations, gain_attn, gain_part, seen_attn)
-        input_grad = hidden_grad + input_part
-        grad_query, grad_key, grad_value = [grad_qkv[:, part * width : (part + 1) * width] for part in range(3)]
-        hidden = w_gate.shape[1]
-        grad_gate, grad_up = grad_both[:, :hidden].astype(jnp.float32), grad_both[:, hidden:].astype(jnp.float32)
-        grad_down, grad_gate, grad_up = lax.optimization_barrier((grad_down, grad_gate, grad_up))
-        grad_down = grad_down.astype(jnp.float32)
+        output, input_grad, grad_query, grad_key, grad_value, grad_out, grad_gate, grad_up, grad_down = finish(
+            hidden_state, down, hidden_grad, input_part, grad_both, grad_down, grad_qkv, grad_out
+        )
         return (
             output, input_grad, gain_sums[0], grad_query, grad_key, grad_value, grad_out, gain_sums[1],
             grad_gate, grad_up, grad_down,

time: 614 us -> 598 us (0.974)
  other arithmetic: 19 us -> 1.82 us
    pallas_call x1 -> x2, Pallas kernels: 155 us -> 168 us  [the longest x1 157 us: feed(): pl.pallas_call(lambda *refs: feed_kernel(chips, *refs), in_specs=[VMEM] +...]
    add x2 -> x0, other arithmetic: 7.16 us -> none  [the longest x1 4 us: body(): input_grad = hidden_grad + input_part]
    convert_element_type x2 -> x0, other arithmetic: 6.91 us -> none  [the longest x1 4.01 us: body(): grad_both[:, hidden:].astype(jnp.float32)]
  transfers between devices with their start and end apart: 5 -> 5, of which waited for: 0 -> 1; matrix products, arithmetic and copies ran while one was open for 3% -> 1% of each run, Pallas kernels for 68% -> 69%
where the time goes in v5:
time: 598 us; the launch traced here: 597 us
  Pallas kernels  578 us (97%)
  between operations  13.9 us (2%)
    pallas_call x1, Pallas kernels, feed(): pl.pallas_call(lambda *refs: feed_kernel(chips, *refs), in_specs=[VMEM] +...  157 us
    pallas_call x1, Pallas kernels, back(): pl.pallas_call(lambda *refs: back_kernel(chips, shards, *refs), in_specs=...  120 us
    pallas_call x1, Pallas kernels, attend(): pl.pallas_call(lambda *refs: attend_kernel(chips, *refs), in_specs=[VMEM]...  102 us
    pallas_call x1, Pallas kernels, spread(): pl.pallas_call(lambda *refs: spread_kernel(chips, shards, *refs), in_spec...  98.6 us
    pallas_call x1, Pallas kernels, project(): pl.pallas_call(lambda *refs: project_kernel(chips, shards, *refs), in_spe...  89.1 us
  transfers between devices with their start and end apart: 5, of which 1 were waited for; matrix products, arithmetic and copies ran while one was open for 1% of the time, Pallas kernels for 69%

profile of v5, /device:TPU:0, one launch (start us, length us, event | category | flops | bytes accessed | tf_op | source)
XLA Modules:
  0.0 597.3 jit_solution(7624755452650211844)
XLA Ops:
  7.2 0.0 all-gather.4.cloned.1.call-start
  7.2 0.7 all-gather.4.cloned.1.call-update
  7.9 0.0 all-gather.8.cloned.1.call-start
  8.0 0.7 all-gather.8.cloned.1.call-update
  8.7 0.0 all-gather.6.cloned.1.call-start
  8.7 1.8 multiply_sine_fusion
  10.5 89.1 %project.1 = (bf16[2048,2048]{1,0:T(8,128)(2,1)}, bf16[2048,768]{1,0:T(8,128)(2,1)}, bf16[2048,768]{1,0:T(8,128)(2,1)}, bf16[256,2048]{1,0:T(8,128)(2,1)}, bf16[...) custom-call(f32[256,2048]{1,0:T(8,128)} %refs_2_.5, ...), custom_call_target="tpu_custom_call" | custom-call | flops 6442450944 | bytes 16777216 | tf_op jit(solution)/shard_map/project/pallas_call | solution.py:469
  99.6 0.0 all-gather.6.cloned.1.call-update
  99.7 0.0 reduce-scatter.3.cloned.1.call-start
  99.7 0.0 all-gather.4.cloned.1.call-done.refs_4_
  99.7 101.6 %attend.1 = (f32[256,2048]{1,0:T(8,128)}, bf16[256,2048]{1,0:T(8,128)(2,1)}, bf16[2048,256]{1,0:T(8,128)(2,1)}, f32[4,2048]{1,0:T(4,128)}, bf16[2048,2048]{1,0:T(8,128)(2,1)}) custom-call(f32[256,2048]{1,0:T(8,128)} %refs_2_.4, f32[1,2048]{1,0:T(1,128)} %bitcast.8, bf16[2048,768]{1,0:T(8,128)(2,1)} %get-tuple-element.48.refs_2_.refs_5_, ...), custom_call_target="tpu_custom_call" | custom-call | flops 4294967296 | bytes 16777216 | tf_op jit(solution)/shard_map/attend/pallas_call | solution.py:586
  201.4 0.0 all-gather.8.cloned.1.call-done.refs_6_
  201.4 0.5 all-gather.6.cloned.1.call-done.refs_5_
  201.9 157.1 %feed.1 = (f32[256,2048]{1,0:T(8,128)}, bf16[256,2048]{1,0:T(8,128)(2,1)}, f32[1,2048]{1,0:T(1,128)}, bf16[2048,1024]{1,0:T(8,128)(2,1)}, bf16[2048,2048]{1,0:T(8,128)(2,1)}, /*index=5*/bf16[2048,2048]{1,0:T(8,128)(2,1)}) custom-call(f32[1,2048]{1,0:T(1,128)} %bitcast.9, f32[256,2048]{1,0:T(8,128)} %get-tuple-element.50.refs_1_.hidden, f32[256,2048]{1,0:T(8,128)} %refs_2_.4, ...), custom_call_target="tpu_custom_call" | custom-call | flops 68719476736 | bytes 41943040 | tf_op jit(solution)/shard_map/feed/pallas_call | solution.py:1232
  359.0 0.0 reduce-scatter.3.cloned.1.call-update
  359.0 0.0 reduce-scatter.5.cloned.1.call-start
  359.1 120.4 %back.1 = (f32[256,2048]{1,0:T(8,128)}, bf16[2048,2048]{1,0:T(8,128)(2,1)}, bf16[2048,768]{1,0:T(8,128)(2,1)}, bf16[1024,2048]{1,0:T(8,128)(2,1)}, f32[256,512]{1,0:T(8,128)}) custom-call(bf16[256,2048]{1,0:T(8,128)(2,1)} %get-tuple-element.54.refs_0_, bf16[2048,2048]{1,0:T(8,128)(2,1)} %get-tuple-element.55.refs_1_, ...), custom_call_target="tpu_custom_call" | custom-call | flops 1048576 | bytes 1048576 | tf_op jit(solution)/shard_map/back/pallas_call | solution.py:810
  479.4 0.0 reduce-scatter.5.cloned.1.call-update
  479.5 0.0 reduce-scatter.3.cloned.1.call-done.both
  479.5 98.6 %spread.1 = (f32[256,2048]{1,0:T(8,128)}, f32[512,768]{1,0:T(8,128)}, f32[2,2048]{1,0:T(2,128)}) custom-call(bf16[2048,768]{1,0:T(8,128)(2,1)} %get-tuple-element.66.refs_0_, bf16[2048,768]{1,0:T(8,128)(2,1)} %get-tuple-element.67.refs_1_, f32[256,2048]{1,0:T(8,128)} %refs_2_.5, f32[1,2048]{1,0:T(1,128)} %bitcast.5, f32[1,2048]{1,0:T(1,128)} %get-tuple-element.68.refs_4_, ...), custom_call_target="tpu_custom_call" | custom-call | flops 1048576 | bytes 1048576 | tf_op jit(solution)/shard_map/spread/pallas_call | solution.py:982
  578.1 1.4 fusion
  579.5 0.0 reduce-scatter.5.cloned.1.call-done.grad_down
  579.5 11.2 %finish.1 = (f32[256,2048]{1,0:T(8,128)}, f32[256,2048]{1,0:T(8,128)}, f32[512,256]{1,0:T(8,128)}, f32[512,256]{1,0:T(8,128)}, f32[512,256]{1,0:T(8,128)}, /*ind...) custom-call(f32[256,2048]{1,0:T(8,128)} %get-tuple-element.50.refs_1_.hidden, ...), custom_call_target="tpu_custom_call" | custom-call | tf_op jit(solution)/shard_map/finish/pallas_call | solution.py:1290
  (2 shorter events, 0.0 us)
Async XLA Ops:
  7.2 92.6 %all-gather.4.cloned.1.call-start = ((), (), s32[]{:S(2)}) async-start(), calls=%async_computation.2 | async-start | bytes 1310720 | tf_op jit(solution)/shard_map/all_gather | solution.py:1314
  7.9 193.5 %all-gather.8.cloned.1.call-start = ((), (), s32[]{:S(2)}) async-start(), calls=%async_computation.4 | async-start | bytes 5242880 | tf_op jit(solution)/shard_map/all_gather | solution.py:1315
  8.7 193.3 %all-gather.6.cloned.1.call-start = ((), (), s32[]{:S(2)}) async-start(), calls=%async_computation.3 | async-start | bytes 10485760 | tf_op jit(solution)/shard_map/all_gather | solution.py:1320
  99.7 379.8 %reduce-scatter.3.cloned.1.call-start = ((), (), s32[]{:S(2)}) async-start(), calls=%async_computation.5 | async-start | bytes 10485760 | tf_op jit(solution)/shard_map/reduce_scatter | solution.py:1327
  359.0 220.5 %reduce-scatter.5.cloned.1.call-start = ((), (), s32[]{:S(2)}) async-start(), calls=%async_computation.6 | async-start | bytes 5242880 | tf_op jit(solution)/shard_map/reduce_scatter | solution.py:1327
Sparse Core Ops, SparseCore 0:
  9.8 49.0 all-gather.3
  60.7 51.6 all-gather.7
  114.3 87.6 all-gather.5
  359.1 85.2 reduce-scatter.2
  479.6 81.4 reduce-scatter.4

commit v6 on v5

--- a/solution.py
+++ b/solution.py
@@ -253,6 +253,77 @@
     lax.fori_loop(0, rows // NORM_ROWS, step, 0)
 
 
+class Grid:
+    def __init__(self, shards):
+        self.shards, self.across = shards, shards // 2
+        self.me = lax.axis_index("fsdp")
+        self.row, self.column = self.me // self.across, self.me % self.across
+        self.others = [(self.me + ahead) % shards for ahead in range(1, shards)]
+        self.mates = [self.row * self.across + (self.column + ahead) % self.across for ahead in range(1, self.across)]
+        self.twin = (1 - self.row) * self.across + self.column
+        self.near = self.mates + [self.twin]
+
+    def is_near(self, shard):
+        return jnp.logical_or(shard // self.across == self.row, shard % self.across == self.column)
+
+
+class NearShards:
+    scratch = staticmethod(lambda shards: [DMA((shards // 2,)), DMA((shards // 2,))])
+
+    def __init__(self, grid, own, whole, at, send, receive):
+        place = at(whole, grid.me, None)
+        self.copies = [remote(own, place, send.at[i], receive.at[i], {"fsdp": peer}) for i, peer in enumerate(grid.near)]
+
+    def start(self):
+        for copy in self.copies:
+            copy.start()
+
+    def arrive(self):
+        for copy in self.copies:
+            copy.wait_recv()
+
+    def finish(self):
+        for copy in self.copies:
+            copy.wait_send()
+
+
+class FarShards:
+    scratch = staticmethod(lambda shards: [DMA((2, shards // 2 - 1)), DMA((2, shards // 2 - 1))])
+
+    def __init__(self, grid, near, whole, at, send, receive):
+        self.copies = []
+        for i, mate in enumerate(grid.mates):
+            self.copies.append(remote(at(near, mate, 0), at(whole, mate, 0), send.at[0, i], receive.at[0, i], {"fsdp": grid.twin}))
+            self.copies.append(remote(at(near, grid.twin, 1), at(whole, grid.twin, 1), send.at[1, i], receive.at[1, i], {"fsdp": mate}))
+
+    def start(self):
+        for copy in self.copies:
+            copy.start()
+
+    def finish(self):
+        for copy in self.copies:
+            copy.wait_recv()
+            copy.wait_send()
+
+
+def row_shard(depth):
+    def at(ref, shard, half):
+        if half is None:
+            return ref.at[span(shard, depth)]
+        return ref.at[span(2 * shard + half, depth // 2)]
+
+    return at
+
+
+def column_shard(rows, width):
+    def at(ref, shard, half):
+        if half is None:
+            return ref.at[:, span(shard, width)]
+        return ref.at[pl.ds(half * (rows // 2), rows // 2), span(shard, width)]
+
+    return at
+
+
 class HeldScatter(Scatter):
     @staticmethod
     def scratch(chips, rows, depth):
@@ -332,21 +403,24 @@
 
 def project_kernel(
     chips, shards,
-    activations, gain, w_query, w_key, w_value, cosine_t, sine_t, w_gate, w_up,
-    tokens_out, weight_out, qkv_out, keys_out, values_out, cosine_out, sine_out, both_out,
-    weight, qkv, keys_t, values_t, cosine, sine, both, tokens, chunks,
-    chunk_sem, weight_send, weight_recv, weight_keep, table_sem, both_sem, store_sem, *gather_sems,
+    activations, gain, w_query, w_key, w_value, w_out, cosine_t, sine_t, w_down,
+    tokens_out, weight_out, full_out, qkv_out, keys_out, values_out, cosine_out, sine_out, down_near,
+    weight, out_w, qkv, keys_t, values_t, cosine, sine, tokens, chunks,
+    chunk_sem, weight_send, weight_recv, weight_keep, table_sem, store_sem, near_send, near_recv, *gather_sems,
 ):
     line = Line(chips)
     rows = tokens.shape[0]
     pair = 2 * rows
     depth, width = w_query.shape
-    shard = lax.axis_index("fsdp")
-    others = [(shard + ahead) % shards for ahead in range(1, shards)]
+    grid = Grid(shards)
+    shard, others = grid.me, grid.others
     gather = Gather(line, tokens, tokens_out, *gather_sems)
-    parts = (w_query, w_key, w_value)
+    down = NearShards(grid, w_down, down_near, column_shard(*w_down.shape), near_send, near_recv)
+    parts = (w_query, w_key, w_value, w_out)
 
     def place(part):
+        if part == 3:
+            return out_w.at[:, span(shard, depth)]
         return weight.at[span(shard, depth), pl.ds(part * width, width)]
 
     def give(ahead, part):
@@ -355,15 +429,9 @@
     def keep(part):
         return pltpu.make_async_copy(parts[part], place(part), weight_keep.at[part])
 
-    hidden = w_gate.shape[1]
-    joins = [
-        pltpu.make_async_copy(source, both.at[:, pl.ds(side * hidden, hidden)], both_sem.at[side])
-        for side, source in enumerate((w_gate, w_up))
-    ]
-    joined = pltpu.make_async_copy(both, both_out, both_sem.at[2])
     tables = [
         pltpu.make_async_copy(source, out, table_sem.at[i])
-        for i, (source, out) in enumerate(((cosine, cosine_out), (sine, sine_out), (weight, weight_out)))
+        for i, (source, out) in enumerate(((cosine, cosine_out), (sine, sine_out), (weight, weight_out), (out_w, full_out)))
     ]
 
     def stores(chip):
@@ -380,14 +448,14 @@
     by_rows(rows, norm)
     line.greet([{"fsdp": other} for other in others])
     gather.start()
-    for part in range(3):
+    for part in range(4):
         keep(part).start()
         for ahead in range(shards - 1):
             give(ahead, part).start()
     for table, table_t in ((cosine, cosine_t), (sine, sine_t)):
         turn = table_t[...].T
         table[...] = jnp.concatenate([turn] * (LANES // turn.shape[1]), axis=1)
-    for copy in joins + tables[:2]:
+    for copy in tables[:2]:
         copy.start()
 
     def project(chip):
@@ -415,71 +483,72 @@
         def _():
             gather.step(index)
 
-        @pl.when(index == 1)
+        @pl.when(index == 2)
         def _():
             gather.keep().wait()
-            for part in range(3):
+            for part in range(4):
                 keep(part).wait()
                 for ahead in range(shards - 1):
                     give(ahead, part).wait_recv()
-            tables[2].start()
-            for copy in joins:
-                copy.wait()
-            joined.start()
+            for copy in tables[2:]:
+                copy.start()
+            down.start()
 
         def side(which, carry):
             distance = index - 1
-
-            @pl.when(jnp.logical_and(distance >= 0, jnp.logical_or(which == 0, distance > 0)))
-            def _():
-                project(jnp.where(which == 0, line.chip - distance, line.chip + distance))
+            chip = jnp.where(which == 0, line.chip - distance, jnp.where(which == 1, line.chip + distance, line.chip))
+
+            @pl.when(jnp.logical_and(index >= 2, jnp.logical_or(which < 2, index == 2)))
+            def _():
+                project(chip)
 
             return carry
 
-        lax.fori_loop(0, 2, side, 0)
+        lax.fori_loop(0, 3, side, 0)
         return carry
 
     lax.fori_loop(0, chips + 1, step, 0)
     gather.finish(False)
-    for part in range(3):
+    for part in range(4):
         for ahead in range(shards - 1):
             give(ahead, part).wait_send()
-    joined.wait()
     for copy in tables:
         copy.wait()
     for chip in range(chips):
         for copy in stores(chip):
             copy.wait()
-
-
-def project(chips, shards, activations, gain, w_query, w_key, w_value, cosine_t, sine_t, w_gate, w_up):
+    down.arrive()
+    down.finish()
+
+
+def project(chips, shards, activations, gain, w_query, w_key, w_value, w_out, cosine_t, sine_t, w_down):
     rows, depth = activations.shape
     group_rows = 2 * chips * rows
     width = w_query.shape[1]
     shape = jax.ShapeDtypeStruct
     held = [
         shape((depth, 3 * width), low),
+        shape((width, depth), low),
         shape((group_rows, 3 * width), low),
         shape((width, group_rows), low),
         shape((width, group_rows), low),
         shape((SEQ_LEN, LANES), jnp.float32),
         shape((SEQ_LEN, LANES), jnp.float32),
-        shape((w_gate.shape[0], 2 * w_gate.shape[1]), low),
     ]
     return pl.pallas_call(
         lambda *refs: project_kernel(chips, shards, *refs),
-        in_specs=[VMEM] * 7 + [ANYWHERE] * 2,
-        out_specs=[ANYWHERE] * 8,
-        out_shape=[shape((group_rows, depth), low)] + held,
+        in_specs=[VMEM] * 8 + [ANYWHERE],
+        out_specs=[ANYWHERE] * 9,
+        out_shape=[shape((group_rows, depth), low)] + held + [shape((w_down.shape[0], depth), low)],
         scratch_shapes=[pltpu.VMEM(a.shape, a.dtype) for a in held] + [
             pltpu.VMEM((rows, depth), low),
             pltpu.VMEM((2 * rows, depth), low),
-            DMA, DMA((shards - 1, 3)), DMA((shards - 1, 3)), DMA((3,)), DMA((3,)), DMA((3,)), DMA((3, chips)),
-        ] + Gather.scratch(chips),
+            DMA, DMA((shards - 1, 4)), DMA((shards - 1, 4)), DMA((4,)), DMA((4,)), DMA((3, chips)),
+        ] + NearShards.scratch(shards) + Gather.scratch(chips),
         compiler_params=pltpu.CompilerParams(collective_id=1, has_side_effects=True, vmem_limit_bytes=63 << 20),
         cost_estimate=pl.CostEstimate(flops=6 * group_rows * depth * width, bytes_accessed=4 * group_rows * depth, transcendentals=0),
         name="project",
-    )(activations, gain, w_query, w_key, w_value, cosine_t, sine_t, w_gate, w_up)
+    )(activations, gain, w_query, w_key, w_value, w_out, cosine_t, sine_t, w_down)
 
 
 def attend_chunk(chunk, rows, qkv, values_t, heads_ref, acc, out, top_ref, sum_ref):
@@ -516,14 +585,20 @@
 
 
 def attend_kernel(
-    chips,
+    chips, shards,
     cotangent, gain, *refs,
 ):
-    sources, (hidden, tokens, mixed, totals, grads_out) = refs[:4], refs[4:9]
-    loads = Loads(sources, refs[9:14])
+    sources, (w_gate, w_up, down_near) = refs[:4], refs[4:7]
+    hidden, tokens, mixed, totals, grads_out, gate_all, up_all, down_far = refs[7:15]
+    loads = Loads(sources, refs[15:20])
     qkv, values_t, w_out, activations = loads.refs
-    heads_ref, acc, out, top_ref, sum_ref, grads = refs[14:20]
-    sems = refs[20:]
+    heads_ref, acc, out, top_ref, sum_ref, grads = refs[20:26]
+    grid = Grid(shards)
+    rows_of = row_shard(w_gate.shape[0])
+    down = FarShards(grid, down_near, down_far, column_shard(down_near.shape[0], down_near.shape[1] // shards), *refs[26:28])
+    gate_near, gate_far = NearShards(grid, w_gate, gate_all, rows_of, *refs[28:30]), FarShards(grid, gate_all, gate_all, rows_of, *refs[30:32])
+    up_near, up_far = NearShards(grid, w_up, up_all, rows_of, *refs[32:34]), FarShards(grid, up_all, up_all, rows_of, *refs[34:36])
+    sems = refs[36:]
     loads.start()
     line = Line(chips)
     rows, depth = hidden.shape
@@ -531,8 +606,10 @@
     scatter = Scatter(line, hidden, *sems[:8])
     grads[...] = cotangent[...].astype(low)
     gather = Gather(line, grads, grads_out, *sems[8:])
-    line.greet()
+    line.greet([{"fsdp": peer} for peer in grid.near])
     gather.start()
+    gate_near.start()
+    down.start()
     loads.wait(0, 1, 2, 3)
 
     def step(index, carry):
@@ -558,6 +635,20 @@
         def _():
             gather.step(index)
 
+        @pl.when(index == 1)
+        def _():
+            up_near.start()
+
+        @pl.when(index == min(2, chips))
+        def _():
+            gate_near.arrive()
+            gate_far.start()
+
+        @pl.when(index == min(3, chips))
+        def _():
+            up_near.arrive()
+            up_far.start()
+
         @pl.when(index >= 1)
         def _():
             scatter.step(index - 1)
@@ -574,9 +665,13 @@
     by_rows(rows, norm)
     scatter.finish()
     gather.finish(True)
-
-
-def attend(chips, qkv, values_t, w_out, activations, cotangent, gain):
+    for near in (gate_near, up_near):
+        near.finish()
+    for far in (down, gate_far, up_far):
+        far.finish()
+
+
+def attend(chips, shards, qkv, values_t, w_out, activations, cotangent, gain, w_gate, w_up, down_near):
     rows, depth = activations.shape
     pair = 2 * rows
     group_rows = chips * pair
@@ -584,15 +679,18 @@
     heads = width // HEAD_DIM
     shape = jax.ShapeDtypeStruct
     return pl.pallas_call(
-        lambda *refs: attend_kernel(chips, *refs),
-        in_specs=[VMEM] * 2 + [ANYWHERE] * 4,
-        out_specs=[VMEM] * 4 + [ANYWHERE],
+        lambda *refs: attend_kernel(chips, shards, *refs),
+        in_specs=[VMEM] * 2 + [ANYWHERE] * 7,
+        out_specs=[VMEM] * 4 + [ANYWHERE] * 4,
         out_shape=[
             shape((rows, depth), jnp.float32),
             shape((rows, depth), low),
             shape((group_rows, width), low),
             shape((heads, group_rows), jnp.float32),
             shape((group_rows, depth), low),
+            shape((depth, w_gate.shape[1]), low),
+            shape((depth, w_gate.shape[1]), low),
+            shape(down_near.shape, low),
         ],
         scratch_shapes=Loads.scratch(qkv, values_t, w_out, activations) + [
             pltpu.VMEM((heads, pair, width), low),
@@ -601,11 +699,11 @@
             pltpu.VMEM((heads, pair), jnp.float32),
             pltpu.VMEM((heads, pair), jnp.float32),
             pltpu.VMEM((rows, depth), low),
-        ] + Scatter.scratch(chips, rows, depth) + Gather.scratch(chips),
+        ] + FarShards.scratch(shards) + (NearShards.scratch(shards) + FarShards.scratch(shards)) * 2 + Scatter.scratch(chips, rows, depth) + Gather.scratch(chips),
         compiler_params=pltpu.CompilerParams(collective_id=2, has_side_effects=True, vmem_limit_bytes=63 << 20),
         cost_estimate=pl.CostEstimate(flops=2 * group_rows * (SEQ_LEN + depth) * width, bytes_accessed=4 * group_rows * depth, transcendentals=group_rows * SEQ_LEN * heads // 2),
         name="attend",
-    )(cotangent, gain, qkv, values_t, w_out, activations)
+    )(cotangent, gain, qkv, values_t, w_out, activations, w_gate, w_up, down_near)
 
 
 def back_chunk(chunk, rows, grad, qkv, keys_t, mixed, totals, dkey, dvalue, heads_ref, grads_ref, acc, inner_ref):
@@ -646,14 +744,14 @@
 
 def back_kernel(
     chips, shards,
-    branch, terms, inner, grads, *refs,
+    branch, terms, inner, grads, grad_both, *refs,
 ):
-    sources, (down, branch_out, qkv_grad, grad_down, grad_out) = refs[:7], refs[7:12]
-    loads = Loads(sources, refs[12:20])
+    sources, (down, branch_out, qkv_grad, grad_down, grad_out, both_from) = refs[:7], refs[7:13]
+    loads = Loads(sources, refs[13:21])
     w_out, qkv, keys_t, mixed, totals, cosine, sine = loads.refs
-    inner_chunk, grad_chunk, down_sum, down_tile, out_sum, out_stage, out_from, branch_chunk, dkey, dvalue = refs[20:30]
-    heads_ref, grads_ref, acc, inner_ref, inner_sem, grad_sem, branch_sem, tile_sem, out_send, out_recv = refs[30:40]
-    sems = refs[40:]
+    inner_chunk, grad_chunk, down_sum, down_tile, out_sum, out_stage, out_from, branch_chunk, dkey, dvalue = refs[21:31]
+    heads_ref, grads_ref, acc, inner_ref, inner_sem, grad_sem, branch_sem, tile_sem, out_send, out_recv, both_send, both_recv = refs[31:43]
+    sems = refs[43:]
     line = Line(chips)
     rows, depth = down.shape
     pair = 2 * rows
@@ -674,12 +772,18 @@
     def give(turn):
         return remote(out_stage.at[turn], out_from.at[turn], out_send.at[turn], out_recv.at[turn], {"fsdp": others[turn]})
 
+    def hand(turn):
+        source = grad_both.at[span(others[turn], grad_both.shape[0] // shards)]
+        return remote(source, both_from.at[turn], both_send.at[turn], both_recv.at[turn], {"fsdp": others[turn]})
+
     def keep_tile(place):
         return pltpu.make_async_copy(down_tile, grad_down.at[span(place, 256)], tile_sem)
 
     loads.start()
     line.greet([{"fsdp": other} for other in others])
     gather.start()
+    for turn in range(shards - 1):
+        hand(turn).start()
     out_sum[...] = jnp.zeros_like(out_sum)
     dkey[...] = jnp.zeros_like(dkey)
     dvalue[...] = jnp.zeros_like(dvalue)
@@ -794,11 +898,14 @@
     for turn in range(shards - 1):
         give(turn).wait_send()
     keep_tile(down_sum.shape[0] // 256 - 1).wait()
+    for turn in range(shards - 1):
+        hand(turn).wait_recv()
+        hand(turn).wait_send()
     scatter.finish()
     gather.finish(False)
 
 
-def back(chips, shards, branch, terms, inner, grads, w_out, qkv, keys_t, mixed, totals, cosine, sine):
+def back(chips, shards, branch, terms, inner, grads, grad_both, w_out, qkv, keys_t, mixed, totals, cosine, sine):
     rows, depth = branch.shape
     pair = 2 * rows
     group_rows = chips * pair
@@ -809,14 +916,15 @@
     held = (w_out, qkv, keys_t, mixed, totals, cosine, sine)
     return pl.pallas_call(
         lambda *refs: back_kernel(chips, shards, *refs),
-        in_specs=[VMEM] + [ANYWHERE] * 10,
-        out_specs=[VMEM, ANYWHERE, VMEM, ANYWHERE, VMEM],
+        in_specs=[VMEM] + [ANYWHERE] * 11,
+        out_specs=[VMEM, ANYWHERE, VMEM, ANYWHERE, VMEM, ANYWHERE],
         out_shape=[
             shape((rows, depth), jnp.float32),
             shape((group_rows, depth), low),
             shape((group_rows, 3 * width), low),
             shape((hidden, depth), low),
             shape((width, depth // shards), jnp.float32),
+            shape((shards - 1, depth // shards, grad_both.shape[1]), low),
         ],
         scratch_shapes=Loads.scratch(*held) + [
             pltpu.VMEM((pair, hidden), low),
@@ -833,20 +941,20 @@
             pltpu.VMEM((heads, pair, width), low),
             pltpu.VMEM((width, pair), jnp.float32),
             pltpu.VMEM((8, pair), jnp.float32),
-            DMA, DMA, DMA, DMA, DMA((shards - 1,)), DMA((shards - 1,)),
+            DMA, DMA, DMA, DMA, DMA((shards - 1,)), DMA((shards - 1,)), DMA((shards - 1,)), DMA((shards - 1,)),
         ] + HeldScatter.scratch(chips, rows, depth) + Gather.scratch(chips),
         compiler_params=pltpu.CompilerParams(collective_id=4, has_side_effects=True, vmem_limit_bytes=67043328),
         cost_estimate=pl.CostEstimate(flops=1 << 20, bytes_accessed=1 << 20, transcendentals=0),
         name="back",
-    )(branch, terms, inner, grads, *held)
+    )(branch, terms, inner, grads, grad_both, *held)
 
 
 def spread_kernel(
     chips, shards,
-    qkv_grad, weight, activations, gain, gain_part, attn_tokens,
-    input_part, grad_qkv, gain_sum,
+    qkv_grad, weight, activations, gain, gain_part, attn_tokens, grad_down,
+    input_part, grad_qkv, gain_sum, down_from,
     attn_cols, qkv_stage, qkv_from, gains, gains_tp, gains_fsdp,
-    attn_sem, qkv_send, qkv_recv, tp_send, tp_recv, fsdp_send, fsdp_recv, *sems,
+    attn_sem, qkv_send, qkv_recv, down_send, down_recv, tp_send, tp_recv, fsdp_send, fsdp_recv, *sems,
 ):
     line = Line(chips)
     size = 2 * chips
@@ -865,6 +973,10 @@
     def give(turn):
         return remote(qkv_stage.at[turn], qkv_from.at[turn], qkv_send.at[turn], qkv_recv.at[turn], {"fsdp": peer(turn)})
 
+    def hand(turn):
+        source = grad_down.at[:, span(peer(turn), columns)]
+        return remote(source, down_from.at[turn], down_send.at[turn], down_recv.at[turn], {"fsdp": peer(turn)})
+
     def tell_tp(ahead):
         return remote(gains, gains_tp.at[line.me], tp_send.at[ahead - 1], tp_recv.at[line.me], {"tp": (line.me + ahead) % size})
 
@@ -877,6 +989,8 @@
     for ahead in range(1, shards):
         hello({"fsdp": (shard + ahead) % shards})
     pl.semaphore_wait(pltpu.get_barrier_semaphore(), size - 1 + shards - 1)
+    for turn in range(shards - 1):
+        hand(turn).start()
 
     def weights(turn, carry):
         @pl.when(turn < shards - 1)
@@ -930,9 +1044,6 @@
         return carry
 
     lax.fori_loop(0, chips + 1, step, 0)
-    for turn in range(shards - 1):
-        give(turn).wait_recv()
-        grad_qkv[...] += qkv_from[turn].astype(jnp.float32)
     gains[0:1, :] = jnp.zeros((1, depth), jnp.float32)
     gains[1:2, :] = gain_part[...]
 
@@ -968,11 +1079,16 @@
     for ahead in range(1, shards):
         tell_fsdp(ahead).wait_send()
     for turn in range(shards - 1):
+        give(turn).wait_recv()
+        grad_qkv[...] += qkv_from[turn].astype(jnp.float32)
+    for turn in range(shards - 1):
         give(turn).wait_send()
+        hand(turn).wait_recv()
+        hand(turn).wait_send()
     scatter.finish()
 
 
-def spread(chips, shards, qkv_grad, weight, activations, gain, gain_part, attn_tokens):
+def spread(chips, shards, qkv_grad, weight, activations, gain, gain_part, attn_tokens, grad_down):
     group_rows = qkv_grad.shape[0]
     rows, depth = activations.shape
     width = qkv_grad.shape[1] // 3
@@ -981,12 +1097,13 @@
     shape = jax.ShapeDtypeStruct
     return pl.pallas_call(
         lambda *refs: spread_kernel(chips, shards, *refs),
-        in_specs=[VMEM] * 5 + [ANYWHERE],
-        out_specs=[VMEM] * 3,
+        in_specs=[VMEM] * 5 + [ANYWHERE] * 2,
+        out_specs=[VMEM] * 3 + [ANYWHERE],
         out_shape=[
             shape((rows, depth), jnp.float32),
             shape((columns, 3 * width), jnp.float32),
             shape((2, depth), jnp.float32),
+            shape((shards - 1, grad_down.shape[0], columns), low),
         ],
         scratch_shapes=[
             pltpu.VMEM((2, group_rows, columns), low),
@@ -995,13 +1112,13 @@
             pltpu.VMEM((2, depth), jnp.float32),
             pltpu.VMEM((size, 2, depth), jnp.float32),
             pltpu.VMEM((shards, 2, depth), jnp.float32),
-            DMA((2,)), DMA((shards - 1,)), DMA((shards - 1,)),
+            DMA((2,)), DMA((shards - 1,)), DMA((shards - 1,)), DMA((shards - 1,)), DMA((shards - 1,)),
             DMA((size - 1,)), DMA((size,)), DMA((shards - 1,)), DMA((shards,)),
         ] + Scatter.scratch(chips, rows, depth),
         compiler_params=pltpu.CompilerParams(collective_id=5, has_side_effects=True, vmem_limit_bytes=63 << 20),
         cost_estimate=pl.CostEstimate(flops=1 << 20, bytes_accessed=1 << 20, transcendentals=0),
         name="spread",
-    )(qkv_grad, weight, activations, gain, gain_part, attn_tokens)
+    )(qkv_grad, weight, activations, gain, gain_part, attn_tokens, grad_down)
 
 
 def chip_at(place, chips):
@@ -1013,8 +1130,8 @@
 
 
 def feed_kernel(
-    chips,
-    gain, hidden_hbm, cotangent_hbm, tokens, grads_hbm, both_hbm, down_hbm,
+    chips, shards,
+    gain, hidden_hbm, cotangent_hbm, tokens, grads_hbm, w_gate, w_up, w_down, gate_all, up_all, down_near, down_far,
     hidden_grad, branch, gain_part, inner_out, grad_both, down_out,
     hidden_state, cotangent, state_sem, down_tile, down_sem, tokens_all, gate_w, up_w, down_w, grads, inner, gate_grad, up_grad, term, from_core, from_ring, total, tile_gate, tile_up,
     load_sem, own_sem, grad_sem, store_sem, tile_sem,
@@ -1030,7 +1147,36 @@
     before = {"tp": 2 * chip_at((place + chips - 1) % chips, chips) + core}
     partner = {"tp": 2 * chip + 1 - core}
 
-    loads = [pltpu.make_async_copy(a, b, load_sem.at[i]) for i, (a, b) in enumerate(((both_hbm.at[:, pl.ds(0, width)], gate_w), (both_hbm.at[:, pl.ds(width, width)], up_w), (down_hbm, down_w)))]
+    grid = Grid(shards)
+    rows_of, columns_of = row_shard(w_gate.shape[0]), column_shard(*w_down.shape)
+
+    def load(array, source, shard, whole):
+        at = columns_of if array == 2 else rows_of
+        target = at((gate_w, up_w, down_w)[array], shard, None)
+        return pltpu.make_async_copy(at(source, shard, None) if whole else source, target, load_sem.at[array, shard])
+
+    def load_weights():
+        for shard in range(shards):
+            own, near = grid.me == shard, grid.is_near(shard)
+
+            @pl.when(own)
+            def _():
+                for array, source in enumerate((w_gate, w_up, w_down)):
+                    load(array, source, shard, False).start()
+
+            @pl.when(jnp.logical_not(own))
+            def _():
+                for array, source in enumerate((gate_all, up_all)):
+                    load(array, source, shard, True).start()
+
+            @pl.when(jnp.logical_and(near, jnp.logical_not(own)))
+            def _():
+                load(2, down_near, shard, True).start()
+
+            @pl.when(jnp.logical_not(near))
+            def _():
+                load(2, down_far, shard, True).start()
+
     own = pltpu.make_async_copy(tokens, tokens_all.at[span(me, rows)], own_sem)
     states = Loads((hidden_hbm, cotangent_hbm), (hidden_state, cotangent, state_sem))
 
@@ -1080,8 +1226,7 @@
 
     own.start()
     fetch(0).start()
-    for load in loads:
-        load.start()
+    load_weights()
     own.wait()
     for device in (following, before, partner):
         hello(device)
@@ -1105,8 +1250,9 @@
 
         @pl.when(slot == 0)
         def _():
-            for load in loads:
-                load.wait()
+            for shard in range(shards):
+                for array, source in enumerate((gate_all, up_all, down_near)):
+                    load(array, source, shard, True).wait()
 
         @pl.when(slot == 1)
         def _():
@@ -1223,15 +1369,15 @@
             copy.wait()
 
 
-def feed(chips, hidden_state, cotangent, gain, tokens, grads, both_w, down_w):
+def feed(chips, shards, hidden_state, cotangent, gain, tokens, grads, w_gate, w_up, w_down, gate_all, up_all, down_near, down_far):
     rows, depth = tokens.shape
     pair = 2 * rows
     group_rows = chips * pair
-    width = down_w.shape[0]
+    width = w_down.shape[0]
     shape = jax.ShapeDtypeStruct
     return pl.pallas_call(
-        lambda *refs: feed_kernel(chips, *refs),
-        in_specs=[VMEM] + [ANYWHERE] * 6,
+        lambda *refs: feed_kernel(chips, shards, *refs),
+        in_specs=[VMEM] + [ANYWHERE] * 11,
         out_specs=[VMEM] * 3 + [ANYWHERE] * 3,
         out_shape=[
             shape((rows, depth), jnp.float32),
@@ -1247,7 +1393,7 @@
             pltpu.VMEM((group_rows, depth), low),
             pltpu.VMEM((depth, width), low),
             pltpu.VMEM((depth, width), low),
-            pltpu.VMEM(down_w.shape, low),
+            pltpu.VMEM((width, depth), low),
             pltpu.VMEM((2, pair, depth), low),
             pltpu.VMEM((chips, pair, width), low),
             pltpu.VMEM((group_rows, width), low),
@@ -1258,17 +1404,20 @@
             pltpu.VMEM((2, rows, depth), low),
             pltpu.VMEM((2, 256, width), low),
             pltpu.VMEM((2, 256, width), low),
-            DMA((3,)), DMA, DMA((2,)), DMA((chips,)), DMA((2, 2)),
+            DMA((3, shards)), DMA, DMA((2,)), DMA((chips,)), DMA((2, 2)),
             DMA((chips,)), DMA((chips,)), DMA((chips,)), DMA((chips,)),
             DMA, DMA((3,)), DMA((2,)), DMA((chips - 1,)),
         ],
         compiler_params=pltpu.CompilerParams(collective_id=3, has_side_effects=True, vmem_limit_bytes=67043328),
         cost_estimate=pl.CostEstimate(flops=16 * group_rows * depth * width, bytes_accessed=10 * group_rows * depth, transcendentals=group_rows * width),
         name="feed",
-    )(gain, hidden_state, cotangent, tokens, grads, both_w, down_w)
-
-
-def finish_kernel(hidden, down, hidden_grad, input_part, both, grad_down, grad_qkv, grad_out, output, input_grad, query, key, value, out, gate, up, down_out):
+    )(gain, hidden_state, cotangent, tokens, grads, w_gate, w_up, w_down, gate_all, up_all, down_near, down_far)
+
+
+def finish_kernel(
+    shard_ref, hidden, down, hidden_grad, input_part, both, both_from, grad_down, down_from, grad_qkv, grad_out,
+    output, input_grad, query, key, value, out, gate, up, down_out,
+):
     output[...] = hidden[...] + down[...]
     input_grad[...] = hidden_grad[...] + input_part[...]
     width = query.shape[1]
@@ -1276,25 +1425,44 @@
         ref[...] = grad_qkv[:, pl.ds(part * width, width)]
     out[...] = grad_out[...]
     wide = gate.shape[1]
-    gate[...] = both[:, pl.ds(0, wide)].astype(jnp.float32)
-    up[...] = both[:, pl.ds(wide, wide)].astype(jnp.float32)
-    down_out[...] = grad_down[...].astype(jnp.float32)
-
-
-def finish(*operands):
+    for side, ref in enumerate((gate, up)):
+        columns = pl.ds(side * wide, wide)
+        total = both[:, columns].astype(jnp.float32)
+        for turn in range(both_from.shape[0]):
+            total = total + both_from[turn, :, columns].astype(jnp.float32)
+        ref[...] = total
+    total = grad_down[...].astype(jnp.float32)
+    for turn in range(down_from.shape[0]):
+        total = total + down_from[turn].astype(jnp.float32)
+    down_out[...] = total
+
+
+def finish(shard, hidden, down, hidden_grad, input_part, both, both_from, grad_down, down_from, grad_qkv, grad_out):
     steps = 8
-    hidden, _, _, _, both, grad_down, grad_qkv, grad_out = operands
-    shape = lambda a, parts: jax.ShapeDtypeStruct((a.shape[0], a.shape[1] // parts), jnp.float32)
-    results = [shape(hidden, 1)] * 2 + [shape(grad_qkv, 3)] * 3 + [shape(grad_out, 1)] + [shape(both, 2)] * 2 + [shape(grad_down, 1)]
-    spec = lambda a: pl.BlockSpec((a.shape[0] // steps, a.shape[1]), lambda i: (i, 0))
+    shape = jax.ShapeDtypeStruct
+    columns = down_from.shape[2]
+    results = [shape(hidden.shape, jnp.float32)] * 2
+    results += [shape((columns, grad_qkv.shape[1] // 3), jnp.float32)] * 3 + [shape(grad_out.shape, jnp.float32)]
+    results += [shape((columns, both.shape[1] // 2), jnp.float32)] * 2 + [shape((grad_down.shape[0], columns), jnp.float32)]
+    spec = lambda a: pl.BlockSpec((a.shape[0] // steps, a.shape[1]), lambda i, s: (i, 0))
+    spec3 = lambda a: pl.BlockSpec((a.shape[0], a.shape[1] // steps, a.shape[2]), lambda i, s: (0, i, 0))
     return pl.pallas_call(
         finish_kernel,
-        grid=(steps,),
-        in_specs=[spec(a) for a in operands],
-        out_specs=[spec(a) for a in results],
+        grid_spec=pltpu.PrefetchScalarGridSpec(
+            num_scalar_prefetch=1,
+            grid=(steps,),
+            in_specs=[
+                spec(hidden), spec(down), spec(hidden_grad), spec(input_part),
+                pl.BlockSpec((columns // steps, both.shape[1]), lambda i, s: (s[0] * steps + i, 0)),
+                spec3(both_from),
+                pl.BlockSpec((grad_down.shape[0] // steps, columns), lambda i, s: (i, s[0])),
+                spec3(down_from), spec(grad_qkv), spec(grad_out),
+            ],
+            out_specs=[spec(a) for a in results],
+        ),
         out_shape=results,
         name="finish",
-    )(*operands)
+    )(shard.reshape(1), hidden, down, hidden_grad, input_part, both, both_from, grad_down, down_from, grad_qkv, grad_out)
 
 
 def rope_tables():
@@ -1310,31 +1478,26 @@
     chips, shards = mesh.shape["tp"] // 2, mesh.shape["fsdp"]
 
     def body(activations, gain_attn, w_query, w_key, w_value, w_out, gain_mlp, w_gate, w_up, w_down, cotangent):
-        width = w_query.shape[1]
-        full_out = lax.all_gather(w_out, "fsdp", axis=1, tiled=True)
-        full_down = lax.all_gather(w_down, "fsdp", axis=1, tiled=True)
         gain_attn, gain_mlp = gain_attn[None, :], gain_mlp[None, :]
-        seen_attn, w_qkv, qkv, keys_t, values_t, cosine, sine, both = project(
-            chips, shards, activations, gain_attn, w_query, w_key, w_value, *rope_tables(), w_gate, w_up
+        seen_attn, w_qkv, full_out, qkv, keys_t, values_t, cosine, sine, down_near = project(
+            chips, shards, activations, gain_attn, w_query, w_key, w_value, w_out, *rope_tables(), w_down
         )
-        full_both = lax.all_gather(both, "fsdp", axis=0, tiled=True)
-        hidden_state, normed_mlp, mixed, totals, seen_grad = attend(chips, qkv, values_t, full_out, activations, cotangent, gain_mlp)
+        hidden_state, normed_mlp, mixed, totals, seen_grad, gate_all, up_all, down_far = attend(
+            chips, shards, qkv, values_t, full_out, activations, cotangent, gain_mlp, w_gate, w_up, down_near
+        )
         hidden_grad, branch_grad, gain_part, inner, grad_both, terms = feed(
-            chips, hidden_state, cotangent, gain_mlp, normed_mlp, seen_grad, full_both, full_down
+            chips, shards, hidden_state, cotangent, gain_mlp, normed_mlp, seen_grad,
+            w_gate, w_up, w_down, gate_all, up_all, down_near, down_far,
         )
-
-        def over_fsdp(grad, dimension):
-            return lax.psum_scatter(grad, "fsdp", scatter_dimension=dimension, tiled=True)
-
-        grad_both = over_fsdp(grad_both, 0)
-        down, _, qkv_grad, grad_down, grad_out = back(
-            chips, shards, branch_grad, terms, inner, seen_grad, full_out, qkv, keys_t, mixed, totals, cosine, sine
+        down, _, qkv_grad, grad_down, grad_out, both_from = back(
+            chips, shards, branch_grad, terms, inner, seen_grad, grad_both, full_out, qkv, keys_t, mixed, totals, cosine, sine
         )
-        grad_down = over_fsdp(grad_down, 1)
-        qkv_grad, grad_both = lax.optimization_barrier((qkv_grad, grad_both))
-        input_part, grad_qkv, gain_sums = spread(chips, shards, qkv_grad, w_qkv, activations, gain_attn, gain_part, seen_attn)
+        input_part, grad_qkv, gain_sums, down_from = spread(
+            chips, shards, qkv_grad, w_qkv, activations, gain_attn, gain_part, seen_attn, grad_down
+        )
         output, input_grad, grad_query, grad_key, grad_value, grad_out, grad_gate, grad_up, grad_down = finish(
-            hidden_state, down, hidden_grad, input_part, grad_both, grad_down, grad_qkv, grad_out
+            lax.axis_index("fsdp"), hidden_state, down, hidden_grad, input_part,
+            grad_both, both_from, grad_down, down_from, grad_qkv, grad_out,
         )
         return (
             output, input_grad, gain_sums[0], grad_query, grad_key, grad_value, grad_out, gain_sums[1],

time: 598 us -> 582 us (0.973)
  between operations: 13.9 us -> 0.72 us
  transfers between devices with their start and end apart: 5 -> 0, of which waited for: 1 -> 0; matrix products, arithmetic and copies ran while one was open for 1% -> 0% of each run, Pallas kernels for 69% -> 0%
where the time goes in v6:
time: 582 us
  Pallas kernels  579 us (99%)
    pallas_call x1, Pallas kernels, feed(): pl.pallas_call(lambda *refs: feed_kernel(chips, shards, *refs), in_specs=...  157 us
    pallas_call x1, Pallas kernels, back(): pl.pallas_call(lambda *refs: back_kernel(chips, shards, *refs), in_specs=...  118 us
    pallas_call x1, Pallas kernels, attend(): pl.pallas_call(lambda *refs: attend_kernel(chips, shards, *refs), in_spec...  102 us
    pallas_call x1, Pallas kernels, spread(): pl.pallas_call(lambda *refs: spread_kernel(chips, shards, *refs), in_spec...  101 us
    pallas_call x1, Pallas kernels, project(): pl.pallas_call(lambda *refs: project_kernel(chips, shards, *refs), in_spe...  88.5 us
    pallas_call x1, Pallas kernels, finish(): pl.pallas_call(finish_kernel, grid_spec=pltpu.PrefetchScalarGridSpec(num_...  13.3 us

profile of v6, /device:TPU:0, one launch (start us, length us, event | category | flops | bytes accessed | tf_op | source)
XLA Modules:
  0.0 581.8 jit_solution(13664858218965809644)
XLA Ops:
  0.7 1.8 multiply_sine_fusion
  2.5 88.5 %project.1 = (bf16[2048,2048]{1,0:T(8,128)(2,1)}, bf16[2048,768]{1,0:T(8,128)(2,1)}, bf16[256,2048]{1,0:T(8,128)(2,1)}, bf16[2048,768]{1,0:T(8,128)(2,1)}, bf16[...) custom-call(f32[256,2048]{1,0:T(8,128)} %refs_2_.5, ...), custom_call_target="tpu_custom_call" | custom-call | flops 6442450944 | bytes 16777216 | tf_op jit(solution)/shard_map/project/pallas_call | solution.py:538
  90.9 101.5 %attend.1 = (f32[256,2048]{1,0:T(8,128)}, bf16[256,2048]{1,0:T(8,128)(2,1)}, bf16[2048,256]{1,0:T(8,128)(2,1)}, f32[4,2048]{1,0:T(4,128)}, bf16[2048,2048]{1,0:T...) custom-call(f32[256,2048]{1,0:T(8,128)} %refs_2_.4, ...), custom_call_target="tpu_custom_call" | custom-call | flops 4294967296 | bytes 16777216 | tf_op jit(solution)/shard_map/attend/pallas_call | solution.py:681
  192.5 157.0 %feed.1 = (f32[256,2048]{1,0:T(8,128)}, bf16[256,2048]{1,0:T(8,128)(2,1)}, f32[1,2048]{1,0:T(1,128)}, bf16[2048,1024]{1,0:T(8,128)(2,1)}, bf16[2048,2048]{1,0:T(8,128)(2,1)}, /*index=5*/bf16[2048,2048]{1,0:T(8,128)(2,1)}) custom-call(f32[1,2048]{1,0:T(1,128)} %bitcast.10, f32[256,2048]{1,0:T(8,128)} %get-tuple-element.56.refs_1_.hidden, ...), custom_call_target="tpu_custom_call" | custom-call | flops 68719476736 | bytes 41943040 | tf_op jit(solution)/shard_map/feed/pallas_call | solution.py:1378
  349.4 117.9 %back.1 = (f32[256,2048]{1,0:T(8,128)}, bf16[2048,2048]{1,0:T(8,128)(2,1)}, bf16[2048,768]{1,0:T(8,128)(2,1)}, bf16[1024,2048]{1,0:T(8,128)(2,1)}, f32[256,512]{1,0:T(8,128)}, /*index=5*/bf16[3,512,2048]{2,1,0:T(8,128)(2,1)}) custom-call(bf16[256,2048]{1,0:T(8,128)(2,1)} %get-tuple-element.62.refs_0_, bf16[2048,2048]{1,0:T(8,128)(2,1)} %get-tuple-element.63.refs_1_, ...), custom_call_target="tpu_custom_call" | custom-call | flops 1048576 | bytes 1048576 | tf_op jit(solution)/shard_map/back/pallas_call | solution.py:917
  467.3 100.5 %spread.1 = (f32[256,2048]{1,0:T(8,128)}, f32[512,768]{1,0:T(8,128)}, f32[2,2048]{1,0:T(2,128)}, bf16[3,1024,512]{2,1,0:T(8,128)(2,1)}) custom-call(bf16[2048,768]{1,0:T(8,128)(2,1)} %get-tuple-element.73.refs_0_, bf16[2048,768]{1,0:T(8,128)(2,1)} %get-tuple-element.74.refs_1_, f32[256,2048]{1,0:T(8,128)} %refs_2_.5, f32[1,2048]{1,0:T(1,128)} %bitcast.6, ...), custom_call_target="tpu_custom_call" | custom-call | flops 1048576 | bytes 1048576 | tf_op jit(solution)/shard_map/spread/pallas_call | solution.py:1098
  567.8 0.0 copy-start
  567.8 13.3 %finish.1 = (f32[256,2048]{1,0:T(8,128)}, f32[256,2048]{1,0:T(8,128)}, f32[512,256]{1,0:T(8,128)}, f32[512,256]{1,0:T(8,128)}, f32[512,256]{1,0:T(8,128)}, /*ind...) custom-call(s32[1]{0:T(128)} %bitcast.shard_ref, ...), custom_call_target="tpu_custom_call" | custom-call | tf_op jit(solution)/shard_map/finish/pallas_call | solution.py:1449
  581.2 0.0 copy-done
  581.2 0.6 fusion
  (2 shorter events, 0.0 us)
Async XLA Ops:
  567.8 13.3 %copy-start = (f32[2,2048]{1,0:T(2,128)S(1)}, f32[2,2048]{1,0:T(2,128)}, u32[]{:S(2)}) copy-start(f32[2,2048]{1,0:T(2,128)} %get-tuple-element.85) | copy-start | bytes 49156

commit v7 on v6

--- a/solution.py
+++ b/solution.py
@@ -306,6 +306,68 @@
             copy.wait_send()
 
 
+class NearSums:
+    @staticmethod
+    def scratch(shards, rows, columns):
+        across = shards // 2
+        return [
+            pltpu.VMEM((2, across - 1, rows // 2, columns), low),
+            pltpu.VMEM((across, rows // 2, columns), low),
+            DMA((2, across - 1)), DMA((2, across - 1)), DMA((across, 2)), DMA((across, 2)), DMA((across,)),
+        ]
+
+    def __init__(self, grid, part, out, at, relay, base, relay_send, relay_recv, near_send, near_recv, load_sem):
+        self.relay, self.base = relay, base
+        last = grid.across - 1
+        half = base.shape[1]
+
+        def near(source, slot, which, peer):
+            target = out.at[slot, pl.ds(which * half, half)]
+            return remote(source, target, near_send.at[slot, which], near_recv.at[slot, which], {"fsdp": peer})
+
+        self.by_twin, self.by_mate, self.plain, self.joined, self.loads = [], [], [], [], []
+        for i, mate in enumerate(grid.mates):
+            far = (1 - grid.row) * grid.across + mate % grid.across
+            self.by_twin.append(remote(at(part, far, 0), relay.at[0, i], relay_send.at[0, i], relay_recv.at[0, i], {"fsdp": grid.twin}))
+            self.by_mate.append(remote(at(part, far, 1), relay.at[1, i], relay_send.at[1, i], relay_recv.at[1, i], {"fsdp": mate}))
+            self.plain.append(near(at(part, mate, 1), i, 1, mate))
+            self.joined.append(near(relay.at[0, i], i, 0, mate))
+            self.loads.append(pltpu.make_async_copy(at(part, mate, 0), base.at[i], load_sem.at[i]))
+        self.plain.append(near(at(part, grid.twin, 0), last, 0, grid.twin))
+        self.joined.append(near(relay.at[1, 0], last, 1, grid.twin))
+        self.loads.append(pltpu.make_async_copy(at(part, grid.twin, 1), base.at[last], load_sem.at[last]))
+
+    def start(self):
+        for copy in self.by_twin + self.by_mate + self.loads:
+            copy.start()
+
+    def start_plain(self):
+        for copy in self.plain:
+            copy.start()
+
+    def join(self):
+        for copy in self.by_twin + self.by_mate:
+            copy.wait_recv()
+        for copy in self.loads:
+            copy.wait()
+        last = self.base.shape[0] - 1
+        for i in range(last):
+            self.relay[0, i] = (self.base[i].astype(jnp.float32) + self.relay[0, i].astype(jnp.float32)).astype(low)
+        total = self.base[last].astype(jnp.float32)
+        for i in range(last):
+            total = total + self.relay[1, i].astype(jnp.float32)
+        self.relay[1, 0] = total.astype(low)
+        for copy in self.joined:
+            copy.start()
+
+    def finish(self):
+        for copy in self.by_twin + self.by_mate:
+            copy.wait_send()
+        for copy in self.plain + self.joined:
+            copy.wait_recv()
+            copy.wait_send()
+
+
 def row_shard(depth):
     def at(ref, shard, half):
         if half is None:
@@ -327,7 +389,13 @@
 class HeldScatter(Scatter):
     @staticmethod
     def scratch(chips, rows, depth):
-        return [pltpu.VMEM((2, rows, depth), low)] + Scatter.scratch(chips, rows, depth)[1:] + [DMA((2,))]
+        return [
+            pltpu.VMEM((2, rows, depth), low),
+            pltpu.VMEM((chips, rows, depth), low),
+            pltpu.VMEM((chips + 1, rows, depth), low),
+            pltpu.VMEM((2, rows, depth), low),
+            DMA((2,)), DMA((chips,)), DMA((2,)), DMA((chips + 1,)), DMA((2,)),
+        ]
 
     def __init__(self, line, out, held, *refs):
         super().__init__(line, out, *refs[:-1])
@@ -344,6 +412,11 @@
 
     def mine(self, step):
         self.load(step).wait()
+
+        @pl.when(step < self.line.chips - 1)
+        def _():
+            self.load(step + 1).start()
+
         return self.term[step % 2]
 
 
@@ -750,8 +823,9 @@
     loads = Loads(sources, refs[13:21])
     w_out, qkv, keys_t, mixed, totals, cosine, sine = loads.refs
     inner_chunk, grad_chunk, down_sum, down_tile, out_sum, out_stage, out_from, branch_chunk, dkey, dvalue = refs[21:31]
-    heads_ref, grads_ref, acc, inner_ref, inner_sem, grad_sem, branch_sem, tile_sem, out_send, out_recv, both_send, both_recv = refs[31:43]
-    sems = refs[43:]
+    heads_ref, grads_ref, acc, inner_ref, inner_sem, grad_sem, branch_sem, tile_sem, out_send, out_recv = refs[31:41]
+    sums = refs[41:48]
+    sems = refs[48:]
     line = Line(chips)
     rows, depth = down.shape
     pair = 2 * rows
@@ -765,25 +839,24 @@
     def fetch_grad(step):
         return pltpu.make_async_copy(grads.at[span(line.target(step), pair)], grad_chunk, grad_sem)
 
-    shard = lax.axis_index("fsdp")
+    grid = Grid(shards)
+    shard, others = grid.me, grid.others
     columns_out = depth // shards
-    others = [(shard + ahead) % shards for ahead in range(1, shards)]
+    both = NearSums(grid, grad_both, both_from, row_shard(columns_out), *sums)
 
     def give(turn):
         return remote(out_stage.at[turn], out_from.at[turn], out_send.at[turn], out_recv.at[turn], {"fsdp": others[turn]})
 
-    def hand(turn):
-        source = grad_both.at[span(others[turn], grad_both.shape[0] // shards)]
-        return remote(source, both_from.at[turn], both_send.at[turn], both_recv.at[turn], {"fsdp": others[turn]})
-
     def keep_tile(place):
         return pltpu.make_async_copy(down_tile, grad_down.at[span(place, 256)], tile_sem)
 
     loads.start()
+    fetch(0).start()
+    fetch_grad(0).start()
+    scatter.load(0).start()
     line.greet([{"fsdp": other} for other in others])
     gather.start()
-    for turn in range(shards - 1):
-        hand(turn).start()
+    both.start()
     out_sum[...] = jnp.zeros_like(out_sum)
     dkey[...] = jnp.zeros_like(dkey)
     dvalue[...] = jnp.zeros_like(dvalue)
@@ -819,15 +892,8 @@
 
         @pl.when(index < chips)
         def _():
-            fetch(index).start()
-            fetch_grad(index).start()
             scatter.free(index)
-            scatter.load(index).start()
             scatter.share(index).start()
-
-        @pl.when(jnp.logical_and(index >= 1, index < chips))
-        def _():
-            gather.step(index)
 
         @pl.when(index == chips)
         def _():
@@ -836,45 +902,51 @@
                 give(turn).start()
             close()
 
-        def phase(which, carry):
-            done = jnp.maximum(index - 1, 0)
-            late = line.fed(line.target(done))
-            turn = jnp.logical_or(jnp.logical_and(which == 0, jnp.logical_not(late)), jnp.logical_and(which == 3, late))
-
-            @pl.when(jnp.logical_and(index >= 1, turn))
+        def due(done, carry):
+            target = line.target(done)
+            distance = jnp.where(target > line.chip, target - line.chip, line.chip - target)
+
+            @pl.when(distance == chips - index)
             def _():
                 scatter.step(done)
 
-            chunk = jnp.where(which == 1, line.chip - index, line.chip + index)
-            there = jnp.logical_and(chunk >= 0, chunk < chips)
-            turn = jnp.logical_or(which == 1, jnp.logical_and(which == 2, index > 0))
-
-            @pl.when(jnp.logical_and(there, turn))
-            def _():
-                attention(chunk)
-
             return carry
 
-        lax.fori_loop(0, 4, phase, 0)
+        lax.fori_loop(0, chips, due, 0)
+
+        @pl.when(jnp.logical_and(index >= 1, index < chips))
+        def _():
+            gather.step(index)
+
+        @pl.when(index == 1)
+        def _():
+            both.start_plain()
+
+        @pl.when(index == 2)
+        def _():
+            both.join()
 
         @pl.when(index < chips)
         def _():
-            fetch(index).wait()
-            fetch_grad(index).wait()
+            attention(line.target(chips - 1 - index))
+
+        def weights(turn, carry):
+            fetch(turn).wait()
+            fetch_grad(turn).wait()
 
             def tile(place, carry):
                 here = span(place, 256)
                 part = dot(inner_chunk[:, here], grad_chunk[...], TN)
 
-                @pl.when(index == 0)
+                @pl.when(turn == 0)
                 def _():
                     down_sum[here, :] = part
 
-                @pl.when(index > 0)
+                @pl.when(turn > 0)
                 def _():
                     down_sum[here, :] += part
 
-                @pl.when(index == chips - 1)
+                @pl.when(turn == chips - 1)
                 def _():
                     @pl.when(place > 0)
                     def _():
@@ -887,6 +959,14 @@
 
             lax.fori_loop(0, down_sum.shape[0] // 256, tile, 0)
 
+            @pl.when(turn < chips - 1)
+            def _():
+                fetch(turn + 1).start()
+                fetch_grad(turn + 1).start()
+
+            return carry
+
+        lax.fori_loop(jnp.where(index == 0, 0, index + 1), jnp.minimum(index + 2, chips), weights, 0)
         return carry
 
     lax.fori_loop(0, chips + 1, step, 0)
@@ -898,9 +978,7 @@
     for turn in range(shards - 1):
         give(turn).wait_send()
     keep_tile(down_sum.shape[0] // 256 - 1).wait()
-    for turn in range(shards - 1):
-        hand(turn).wait_recv()
-        hand(turn).wait_send()
+    both.finish()
     scatter.finish()
     gather.finish(False)
 
@@ -924,7 +1002,7 @@
             shape((group_rows, 3 * width), low),
             shape((hidden, depth), low),
             shape((width, depth // shards), jnp.float32),
-            shape((shards - 1, depth // shards, grad_both.shape[1]), low),
+            shape((shards // 2, depth // shards, grad_both.shape[1]), low),
         ],
         scratch_shapes=Loads.scratch(*held) + [
             pltpu.VMEM((pair, hidden), low),
@@ -941,8 +1019,8 @@
             pltpu.VMEM((heads, pair, width), low),
             pltpu.VMEM((width, pair), jnp.float32),
             pltpu.VMEM((8, pair), jnp.float32),
-            DMA, DMA, DMA, DMA, DMA((shards - 1,)), DMA((shards - 1,)), DMA((shards - 1,)), DMA((shards - 1,)),
-        ] + HeldScatter.scratch(chips, rows, depth) + Gather.scratch(chips),
+            DMA, DMA, DMA, DMA, DMA((shards - 1,)), DMA((shards - 1,)),
+        ] + NearSums.scratch(shards, depth // shards, grad_both.shape[1]) + HeldScatter.scratch(chips, rows, depth) + Gather.scratch(chips),
         compiler_params=pltpu.CompilerParams(collective_id=4, has_side_effects=True, vmem_limit_bytes=67043328),
         cost_estimate=pl.CostEstimate(flops=1 << 20, bytes_accessed=1 << 20, transcendentals=0),
         name="back",
@@ -951,18 +1029,22 @@
 
 def spread_kernel(
     chips, shards,
-    qkv_grad, weight, activations, gain, gain_part, attn_tokens, grad_down,
+    gain, gain_part, qkv_hbm, weight_hbm, activations_hbm, attn_tokens, grad_down,
     input_part, grad_qkv, gain_sum, down_from,
+    qkv_grad, weight, activations, held_sem,
     attn_cols, qkv_stage, qkv_from, gains, gains_tp, gains_fsdp,
-    attn_sem, qkv_send, qkv_recv, down_send, down_recv, tp_send, tp_recv, fsdp_send, fsdp_recv, *sems,
+    attn_sem, qkv_send, qkv_recv, tp_send, tp_recv, fsdp_send, fsdp_recv, *sems,
 ):
     line = Line(chips)
     size = 2 * chips
     rows, depth = input_part.shape
     pair = 2 * rows
-    shard = lax.axis_index("fsdp")
+    grid = Grid(shards)
+    shard = grid.me
     columns = depth // shards
-    scatter = Scatter(line, input_part, *sems)
+    loads = Loads((qkv_hbm, weight_hbm, activations_hbm), (qkv_grad, weight, activations, held_sem))
+    down = NearSums(grid, grad_down, down_from, column_shard(grad_down.shape[0], columns), *sems[:7])
+    scatter = Scatter(line, input_part, *sems[7:])
 
     def peer(turn):
         return (shard + 1 + turn) % shards
@@ -973,24 +1055,21 @@
     def give(turn):
         return remote(qkv_stage.at[turn], qkv_from.at[turn], qkv_send.at[turn], qkv_recv.at[turn], {"fsdp": peer(turn)})
 
-    def hand(turn):
-        source = grad_down.at[:, span(peer(turn), columns)]
-        return remote(source, down_from.at[turn], down_send.at[turn], down_recv.at[turn], {"fsdp": peer(turn)})
-
     def tell_tp(ahead):
         return remote(gains, gains_tp.at[line.me], tp_send.at[ahead - 1], tp_recv.at[line.me], {"tp": (line.me + ahead) % size})
 
     def tell_fsdp(ahead):
         return remote(gains, gains_fsdp.at[shard], fsdp_send.at[ahead - 1], fsdp_recv.at[shard], {"fsdp": (shard + ahead) % shards})
 
+    loads.start()
     fetch(0).start()
     for ahead in range(1, size):
         hello({"tp": (line.me + ahead) % size})
     for ahead in range(1, shards):
         hello({"fsdp": (shard + ahead) % shards})
     pl.semaphore_wait(pltpu.get_barrier_semaphore(), size - 1 + shards - 1)
-    for turn in range(shards - 1):
-        hand(turn).start()
+    down.start()
+    loads.wait(0, 1)
 
     def weights(turn, carry):
         @pl.when(turn < shards - 1)
@@ -1025,6 +1104,14 @@
             lax.fori_loop(0, depth // 512, tile, 0)
             scatter.share(index).start()
 
+        @pl.when(index == 1)
+        def _():
+            down.start_plain()
+
+        @pl.when(index == 2)
+        def _():
+            down.join()
+
         def phase(which, carry):
             done = jnp.maximum(index - 1, 0)
             late = line.fed(line.target(done))
@@ -1052,11 +1139,15 @@
         input_part[here, :] = part
         gains[0:1, :] += grad
 
+    loads.wait(2)
     by_rows(rows, norm)
 
     gains_tp[line.me] = gains[...]
     for ahead in range(1, size):
         tell_tp(ahead).start()
+    for turn in range(shards - 1):
+        give(turn).wait_recv()
+        grad_qkv[...] += qkv_from[turn].astype(jnp.float32)
     for ahead in range(1, size):
         source = (line.me + ahead) % size
         remote(gains, gains_tp.at[source], tp_send.at[0], tp_recv.at[source], {"tp": source}).wait_recv()
@@ -1079,12 +1170,8 @@
     for ahead in range(1, shards):
         tell_fsdp(ahead).wait_send()
     for turn in range(shards - 1):
-        give(turn).wait_recv()
-        grad_qkv[...] += qkv_from[turn].astype(jnp.float32)
-    for turn in range(shards - 1):
         give(turn).wait_send()
-        hand(turn).wait_recv()
-        hand(turn).wait_send()
+    down.finish()
     scatter.finish()
 
 
@@ -1097,28 +1184,28 @@
     shape = jax.ShapeDtypeStruct
     return pl.pallas_call(
         lambda *refs: spread_kernel(chips, shards, *refs),
-        in_specs=[VMEM] * 5 + [ANYWHERE] * 2,
+        in_specs=[VMEM] * 2 + [ANYWHERE] * 5,
         out_specs=[VMEM] * 3 + [ANYWHERE],
         out_shape=[
             shape((rows, depth), jnp.float32),
             shape((columns, 3 * width), jnp.float32),
             shape((2, depth), jnp.float32),
-            shape((shards - 1, grad_down.shape[0], columns), low),
+            shape((shards // 2, grad_down.shape[0], columns), low),
         ],
-        scratch_shapes=[
+        scratch_shapes=Loads.scratch(qkv_grad, weight, activations) + [
             pltpu.VMEM((2, group_rows, columns), low),
             pltpu.VMEM((shards - 1, columns, 3 * width), low),
             pltpu.VMEM((shards - 1, columns, 3 * width), low),
             pltpu.VMEM((2, depth), jnp.float32),
             pltpu.VMEM((size, 2, depth), jnp.float32),
             pltpu.VMEM((shards, 2, depth), jnp.float32),
-            DMA((2,)), DMA((shards - 1,)), DMA((shards - 1,)), DMA((shards - 1,)), DMA((shards - 1,)),
+            DMA((2,)), DMA((shards - 1,)), DMA((shards - 1,)),
             DMA((size - 1,)), DMA((size,)), DMA((shards - 1,)), DMA((shards,)),
-        ] + Scatter.scratch(chips, rows, depth),
+        ] + NearSums.scratch(shards, grad_down.shape[0], columns) + Scatter.scratch(chips, rows, depth),
         compiler_params=pltpu.CompilerParams(collective_id=5, has_side_effects=True, vmem_limit_bytes=63 << 20),
         cost_estimate=pl.CostEstimate(flops=1 << 20, bytes_accessed=1 << 20, transcendentals=0),
         name="spread",
-    )(qkv_grad, weight, activations, gain, gain_part, attn_tokens, grad_down)
+    )(gain, gain_part, qkv_grad, weight, activations, attn_tokens, grad_down)
 
 
 def chip_at(place, chips):

time: 582 us -> 568 us (0.976)
  Pallas kernels: 579 us -> 564 us
    pallas_call x1, Pallas kernels: 118 us -> 107 us  [back(): pl.pallas_call(lambda *refs: back_kernel(chips, shards, *refs), in_specs=...]
where the time goes in v7:
time: 568 us; the launch traced here: 567 us
  Pallas kernels  564 us (99%)
    pallas_call x1, Pallas kernels, feed(): pl.pallas_call(lambda *refs: feed_kernel(chips, shards, *refs), in_specs=...  157 us
    pallas_call x1, Pallas kernels, back(): pl.pallas_call(lambda *refs: back_kernel(chips, shards, *refs), in_specs=...  107 us
    pallas_call x1, Pallas kernels, attend(): pl.pallas_call(lambda *refs: attend_kernel(chips, shards, *refs), in_spec...  102 us
    pallas_call x1, Pallas kernels, spread(): pl.pallas_call(lambda *refs: spread_kernel(chips, shards, *refs), in_spec...  96.7 us
    pallas_call x1, Pallas kernels, project(): pl.pallas_call(lambda *refs: project_kernel(chips, shards, *refs), in_spe...  88.4 us
    pallas_call x1, Pallas kernels, finish(): pl.pallas_call(finish_kernel, grid_spec=pltpu.PrefetchScalarGridSpec(num_...  12.6 us

profile of v7, /device:TPU:0, one launch (start us, length us, event | category | flops | bytes accessed | tf_op | source)
XLA Modules:
  0.0 566.9 jit_solution(13396593310096203294)
XLA Ops:
  0.7 1.8 multiply_sine_fusion
  2.5 88.4 %project.1 = (bf16[2048,2048]{1,0:T(8,128)(2,1)}, bf16[2048,768]{1,0:T(8,128)(2,1)}, bf16[256,2048]{1,0:T(8,128)(2,1)}, bf16[2048,768]{1,0:T(8,128)(2,1)}, bf16[...) custom-call(f32[256,2048]{1,0:T(8,128)} %refs_4_.3, ...), custom_call_target="tpu_custom_call" | custom-call | flops 6442450944 | bytes 16777216 | tf_op jit(solution)/shard_map/project/pallas_call | solution.py:611
  90.9 101.6 %attend.1 = (f32[256,2048]{1,0:T(8,128)}, bf16[256,2048]{1,0:T(8,128)(2,1)}, bf16[2048,256]{1,0:T(8,128)(2,1)}, f32[4,2048]{1,0:T(4,128)}, bf16[2048,2048]{1,0:T...) custom-call(f32[256,2048]{1,0:T(8,128)} %refs_2_.3, ...), custom_call_target="tpu_custom_call" | custom-call | flops 4294967296 | bytes 16777216 | tf_op jit(solution)/shard_map/attend/pallas_call | solution.py:754
  192.5 157.0 %feed.1 = (f32[256,2048]{1,0:T(8,128)}, bf16[256,2048]{1,0:T(8,128)(2,1)}, f32[1,2048]{1,0:T(1,128)}, bf16[2048,1024]{1,0:T(8,128)(2,1)}, bf16[2048,2048]{1,0:T(8,128)(2,1)}, /*index=5*/bf16[2048,2048]{1,0:T(8,128)(2,1)}) custom-call(f32[1,2048]{1,0:T(1,128)} %bitcast.10, f32[256,2048]{1,0:T(8,128)} %get-tuple-element.56.refs_1_.hidden, ...), custom_call_target="tpu_custom_call" | custom-call | flops 68719476736 | bytes 41943040 | tf_op jit(solution)/shard_map/feed/pallas_call | solution.py:1465
  349.5 107.4 %back.1 = (f32[256,2048]{1,0:T(8,128)}, bf16[2048,2048]{1,0:T(8,128)(2,1)}, bf16[2048,768]{1,0:T(8,128)(2,1)}, bf16[1024,2048]{1,0:T(8,128)(2,1)}, f32[256,512]{1,0:T(8,128)}, /*index=5*/bf16[2,512,2048]{2,1,0:T(8,128)(2,1)}) custom-call(bf16[256,2048]{1,0:T(8,128)(2,1)} %get-tuple-element.62.refs_0_, bf16[2048,2048]{1,0:T(8,128)(2,1)} %get-tuple-element.63.refs_1_, ...), custom_call_target="tpu_custom_call" | custom-call | flops 1048576 | bytes 1048576 | tf_op jit(solution)/shard_map/back/pallas_call | solution.py:995
  456.9 96.7 %spread.1 = (f32[256,2048]{1,0:T(8,128)}, f32[512,768]{1,0:T(8,128)}, f32[2,2048]{1,0:T(2,128)}, bf16[2,1024,512]{2,1,0:T(8,128)(2,1)}) custom-call(f32[1,2048]{1,0:T(1,128)} %bitcast.6, f32[1,2048]{1,0:T(1,128)} %get-tuple-element.73.refs_1_, bf16[2048,768]{1,0:T(8,128)(2,1)} %get-tuple-element.74.refs_2_, bf16[2048,768]{1,0:T(8,128)(2,1)} %get-tuple-element.75.refs_3_, ...), custom_call_target="tpu_custom_call" | custom-call | flops 1048576 | bytes 1048576 | tf_op jit(solution)/shard_map/spread/pallas_call | solution.py:1185
  553.7 0.0 copy-start
  553.7 12.6 %finish.1 = (f32[256,2048]{1,0:T(8,128)}, f32[256,2048]{1,0:T(8,128)}, f32[512,256]{1,0:T(8,128)}, f32[512,256]{1,0:T(8,128)}, f32[512,256]{1,0:T(8,128)}, /*ind...) custom-call(s32[1]{0:T(128)} %bitcast.shard_ref, ...), custom_call_target="tpu_custom_call" | custom-call | tf_op jit(solution)/shard_map/finish/pallas_call | solution.py:1536
  566.3 0.0 copy-done
  566.3 0.6 fusion
  (2 shorter events, 0.0 us)
Async XLA Ops:
  553.7 12.6 %copy-start = (f32[2,2048]{1,0:T(2,128)S(1)}, f32[2,2048]{1,0:T(2,128)}, u32[]{:S(2)}) copy-start(f32[2,2048]{1,0:T(2,128)} %get-tuple-element.85) | copy-start | bytes 49156

commit v8 on v7

--- a/solution.py
+++ b/solution.py
@@ -49,7 +49,7 @@
         self.partner = 2 * self.chip + 1 - self.core
         self.has_left, self.has_right = self.chip > 0, self.chip < chips - 1
 
-    def greet(self, more=()):
+    def hello(self, more=()):
         hello({"tp": self.partner})
 
         @pl.when(self.has_left)
@@ -62,6 +62,8 @@
 
         for device in more:
             hello(device)
+
+    def ready(self, more=()):
         count = 1 + len(more) + jnp.where(self.has_left, 1, 0) + jnp.where(self.has_right, 1, 0)
         pl.semaphore_wait(pltpu.get_barrier_semaphore(), count)
 
@@ -80,66 +82,77 @@
 
 
 class Gather:
-    scratch = staticmethod(lambda chips: [DMA((2 * chips,)), DMA((chips,)), DMA((chips,)), DMA((chips,)), DMA])
-
-    def __init__(self, line, own, out, received, right, left, across, local):
-        self.line, self.own, self.out = line, own, out
+    @staticmethod
+    def scratch(chips, parts=1):
+        return [DMA((2 * chips, parts)), DMA((chips, parts)), DMA((chips, parts)), DMA((chips, parts)), DMA]
+
+    def __init__(self, line, own, out, received, right, left, across, local, parts=1):
+        self.line, self.out = line, out
         self.received, self.right, self.left, self.across, self.local = received, right, left, across, local
-        self.rows = own.shape[0]
-
-    def block(self, index):
-        return self.out.at[span(index, self.rows)]
-
-    def copy(self, source, sems, chip, device, mine):
+        self.parts = parts
+        self.rows = out.shape[0] // (2 * line.chips * parts)
+        self.held = own is None
+        self.own = out.at[span(line.me, self.rows * parts)] if self.held else own
+
+    def block(self, index, part):
+        return self.out.at[span(index * self.parts + part, self.rows)]
+
+    def mine(self, part):
+        return self.own.at[pl.ds(part * self.rows, self.rows)]
+
+    def copy(self, sems, chip, part, device, mine):
         index = 2 * chip + self.line.core
-        return remote(source if mine else self.block(index), self.block(index), sems.at[chip], self.received.at[index], {"tp": device})
+        source = self.mine(part) if mine else self.block(index, part)
+        return remote(source, self.block(index, part), sems.at[chip, part], self.received.at[index, part], {"tp": device})
 
     def keep(self):
-        return pltpu.make_async_copy(self.own, self.block(self.line.me), self.local)
+        return pltpu.make_async_copy(self.own, self.out.at[span(self.line.me, self.rows * self.parts)], self.local)
 
     def start(self):
         line = self.line
-        self.keep().start()
-
-        @pl.when(line.has_right)
-        def _():
-            self.copy(self.own, self.right, line.chip, line.me + 2, True).start()
-
-        @pl.when(line.has_left)
-        def _():
-            self.copy(self.own, self.left, line.chip, line.me - 2, True).start()
-
-        self.copy(self.own, self.across, line.chip, line.partner, True).start()
-
-    def arrive(self, index):
-        remote(self.own, self.block(index), self.right.at[0], self.received.at[index], {"tp": self.line.partner}).wait_recv()
+        if not self.held:
+            self.keep().start()
+        for part in range(self.parts):
+            @pl.when(line.has_right)
+            def _():
+                self.copy(self.right, line.chip, part, line.me + 2, True).start()
+
+            @pl.when(line.has_left)
+            def _():
+                self.copy(self.left, line.chip, part, line.me - 2, True).start()
+
+            self.copy(self.across, line.chip, part, line.partner, True).start()
+
+    def arrive(self, index, part):
+        remote(self.mine(part), self.block(index, part), self.right.at[0, part], self.received.at[index, part], {"tp": self.line.partner}).wait_recv()
 
     def arrive_across(self, chip):
-        self.arrive(2 * chip + 1 - self.line.core)
+        for part in range(self.parts):
+            self.arrive(2 * chip + 1 - self.line.core, part)
 
     def step(self, distance):
         line = self.line
         before, after = line.chip - distance, line.chip + distance
-
-        @pl.when(before >= 0)
-        def _():
-            self.arrive(2 * before + line.core)
-
-            @pl.when(line.has_right)
-            def _():
-                self.copy(None, self.right, before, line.me + 2, False).start()
-
-            self.copy(None, self.across, before, line.partner, False).start()
-
-        @pl.when(after < line.chips)
-        def _():
-            self.arrive(2 * after + line.core)
-
-            @pl.when(line.has_left)
-            def _():
-                self.copy(None, self.left, after, line.me - 2, False).start()
-
-            self.copy(None, self.across, after, line.partner, False).start()
+        for part in range(self.parts):
+            @pl.when(before >= 0)
+            def _():
+                self.arrive(2 * before + line.core, part)
+
+                @pl.when(line.has_right)
+                def _():
+                    self.copy(self.right, before, part, line.me + 2, False).start()
+
+                self.copy(self.across, before, part, line.partner, False).start()
+
+            @pl.when(after < line.chips)
+            def _():
+                self.arrive(2 * after + line.core, part)
+
+                @pl.when(line.has_left)
+                def _():
+                    self.copy(self.left, after, part, line.me - 2, False).start()
+
+                self.copy(self.across, after, part, line.partner, False).start()
 
     def finish(self, arrivals):
         line = self.line
@@ -148,15 +161,16 @@
         for chip in range(line.chips):
             if arrivals:
                 self.arrive_across(chip)
-            self.copy(self.own, self.across, chip, line.partner, True).wait_send()
-
-            @pl.when(jnp.logical_and(line.has_right, chip <= line.chip))
-            def _():
-                self.copy(self.own, self.right, chip, line.me + 2, True).wait_send()
-
-            @pl.when(jnp.logical_and(line.has_left, chip >= line.chip))
-            def _():
-                self.copy(self.own, self.left, chip, line.me - 2, True).wait_send()
+            for part in range(self.parts):
+                self.copy(self.across, chip, part, line.partner, True).wait_send()
+
+                @pl.when(jnp.logical_and(line.has_right, chip <= line.chip))
+                def _():
+                    self.copy(self.right, chip, part, line.me + 2, True).wait_send()
+
+                @pl.when(jnp.logical_and(line.has_left, chip >= line.chip))
+                def _():
+                    self.copy(self.left, chip, part, line.me - 2, True).wait_send()
 
 
 class Scatter:
@@ -476,18 +490,17 @@
 
 def project_kernel(
     chips, shards,
-    activations, gain, w_query, w_key, w_value, w_out, cosine_t, sine_t, w_down,
+    gain, cosine_t, sine_t, activations_hbm, w_query, w_key, w_value, w_out, w_down,
     tokens_out, weight_out, full_out, qkv_out, keys_out, values_out, cosine_out, sine_out, down_near,
-    weight, out_w, qkv, keys_t, values_t, cosine, sine, tokens, chunks,
-    chunk_sem, weight_send, weight_recv, weight_keep, table_sem, store_sem, near_send, near_recv, *gather_sems,
+    weight, out_w, qkv, keys_t, values_t, cosine, sine, tokens, activations,
+    load_sem, weight_send, weight_recv, weight_keep, table_sem, store_sem, near_send, near_recv, *gather_sems,
 ):
     line = Line(chips)
-    rows = tokens.shape[0]
-    pair = 2 * rows
+    rows = activations.shape[0]
     depth, width = w_query.shape
     grid = Grid(shards)
     shard, others = grid.me, grid.others
-    gather = Gather(line, tokens, tokens_out, *gather_sems)
+    gather = Gather(line, None, tokens, *gather_sems, parts=2)
     down = NearShards(grid, w_down, down_near, column_shard(*w_down.shape), near_send, near_recv)
     parts = (w_query, w_key, w_value, w_out)
 
@@ -507,19 +520,26 @@
         for i, (source, out) in enumerate(((cosine, cosine_out), (sine, sine_out), (weight, weight_out), (out_w, full_out)))
     ]
 
-    def stores(chip):
-        here = span(chip, pair)
+    def stores(index):
+        here = span(index, rows)
         return [
-            pltpu.make_async_copy(qkv.at[here], qkv_out.at[here], store_sem.at[0, chip]),
-            pltpu.make_async_copy(keys_t.at[:, here], keys_out.at[:, here], store_sem.at[1, chip]),
-            pltpu.make_async_copy(values_t.at[:, here], values_out.at[:, here], store_sem.at[2, chip]),
+            pltpu.make_async_copy(qkv.at[here], qkv_out.at[here], store_sem.at[0, index]),
+            pltpu.make_async_copy(keys_t.at[:, here], keys_out.at[:, here], store_sem.at[1, index]),
+            pltpu.make_async_copy(values_t.at[:, here], values_out.at[:, here], store_sem.at[2, index]),
+            pltpu.make_async_copy(tokens.at[here], tokens_out.at[here], store_sem.at[3, index]),
         ]
 
-    def norm(here):
-        tokens[here, :] = normed(activations[here, :], gain[...]).astype(low)
-
-    by_rows(rows, norm)
-    line.greet([{"fsdp": other} for other in others])
+    def norm(index, carry):
+        there = span(line.me * (rows // NORM_ROWS) + index, NORM_ROWS)
+        tokens[there, :] = normed(activations[span(index, NORM_ROWS), :], gain[...]).astype(low)
+        return carry
+
+    load = pltpu.make_async_copy(activations_hbm, activations, load_sem)
+    load.start()
+    line.hello([{"fsdp": other} for other in others])
+    load.wait()
+    lax.fori_loop(0, rows // NORM_ROWS, norm, 0)
+    line.ready(others)
     gather.start()
     for part in range(4):
         keep(part).start()
@@ -531,25 +551,19 @@
     for copy in tables[:2]:
         copy.start()
 
-    def project(chip):
-        @pl.when(jnp.logical_and(chip >= 0, chip < chips))
-        def _():
-            gather.arrive_across(chip)
-            load = pltpu.make_async_copy(tokens_out.at[span(chip, pair)], chunks, chunk_sem)
-            load.start()
-            load.wait()
-            here = span(chip, pair)
-            table = span(chip % (SEQ_LEN // pair), pair)
-            for part in range(3):
-                columns = pl.ds(part * width, width)
-                block = dot(chunks[...], weight[:, columns])
-                if part < 2:
-                    block = block * widened(cosine[table, :], width) + turned(block, 1.0) * widened(sine[table, :], width)
-                qkv[here, columns] = block.astype(low)
-                if part:
-                    (keys_t, values_t)[part - 1][:, here] = block.T.astype(low)
-            for copy in stores(chip):
-                copy.start()
+    def project(index):
+        here = span(index, rows)
+        table = span(index % (SEQ_LEN // rows), rows)
+        for part in range(3):
+            columns = pl.ds(part * width, width)
+            block = dot(tokens[here, :], weight[:, columns])
+            if part < 2:
+                block = block * widened(cosine[table, :], width) + turned(block, 1.0) * widened(sine[table, :], width)
+            qkv[here, columns] = block.astype(low)
+            if part:
+                (keys_t, values_t)[part - 1][:, here] = block.T.astype(low)
+        for copy in stores(index):
+            copy.start()
 
     def step(index, carry):
         @pl.when(jnp.logical_and(index >= 1, index < chips))
@@ -558,7 +572,6 @@
 
         @pl.when(index == 2)
         def _():
-            gather.keep().wait()
             for part in range(4):
                 keep(part).wait()
                 for ahead in range(shards - 1):
@@ -567,17 +580,22 @@
                 copy.start()
             down.start()
 
-        def side(which, carry):
-            distance = index - 1
+        def side(turn, carry):
+            distance, which, across = index - 1, turn % 3, turn // 3
             chip = jnp.where(which == 0, line.chip - distance, jnp.where(which == 1, line.chip + distance, line.chip))
-
-            @pl.when(jnp.logical_and(index >= 2, jnp.logical_or(which < 2, index == 2)))
-            def _():
-                project(chip)
+            there = jnp.logical_and(chip >= 0, chip < chips)
+
+            @pl.when(jnp.logical_and(there, jnp.logical_and(index >= 2, jnp.logical_or(which < 2, index == 2))))
+            def _():
+                @pl.when(across == 1)
+                def _():
+                    gather.arrive_across(chip)
+
+                project(2 * chip + jnp.where(across == 1, 1 - line.core, line.core))
 
             return carry
 
-        lax.fori_loop(0, 3, side, 0)
+        lax.fori_loop(0, 6, side, 0)
         return carry
 
     lax.fori_loop(0, chips + 1, step, 0)
@@ -587,8 +605,8 @@
             give(ahead, part).wait_send()
     for copy in tables:
         copy.wait()
-    for chip in range(chips):
-        for copy in stores(chip):
+    for index in range(2 * chips):
+        for copy in stores(index):
             copy.wait()
     down.arrive()
     down.finish()
@@ -610,18 +628,18 @@
     ]
     return pl.pallas_call(
         lambda *refs: project_kernel(chips, shards, *refs),
-        in_specs=[VMEM] * 8 + [ANYWHERE],
+        in_specs=[VMEM] * 3 + [ANYWHERE] * 6,
         out_specs=[ANYWHERE] * 9,
         out_shape=[shape((group_rows, depth), low)] + held + [shape((w_down.shape[0], depth), low)],
         scratch_shapes=[pltpu.VMEM(a.shape, a.dtype) for a in held] + [
-            pltpu.VMEM((rows, depth), low),
-            pltpu.VMEM((2 * rows, depth), low),
-            DMA, DMA((shards - 1, 4)), DMA((shards - 1, 4)), DMA((4,)), DMA((4,)), DMA((3, chips)),
-        ] + NearShards.scratch(shards) + Gather.scratch(chips),
+            pltpu.VMEM((group_rows, depth), low),
+            pltpu.VMEM((rows, depth), jnp.float32),
+            DMA, DMA((shards - 1, 4)), DMA((shards - 1, 4)), DMA((4,)), DMA((4,)), DMA((4, 2 * chips)),
+        ] + NearShards.scratch(shards) + Gather.scratch(chips, 2),
         compiler_params=pltpu.CompilerParams(collective_id=1, has_side_effects=True, vmem_limit_bytes=63 << 20),
         cost_estimate=pl.CostEstimate(flops=6 * group_rows * depth * width, bytes_accessed=4 * group_rows * depth, transcendentals=0),
         name="project",
-    )(activations, gain, w_query, w_key, w_value, w_out, cosine_t, sine_t, w_down)
+    )(gain, cosine_t, sine_t, activations, w_query, w_key, w_value, w_out, w_down)
 
 
 def attend_chunk(chunk, rows, qkv, values_t, heads_ref, acc, out, top_ref, sum_ref):
@@ -659,31 +677,33 @@
 
 def attend_kernel(
     chips, shards,
-    cotangent, gain, *refs,
+    gain, *refs,
 ):
-    sources, (w_gate, w_up, down_near) = refs[:4], refs[4:7]
-    hidden, tokens, mixed, totals, grads_out, gate_all, up_all, down_far = refs[7:15]
-    loads = Loads(sources, refs[15:20])
-    qkv, values_t, w_out, activations = loads.refs
-    heads_ref, acc, out, top_ref, sum_ref, grads = refs[20:26]
+    sources, (w_gate, w_up, down_near) = refs[:5], refs[5:8]
+    hidden, tokens, mixed, totals, grads_out, gate_all, up_all, down_far = refs[8:16]
+    loads = Loads(sources, refs[16:22])
+    cotangent, qkv, values_t, w_out, activations = loads.refs
+    heads_ref, acc, out, top_ref, sum_ref, grads = refs[22:28]
+    loads.start()
+    line = Line(chips)
     grid = Grid(shards)
     rows_of = row_shard(w_gate.shape[0])
-    down = FarShards(grid, down_near, down_far, column_shard(down_near.shape[0], down_near.shape[1] // shards), *refs[26:28])
-    gate_near, gate_far = NearShards(grid, w_gate, gate_all, rows_of, *refs[28:30]), FarShards(grid, gate_all, gate_all, rows_of, *refs[30:32])
-    up_near, up_far = NearShards(grid, w_up, up_all, rows_of, *refs[32:34]), FarShards(grid, up_all, up_all, rows_of, *refs[34:36])
-    sems = refs[36:]
-    loads.start()
-    line = Line(chips)
+    line.hello([{"fsdp": peer} for peer in grid.near])
+    down = FarShards(grid, down_near, down_far, column_shard(down_near.shape[0], down_near.shape[1] // shards), *refs[28:30])
+    gate_near, gate_far = NearShards(grid, w_gate, gate_all, rows_of, *refs[30:32]), FarShards(grid, gate_all, gate_all, rows_of, *refs[32:34])
+    up_near, up_far = NearShards(grid, w_up, up_all, rows_of, *refs[34:36]), FarShards(grid, up_all, up_all, rows_of, *refs[36:38])
+    sems = refs[38:]
     rows, depth = hidden.shape
     pair = 2 * rows
     scatter = Scatter(line, hidden, *sems[:8])
+    loads.wait(0)
     grads[...] = cotangent[...].astype(low)
     gather = Gather(line, grads, grads_out, *sems[8:])
-    line.greet([{"fsdp": peer} for peer in grid.near])
+    line.ready(grid.near)
     gather.start()
     gate_near.start()
     down.start()
-    loads.wait(0, 1, 2, 3)
+    loads.wait(1, 2, 3, 4)
 
     def step(index, carry):
         work = jnp.where(index == chips, chips - 1, index)
@@ -753,7 +773,7 @@
     shape = jax.ShapeDtypeStruct
     return pl.pallas_call(
         lambda *refs: attend_kernel(chips, shards, *refs),
-        in_specs=[VMEM] * 2 + [ANYWHERE] * 7,
+        in_specs=[VMEM] + [ANYWHERE] * 8,
         out_specs=[VMEM] * 4 + [ANYWHERE] * 4,
         out_shape=[
             shape((rows, depth), jnp.float32),
@@ -765,7 +785,7 @@
             shape((depth, w_gate.shape[1]), low),
             shape(down_near.shape, low),
         ],
-        scratch_shapes=Loads.scratch(qkv, values_t, w_out, activations) + [
+        scratch_shapes=Loads.scratch(cotangent, qkv, values_t, w_out, activations) + [
             pltpu.VMEM((heads, pair, width), low),
             pltpu.VMEM((width, pair), jnp.float32),
             pltpu.VMEM((pair, width), low),
@@ -776,7 +796,7 @@
         compiler_params=pltpu.CompilerParams(collective_id=2, has_side_effects=True, vmem_limit_bytes=63 << 20),
         cost_estimate=pl.CostEstimate(flops=2 * group_rows * (SEQ_LEN + depth) * width, bytes_accessed=4 * group_rows * depth, transcendentals=group_rows * SEQ_LEN * heads // 2),
         name="attend",
-    )(cotangent, gain, qkv, values_t, w_out, activations, w_gate, w_up, down_near)
+    )(gain, cotangent, qkv, values_t, w_out, activations, w_gate, w_up, down_near)
 
 
 def back_chunk(chunk, rows, grad, qkv, keys_t, mixed, totals, dkey, dvalue, heads_ref, grads_ref, acc, inner_ref):
@@ -850,11 +870,12 @@
     def keep_tile(place):
         return pltpu.make_async_copy(down_tile, grad_down.at[span(place, 256)], tile_sem)
 
+    line.hello([{"fsdp": other} for other in others])
     loads.start()
     fetch(0).start()
     fetch_grad(0).start()
     scatter.load(0).start()
-    line.greet([{"fsdp": other} for other in others])
+    line.ready(others)
     gather.start()
     both.start()
     out_sum[...] = jnp.zeros_like(out_sum)
@@ -1061,15 +1082,15 @@
     def tell_fsdp(ahead):
         return remote(gains, gains_fsdp.at[shard], fsdp_send.at[ahead - 1], fsdp_recv.at[shard], {"fsdp": (shard + ahead) % shards})
 
-    loads.start()
-    fetch(0).start()
     for ahead in range(1, size):
         hello({"tp": (line.me + ahead) % size})
     for ahead in range(1, shards):
         hello({"fsdp": (shard + ahead) % shards})
+    loads.start()
+    fetch(0).start()
+    loads.wait(0, 1)
     pl.semaphore_wait(pltpu.get_barrier_semaphore(), size - 1 + shards - 1)
     down.start()
-    loads.wait(0, 1)
 
     def weights(turn, carry):
         @pl.when(turn < shards - 1)
@@ -1311,12 +1332,12 @@
     def pass_on(slot):
         return remote(total.at[slot % 2], from_ring.at[slot - 1], total_send.at[slot % 2], total_recv.at[slot - 1], following)
 
+    for device in (following, before, partner):
+        hello(device)
     own.start()
     fetch(0).start()
     load_weights()
     own.wait()
-    for device in (following, before, partner):
-        hello(device)
     pl.semaphore_wait(pltpu.get_barrier_semaphore(), 3)
 
     def step(slot, carry):

time: 568 us -> 562 us (0.989)
  Pallas kernels: 564 us -> 558 us
    pallas_call x1, Pallas kernels: 107 us -> 116 us  [back(): pl.pallas_call(lambda *refs: back_kernel(chips, shards, *refs), in_specs=...]
    pallas_call x1, Pallas kernels: 88.4 us -> 81.7 us  [project(): pl.pallas_call(lambda *refs: project_kernel(chips, shards, *refs), in_spe...]
where the time goes in v8:
time: 562 us; the launch traced here: 561 us
  Pallas kernels  558 us (99%)
    pallas_call x1, Pallas kernels, feed(): pl.pallas_call(lambda *refs: feed_kernel(chips, shards, *refs), in_specs=...  151 us
    pallas_call x1, Pallas kernels, back(): pl.pallas_call(lambda *refs: back_kernel(chips, shards, *refs), in_specs=...  116 us
    pallas_call x1, Pallas kernels, attend(): pl.pallas_call(lambda *refs: attend_kernel(chips, shards, *refs), in_spec...  101 us
    pallas_call x1, Pallas kernels, spread(): pl.pallas_call(lambda *refs: spread_kernel(chips, shards, *refs), in_spec...  95.7 us
    pallas_call x1, Pallas kernels, project(): pl.pallas_call(lambda *refs: project_kernel(chips, shards, *refs), in_spe...  81.7 us
    pallas_call x1, Pallas kernels, finish(): pl.pallas_call(finish_kernel, grid_spec=pltpu.PrefetchScalarGridSpec(num_...  12.6 us

profile of v8, /device:TPU:0, one launch (start us, length us, event | category | flops | bytes accessed | tf_op | source)
XLA Modules:
  0.0 561.2 jit_solution(4670685305686864532)
XLA Ops:
  0.7 1.8 multiply_sine_fusion
  2.5 81.7 %project.1 = (bf16[2048,2048]{1,0:T(8,128)(2,1)}, bf16[2048,768]{1,0:T(8,128)(2,1)}, bf16[256,2048]{1,0:T(8,128)(2,1)}, bf16[2048,768]{1,0:T(8,128)(2,1)}, bf16[...) custom-call(f32[1,2048]{1,0:T(1,128)} %bitcast.5, ...), custom_call_target="tpu_custom_call" | custom-call | flops 6442450944 | bytes 16777216 | tf_op jit(solution)/shard_map/project/pallas_call | solution.py:629
  84.2 100.9 %attend.1 = (f32[256,2048]{1,0:T(8,128)}, bf16[256,2048]{1,0:T(8,128)(2,1)}, bf16[2048,256]{1,0:T(8,128)(2,1)}, f32[4,2048]{1,0:T(4,128)}, bf16[2048,2048]{1,0:T...) custom-call(f32[1,2048]{1,0:T(1,128)} %bitcast.9, ...), custom_call_target="tpu_custom_call" | custom-call | flops 4294967296 | bytes 16777216 | tf_op jit(solution)/shard_map/attend/pallas_call | solution.py:774
  185.1 151.3 %feed.1 = (f32[256,2048]{1,0:T(8,128)}, bf16[256,2048]{1,0:T(8,128)(2,1)}, f32[1,2048]{1,0:T(1,128)}, bf16[2048,1024]{1,0:T(8,128)(2,1)}, bf16[2048,2048]{1,0:T(8,128)(2,1)}, /*index=5*/bf16[2048,2048]{1,0:T(8,128)(2,1)}) custom-call(f32[1,2048]{1,0:T(1,128)} %bitcast.10, f32[256,2048]{1,0:T(8,128)} %get-tuple-element.56.refs_1_.hidden, ...), custom_call_target="tpu_custom_call" | custom-call | flops 68719476736 | bytes 41943040 | tf_op jit(solution)/shard_map/feed/pallas_call | solution.py:1486
  336.4 115.8 %back.1 = (f32[256,2048]{1,0:T(8,128)}, bf16[2048,2048]{1,0:T(8,128)(2,1)}, bf16[2048,768]{1,0:T(8,128)(2,1)}, bf16[1024,2048]{1,0:T(8,128)(2,1)}, f32[256,512]{1,0:T(8,128)}, /*index=5*/bf16[2,512,2048]{2,1,0:T(8,128)(2,1)}) custom-call(bf16[256,2048]{1,0:T(8,128)(2,1)} %get-tuple-element.62.refs_0_, bf16[2048,2048]{1,0:T(8,128)(2,1)} %get-tuple-element.63.refs_1_, ...), custom_call_target="tpu_custom_call" | custom-call | flops 1048576 | bytes 1048576 | tf_op jit(solution)/shard_map/back/pallas_call | solution.py:1016
  452.3 95.7 %spread.1 = (f32[256,2048]{1,0:T(8,128)}, f32[512,768]{1,0:T(8,128)}, f32[2,2048]{1,0:T(2,128)}, bf16[2,1024,512]{2,1,0:T(8,128)(2,1)}) custom-call(f32[1,2048]{1,0:T(1,128)} %bitcast.6, f32[1,2048]{1,0:T(1,128)} %get-tuple-element.73.refs_1_, bf16[2048,768]{1,0:T(8,128)(2,1)} %get-tuple-element.74.refs_2_, bf16[2048,768]{1,0:T(8,128)(2,1)} %get-tuple-element.75.refs_3_, ...), custom_call_target="tpu_custom_call" | custom-call | flops 1048576 | bytes 1048576 | tf_op jit(solution)/shard_map/spread/pallas_call | solution.py:1206
  548.0 0.0 copy-start
  548.0 12.6 %finish.1 = (f32[256,2048]{1,0:T(8,128)}, f32[256,2048]{1,0:T(8,128)}, f32[512,256]{1,0:T(8,128)}, f32[512,256]{1,0:T(8,128)}, f32[512,256]{1,0:T(8,128)}, /*ind...) custom-call(s32[1]{0:T(128)} %bitcast.shard_ref, ...), custom_call_target="tpu_custom_call" | custom-call | tf_op jit(solution)/shard_map/finish/pallas_call | solution.py:1557
  560.6 0.0 copy-done
  560.6 0.6 fusion
  (2 shorter events, 0.0 us)
Async XLA Ops:
  548.0 12.6 %copy-start = (f32[2,2048]{1,0:T(2,128)S(1)}, f32[2,2048]{1,0:T(2,128)}, u32[]{:S(2)}) copy-start(f32[2,2048]{1,0:T(2,128)} %get-tuple-element.85) | copy-start | bytes 49156

commit v9 on v8

--- a/solution.py
+++ b/solution.py
@@ -1,5 +1,6 @@
 import jax
 import jax.numpy as jnp
+import numpy as np
 from jax import lax
 from jax.experimental import pallas as pl
 from jax.experimental.pallas import tpu as pltpu
@@ -176,13 +177,13 @@
 class Scatter:
     @staticmethod
     def scratch(chips, rows, depth):
-        shares = min(chips, 4)
+        slots = chips // 2 + 1
         return [
-            pltpu.VMEM((2, 2 * rows, depth), low),
-            pltpu.VMEM((shares, rows, depth), low),
+            pltpu.VMEM((slots, 2 * rows, depth), low),
+            pltpu.VMEM((chips, rows, depth), low),
             pltpu.VMEM((chips + 1, rows, depth), low),
             pltpu.VMEM((2, rows, depth), low),
-            DMA((2,)), DMA((shares,)), DMA((2,)), DMA((chips + 1,)),
+            DMA((slots,)), DMA((chips,)), DMA((2,)), DMA((chips + 1,)),
         ]
 
     def __init__(self, line, out, term, shares, lines, total, share_send, share_recv, line_send, line_recv):
@@ -190,14 +191,29 @@
         self.term, self.shares, self.lines, self.total = term, shares, lines, total
         self.share_send, self.share_recv, self.line_send, self.line_recv = share_send, share_recv, line_send, line_recv
         self.rows = out.shape[0]
+        self.slots = term.shape[0]
 
     def share(self, step):
-        slot = step % self.shares.shape[0]
-        source = self.term.at[step % 2, span(1 - self.line.core, self.rows)]
-        return remote(source, self.shares.at[slot], self.share_send.at[step % 2], self.share_recv.at[slot], {"tp": self.line.partner})
+        slot = step % self.slots
+        source = self.term.at[slot, span(1 - self.line.core, self.rows)]
+        return remote(source, self.shares.at[step], self.share_send.at[slot], self.share_recv.at[step], {"tp": self.line.partner})
+
+    def due(self, index, fed):
+        def one(step, carry):
+            target = self.line.target(step)
+            distance = jnp.where(target > self.line.chip, target - self.line.chip, self.line.chip - target)
+            turn = True if fed is None else self.line.fed(target) == fed
+
+            @pl.when(jnp.logical_and(distance == self.line.chips - index, turn))
+            def _():
+                self.step(step)
+
+            return carry
+
+        return one
 
     def mine(self, step):
-        return self.term[step % 2, span(self.line.core, self.rows), :]
+        return self.term[step % self.slots, span(self.line.core, self.rows), :]
 
     def pass_on(self, step):
         line, target = self.line, self.line.target(step)
@@ -211,14 +227,14 @@
         self.out[...] += self.lines[slot].astype(jnp.float32)
 
     def free(self, step):
-        @pl.when(step >= 2)
-        def _():
-            self.share(step - 2).wait_send()
+        @pl.when(step >= self.slots)
+        def _():
+            self.share(step - self.slots).wait_send()
 
     def step(self, step):
         line, target = self.line, self.line.target(step)
         self.share(step).wait_recv()
-        self.out[...] = self.mine(step).astype(jnp.float32) + self.shares[step % self.shares.shape[0]].astype(jnp.float32)
+        self.out[...] = self.mine(step).astype(jnp.float32) + self.shares[step].astype(jnp.float32)
 
         @pl.when(jnp.logical_and(target >= line.chip, line.has_left))
         def _():
@@ -241,7 +257,7 @@
         chips = self.line.chips
         for step in range(max(0, chips - 3), chips - 1):
             self.pass_on(step).wait_send()
-        for step in range(max(0, chips - 2), chips):
+        for step in range(max(0, chips - self.slots), chips):
             self.share(step).wait_send()
 
 
@@ -420,9 +436,8 @@
         return pltpu.make_async_copy(source, self.term.at[step % 2], self.load_sem.at[step % 2])
 
     def share(self, step):
-        slot = step % self.shares.shape[0]
         source = self.held.at[span(2 * self.line.target(step) + 1 - self.line.core, self.rows)]
-        return remote(source, self.shares.at[slot], self.share_send.at[step % 2], self.share_recv.at[slot], {"tp": self.line.partner})
+        return remote(source, self.shares.at[step], self.share_send.at[step % 2], self.share_recv.at[step], {"tp": self.line.partner})
 
     def mine(self, step):
         self.load(step).wait()
@@ -490,7 +505,7 @@
 
 def project_kernel(
     chips, shards,
-    gain, cosine_t, sine_t, activations_hbm, w_query, w_key, w_value, w_out, w_down,
+    gain, inverse, activations_hbm, w_query, w_key, w_value, w_out, w_down,
     tokens_out, weight_out, full_out, qkv_out, keys_out, values_out, cosine_out, sine_out, down_near,
     weight, out_w, qkv, keys_t, values_t, cosine, sine, tokens, activations,
     load_sem, weight_send, weight_recv, weight_keep, table_sem, store_sem, near_send, near_recv, *gather_sems,
@@ -545,8 +560,9 @@
         keep(part).start()
         for ahead in range(shards - 1):
             give(ahead, part).start()
-    for table, table_t in ((cosine, cosine_t), (sine, sine_t)):
-        turn = table_t[...].T
+    position = lax.broadcasted_iota(jnp.int32, (inverse.shape[0], SEQ_LEN), 1).astype(jnp.float32)
+    angle = position * inverse[...]
+    for table, turn in ((cosine, jnp.cos(angle).T), (sine, jnp.sin(angle).T)):
         table[...] = jnp.concatenate([turn] * (LANES // turn.shape[1]), axis=1)
     for copy in tables[:2]:
         copy.start()
@@ -612,7 +628,7 @@
     down.finish()
 
 
-def project(chips, shards, activations, gain, w_query, w_key, w_value, w_out, cosine_t, sine_t, w_down):
+def project(chips, shards, activations, gain, w_query, w_key, w_value, w_out, inverse, w_down):
     rows, depth = activations.shape
     group_rows = 2 * chips * rows
     width = w_query.shape[1]
@@ -628,7 +644,7 @@
     ]
     return pl.pallas_call(
         lambda *refs: project_kernel(chips, shards, *refs),
-        in_specs=[VMEM] * 3 + [ANYWHERE] * 6,
+        in_specs=[VMEM] * 2 + [ANYWHERE] * 6,
         out_specs=[ANYWHERE] * 9,
         out_shape=[shape((group_rows, depth), low)] + held + [shape((w_down.shape[0], depth), low)],
         scratch_shapes=[pltpu.VMEM(a.shape, a.dtype) for a in held] + [
@@ -639,7 +655,7 @@
         compiler_params=pltpu.CompilerParams(collective_id=1, has_side_effects=True, vmem_limit_bytes=63 << 20),
         cost_estimate=pl.CostEstimate(flops=6 * group_rows * depth * width, bytes_accessed=4 * group_rows * depth, transcendentals=0),
         name="project",
-    )(gain, cosine_t, sine_t, activations, w_query, w_key, w_value, w_out, w_down)
+    )(gain, inverse, activations, w_query, w_key, w_value, w_out, w_down)
 
 
 def attend_chunk(chunk, rows, qkv, values_t, heads_ref, acc, out, top_ref, sum_ref):
@@ -705,24 +721,31 @@
     down.start()
     loads.wait(1, 2, 3, 4)
 
+    def term(index):
+        chunk = line.target(index)
+        attend_chunk(chunk, pair, qkv, values_t, heads_ref, acc, out, top_ref, sum_ref)
+        mixed[span(chunk, pair), :] = out[...]
+        totals[:, span(chunk, pair)] = top_ref[...] + jnp.log(sum_ref[...])
+        scatter.free(index)
+
+        def tile(place, carry):
+            columns = span(place, 512)
+            scatter.term[index % scatter.slots, :, columns] = dot(out[...], w_out[:, columns]).astype(low)
+            return carry
+
+        lax.fori_loop(0, depth // 512, tile, 0)
+        scatter.share(index).start()
+
     def step(index, carry):
-        work = jnp.where(index == chips, chips - 1, index)
-
-        @pl.when(jnp.logical_or(index < chips - 1, index == chips))
-        def _():
-            chunk = line.target(work)
-            attend_chunk(chunk, pair, qkv, values_t, heads_ref, acc, out, top_ref, sum_ref)
-            mixed[span(chunk, pair), :] = out[...]
-            totals[:, span(chunk, pair)] = top_ref[...] + jnp.log(sum_ref[...])
-            scatter.free(work)
-
-            def tile(place, carry):
-                columns = span(place, 512)
-                scatter.term[work % 2, :, columns] = dot(out[...], w_out[:, columns]).astype(low)
-                return carry
-
-            lax.fori_loop(0, depth // 512, tile, 0)
-            scatter.share(work).start()
+        def phase(which, carry):
+            @pl.when(jnp.logical_and(which == 1, index < chips))
+            def _():
+                term(index)
+
+            lax.fori_loop(0, jnp.where(which == 1, 0, chips), scatter.due(index, which == 2), 0)
+            return carry
+
+        lax.fori_loop(0, 3, phase, 0)
 
         @pl.when(jnp.logical_and(index >= 1, index < chips))
         def _():
@@ -741,10 +764,6 @@
         def _():
             up_near.arrive()
             up_far.start()
-
-        @pl.when(index >= 1)
-        def _():
-            scatter.step(index - 1)
 
         return carry
 
@@ -923,17 +942,7 @@
                 give(turn).start()
             close()
 
-        def due(done, carry):
-            target = line.target(done)
-            distance = jnp.where(target > line.chip, target - line.chip, line.chip - target)
-
-            @pl.when(distance == chips - index)
-            def _():
-                scatter.step(done)
-
-            return carry
-
-        lax.fori_loop(0, chips, due, 0)
+        lax.fori_loop(0, chips, scatter.due(index, None), 0)
 
         @pl.when(jnp.logical_and(index >= 1, index < chips))
         def _():
@@ -1111,44 +1120,41 @@
 
         return carry
 
+    def term(index):
+        scatter.free(index)
+        here = span(line.target(index), pair)
+
+        def tile(place, carry):
+            there = span(place, 512)
+            scatter.term[index % scatter.slots, :, there] = dot(qkv_grad[here, :], weight[there, :], NT).astype(low)
+            return carry
+
+        lax.fori_loop(0, depth // 512, tile, 0)
+        scatter.share(index).start()
+
     def step(index, carry):
-        @pl.when(index < chips)
-        def _():
-            here = span(line.target(index), pair)
-            scatter.free(index)
-
-            def tile(place, carry):
-                there = span(place, 512)
-                scatter.term[index % 2, :, there] = dot(qkv_grad[here, :], weight[there, :], NT).astype(low)
-                return carry
-
-            lax.fori_loop(0, depth // 512, tile, 0)
-            scatter.share(index).start()
-
-        @pl.when(index == 1)
-        def _():
-            down.start_plain()
-
-        @pl.when(index == 2)
-        def _():
-            down.join()
-
         def phase(which, carry):
-            done = jnp.maximum(index - 1, 0)
-            late = line.fed(line.target(done))
-            turn = jnp.logical_or(jnp.logical_and(which == 0, jnp.logical_not(late)), jnp.logical_and(which == 2, late))
-
-            @pl.when(jnp.logical_and(index >= 1, turn))
-            def _():
-                scatter.step(done)
-
-            @pl.when(jnp.logical_and(which == 1, index < 2))
+            @pl.when(jnp.logical_and(which == 1, index < chips))
+            def _():
+                term(index)
+
+            @pl.when(jnp.logical_and(which == 2, index < 2))
             def _():
                 lax.fori_loop(index, jnp.where(index == 0, 1, shards), weights, 0)
 
+            @pl.when(jnp.logical_and(which == 2, index == 1))
+            def _():
+                down.start_plain()
+
+            @pl.when(jnp.logical_and(which == 2, index == 2))
+            def _():
+                down.join()
+
+            outer = jnp.logical_or(which == 0, which == 3)
+            lax.fori_loop(0, jnp.where(outer, chips, 0), scatter.due(index, which == 3), 0)
             return carry
 
-        lax.fori_loop(0, 3, phase, 0)
+        lax.fori_loop(0, 4, phase, 0)
         return carry
 
     lax.fori_loop(0, chips + 1, step, 0)
@@ -1573,13 +1579,9 @@
     )(shard.reshape(1), hidden, down, hidden_grad, input_part, both, both_from, grad_down, down_from, grad_qkv, grad_out)
 
 
-def rope_tables():
-    half = HEAD_DIM // 2
-    positions = jnp.arange(SEQ_LEN, dtype=jnp.int32).astype(jnp.float32)
-    column = jnp.arange(half, dtype=jnp.int32)
-    inverse = jnp.power(jnp.float32(rope_base), -2.0 * column.astype(jnp.float32) / HEAD_DIM)
-    angle = positions[None, :] * inverse[:, None]
-    return (jnp.cos(angle), jnp.sin(angle))
+def rope_frequencies():
+    column = np.arange(HEAD_DIM // 2)
+    return jnp.asarray((rope_base ** (-2.0 * column / HEAD_DIM)).astype(np.float32)[:, None])
 
 
 def make_body(mesh):
@@ -1588,7 +1590,7 @@
     def body(activations, gain_attn, w_query, w_key, w_value, w_out, gain_mlp, w_gate, w_up, w_down, cotangent):
         gain_attn, gain_mlp = gain_attn[None, :], gain_mlp[None, :]
         seen_attn, w_qkv, full_out, qkv, keys_t, values_t, cosine, sine, down_near = project(
-            chips, shards, activations, gain_attn, w_query, w_key, w_value, w_out, *rope_tables(), w_down
+            chips, shards, activations, gain_attn, w_query, w_key, w_value, w_out, rope_frequencies(), w_down
         )
         hidden_state, normed_mlp, mixed, totals, seen_grad, gate_all, up_all, down_far = attend(
             chips, shards, qkv, values_t, full_out, activations, cotangent, gain_mlp, w_gate, w_up, down_near

time: 562 us -> 546 us (0.972)
  Pallas kernels: 558 us -> 544 us
where the time goes in v9:
time: 546 us
  Pallas kernels  544 us (100%)
    pallas_call x1, Pallas kernels, feed(): pl.pallas_call(lambda *refs: feed_kernel(chips, shards, *refs), in_specs=...  146 us
    pallas_call x1, Pallas kernels, back(): pl.pallas_call(lambda *refs: back_kernel(chips, shards, *refs), in_specs=...  112 us
    pallas_call x1, Pallas kernels, attend(): pl.pallas_call(lambda *refs: attend_kernel(chips, shards, *refs), in_spec...  98.3 us
    pallas_call x1, Pallas kernels, spread(): pl.pallas_call(lambda *refs: spread_kernel(chips, shards, *refs), in_spec...  94.1 us
    pallas_call x1, Pallas kernels, project(): pl.pallas_call(lambda *refs: project_kernel(chips, shards, *refs), in_spe...  81.3 us
    pallas_call x1, Pallas kernels, finish(): pl.pallas_call(finish_kernel, grid_spec=pltpu.PrefetchScalarGridSpec(num_...  12.6 us

profile of v9, /device:TPU:0, one launch (start us, length us, event | category | flops | bytes accessed | tf_op | source)
XLA Modules:
  0.0 545.7 jit_solution(4641989855615949088)
XLA Ops:
  0.6 81.3 %project.1 = (bf16[2048,2048]{1,0:T(8,128)(2,1)}, bf16[2048,768]{1,0:T(8,128)(2,1)}, bf16[256,2048]{1,0:T(8,128)(2,1)}, bf16[2048,768]{1,0:T(8,128)(2,1)}, bf16[...) custom-call(f32[1,2048]{1,0:T(1,128)} %bitcast.5, ...), custom_call_target="tpu_custom_call" | custom-call | flops 6442450944 | bytes 16777216 | tf_op jit(solution)/shard_map/project/pallas_call | solution.py:645
  82.0 98.3 %attend.1 = (f32[256,2048]{1,0:T(8,128)}, bf16[256,2048]{1,0:T(8,128)(2,1)}, bf16[2048,256]{1,0:T(8,128)(2,1)}, f32[4,2048]{1,0:T(4,128)}, bf16[2048,2048]{1,0:T...) custom-call(f32[1,2048]{1,0:T(1,128)} %bitcast.9, ...), custom_call_target="tpu_custom_call" | custom-call | flops 4294967296 | bytes 16777216 | tf_op jit(solution)/shard_map/attend/pallas_call | solution.py:793
  180.3 145.9 %feed.1 = (f32[256,2048]{1,0:T(8,128)}, bf16[256,2048]{1,0:T(8,128)(2,1)}, f32[1,2048]{1,0:T(1,128)}, bf16[2048,1024]{1,0:T(8,128)(2,1)}, bf16[2048,2048]{1,0:T(8,128)(2,1)}, /*index=5*/bf16[2048,2048]{1,0:T(8,128)(2,1)}) custom-call(f32[1,2048]{1,0:T(1,128)} %bitcast.10, f32[256,2048]{1,0:T(8,128)} %get-tuple-element.56.refs_1_.hidden, ...), custom_call_target="tpu_custom_call" | custom-call | flops 68719476736 | bytes 41943040 | tf_op jit(solution)/shard_map/feed/pallas_call | solution.py:1492
  326.2 112.3 %back.1 = (f32[256,2048]{1,0:T(8,128)}, bf16[2048,2048]{1,0:T(8,128)(2,1)}, bf16[2048,768]{1,0:T(8,128)(2,1)}, bf16[1024,2048]{1,0:T(8,128)(2,1)}, f32[256,512]{1,0:T(8,128)}, /*index=5*/bf16[2,512,2048]{2,1,0:T(8,128)(2,1)}) custom-call(bf16[256,2048]{1,0:T(8,128)(2,1)} %get-tuple-element.62.refs_0_, bf16[2048,2048]{1,0:T(8,128)(2,1)} %get-tuple-element.63.refs_1_, ...), custom_call_target="tpu_custom_call" | custom-call | flops 1048576 | bytes 1048576 | tf_op jit(solution)/shard_map/back/pallas_call | solution.py:1025
  438.4 94.1 %spread.1 = (f32[256,2048]{1,0:T(8,128)}, f32[512,768]{1,0:T(8,128)}, f32[2,2048]{1,0:T(2,128)}, bf16[2,1024,512]{2,1,0:T(8,128)(2,1)}) custom-call(f32[1,2048]{1,0:T(1,128)} %bitcast.6, f32[1,2048]{1,0:T(1,128)} %get-tuple-element.73.refs_1_, bf16[2048,768]{1,0:T(8,128)(2,1)} %get-tuple-element.74.refs_2_, bf16[2048,768]{1,0:T(8,128)(2,1)} %get-tuple-element.75.refs_3_, ...), custom_call_target="tpu_custom_call" | custom-call | flops 1048576 | bytes 1048576 | tf_op jit(solution)/shard_map/spread/pallas_call | solution.py:1212
  532.5 0.0 copy-start
  532.5 12.6 %finish.1 = (f32[256,2048]{1,0:T(8,128)}, f32[256,2048]{1,0:T(8,128)}, f32[512,256]{1,0:T(8,128)}, f32[512,256]{1,0:T(8,128)}, f32[512,256]{1,0:T(8,128)}, /*ind...) custom-call(s32[1]{0:T(128)} %bitcast.shard_ref, ...), custom_call_target="tpu_custom_call" | custom-call | tf_op jit(solution)/shard_map/finish/pallas_call | solution.py:1563
  545.1 0.0 copy-done
  545.1 0.6 fusion
Async XLA Ops:
  532.5 12.6 %copy-start = (f32[2,2048]{1,0:T(2,128)S(1)}, f32[2,2048]{1,0:T(2,128)}, u32[]{:S(2)}) copy-start(f32[2,2048]{1,0:T(2,128)} %get-tuple-element.85) | copy-start | bytes 49156

commit v10 on v9

--- a/solution.py
+++ b/solution.py
@@ -275,9 +275,11 @@
     return scale * (scaled - unit * jnp.mean(scaled * unit, axis=-1, keepdims=True)), jnp.sum(grad * unit, axis=0, keepdims=True)
 
 
-def by_rows(rows, work):
+def by_rows(rows, work, stores=None):
     def step(index, carry):
         work(span(index, NORM_ROWS))
+        if stores:
+            stores.start(index)
         return carry
 
     lax.fori_loop(0, rows // NORM_ROWS, step, 0)
@@ -465,6 +467,28 @@
     def wait(self, *which):
         for i in which:
             self.copies[i].wait()
+
+
+class RowStores:
+    @staticmethod
+    def scratch(size, count, *results):
+        return [pltpu.VMEM(a.shape, a.dtype) for a in results] + [DMA((len(results), count))]
+
+    def __init__(self, size, count, refs, outs, sems):
+        self.size, self.count, self.refs, self.outs, self.sems = size, count, refs, outs, sems
+
+    def copies(self, index):
+        here = span(index, self.size)
+        return [pltpu.make_async_copy(a.at[here], b.at[here], self.sems.at[i, index]) for i, (a, b) in enumerate(zip(self.refs, self.outs))]
+
+    def start(self, index):
+        for copy in self.copies(index):
+            copy.start()
+
+    def wait(self):
+        for index in range(self.count):
+            for copy in self.copies(index):
+                copy.wait()
 
 
 def turned(block, sign):
@@ -696,7 +720,9 @@
     gain, *refs,
 ):
     sources, (w_gate, w_up, down_near) = refs[:5], refs[5:8]
-    hidden, tokens, mixed, totals, grads_out, gate_all, up_all, down_far = refs[8:16]
+    hidden_out, tokens_out, mixed_out, totals, grads_out, gate_all, up_all, down_far = refs[8:16]
+    hidden, tokens, rows_sem, mixed, mixed_sem = refs[-5:]
+    refs = refs[:-5]
     loads = Loads(sources, refs[16:22])
     cotangent, qkv, values_t, w_out, activations = loads.refs
     heads_ref, acc, out, top_ref, sum_ref, grads = refs[22:28]
@@ -711,6 +737,8 @@
     sems = refs[38:]
     rows, depth = hidden.shape
     pair = 2 * rows
+    states = RowStores(NORM_ROWS, rows // NORM_ROWS, (hidden, tokens), (hidden_out, tokens_out), rows_sem)
+    blends = RowStores(pair, chips, (mixed,), (mixed_out,), mixed_sem)
     scatter = Scatter(line, hidden, *sems[:8])
     loads.wait(0)
     grads[...] = cotangent[...].astype(low)
@@ -725,6 +753,7 @@
         chunk = line.target(index)
         attend_chunk(chunk, pair, qkv, values_t, heads_ref, acc, out, top_ref, sum_ref)
         mixed[span(chunk, pair), :] = out[...]
+        blends.start(chunk)
         totals[:, span(chunk, pair)] = top_ref[...] + jnp.log(sum_ref[...])
         scatter.free(index)
 
@@ -774,9 +803,11 @@
         hidden[here, :] = state
         tokens[here, :] = normed(state, gain[...]).astype(low)
 
-    by_rows(rows, norm)
+    by_rows(rows, norm, states)
     scatter.finish()
     gather.finish(True)
+    blends.wait()
+    states.wait()
     for near in (gate_near, up_near):
         near.finish()
     for far in (down, gate_far, up_far):
@@ -790,14 +821,12 @@
     width = w_out.shape[0]
     heads = width // HEAD_DIM
     shape = jax.ShapeDtypeStruct
+    stored = [shape((rows, depth), jnp.float32), shape((rows, depth), low), shape((group_rows, width), low)]
     return pl.pallas_call(
         lambda *refs: attend_kernel(chips, shards, *refs),
         in_specs=[VMEM] + [ANYWHERE] * 8,
-        out_specs=[VMEM] * 4 + [ANYWHERE] * 4,
-        out_shape=[
-            shape((rows, depth), jnp.float32),
-            shape((rows, depth), low),
-            shape((group_rows, width), low),
+        out_specs=[ANYWHERE] * 3 + [VMEM] + [ANYWHERE] * 4,
+        out_shape=stored + [
             shape((heads, group_rows), jnp.float32),
             shape((group_rows, depth), low),
             shape((depth, w_gate.shape[1]), low),
@@ -811,7 +840,8 @@
             pltpu.VMEM((heads, pair), jnp.float32),
             pltpu.VMEM((heads, pair), jnp.float32),
             pltpu.VMEM((rows, depth), low),
-        ] + FarShards.scratch(shards) + (NearShards.scratch(shards) + FarShards.scratch(shards)) * 2 + Scatter.scratch(chips, rows, depth) + Gather.scratch(chips),
+        ] + FarShards.scratch(shards) + (NearShards.scratch(shards) + FarShards.scratch(shards)) * 2 + Scatter.scratch(chips, rows, depth) + Gather.scratch(chips)
+        + RowStores.scratch(NORM_ROWS, rows // NORM_ROWS, *stored[:2]) + RowStores.scratch(pair, chips, stored[2]),
         compiler_params=pltpu.CompilerParams(collective_id=2, has_side_effects=True, vmem_limit_bytes=63 << 20),
         cost_estimate=pl.CostEstimate(flops=2 * group_rows * (SEQ_LEN + depth) * width, bytes_accessed=4 * group_rows * depth, transcendentals=group_rows * SEQ_LEN * heads // 2),
         name="attend",
@@ -858,7 +888,9 @@
     chips, shards,
     branch, terms, inner, grads, grad_both, *refs,
 ):
-    sources, (down, branch_out, qkv_grad, grad_down, grad_out, both_from) = refs[:7], refs[7:13]
+    sources, (down, branch_out, qkv_out, grad_down, grad_out, both_from) = refs[:7], refs[7:13]
+    qkv_grad, qkv_sem = refs[-2:]
+    refs = refs[:-2]
     loads = Loads(sources, refs[13:21])
     w_out, qkv, keys_t, mixed, totals, cosine, sine = loads.refs
     inner_chunk, grad_chunk, down_sum, down_tile, out_sum, out_stage, out_from, branch_chunk, dkey, dvalue = refs[21:31]
@@ -869,6 +901,7 @@
     rows, depth = down.shape
     pair = 2 * rows
     width = w_out.shape[0]
+    results = RowStores(pair, chips, (qkv_grad,), (qkv_out,), qkv_sem)
     scatter = HeldScatter(line, down, terms, *sems[:9])
     gather = Gather(line, branch, branch_out, *sems[9:])
 
@@ -920,6 +953,7 @@
             here = span(chunk, pair)
             qkv_grad[here, pl.ds(width, width)] = unrotated(dkey[here, :], chunk)
             qkv_grad[here, pl.ds(2 * width, width)] = dvalue[here, :].astype(low)
+            results.start(chunk)
             return carry
 
         lax.fori_loop(0, chips, part, 0)
@@ -1009,6 +1043,7 @@
         give(turn).wait_send()
     keep_tile(down_sum.shape[0] // 256 - 1).wait()
     both.finish()
+    results.wait()
     scatter.finish()
     gather.finish(False)
 
@@ -1025,7 +1060,7 @@
     return pl.pallas_call(
         lambda *refs: back_kernel(chips, shards, *refs),
         in_specs=[VMEM] + [ANYWHERE] * 11,
-        out_specs=[VMEM, ANYWHERE, VMEM, ANYWHERE, VMEM, ANYWHERE],
+        out_specs=[VMEM, ANYWHERE, ANYWHERE, ANYWHERE, VMEM, ANYWHERE],
         out_shape=[
             shape((rows, depth), jnp.float32),
             shape((group_rows, depth), low),
@@ -1050,7 +1085,8 @@
             pltpu.VMEM((width, pair), jnp.float32),
             pltpu.VMEM((8, pair), jnp.float32),
             DMA, DMA, DMA, DMA, DMA((shards - 1,)), DMA((shards - 1,)),
-        ] + NearSums.scratch(shards, depth // shards, grad_both.shape[1]) + HeldScatter.scratch(chips, rows, depth) + Gather.scratch(chips),
+        ] + NearSums.scratch(shards, depth // shards, grad_both.shape[1]) + HeldScatter.scratch(chips, rows, depth) + Gather.scratch(chips)
+        + RowStores.scratch(pair, chips, shape((group_rows, 3 * width), low)),
         compiler_params=pltpu.CompilerParams(collective_id=4, has_side_effects=True, vmem_limit_bytes=67043328),
         cost_estimate=pl.CostEstimate(flops=1 << 20, bytes_accessed=1 << 20, transcendentals=0),
         name="back",
@@ -1060,8 +1096,8 @@
 def spread_kernel(
     chips, shards,
     gain, gain_part, qkv_hbm, weight_hbm, activations_hbm, attn_tokens, grad_down,
-    input_part, grad_qkv, gain_sum, down_from,
-    qkv_grad, weight, activations, held_sem,
+    input_out, qkv_out, gain_sum, down_from,
+    input_part, rows_sem, grad_qkv, sum_sem, qkv_grad, weight, activations, held_sem,
     attn_cols, qkv_stage, qkv_from, gains, gains_tp, gains_fsdp,
     attn_sem, qkv_send, qkv_recv, tp_send, tp_recv, fsdp_send, fsdp_recv, *sems,
 ):
@@ -1167,7 +1203,8 @@
         gains[0:1, :] += grad
 
     loads.wait(2)
-    by_rows(rows, norm)
+    results = RowStores(NORM_ROWS, rows // NORM_ROWS, (input_part,), (input_out,), rows_sem)
+    by_rows(rows, norm, results)
 
     gains_tp[line.me] = gains[...]
     for ahead in range(1, size):
@@ -1175,6 +1212,8 @@
     for turn in range(shards - 1):
         give(turn).wait_recv()
         grad_qkv[...] += qkv_from[turn].astype(jnp.float32)
+    summed = RowStores(columns, 1, (grad_qkv,), (qkv_out,), sum_sem)
+    summed.start(0)
     for ahead in range(1, size):
         source = (line.me + ahead) % size
         remote(gains, gains_tp.at[source], tp_send.at[0], tp_recv.at[source], {"tp": source}).wait_recv()
@@ -1199,6 +1238,8 @@
     for turn in range(shards - 1):
         give(turn).wait_send()
     down.finish()
+    results.wait()
+    summed.wait()
     scatter.finish()
 
 
@@ -1209,17 +1250,16 @@
     columns = depth // shards
     size = 2 * chips
     shape = jax.ShapeDtypeStruct
+    stored = [shape((rows, depth), jnp.float32), shape((columns, 3 * width), jnp.float32)]
     return pl.pallas_call(
         lambda *refs: spread_kernel(chips, shards, *refs),
         in_specs=[VMEM] * 2 + [ANYWHERE] * 5,
-        out_specs=[VMEM] * 3 + [ANYWHERE],
-        out_shape=[
-            shape((rows, depth), jnp.float32),
-            shape((columns, 3 * width), jnp.float32),
+        out_specs=[ANYWHERE] * 2 + [VMEM, ANYWHERE],
+        out_shape=stored + [
             shape((2, depth), jnp.float32),
             shape((shards // 2, grad_down.shape[0], columns), low),
         ],
-        scratch_shapes=Loads.scratch(qkv_grad, weight, activations) + [
+        scratch_shapes=RowStores.scratch(NORM_ROWS, rows // NORM_ROWS, stored[0]) + RowStores.scratch(columns, 1, stored[1]) + Loads.scratch(qkv_grad, weight, activations) + [
             pltpu.VMEM((2, group_rows, columns), low),
             pltpu.VMEM((shards - 1, columns, 3 * width), low),
             pltpu.VMEM((shards - 1, columns, 3 * width), low),
@@ -1246,8 +1286,8 @@
 def feed_kernel(
     chips, shards,
     gain, hidden_hbm, cotangent_hbm, tokens, grads_hbm, w_gate, w_up, w_down, gate_all, up_all, down_near, down_far,
-    hidden_grad, branch, gain_part, inner_out, grad_both, down_out,
-    hidden_state, cotangent, state_sem, down_tile, down_sem, tokens_all, gate_w, up_w, down_w, grads, inner, gate_grad, up_grad, term, from_core, from_ring, total, tile_gate, tile_up,
+    hidden_grad_out, branch_out, gain_part, inner_out, grad_both, down_out,
+    hidden_grad, branch, rows_sem, hidden_state, cotangent, state_sem, down_tile, down_sem, tokens_all, gate_w, up_w, down_w, grads, inner, gate_grad, up_grad, term, from_core, from_ring, total, tile_gate, tile_up,
     load_sem, own_sem, grad_sem, store_sem, tile_sem,
     ring_send, ring_recv, core_send, core_recv, share_send, share_recv, total_send, total_recv,
 ):
@@ -1262,34 +1302,42 @@
     partner = {"tp": 2 * chip + 1 - core}
 
     grid = Grid(shards)
-    rows_of, columns_of = row_shard(w_gate.shape[0]), column_shard(*w_down.shape)
-
-    def load(array, source, shard, whole):
-        at = columns_of if array == 2 else rows_of
-        target = at((gate_w, up_w, down_w)[array], shard, None)
-        return pltpu.make_async_copy(at(source, shard, None) if whole else source, target, load_sem.at[array, shard])
-
-    def load_weights():
+    part = w_gate.shape[0]
+
+    def load(array, source, shard, tile, whole):
+        cut = span(tile, 256)
+        if array == 2:
+            place = lambda ref: ref.at[cut, span(shard, part)]
+            own = lambda ref: ref.at[cut]
+        else:
+            place = lambda ref: ref.at[span(shard, part), cut]
+            own = lambda ref: ref.at[:, cut]
+        target = place((gate_w, up_w, down_w)[array])
+        return pltpu.make_async_copy(place(source) if whole else own(source), target, load_sem.at[array, shard, tile])
+
+    def load_weights(tile, carry):
         for shard in range(shards):
             own, near = grid.me == shard, grid.is_near(shard)
 
             @pl.when(own)
             def _():
                 for array, source in enumerate((w_gate, w_up, w_down)):
-                    load(array, source, shard, False).start()
+                    load(array, source, shard, tile, False).start()
 
             @pl.when(jnp.logical_not(own))
             def _():
                 for array, source in enumerate((gate_all, up_all)):
-                    load(array, source, shard, True).start()
+                    load(array, source, shard, tile, True).start()
 
             @pl.when(jnp.logical_and(near, jnp.logical_not(own)))
             def _():
-                load(2, down_near, shard, True).start()
+                load(2, down_near, shard, tile, True).start()
 
             @pl.when(jnp.logical_not(near))
             def _():
-                load(2, down_far, shard, True).start()
+                load(2, down_far, shard, tile, True).start()
+
+        return carry
 
     own = pltpu.make_async_copy(tokens, tokens_all.at[span(me, rows)], own_sem)
     states = Loads((hidden_hbm, cotangent_hbm), (hidden_state, cotangent, state_sem))
@@ -1342,7 +1390,7 @@
         hello(device)
     own.start()
     fetch(0).start()
-    load_weights()
+    lax.fori_loop(0, width // 256, load_weights, 0)
     own.wait()
     pl.semaphore_wait(pltpu.get_barrier_semaphore(), 3)
 
@@ -1362,12 +1410,6 @@
 
         to_core(slot).start()
 
-        @pl.when(slot == 0)
-        def _():
-            for shard in range(shards):
-                for array, source in enumerate((gate_all, up_all, down_near)):
-                    load(array, source, shard, True).wait()
-
         @pl.when(slot == 1)
         def _():
             states.start()
@@ -1377,6 +1419,13 @@
 
         def narrow(tile, carry):
             columns = span(tile, 256)
+
+            @pl.when(slot == 0)
+            def _():
+                for shard in range(shards):
+                    for array, source in enumerate((gate_all, up_all, down_near)):
+                        load(array, source, shard, tile, True).wait()
+
             token = tokens_all[wide_rows, :]
             gate = dot(token, gate_w[:, columns])
             up = dot(token, up_w[:, columns])
@@ -1388,7 +1437,7 @@
             gate_grad[wide_rows, columns] = (grad * up * squash * (1.0 + gate * (1.0 - squash))).astype(low)
             return carry
 
-        lax.fori_loop(0, width // 256, narrow, 0)
+        lax.fori_loop(0, width // 256, narrow, 0, unroll=2)
         store(slot).start()
 
         @pl.when(slot > 0)
@@ -1469,7 +1518,8 @@
         branch[here, :] = full.astype(low)
         gain_part[...] += gain_grad
 
-    by_rows(rows, norm)
+    results = RowStores(NORM_ROWS, rows // NORM_ROWS, (hidden_grad, branch), (hidden_grad_out, branch_out), rows_sem)
+    by_rows(rows, norm, results)
     share(chips - 1).wait_send()
     for slot in range(chips):
         to_core(slot).wait_send()
@@ -1481,6 +1531,7 @@
     for index in range(depth // 256 - 2, depth // 256):
         for copy in tiles(index):
             copy.wait()
+    results.wait()
 
 
 def feed(chips, shards, hidden_state, cotangent, gain, tokens, grads, w_gate, w_up, w_down, gate_all, up_all, down_near, down_far):
@@ -1489,19 +1540,18 @@
     group_rows = chips * pair
     width = w_down.shape[0]
     shape = jax.ShapeDtypeStruct
+    stored = [shape((rows, depth), jnp.float32), shape((rows, depth), low)]
     return pl.pallas_call(
         lambda *refs: feed_kernel(chips, shards, *refs),
         in_specs=[VMEM] + [ANYWHERE] * 11,
-        out_specs=[VMEM] * 3 + [ANYWHERE] * 3,
-        out_shape=[
-            shape((rows, depth), jnp.float32),
-            shape((rows, depth), low),
+        out_specs=[ANYWHERE] * 2 + [VMEM] + [ANYWHERE] * 3,
+        out_shape=stored + [
             shape((1, depth), jnp.float32),
             shape((group_rows, width), low),
             shape((depth, 2 * width), low),
             shape((group_rows, depth), low),
         ],
-        scratch_shapes=Loads.scratch(hidden_state, cotangent) + [
+        scratch_shapes=RowStores.scratch(NORM_ROWS, rows // NORM_ROWS, *stored) + Loads.scratch(hidden_state, cotangent) + [
             pltpu.VMEM((2, pair, 256), low),
             DMA((2,)),
             pltpu.VMEM((group_rows, depth), low),
@@ -1518,7 +1568,7 @@
             pltpu.VMEM((2, rows, depth), low),
             pltpu.VMEM((2, 256, width), low),
             pltpu.VMEM((2, 256, width), low),
-            DMA((3, shards)), DMA, DMA((2,)), DMA((chips,)), DMA((2, 2)),
+            DMA((3, shards, width // 256)), DMA, DMA((2,)), DMA((chips,)), DMA((2, 2)),
             DMA((chips,)), DMA((chips,)), DMA((chips,)), DMA((chips,)),
             DMA, DMA((3,)), DMA((2,)), DMA((chips - 1,)),
         ],
@@ -1529,9 +1579,11 @@
 
 
 def finish_kernel(
-    shard_ref, hidden, down, hidden_grad, input_part, both, both_from, grad_down, down_from, grad_qkv, grad_out,
-    output, input_grad, query, key, value, out, gate, up, down_out,
+    shard_ref, hidden, down, hidden_grad, input_part, both, both_from, grad_down, down_from, grad_qkv, grad_out, gains,
+    output, input_grad, query, key, value, out, gate, up, down_out, gain_attn, gain_mlp,
 ):
+    gain_attn[...] = gains[0:1, :]
+    gain_mlp[...] = gains[1:2, :]
     output[...] = hidden[...] + down[...]
     input_grad[...] = hidden_grad[...] + input_part[...]
     width = query.shape[1]
@@ -1551,7 +1603,7 @@
     down_out[...] = total
 
 
-def finish(shard, hidden, down, hidden_grad, input_part, both, both_from, grad_down, down_from, grad_qkv, grad_out):
+def finish(shard, hidden, down, hidden_grad, input_part, both, both_from, grad_down, down_from, grad_qkv, grad_out, gains):
     steps = 8
     shape = jax.ShapeDtypeStruct
     columns = down_from.shape[2]
@@ -1571,12 +1623,13 @@
                 spec3(both_from),
                 pl.BlockSpec((grad_down.shape[0] // steps, columns), lambda i, s: (i, s[0])),
                 spec3(down_from), spec(grad_qkv), spec(grad_out),
+                pl.BlockSpec(gains.shape, lambda i, s: (0, 0)),
             ],
-            out_specs=[spec(a) for a in results],
+            out_specs=[spec(a) for a in results] + [pl.BlockSpec((1, gains.shape[1]), lambda i, s: (0, 0))] * 2,
         ),
-        out_shape=results,
+        out_shape=results + [shape((1, gains.shape[1]), jnp.float32)] * 2,
         name="finish",
-    )(shard.reshape(1), hidden, down, hidden_grad, input_part, both, both_from, grad_down, down_from, grad_qkv, grad_out)
+    )(shard.reshape(1), hidden, down, hidden_grad, input_part, both, both_from, grad_down, down_from, grad_qkv, grad_out, gains)
 
 
 def rope_frequencies():
@@ -1605,12 +1658,12 @@
         input_part, grad_qkv, gain_sums, down_from = spread(
             chips, shards, qkv_grad, w_qkv, activations, gain_attn, gain_part, seen_attn, grad_down
         )
-        output, input_grad, grad_query, grad_key, grad_value, grad_out, grad_gate, grad_up, grad_down = finish(
+        output, input_grad, grad_query, grad_key, grad_value, grad_out, grad_gate, grad_up, grad_down, gain_attn, gain_mlp = finish(
             lax.axis_index("fsdp"), hidden_state, down, hidden_grad, input_part,
-            grad_both, both_from, grad_down, down_from, grad_qkv, grad_out,
+            grad_both, both_from, grad_down, down_from, grad_qkv, grad_out, gain_sums,
         )
         return (
-            output, input_grad, gain_sums[0], grad_query, grad_key, grad_value, grad_out, gain_sums[1],
+            output, input_grad, gain_attn[0], grad_query, grad_key, grad_value, grad_out, gain_mlp[0],
             grad_gate, grad_up, grad_down,
         )
 

time: 546 us -> 543 us (level)
  no operation moved by 1% of the time
where the time goes in v10:
time: 543 us; the launch traced here: 542 us
  Pallas kernels  541 us (100%)
    pallas_call x1, Pallas kernels, feed(): pl.pallas_call(lambda *refs: feed_kernel(chips, shards, *refs), in_specs=...  146 us
    pallas_call x1, Pallas kernels, back(): pl.pallas_call(lambda *refs: back_kernel(chips, shards, *refs), in_specs=...  110 us
    pallas_call x1, Pallas kernels, attend(): pl.pallas_call(lambda *refs: attend_kernel(chips, shards, *refs), in_spec...  97.9 us
    pallas_call x1, Pallas kernels, spread(): pl.pallas_call(lambda *refs: spread_kernel(chips, shards, *refs), in_spec...  92.8 us
    pallas_call x1, Pallas kernels, project(): pl.pallas_call(lambda *refs: project_kernel(chips, shards, *refs), in_spe...  81.3 us
    pallas_call x1, Pallas kernels, finish(): pl.pallas_call(finish_kernel, grid_spec=pltpu.PrefetchScalarGridSpec(num_...  12.6 us

profile of v10, /device:TPU:0, one launch (start us, length us, event | category | flops | bytes accessed | tf_op | source)
XLA Modules:
  0.0 541.9 jit_solution(14014933676521271249)
XLA Ops:
  0.6 81.3 %project.1 = (bf16[2048,2048]{1,0:T(8,128)(2,1)}, bf16[2048,768]{1,0:T(8,128)(2,1)}, bf16[256,2048]{1,0:T(8,128)(2,1)}, bf16[2048,768]{1,0:T(8,128)(2,1)}, bf16[...) custom-call(f32[1,2048]{1,0:T(1,128)} %bitcast.5, ...), custom_call_target="tpu_custom_call" | custom-call | flops 6442450944 | bytes 16777216 | tf_op jit(solution)/shard_map/project/pallas_call | solution.py:669
  82.0 97.9 %attend.1 = (f32[256,2048]{1,0:T(8,128)}, bf16[256,2048]{1,0:T(8,128)(2,1)}, bf16[2048,256]{1,0:T(8,128)(2,1)}, f32[4,2048]{1,0:T(4,128)}, bf16[2048,2048]{1,0:T...) custom-call(f32[1,2048]{1,0:T(1,128)} %bitcast.7, ...), custom_call_target="tpu_custom_call" | custom-call | flops 4294967296 | bytes 16777216 | tf_op jit(solution)/shard_map/attend/pallas_call | solution.py:825
  179.9 146.0 %feed.1 = (f32[256,2048]{1,0:T(8,128)}, bf16[256,2048]{1,0:T(8,128)(2,1)}, f32[1,2048]{1,0:T(1,128)}, bf16[2048,1024]{1,0:T(8,128)(2,1)}, bf16[2048,2048]{1,0:T(8,128)(2,1)}, /*index=5*/bf16[2048,2048]{1,0:T(8,128)(2,1)}) custom-call(f32[1,2048]{1,0:T(1,128)} %bitcast.8, f32[256,2048]{1,0:T(8,128)} %get-tuple-element.58.refs_1_.hidden, f32[256,2048]{1,0:T(8,128)} %refs_2_.3, ...), custom_call_target="tpu_custom_call" | custom-call | flops 68719476736 | bytes 41943040 | tf_op jit(solution)/shard_map/feed/pallas_call | solution.py:1544
  325.9 110.4 %back.1 = (f32[256,2048]{1,0:T(8,128)}, bf16[2048,2048]{1,0:T(8,128)(2,1)}, bf16[2048,768]{1,0:T(8,128)(2,1)}, bf16[1024,2048]{1,0:T(8,128)(2,1)}, f32[256,512]{1,0:T(8,128)}, /*index=5*/bf16[2,512,2048]{2,1,0:T(8,128)(2,1)}) custom-call(bf16[256,2048]{1,0:T(8,128)(2,1)} %get-tuple-element.64.refs_0_, bf16[2048,2048]{1,0:T(8,128)(2,1)} %get-tuple-element.65.refs_1_, ...), custom_call_target="tpu_custom_call" | custom-call | flops 1048576 | bytes 1048576 | tf_op jit(solution)/shard_map/back/pallas_call | solution.py:1060
  436.3 92.8 %spread.1 = (f32[256,2048]{1,0:T(8,128)}, f32[512,768]{1,0:T(8,128)}, f32[2,2048]{1,0:T(2,128)}, bf16[2,1024,512]{2,1,0:T(8,128)(2,1)}) custom-call(f32[1,2048]{1,0:T(1,128)} %bitcast.6, f32[1,2048]{1,0:T(1,128)} %get-tuple-element.75.refs_1_, bf16[2048,768]{1,0:T(8,128)(2,1)} %get-tuple-element.76.refs_2_, bf16[2048,768]{1,0:T(8,128)(2,1)} %get-tuple-element.77.refs_3_, ...), custom_call_target="tpu_custom_call" | custom-call | flops 1048576 | bytes 1048576 | tf_op jit(solution)/shard_map/spread/pallas_call | solution.py:1254
  529.2 12.6 %finish.1 = (f32[256,2048]{1,0:T(8,128)}, f32[256,2048]{1,0:T(8,128)}, f32[512,256]{1,0:T(8,128)}, f32[512,256]{1,0:T(8,128)}, f32[512,256]{1,0:T(8,128)}, /*ind...) custom-call(s32[1]{0:T(128)} %bitcast.shard_ref, ...), custom_call_target="tpu_custom_call" | custom-call | tf_op jit(solution)/shard_map/finish/pallas_call | solution.py:1615

commit v11 on v10

--- a/solution.py
+++ b/solution.py
@@ -903,7 +903,7 @@
     width = w_out.shape[0]
     results = RowStores(pair, chips, (qkv_grad,), (qkv_out,), qkv_sem)
     scatter = HeldScatter(line, down, terms, *sems[:9])
-    gather = Gather(line, branch, branch_out, *sems[9:])
+    gather = Gather(line, branch, branch_out, *sems[9:], parts=2)
 
     def fetch(step):
         return pltpu.make_async_copy(inner.at[span(line.target(step), pair)], inner_chunk, inner_sem)
@@ -1085,7 +1085,7 @@
             pltpu.VMEM((width, pair), jnp.float32),
             pltpu.VMEM((8, pair), jnp.float32),
             DMA, DMA, DMA, DMA, DMA((shards - 1,)), DMA((shards - 1,)),
-        ] + NearSums.scratch(shards, depth // shards, grad_both.shape[1]) + HeldScatter.scratch(chips, rows, depth) + Gather.scratch(chips)
+        ] + NearSums.scratch(shards, depth // shards, grad_both.shape[1]) + HeldScatter.scratch(chips, rows, depth) + Gather.scratch(chips, 2)
         + RowStores.scratch(pair, chips, shape((group_rows, 3 * width), low)),
         compiler_params=pltpu.CompilerParams(collective_id=4, has_side_effects=True, vmem_limit_bytes=67043328),
         cost_estimate=pl.CostEstimate(flops=1 << 20, bytes_accessed=1 << 20, transcendentals=0),
@@ -1604,7 +1604,7 @@
 
 
 def finish(shard, hidden, down, hidden_grad, input_part, both, both_from, grad_down, down_from, grad_qkv, grad_out, gains):
-    steps = 8
+    steps = 4
     shape = jax.ShapeDtypeStruct
     columns = down_from.shape[2]
     results = [shape(hidden.shape, jnp.float32)] * 2

time: 543 us -> 541 us (level)
  no operation moved by 1% of the time
where the time goes in v11:
time: 541 us; the launch traced here: 540 us
  Pallas kernels  539 us (100%)
    pallas_call x1, Pallas kernels, feed(): pl.pallas_call(lambda *refs: feed_kernel(chips, shards, *refs), in_specs=...  146 us
    pallas_call x1, Pallas kernels, back(): pl.pallas_call(lambda *refs: back_kernel(chips, shards, *refs), in_specs=...  109 us
    pallas_call x1, Pallas kernels, attend(): pl.pallas_call(lambda *refs: attend_kernel(chips, shards, *refs), in_spec...  97.9 us
    pallas_call x1, Pallas kernels, spread(): pl.pallas_call(lambda *refs: spread_kernel(chips, shards, *refs), in_spec...  94 us
    pallas_call x1, Pallas kernels, project(): pl.pallas_call(lambda *refs: project_kernel(chips, shards, *refs), in_spe...  81.3 us
    pallas_call x1, Pallas kernels, finish(): pl.pallas_call(finish_kernel, grid_spec=pltpu.PrefetchScalarGridSpec(num_...  11.2 us

profile of v11, /device:TPU:0, one launch (start us, length us, event | category | flops | bytes accessed | tf_op | source)
XLA Modules:
  0.0 540.0 jit_solution(2556981686525611933)
XLA Ops:
  0.6 81.3 %project.1 = (bf16[2048,2048]{1,0:T(8,128)(2,1)}, bf16[2048,768]{1,0:T(8,128)(2,1)}, bf16[256,2048]{1,0:T(8,128)(2,1)}, bf16[2048,768]{1,0:T(8,128)(2,1)}, bf16[...) custom-call(f32[1,2048]{1,0:T(1,128)} %bitcast.5, ...), custom_call_target="tpu_custom_call" | custom-call | flops 6442450944 | bytes 16777216 | tf_op jit(solution)/shard_map/project/pallas_call | solution.py:669
  82.0 97.9 %attend.1 = (f32[256,2048]{1,0:T(8,128)}, bf16[256,2048]{1,0:T(8,128)(2,1)}, bf16[2048,256]{1,0:T(8,128)(2,1)}, f32[4,2048]{1,0:T(4,128)}, bf16[2048,2048]{1,0:T...) custom-call(f32[1,2048]{1,0:T(1,128)} %bitcast.7, ...), custom_call_target="tpu_custom_call" | custom-call | flops 4294967296 | bytes 16777216 | tf_op jit(solution)/shard_map/attend/pallas_call | solution.py:825
  179.9 146.0 %feed.1 = (f32[256,2048]{1,0:T(8,128)}, bf16[256,2048]{1,0:T(8,128)(2,1)}, f32[1,2048]{1,0:T(1,128)}, bf16[2048,1024]{1,0:T(8,128)(2,1)}, bf16[2048,2048]{1,0:T(8,128)(2,1)}, /*index=5*/bf16[2048,2048]{1,0:T(8,128)(2,1)}) custom-call(f32[1,2048]{1,0:T(1,128)} %bitcast.8, f32[256,2048]{1,0:T(8,128)} %get-tuple-element.58.refs_1_.hidden, f32[256,2048]{1,0:T(8,128)} %refs_2_.3, ...), custom_call_target="tpu_custom_call" | custom-call | flops 68719476736 | bytes 41943040 | tf_op jit(solution)/shard_map/feed/pallas_call | solution.py:1544
  325.9 108.6 %back.1 = (f32[256,2048]{1,0:T(8,128)}, bf16[2048,2048]{1,0:T(8,128)(2,1)}, bf16[2048,768]{1,0:T(8,128)(2,1)}, bf16[1024,2048]{1,0:T(8,128)(2,1)}, f32[256,512]{1,0:T(8,128)}, /*index=5*/bf16[2,512,2048]{2,1,0:T(8,128)(2,1)}) custom-call(bf16[256,2048]{1,0:T(8,128)(2,1)} %get-tuple-element.64.refs_0_, bf16[2048,2048]{1,0:T(8,128)(2,1)} %get-tuple-element.65.refs_1_, ...), custom_call_target="tpu_custom_call" | custom-call | flops 1048576 | bytes 1048576 | tf_op jit(solution)/shard_map/back/pallas_call | solution.py:1060
  434.5 94.0 %spread.1 = (f32[256,2048]{1,0:T(8,128)}, f32[512,768]{1,0:T(8,128)}, f32[2,2048]{1,0:T(2,128)}, bf16[2,1024,512]{2,1,0:T(8,128)(2,1)}) custom-call(f32[1,2048]{1,0:T(1,128)} %bitcast.6, f32[1,2048]{1,0:T(1,128)} %get-tuple-element.75.refs_1_, bf16[2048,768]{1,0:T(8,128)(2,1)} %get-tuple-element.76.refs_2_, bf16[2048,768]{1,0:T(8,128)(2,1)} %get-tuple-element.77.refs_3_, ...), custom_call_target="tpu_custom_call" | custom-call | flops 1048576 | bytes 1048576 | tf_op jit(solution)/shard_map/spread/pallas_call | solution.py:1254
  528.6 11.2 %finish.1 = (f32[256,2048]{1,0:T(8,128)}, f32[256,2048]{1,0:T(8,128)}, f32[512,256]{1,0:T(8,128)}, f32[512,256]{1,0:T(8,128)}, f32[512,256]{1,0:T(8,128)}, /*ind...) custom-call(s32[1]{0:T(128)} %bitcast.shard_ref, ...), custom_call_target="tpu_custom_call" | custom-call | tf_op jit(solution)/shard_map/finish/pallas_call | solution.py:1615

commit v12 on v11

--- a/solution.py
+++ b/solution.py
@@ -1136,6 +1136,7 @@
     loads.wait(0, 1)
     pl.semaphore_wait(pltpu.get_barrier_semaphore(), size - 1 + shards - 1)
     down.start()
+    down.start_plain()
 
     def weights(turn, carry):
         @pl.when(turn < shards - 1)
@@ -1177,10 +1178,6 @@
             @pl.when(jnp.logical_and(which == 2, index < 2))
             def _():
                 lax.fori_loop(index, jnp.where(index == 0, 1, shards), weights, 0)
-
-            @pl.when(jnp.logical_and(which == 2, index == 1))
-            def _():
-                down.start_plain()
 
             @pl.when(jnp.logical_and(which == 2, index == 2))
             def _():

time: 541 us -> 541 us (level)
  no operation moved by 1% of the time
where the time goes in v12:
time: 541 us; the launch traced here: 540 us
  Pallas kernels  539 us (100%)
    pallas_call x1, Pallas kernels, feed(): pl.pallas_call(lambda *refs: feed_kernel(chips, shards, *refs), in_specs=...  146 us
    pallas_call x1, Pallas kernels, back(): pl.pallas_call(lambda *refs: back_kernel(chips, shards, *refs), in_specs=...  109 us
    pallas_call x1, Pallas kernels, attend(): pl.pallas_call(lambda *refs: attend_kernel(chips, shards, *refs), in_spec...  97.9 us
    pallas_call x1, Pallas kernels, spread(): pl.pallas_call(lambda *refs: spread_kernel(chips, shards, *refs), in_spec...  94 us
    pallas_call x1, Pallas kernels, project(): pl.pallas_call(lambda *refs: project_kernel(chips, shards, *refs), in_spe...  81.3 us
    pallas_call x1, Pallas kernels, finish(): pl.pallas_call(finish_kernel, grid_spec=pltpu.PrefetchScalarGridSpec(num_...  11.2 us

profile of v12, /device:TPU:0, one launch (start us, length us, event | category | flops | bytes accessed | tf_op | source)
XLA Modules:
  0.0 540.0 jit_solution(2783783401631207273)
XLA Ops:
  0.6 81.3 %project.1 = (bf16[2048,2048]{1,0:T(8,128)(2,1)}, bf16[2048,768]{1,0:T(8,128)(2,1)}, bf16[256,2048]{1,0:T(8,128)(2,1)}, bf16[2048,768]{1,0:T(8,128)(2,1)}, bf16[...) custom-call(f32[1,2048]{1,0:T(1,128)} %bitcast.5, ...), custom_call_target="tpu_custom_call" | custom-call | flops 6442450944 | bytes 16777216 | tf_op jit(solution)/shard_map/project/pallas_call | solution.py:669
  82.0 97.9 %attend.1 = (f32[256,2048]{1,0:T(8,128)}, bf16[256,2048]{1,0:T(8,128)(2,1)}, bf16[2048,256]{1,0:T(8,128)(2,1)}, f32[4,2048]{1,0:T(4,128)}, bf16[2048,2048]{1,0:T...) custom-call(f32[1,2048]{1,0:T(1,128)} %bitcast.7, ...), custom_call_target="tpu_custom_call" | custom-call | flops 4294967296 | bytes 16777216 | tf_op jit(solution)/shard_map/attend/pallas_call | solution.py:825
  179.9 146.0 %feed.1 = (f32[256,2048]{1,0:T(8,128)}, bf16[256,2048]{1,0:T(8,128)(2,1)}, f32[1,2048]{1,0:T(1,128)}, bf16[2048,1024]{1,0:T(8,128)(2,1)}, bf16[2048,2048]{1,0:T(8,128)(2,1)}, /*index=5*/bf16[2048,2048]{1,0:T(8,128)(2,1)}) custom-call(f32[1,2048]{1,0:T(1,128)} %bitcast.8, f32[256,2048]{1,0:T(8,128)} %get-tuple-element.58.refs_1_.hidden, f32[256,2048]{1,0:T(8,128)} %refs_2_.3, ...), custom_call_target="tpu_custom_call" | custom-call | flops 68719476736 | bytes 41943040 | tf_op jit(solution)/shard_map/feed/pallas_call | solution.py:1541
  325.9 108.6 %back.1 = (f32[256,2048]{1,0:T(8,128)}, bf16[2048,2048]{1,0:T(8,128)(2,1)}, bf16[2048,768]{1,0:T(8,128)(2,1)}, bf16[1024,2048]{1,0:T(8,128)(2,1)}, f32[256,512]{1,0:T(8,128)}, /*index=5*/bf16[2,512,2048]{2,1,0:T(8,128)(2,1)}) custom-call(bf16[256,2048]{1,0:T(8,128)(2,1)} %get-tuple-element.64.refs_0_, bf16[2048,2048]{1,0:T(8,128)(2,1)} %get-tuple-element.65.refs_1_, ...), custom_call_target="tpu_custom_call" | custom-call | flops 1048576 | bytes 1048576 | tf_op jit(solution)/shard_map/back/pallas_call | solution.py:1060
  434.5 94.0 %spread.1 = (f32[256,2048]{1,0:T(8,128)}, f32[512,768]{1,0:T(8,128)}, f32[2,2048]{1,0:T(2,128)}, bf16[2,1024,512]{2,1,0:T(8,128)(2,1)}) custom-call(f32[1,2048]{1,0:T(1,128)} %bitcast.6, f32[1,2048]{1,0:T(1,128)} %get-tuple-element.75.refs_1_, bf16[2048,768]{1,0:T(8,128)(2,1)} %get-tuple-element.76.refs_2_, bf16[2048,768]{1,0:T(8,128)(2,1)} %get-tuple-element.77.refs_3_, ...), custom_call_target="tpu_custom_call" | custom-call | flops 1048576 | bytes 1048576 | tf_op jit(solution)/shard_map/spread/pallas_call | solution.py:1251
  528.6 11.2 %finish.1 = (f32[256,2048]{1,0:T(8,128)}, f32[256,2048]{1,0:T(8,128)}, f32[512,256]{1,0:T(8,128)}, f32[512,256]{1,0:T(8,128)}, f32[512,256]{1,0:T(8,128)}, /*ind...) custom-call(s32[1]{0:T(128)} %bitcast.shard_ref, ...), custom_call_target="tpu_custom_call" | custom-call | tf_op jit(solution)/shard_map/finish/pallas_call | solution.py:1612
